TPU v7x, 128 devices: a whole 4x4x4 slice. The times are simulated.
128 devices in a mesh: cfg: 2 (over z_lo), seq: 8 (over x, core), blk: 8 (over z_hi, y).
Axes of the slice: x: 4, y: 4, z: 4 (z_hi: 2, z_lo: 2; z = z_hi * 2 + z_lo), core: 2. Of those that a mesh axis runs over, the one named last changes fastest.
Arguments:
- hidden: bfloat16 [2, 3072, 5120], P('cfg', 'seq', 'blk'), may hold values from -2.5 to 2.5
- modulation: float32 [3, 5120], replicated, may hold values from -4 to 4
- in_projection: bfloat16 [5120, 3, 3072], P(('cfg', 'seq'), None, 'blk'), may hold values from -0.078125 to 0.078125
- out_projection: bfloat16 [3072, 5120], P('blk', ('cfg', 'seq')), may hold values from -0.15625 to 0.15625
- lengths: int32 [5], replicated, may hold values from 1 to 1536, 3072 in all
- positions: int32 [3, 3072], P(None, 'seq'), may hold values from 0 to 63
- guidance: float32 [1], replicated, may hold values from 2 to 5
Outputs:
- guided: float32 [8, 2, 192, 5120], P('seq', 'cfg', None, 'blk')
Inputs may be any that keep to these rules, and one draw needn't show every extreme that they name: The clip lengths sum to 3072 and the longest is exactly 1536.
All inputs are finite; a program needn't handle non-finite values.
Results may differ from a plain program's by a relative error of at most 0.012.
The roundings to bfloat16 on the way count: a program that leaves them out, or rounds other values in their place, can miss the bound.
Values may be sent and summed in bfloat16 or wider, within the bound.
A program may use at most 128 MiB of HBM per device.

v0:
```python
import jax
import jax.numpy as jnp
import numpy as np
from jax import lax
from jax.sharding import PartitionSpec as P

HEAD_DIM = 128


def from_partner(array, axis, distance):
    return lax.ppermute(array, axis, [(i, i ^ 1 << distance) for i in range(lax.axis_size(axis))])


def rotary_angles(head_width):
    third = head_width // 6
    first_dim = head_width - 4 * third
    other_dim = 2 * third
    pair_index = np.arange(head_width) // 2
    first_pairs = first_dim // 2
    other_pairs = other_dim // 2
    in_first = pair_index < first_pairs
    in_second = (pair_index >= first_pairs) & (pair_index < first_pairs + other_pairs)
    in_third = pair_index >= first_pairs + other_pairs
    row_first = np.where(in_first, 10000.0 ** (-2.0 * pair_index / first_dim), 0.0)
    row_second = np.where(
        in_second, 10000.0 ** (-2.0 * (pair_index - first_pairs) / other_dim), 0.0
    )
    row_third = np.where(
        in_third, 10000.0 ** (-2.0 * (pair_index - first_pairs - other_pairs) / other_dim), 0.0
    )
    return np.stack([row_first, row_second, row_third]).astype(np.float32)


def turn_matrix(head_width):
    row_index = np.arange(head_width)[:, None]
    col_index = np.arange(head_width)[None, :]
    upper = np.where((col_index == row_index + 1) & (row_index % 2 == 0), 1.0, 0.0)
    lower = np.where((col_index == row_index - 1) & (row_index % 2 == 1), -1.0, 0.0)
    return (upper + lower).astype(np.float32)


def layer_norm(inputs):
    row_mean = jnp.mean(inputs, -1, keepdims=True)
    centered = inputs - row_mean
    variance = jnp.mean(centered * centered, -1, keepdims=True)
    return centered * lax.rsqrt(variance + 1e-06)


def rms_norm(inputs):
    return inputs * lax.rsqrt(jnp.mean(inputs * inputs, -1, keepdims=True) + 1e-06)


def rotate(inputs, cosine, sine, turning):
    turned = jnp.einsum("thd,de->the", inputs, turning, precision=lax.Precision.HIGHEST)
    return inputs * cosine + turned * sine


def clip_index(clip_ends, first_row, count):
    token_index = first_row + jnp.arange(count, dtype=jnp.int32)
    return jnp.sum((token_index[:, None] >= clip_ends[None, :]).astype(jnp.int32), 1)


def local(hidden, modulation, in_projection, out_projection, lengths, positions, guidance):
    states = hidden[0]
    tok_count = states.shape[0]
    feat_width = states.shape[1]
    half_rows = tok_count // 2
    inner_width = in_projection.shape[2]
    head_count = inner_width // HEAD_DIM
    full_states = lax.all_gather(states, "blk", axis=1, tiled=True)
    modulated = (
        layer_norm(full_states.astype(jnp.float32)) * (1.0 + modulation[1]) + modulation[0]
    ).astype(jnp.bfloat16)
    piece = lax.all_gather(in_projection, ("cfg", "seq"), axis=0, tiled=True)
    mixed = jnp.dot(
        modulated,
        piece.reshape(piece.shape[0], 3 * inner_width),
        preferred_element_type=jnp.float32,
    )
    mixed = mixed.reshape(tok_count, 3, head_count, HEAD_DIM)
    angle_table = jnp.asarray(rotary_angles(HEAD_DIM))
    turning = jnp.asarray(turn_matrix(HEAD_DIM))
    angles = jnp.einsum(
        "at,ae->te", positions.astype(jnp.float32), angle_table, precision=lax.Precision.HIGHEST
    )
    cosine = jnp.cos(angles)[:, None, :]
    sine = jnp.sin(angles)[:, None, :]
    queries = rotate(rms_norm(mixed[:, 0]), cosine, sine, turning).astype(jnp.bfloat16)
    key_rows = rotate(rms_norm(mixed[:, 1]), cosine, sine, turning).astype(jnp.bfloat16)
    value_rows = mixed[:, 2].astype(jnp.bfloat16)
    clip_ends = jnp.cumsum(lengths)
    query_clip = clip_index(clip_ends, lax.axis_index("seq") * tok_count, tok_count)
    score_scale = HEAD_DIM ** (-0.5)
    start_state = (
        jnp.zeros((tok_count, head_count, HEAD_DIM), jnp.float32),
        jnp.zeros((head_count, tok_count), jnp.float32),
    )
    first_row = jnp.int32(0)
    key_piece = lax.all_gather(key_rows, "seq", axis=0, tiled=True)
    value_piece = lax.all_gather(value_rows, "seq", axis=0, tiled=True)
    row_count = key_piece.shape[0]
    key_block = 512 if row_count % 512 == 0 else row_count

    def key_step(block_index, running):
        numerator, denominator = running
        key_slab = lax.dynamic_slice_in_dim(key_piece, block_index * key_block, key_block, 0)
        value_slab = lax.dynamic_slice_in_dim(value_piece, block_index * key_block, key_block, 0)
        key_clip = clip_index(clip_ends, first_row + block_index * key_block, key_block)
        scores = (
            jnp.einsum("qhd,khd->hqk", queries, key_slab, preferred_element_type=jnp.float32)
            * score_scale
        )
        same_clip = query_clip[:, None] == key_clip[None, :]
        weights = jnp.where(same_clip[None], jnp.exp(scores), 0.0)
        numerator = numerator + jnp.einsum(
            "hqk,khd->qhd",
            weights.astype(jnp.bfloat16),
            value_slab,
            preferred_element_type=jnp.float32,
        )
        denominator = denominator + jnp.sum(weights, -1)
        return (numerator, denominator)

    numerator, denominator = lax.fori_loop(0, row_count // key_block, key_step, start_state)
    attended = (
        (numerator / jnp.transpose(denominator)[:, :, None])
        .astype(jnp.bfloat16)
        .reshape(tok_count, inner_width)
    )
    col_start = lax.axis_index("blk") * feat_width
    own_inputs = states.astype(jnp.float32)
    cfg_index = lax.axis_index("cfg")
    partial_out = jnp.dot(
        attended,
        lax.all_gather(out_projection, ("cfg", "seq"), axis=1, tiled=True),
        preferred_element_type=jnp.float32,
    )
    projected = lax.psum_scatter(partial_out, "blk", scatter_dimension=1, tiled=True)
    gate_vector = lax.dynamic_slice_in_dim(modulation[2], col_start, feat_width, 0)
    block_out = own_inputs + gate_vector * projected
    other_out = from_partner(block_out, "cfg", 0)
    mine_rows = lax.dynamic_slice_in_dim(block_out, cfg_index * half_rows, half_rows, 0)
    their_rows = lax.dynamic_slice_in_dim(other_out, cfg_index * half_rows, half_rows, 0)
    is_cond = cfg_index == 0
    cond_rows = jnp.where(is_cond, mine_rows, their_rows)
    uncond_rows = jnp.where(is_cond, their_rows, mine_rows)
    guided = uncond_rows + guidance[0] * (cond_rows - uncond_rows)
    return guided.reshape(1, 1, half_rows, feat_width)


def solution(mesh):
    return jax.shard_map(
        local,
        mesh=mesh,
        in_specs=(
            P("cfg", "seq", "blk"),
            P(),
            P(("cfg", "seq"), None, "blk"),
            P("blk", ("cfg", "seq")),
            P(),
            P(None, "seq"),
            P(),
        ),
        out_specs=P("seq", "cfg", None, "blk"),
        check_vma=False,
    )
```

profile of v0, /device:TPU:0, one launch (start us, length us, event | category | flops | bytes accessed | tf_op | source)
XLA Modules:
  0.0 421.1 jit_solution(1140254993012736413)
XLA Ops:
  6.5 0.7 all-gather.14.cloned.1.call-update
  7.3 0.7 all-gather.8.cloned.1.call-update
  8.1 1.1 fusion.38
  9.2 72.2 %all-gather.14.cloned.1.call-done = bf16[1,384,5120]{2,1,0:T(8,128)(2,1)} async-done(((bf16[1,384,640]{2,1,0:T(8,128)(2,1)}), bf16[1,384,5120]{2,1,0:T(8,128)(2,1)}) %all-gather.14.cloned.1.call-update) | async-done | bytes 3932176 | tf_op jit(solution)/shard_map/all_gather | solution.py:70
  81.3 2.9 convert_reduce_fusion.1
  84.2 0.4 copy-done
  84.6 1.2 fusion.17
  85.8 63.0 %all-gather.8.cloned.1.call-done = bf16[5120,3,384]{2,0,1:T(8,128)(2,1)} async-done(((bf16[320,3,384]{2,0,1:T(8,128)(2,1)}), bf16[5120,3,384]{2,0,1:T(8,128)(2,1)}) %all-gather.8.cloned.1.call-update) | async-done | bytes 11796496 | tf_op jit(solution)/shard_map/all_gather | solution.py:74
  148.8 16.2 %copy.34 = bf16[5120,3,384]{0,2,1:T(8,128)(2,1)} copy(bf16[5120,3,384]{2,0,1:T(8,128)(2,1)} %all-gather.8.cloned.1.call-done) | data formatting | bytes 23592960 | tf_op jit(solution)/shard_map/all_gather | solution.py:74
  165.1 10.7 %fusion.22 = f32[384,3,3,128]{0,3,2,1:T(8,128)S(1)} fusion(bf16[3,3,128,5120]{3,2,1,0:T(8,128)(2,1)} %bitcast.94, bf16[1,384,5120]{2,1,0:T(8,128)(2,1)} %all-gather.14.cloned.1.call-done, f32[5120]{0:T(1024)S(1)} %bitcast.98, f32[5120]{0:T(1024)S(1)} %bitcast.99, f32[384]{0:T(512)S(1)} %add_rsqrt_fusion.2, f32[384]{0:T(512)S(1)} %broadcast_multiply_fusion), kind=kOutput, calls=%fused_computation.29 | convolution fusion | flops 4541644800 | bytes 17542144 | tf_op jit(solution)/shard_map/dot_general | solution.py:75
  175.7 0.7 slice.48
  176.6 1.1 cosine_bitcast_fusion
  177.7 0.1 multiply_reduce_fusion
  177.8 1.4 fusion.30
  179.3 0.5 all-gather.12.cloned.1.call-update
  179.8 0.2 reduce-scatter.2.cloned.1.call-start
  180.1 0.2 reduce-window.8
  180.3 0.1 convert_reduce_fusion.2
  180.3 0.7 fusion.31
  181.0 0.2 copy.40
  181.3 22.3 %all-gather.16.cloned.1.call-done = bf16[3072,1,3,128]{0,3,2,1:T(8,128)(2,1)} async-done(((bf16[384,1,3,128]{0,3,2,1:T(8,128)(2,1)}), bf16[3072,1,3,128]{0,3,2,1:T(8,128)(2,1)}) %all-gather.16.cloned.1.call-update) | async-done | bytes 2359312 | tf_op jit(solution)/shard_map/all_gather | solution.py:100
  203.6 27.7 %all-gather.10.cloned.1.call-done = bf16[3072,3,128]{0,2,1:T(8,128)(2,1)} async-done(((bf16[384,3,128]{0,2,1:T(8,128)(2,1)}), bf16[3072,3,128]{0,2,1:T(8,128)(2,1)}) %all-gather.10.cloned.1.call-update) | async-done | bytes 2359312 | tf_op jit(solution)/shard_map/all_gather | solution.py:99
  231.3 22.9 %while.16 = (s32[]{:T(128)}, f32[384,3,128]{0,2,1:T(8,128)S(1)}, f32[3,384]{1,0:T(4,128)S(1)}, bf16[3072,3,128]{0,2,1:T(8,128)(2,1)}, s32[384]{0:T(512)S(1)}, /*...) while((s32[]{:T(128)}, f32[384,3,128]{0,2,1:T(8,128)S(1)}, ...), condition=%wide.region_9.10_spmd.clone, body=%wide.region_6.9_spmd.clone.sunk | while | flops 306029184 | bytes 7597782 | solution.py:124
  231.4 0.2 broadcast_compare_fusion.2
  231.6 1.8 fusion.57
  233.4 1.7 fusion.58
  235.2 0.2 broadcast_compare_fusion.2
  235.4 1.8 fusion.57
  237.2 1.7 fusion.58
  239.0 0.2 broadcast_compare_fusion.2
  239.2 1.8 fusion.57
  241.0 1.7 fusion.58
  242.8 0.2 broadcast_compare_fusion.2
  243.0 1.8 fusion.57
  244.8 1.7 fusion.58
  246.6 0.2 broadcast_compare_fusion.2
  246.8 1.9 fusion.57
  248.7 1.7 fusion.58
  250.5 0.2 broadcast_compare_fusion.2
  250.6 1.9 fusion.57
  252.5 1.7 fusion.58
  254.3 15.6 %all-gather.12.cloned.1.call-done = bf16[384,5120]{0,1:T(8,128)(2,1)} async-done(((bf16[384,320]{0,1:T(8,128)(2,1)}), bf16[384,5120]{0,1:T(8,128)(2,1)}) %all-gather.12.cloned.1.call-update) | async-done | bytes 3932176 | tf_op jit(solution)/shard_map/all_gather | solution.py:135
  269.9 7.4 %fusion.41 = f32[384,5120]{1,0:T(8,128)} fusion(bf16[384,384]{0,1:T(8,128)(2,1)S(1)} %bitcast.96, bf16[384,5120]{0,1:T(8,128)(2,1)} %all-gather.12.cloned.1.call-done), kind=kOutput, calls=%fused_computation.65 | convolution fusion | flops 1509949440 | bytes 12091392 | tf_op jit(solution)/shard_map/dot_general | solution.py:133
  277.4 111.9 %reduce-scatter.2.cloned.1.call-done = f32[384,640]{1,0:T(8,128)} async-done(((f32[384,5120]{1,0:T(8,128)}), f32[384,640]{1,0:T(8,128)}) %reduce-scatter.2.cloned.1.call-update) | async-done | bytes 983056 | tf_op jit(solution)/shard_map/reduce_scatter | solution.py:138
  389.3 1.3 convert_add_fusion
  390.6 0.7 collective-permute-start
  392.0 21.4 %collective-permute-done = f32[384,640]{1,0:T(8,128)S(1)} collective-permute-done((f32[384,640]{1,0:T(8,128)S(1)}, f32[384,640]{1,0:T(8,128)S(1)}, u32[]{:S(2)}, u32[]{:S(2)}) %collective-permute-start) | collective-permute-done | bytes 983072 | tf_op jit(solution)/shard_map/ppermute | solution.py:11
  413.3 0.9 add_bitcast_fusion
  (46 shorter events, 1.0 us)
Async XLA Ops:
  6.5 74.8 %all-gather.14.cloned.1.call-start = ((), (), s32[]{:S(2)}) async-start(), calls=%async_computation.5 | async-start | bytes 4423680 | tf_op jit(solution)/shard_map/all_gather | solution.py:70
  7.3 141.6 %all-gather.8.cloned.1.call-start = ((), (), s32[]{:S(2)}) async-start(), calls=%async_computation.1 | async-start | bytes 12533760 | tf_op jit(solution)/shard_map/all_gather | solution.py:74
  8.0 195.6 %all-gather.16.cloned.1.call-start = ((), (), s32[]{:S(2)}) async-start(), calls=%async_computation.6 | async-start | bytes 2654208 | tf_op jit(solution)/shard_map/all_gather | solution.py:100
  81.3 3.3 copy-start
  165.0 11.5 %copy-start.3 = (s32[3,384]{1,0:T(4,128)S(1)}, s32[3,384]{1,0:T(4,128)}, u32[]{:S(2)}) copy-start(s32[3,384]{1,0:T(4,128)} %param.16) | copy-start | bytes 13828
  165.0 11.5 %copy-start.4 = (f32[3,128]{1,0:T(4,128)S(1)}, f32[3,128]{1,0:T(4,128)}, u32[]{:S(2)}) copy-start(f32[3,128]{1,0:T(4,128)} %constant.88.clone) | copy-start | bytes 4612
  165.1 12.7 %copy-start.2 = (f32[128,128,1]{1,0,2:T(8,128)S(1)}, f32[128,128,1]{1,0,2:T(8,128)}, u32[]{:S(2)}) copy-start(f32[128,128,1]{1,0,2:T(8,128)} %constant.91) | copy-start | bytes 196612
  175.7 4.3 %copy-start.5 = (s32[5]{0:T(128)S(1)}, s32[5]{0:T(128)}, u32[]{:S(2)}) copy-start(s32[5]{0:T(128)} %param.15) | copy-start | bytes 64
  176.5 54.8 %all-gather.10.cloned.1.call-start = ((), (), s32[]{:S(2)}) async-start(), calls=%async_computation.2 | async-start | bytes 2654208 | tf_op jit(solution)/shard_map/all_gather | solution.py:99
  179.2 90.7 %all-gather.12.cloned.1.call-start = ((), (), s32[]{:S(2)}) async-start(), calls=%async_computation.3 | async-start | bytes 4177920 | tf_op jit(solution)/shard_map/all_gather | solution.py:135
  179.8 209.5 %reduce-scatter.2.cloned.1.call-start = ((), (), s32[]{:S(2)}) async-start(), calls=%async_computation.4 | async-start | bytes 8847360 | tf_op jit(solution)/shard_map/reduce_scatter | solution.py:138
  277.3 112.0 %copy-start.1 = (bf16[1,384,640]{2,1,0:T(8,128)(2,1)S(1)}, bf16[1,384,640]{2,1,0:T(8,128)(2,1)}, u32[]{:S(2)}) copy-start(bf16[1,384,640]{2,1,0:T(8,128)(2,1)} %param.11) | copy-start | bytes 1474564
  390.6 22.8 %collective-permute-start = (f32[384,640]{1,0:T(8,128)S(1)}, f32[384,640]{1,0:T(8,128)S(1)}, u32[]{:S(2)}, u32[]{:S(2)}) collective-permute-start(f32[384,640]{1,0:T(8,128)S(1)} %convert_add_fusion), channel_id=1, source_target_pairs={{0,64},{64,0},{1,65},{65,1},{2,66},{66,2},{3,67},{67,3},{4,68},{68... | collective-permute-start | bytes 2949128 | tf_op jit(solution)/shard_map/ppermute | solution.py:11
Sparse Core Ops, SparseCore 0:
  9.7 71.6 all-gather.13
  83.0 65.7 all-gather.7
  176.6 26.8 all-gather.15
  205.1 26.1 all-gather.9
  232.8 36.9 all-gather.11
  277.5 111.7 reduce-scatter.1
where the time goes:
time: 422 us; the launch traced here: 421 us
  waiting for transfers between devices  336 us (80%)
  matrix products  42.3 us (10%)
  local copies, waits for them, and re-layouts  17.6 us (4%)
  between operations  14.2 us (3%)
  other arithmetic  9.41 us (2%)
    reduce_scatter x1, waiting for transfers between devices, local(): lax.psum_scatter(partial_out, 'blk', scatter_dimension=1, tiled=True)  112 us
    all_gather x1, waiting for transfers between devices, local(): full_states = lax.all_gather(states, 'blk', axis=1, tiled=True)  72.2 us
    all_gather x1, waiting for transfers between devices, local(): piece = lax.all_gather(in_projection, ('cfg', 'seq'), axis=0, tiled=True)  63 us
    all_gather x1, waiting for transfers between devices, local(): key_piece = lax.all_gather(key_rows, 'seq', axis=0, tiled=True)  27.7 us
    all_gather x1, waiting for transfers between devices, local(): value_piece = lax.all_gather(value_rows, 'seq', axis=0, tiled=True)  22.3 us
    ppermute x1, waiting for transfers between devices, from_partner(): lax.ppermute(array, axis, [(i, i ^ 1 << distance) for i in range(lax.axis...  21.4 us
    all_gather x1, local copies, waits for them, and re-layouts, local(): piece = lax.all_gather(in_projection, ('cfg', 'seq'), axis=0, tiled=True)  16.2 us
    all_gather x1, waiting for transfers between devices, local(): lax.all_gather(out_projection, ('cfg', 'seq'), axis=1, tiled=True)  15.6 us
  transfers between devices with their start and end apart: 7, of which 7 were waited for; matrix products, arithmetic and copies ran while one was open for 8% of the time, Pallas kernels for 0%

commit v1 on v0

v1 whole, which is shorter than its diff:
```python
import jax
import jax.numpy as jnp
import numpy as np
from jax import lax
from jax.sharding import Mesh, PartitionSpec as P

HEAD_DIM = 128
SEQ = ("x", "core")
BLK = ("zhi", "y")
SWAP = [(0, 1), (1, 0)]


def rotary_angles(head_width):
    third = head_width // 6
    first_dim = head_width - 4 * third
    other_dim = 2 * third
    pair_index = np.arange(head_width) // 2
    first_pairs = first_dim // 2
    other_pairs = other_dim // 2
    in_first = pair_index < first_pairs
    in_second = (pair_index >= first_pairs) & (pair_index < first_pairs + other_pairs)
    in_third = pair_index >= first_pairs + other_pairs
    row_first = np.where(in_first, 10000.0 ** (-2.0 * pair_index / first_dim), 0.0)
    row_second = np.where(
        in_second, 10000.0 ** (-2.0 * (pair_index - first_pairs) / other_dim), 0.0
    )
    row_third = np.where(
        in_third, 10000.0 ** (-2.0 * (pair_index - first_pairs - other_pairs) / other_dim), 0.0
    )
    return np.stack([row_first, row_second, row_third]).astype(np.float32)


def turn_matrix(head_width):
    row_index = np.arange(head_width)[:, None]
    col_index = np.arange(head_width)[None, :]
    upper = np.where((col_index == row_index + 1) & (row_index % 2 == 0), 1.0, 0.0)
    lower = np.where((col_index == row_index - 1) & (row_index % 2 == 1), -1.0, 0.0)
    return (upper + lower).astype(np.float32)


def layer_norm(inputs):
    row_mean = jnp.mean(inputs, -1, keepdims=True)
    centered = inputs - row_mean
    variance = jnp.mean(centered * centered, -1, keepdims=True)
    return centered * lax.rsqrt(variance + 1e-06)


def rms_norm(inputs):
    return inputs * lax.rsqrt(jnp.mean(inputs * inputs, -1, keepdims=True) + 1e-06)


def rotate(inputs, cosine, sine, turning):
    turned = jnp.einsum("thd,de->the", inputs, turning, precision=lax.Precision.HIGHEST)
    return inputs * cosine + turned * sine


def clip_of(clip_ends, token_index):
    return jnp.sum((token_index[:, None] >= clip_ends[None, :]).astype(jnp.int32), 1)


def local(hidden, modulation, in_projection, out_projection, lengths, positions, guidance):
    cfg = lax.axis_index("cfg")
    core = lax.axis_index("core")
    seq = lax.axis_index("x") * 2 + core
    states = hidden[0]
    tok_count = states.shape[0]
    half_rows = tok_count // 2
    n_blk = lax.axis_size(BLK)
    inner_width = in_projection.shape[2]
    head_count = inner_width // HEAD_DIM

    sent_rows = lax.dynamic_slice_in_dim(states, (1 - cfg) * half_rows, half_rows, 0)
    other_rows = lax.ppermute(sent_rows, "cfg", SWAP)
    mine_rows = lax.dynamic_slice_in_dim(states, cfg * half_rows, half_rows, 0)
    is_cond = cfg == 0
    cond_rows = jnp.where(is_cond, mine_rows, other_rows).astype(jnp.float32)
    uncond_rows = jnp.where(is_cond, other_rows, mine_rows).astype(jnp.float32)
    scale = guidance[0]
    hidden_part = uncond_rows + scale * (cond_rows - uncond_rows)

    full_states = lax.all_gather(states, BLK, axis=1, tiled=True)
    modulated = (
        layer_norm(full_states.astype(jnp.float32)) * (1.0 + modulation[1]) + modulation[0]
    ).astype(jnp.bfloat16)

    w_mine = lax.all_gather(in_projection, ("cfg", "x"), axis=0, tiled=True)
    w_other = lax.ppermute(w_mine, "core", SWAP)
    rows = in_projection.shape[0]
    n_pairs = w_mine.shape[0] // rows
    mod4 = modulated.reshape(tok_count, n_pairs, 2, rows)
    mod_mine = lax.dynamic_index_in_dim(mod4, core, axis=2, keepdims=False)
    mod_other = lax.dynamic_index_in_dim(mod4, 1 - core, axis=2, keepdims=False)
    mixed = jnp.einsum(
        "tjd,jdqe->tqe",
        mod_mine,
        w_mine.reshape(n_pairs, rows, 3, inner_width),
        preferred_element_type=jnp.float32,
    ) + jnp.einsum(
        "tjd,jdqe->tqe",
        mod_other,
        w_other.reshape(n_pairs, rows, 3, inner_width),
        preferred_element_type=jnp.float32,
    )
    mixed = mixed.reshape(tok_count, 3, head_count, HEAD_DIM)

    angle_table = jnp.asarray(rotary_angles(HEAD_DIM))
    turning = jnp.asarray(turn_matrix(HEAD_DIM))
    angles = jnp.einsum(
        "at,ae->te", positions.astype(jnp.float32), angle_table, precision=lax.Precision.HIGHEST
    )
    cosine = jnp.cos(angles)[:, None, :]
    sine = jnp.sin(angles)[:, None, :]
    queries = rotate(rms_norm(mixed[:, 0]), cosine, sine, turning).astype(jnp.bfloat16)
    key_rows = rotate(rms_norm(mixed[:, 1]), cosine, sine, turning).astype(jnp.bfloat16)
    value_rows = mixed[:, 2].astype(jnp.bfloat16)

    kv = jnp.stack([key_rows, value_rows], axis=1)
    kv_mine = lax.all_gather(kv, "x", axis=0, tiled=True)
    kv_other = lax.ppermute(kv_mine, "core", SWAP)
    kv_all = jnp.concatenate([kv_mine, kv_other], axis=0)
    key_piece = kv_all[:, 0]
    value_piece = kv_all[:, 1]
    row_count = key_piece.shape[0]
    n_x = kv_mine.shape[0] // tok_count

    clip_ends = jnp.cumsum(lengths)
    query_clip = clip_of(clip_ends, seq * tok_count + jnp.arange(tok_count, dtype=jnp.int32))
    key_row = jnp.arange(row_count, dtype=jnp.int32)
    key_block = key_row // tok_count
    key_core = jnp.where(key_block < n_x, core, 1 - core)
    key_token = ((key_block % n_x) * 2 + key_core) * tok_count + key_row % tok_count
    key_clip_all = clip_of(clip_ends, key_token)

    score_scale = HEAD_DIM ** (-0.5)
    start_state = (
        jnp.zeros((tok_count, head_count, HEAD_DIM), jnp.float32),
        jnp.zeros((head_count, tok_count), jnp.float32),
    )
    key_block_size = 512 if row_count % 512 == 0 else row_count

    def key_step(block_index, running):
        numerator, denominator = running
        key_slab = lax.dynamic_slice_in_dim(key_piece, block_index * key_block_size, key_block_size, 0)
        value_slab = lax.dynamic_slice_in_dim(value_piece, block_index * key_block_size, key_block_size, 0)
        key_clip = lax.dynamic_slice_in_dim(key_clip_all, block_index * key_block_size, key_block_size, 0)
        scores = (
            jnp.einsum("qhd,khd->hqk", queries, key_slab, preferred_element_type=jnp.float32)
            * score_scale
        )
        same_clip = query_clip[:, None] == key_clip[None, :]
        weights = jnp.where(same_clip[None], jnp.exp(scores), 0.0)
        numerator = numerator + jnp.einsum(
            "hqk,khd->qhd",
            weights.astype(jnp.bfloat16),
            value_slab,
            preferred_element_type=jnp.float32,
        )
        denominator = denominator + jnp.sum(weights, -1)
        return (numerator, denominator)

    numerator, denominator = lax.fori_loop(0, row_count // key_block_size, key_step, start_state)
    attended = (
        (numerator / jnp.transpose(denominator)[:, :, None])
        .astype(jnp.bfloat16)
        .reshape(tok_count, inner_width)
    )

    wo_mine = lax.all_gather(out_projection, ("cfg", "x"), axis=1, tiled=True)
    wo_other = lax.ppermute(wo_mine, "core", SWAP)
    cols = out_projection.shape[1]
    wo_mine = wo_mine.reshape(inner_width, n_blk, cols)
    wo_other = wo_other.reshape(inner_width, n_blk, cols)
    first_core = core == 0
    wo_full = jnp.stack(
        [jnp.where(first_core, wo_mine, wo_other), jnp.where(first_core, wo_other, wo_mine)], axis=2
    ).reshape(inner_width, n_blk, 2 * cols)

    weight = jnp.where(is_cond, scale, 1.0 - scale)
    gate = modulation[2].reshape(n_blk, 2 * cols) * weight
    partial = jnp.einsum(
        "rte,ebn->rbtn",
        attended.reshape(2, half_rows, inner_width),
        wo_full,
        preferred_element_type=jnp.float32,
    ) * gate[None, :, None, :]
    projected = lax.psum_scatter(
        partial.reshape(2 * n_blk, half_rows, 2 * cols),
        ("cfg",) + BLK,
        scatter_dimension=0,
        tiled=True,
    )
    guided = hidden_part + projected[0]
    return guided.reshape(1, 1, half_rows, 2 * cols)


def solution(mesh):
    devices = mesh.devices.reshape(2, 4, 2, 2, 4)
    own = Mesh(devices, ("cfg", "x", "core", "zhi", "y"))
    return jax.shard_map(
        local,
        mesh=own,
        in_specs=(
            P("cfg", SEQ, BLK),
            P(),
            P(("cfg",) + SEQ, None, BLK),
            P(BLK, ("cfg",) + SEQ),
            P(),
            P(None, SEQ),
            P(),
        ),
        out_specs=P(SEQ, "cfg", None, BLK),
        check_vma=False,
    )
```

time: 422 us -> 383 us (0.908)
  waiting for transfers between devices: 336 us -> 288 us
  other arithmetic: 9.41 us -> 17.8 us
    reduce_scatter x1, waiting for transfers between devices: 112 us -> 89.8 us  [local(): lax.psum_scatter(partial.reshape(2 * n_blk, half_rows, 2 * cols), ('cfg',...]
    all_gather x1 -> x0, local copies, waits for them, and re-layouts: 16.2 us -> none  [local(): piece = lax.all_gather(in_projection, ('cfg', 'seq'), axis=0, tiled=True)]
    ppermute x1 -> x4, waiting for transfers between devices: 21.4 us -> 6.81 us  [the longest x1 6.8 us: local(): other_rows = lax.ppermute(sent_rows, 'cfg', SWAP)]
    all_gather x5 -> x4, waiting for transfers between devices: 201 us -> 191 us  [the longest x1 70.6 us: local(): w_mine = lax.all_gather(in_projection, ('cfg', 'x'), axis=0, tiled=True)]
    unnamed x13 -> x27, local copies, waits for them, and re-layouts: 0.66 us -> 5.26 us
    dynamic_slice x1 -> x7, local copies, waits for them, and re-layouts: 0.02 us -> 4.57 us  [the longest x6 4.55 us: key_step(): lax.dynamic_slice_in_dim(key_clip_all, block_index * key_block_size, key_...]
    dot_general x2 -> x3, matrix products: 18.1 us -> 13.6 us  [the longest x1 6.02 us: local(): jnp.einsum('tjd,jdqe->tqe', mod_other, w_other.reshape(n_pairs, rows, 3,...]
  transfers between devices with their start and end apart: 7 -> 9, of which waited for: 7 -> 6; matrix products, arithmetic and copies ran while one was open for 8% -> 9% of each run, Pallas kernels for 0% -> 0%
where the time goes in v1:
time: 383 us; the launch traced here: 382 us
  waiting for transfers between devices  288 us (75%)
  matrix products  39.3 us (10%)
  local copies, waits for them, and re-layouts  20.7 us (5%)
  other arithmetic  17.8 us (5%)
  between operations  14.1 us (4%)
    reduce_scatter x1, waiting for transfers between devices, local(): lax.psum_scatter(partial.reshape(2 * n_blk, half_rows, 2 * cols), ('cfg',...  89.8 us
    all_gather x1, waiting for transfers between devices, local(): w_mine = lax.all_gather(in_projection, ('cfg', 'x'), axis=0, tiled=True)  70.6 us
    all_gather x1, waiting for transfers between devices, local(): full_states = lax.all_gather(states, BLK, axis=1, tiled=True)  66.6 us
    all_gather x1, waiting for transfers between devices, local(): kv_mine = lax.all_gather(kv, 'x', axis=0, tiled=True)  33 us
    all_gather x1, waiting for transfers between devices, local(): wo_mine = lax.all_gather(out_projection, ('cfg', 'x'), axis=1, tiled=True)  20.4 us
    dot_general x6, matrix products, key_step(): jnp.einsum('qhd,khd->hqk', queries, key_slab, preferred_element_type=jnp....  10.4 us
    dot_general x6, matrix products, key_step(): jnp.einsum('hqk,khd->qhd', weights.astype(jnp.bfloat16), value_slab, pref...  10.4 us
  transfers between devices with their start and end apart: 9, of which 6 were waited for; matrix products, arithmetic and copies ran while one was open for 9% of the time, Pallas kernels for 0%

profile of v1, /device:TPU:0, one launch (start us, length us, event | category | flops | bytes accessed | tf_op | source)
XLA Modules:
  0.0 382.0 jit_solution(14357220380822101249)
XLA Ops:
  6.5 0.7 all-gather.8.cloned.1.call-update
  7.3 2.0 copy.34
  9.4 70.6 %all-gather.8.cloned.1.call-done = bf16[2560,3,384]{2,0,1:T(8,128)(2,1)} async-done(((bf16[320,3,384]{2,0,1:T(8,128)(2,1)}), bf16[2560,3,384]{2,0,1:T(8,128)(2,1)}) %all-gather.8.cloned.1.call-update) | async-done | bytes 5898256 | tf_op jit(solution)/shard_map/all_gather | solution.py:86
  80.8 1.8 cosine_bitcast_fusion
  82.8 1.1 slice_add_fusion
  84.0 66.6 %all-gather.12.cloned.1.call-done = bf16[1,384,5120]{1,2,0:T(8,128)(2,1)} async-done(((bf16[1,384,640]{1,2,0:T(8,128)(2,1)}), bf16[1,384,5120]{1,2,0:T(8,128)(2,1)}) %all-gather.12.cloned.1.call-update) | async-done | bytes 3932176 | tf_op jit(solution)/shard_map/all_gather | solution.py:81
  150.6 3.0 convert_reduce_fusion
  153.9 1.1 fusion.17
  155.0 2.9 fusion.20
  158.0 3.3 fusion.23
  161.3 6.0 %bitcast_add_fusion = f32[384,3,384]{0,2,1:T(8,128)S(1)} fusion(f32[384,3,384,1]{0,2,3,1:T(8,128)S(1)} %fusion.23, bf16[8,320,3,384]{3,1,0,2:T(8,128)(2,1)} %bitcast.18, bf16[384,8,2,320]{0,3,2,1:T(8,128)(2,1)S(1)} %bitcast.133, s32[]{:T(128)S(6)} %select_n.127), kind=kOutput, calls=%fused_computation.38 | convolution fusion | flops 2265366528 | bytes 11403268 | tf_op jit(solution)/shard_map/tjd,jdqe->tqe/dot_general | solution.py:98
  167.4 1.0 fusion.59
  169.8 0.9 pad_maximum_fusion.1
  170.7 20.4 %all-gather.6.cloned.1.call-done = bf16[384,2560]{0,1:T(8,128)(2,1)} async-done(((bf16[384,320]{0,1:T(8,128)(2,1)}), bf16[384,2560]{0,1:T(8,128)(2,1)}) %all-gather.6.cloned.1.call-update) | async-done | bytes 1966096 | tf_op jit(solution)/shard_map/all_gather | solution.py:168
  191.9 33.0 %all-gather.10.cloned.1.call-done = bf16[1536,2,3,128]{3,0,2,1:T(8,128)(2,1)} async-done(((bf16[384,2,3,128]{3,0,2,1:T(8,128)(2,1)}), bf16[1536,2,3,128]{3,0,2,1:T(8,128)(2,1)}) %all-gather.10.cloned.1.call-update) | async-done | bytes 2359312 | tf_op jit(solution)/shard_map/all_gather | solution.py:118
  225.7 1.9 broadcast_select_fusion.1
  227.6 2.3 pad_maximum_fusion
  229.9 1.3 copy.54
  231.5 2.5 fusion.32
  234.1 2.0 constant_dynamic-update-slice_fusion
  236.1 2.5 slice_bitcast_fusion
  238.6 26.7 %while.16 = (s32[]{:T(128)}, f32[384,3,128]{0,2,1:T(8,128)S(1)}, f32[3,384]{1,0:T(4,128)S(1)}, bf16[3072,3,128]{2,0,1:T(8,128)(2,1)}, s32[384]{0:T(512)S(1)}, /*...) while((s32[]{:T(128)}, f32[384,3,128]{0,2,1:T(8,128)S(1)}, ...), condition=%wide.region_9.10_spmd.clone, body=%wide.region_7.9_spmd.clone.sunk | while | flops 306021504 | bytes 7595706 | solution.py:161
  238.6 0.8 dynamic_slice.70
  239.5 1.7 fusion.77
  241.2 1.7 fusion.78
  243.0 0.8 dynamic_slice.70
  244.0 1.7 fusion.77
  245.7 1.7 fusion.78
  247.5 0.8 dynamic_slice.70
  248.4 1.7 fusion.77
  250.2 1.7 fusion.78
  251.9 0.8 dynamic_slice.70
  252.9 1.7 fusion.77
  254.6 1.7 fusion.78
  256.4 0.8 dynamic_slice.70
  257.3 1.7 fusion.77
  259.0 1.7 fusion.78
  260.8 0.8 dynamic_slice.70
  261.7 1.7 fusion.77
  263.5 1.7 fusion.78
  265.5 0.8 copy.50
  266.3 4.3 %multiply_bitcast_fusion = f32[2,8,192,640]{3,2,0,1:T(8,128)S(1)} fusion(f32[8,640]{1,0:T(8,128)S(1)} %copy-done.5, bf16[384,8,640,1]{0,2,3,1:T(8,128)(2,1)} %bitcast.129, bf16[2,192,384]{2,1,0:T(8,128)(2,1)S(1)} %copy.50), kind=kOutput, calls=%fused_computation.26 | convolution fusion | flops 1511915520 | bytes 12111872 | tf_op jit(solution)/shard_map/rte,ebn->rbtn/dot_general | solution.py:180
  270.7 3.6 copy.43
  274.3 1.0 copy-done.2
  275.3 1.6 collective-permute-start
  276.9 6.8 %collective-permute-done = bf16[192,640]{1,0:T(8,128)(2,1)S(1)} collective-permute-done((bf16[192,640]{1,0:T(8,128)(2,1)S(1)}, bf16[192,640]{1,0:T(8,128)(2,1)S(1)}, u32[]{:S(2)}, u32[]{:S(2)}) %collective-permute-start) | collective-permute-done | bytes 245792 | tf_op jit(solution)/shard_map/ppermute | solution.py:73
  283.7 89.8 %reduce-scatter.2.cloned.1.call-done = f32[1,192,640]{2,1,0:T(8,128)} async-done(((f32[16,192,640]{2,1,0:T(8,128)}), f32[1,192,640]{2,1,0:T(8,128)}) %reduce-scatter.2.cloned.1.call-update) | async-done | bytes 491536 | tf_op jit(solution)/shard_map/reduce_scatter | solution.py:186
  373.6 1.9 fusion.38
  (73 shorter events, 5.7 us)
Async XLA Ops:
  6.5 73.5 %all-gather.8.cloned.1.call-start = ((), (), s32[]{:S(2)}) async-start(), calls=%async_computation.2 | async-start | bytes 6635520 | tf_op jit(solution)/shard_map/all_gather | solution.py:86
  7.3 143.4 %all-gather.12.cloned.1.call-start = ((), (), s32[]{:S(2)}) async-start(), calls=%async_computation.5 | async-start | bytes 4423680 | tf_op jit(solution)/shard_map/all_gather | solution.py:81
  9.3 181.8 %all-gather.6.cloned.1.call-start = ((), (), s32[]{:S(2)}) async-start(), calls=%async_computation.1 | async-start | bytes 2211840 | tf_op jit(solution)/shard_map/all_gather | solution.py:168
  80.0 81.2 %collective-permute-start.2 = (bf16[2560,3,384]{2,0,1:T(8,128)(2,1)}, bf16[2560,3,384]{2,0,1:T(8,128)(2,1)}, u32[]{:S(2)}, u32[]{:S(2)}) collective-permute-start(bf16[2560,3,384]{2,0,1:T(8,128)(2,1)} %all-gather.8.cloned.1.call-done), channel_id=1, source_target_pairs={{0,8},{8,0},{1,9},{9,1},{2,10},{10,2},{3,11},{11,3},{4,12},{12,4},... | collective-permute-start | bytes 17694728 | tf_op jit(solution)/shard_map/ppermute | solution.py:87
  80.1 144.8 %all-gather.10.cloned.1.call-start = ((), (), s32[]{:S(2)}) async-start(), calls=%async_computation.3 | async-start | bytes 2949120 | tf_op jit(solution)/shard_map/all_gather | solution.py:118
  82.7 86.4 %copy-start.3 = (f32[384,128]{1,0:T(8,128)}, f32[384,128]{1,0:T(8,128)S(1)}, u32[]{:S(2)}) copy-start(f32[384,128]{1,0:T(8,128)S(1)} %copy.36) | copy-start | bytes 589828
  82.8 86.2 %copy-start.4 = (f32[384,128]{1,0:T(8,128)}, f32[384,128]{1,0:T(8,128)S(1)}, u32[]{:S(2)}) copy-start(f32[384,128]{1,0:T(8,128)S(1)} %copy.37) | copy-start | bytes 589828
  150.6 3.3 copy-start
  153.9 4.0 %slice-start = ((s8[5898240]{0:T(1024)(128)(4,1)}), s8[4194304]{0:T(1024)(128)(4,1)S(1)}, s32[]{:S(2)}) async-start(s8[5898240]{0:T(1024)(128)(4,1)} %bitcast.141), calls=%async_computation.6 | async-start | bytes 8388608
  155.0 2.9 slice-start.1
  167.3 1.8 copy-start.7
  167.4 23.8 %copy-start.8 = (s32[5]{0:T(128)S(1)}, s32[5]{0:T(128)}, u32[]{:S(2)}) copy-start(s32[5]{0:T(128)} %param.15) | copy-start | bytes 64
  170.7 202.9 %reduce-scatter.2.cloned.1.call-start = ((), (), s32[]{:S(2)}) async-start(), calls=%async_computation.4 | async-start | bytes 8355840 | tf_op jit(solution)/shard_map/reduce_scatter | solution.py:186
  191.1 34.6 %collective-permute-start.1 = (bf16[384,2560]{0,1:T(8,128)(2,1)}, bf16[384,2560]{0,1:T(8,128)(2,1)S(1)}, u32[]{:S(2)}, u32[]{:S(2)}) collective-permute-start(bf16[384,2560]{0,1:T(8,128)(2,1)} %all-gather.6.cloned.1.call-done), channel_id=1, source_target_pairs={{0,8},{8,0},{1,9},{9,1},{2,10},{10,2},{3,11},{11,3},{4,12},{12,4},... | collective-permute-start | bytes 5898248 | tf_op jit(solution)/shard_map/ppermute | solution.py:169
  224.9 9.2 %collective-permute-start.3 = (bf16[1536,2,3,128]{3,0,2,1:T(8,128)(2,1)}, bf16[1536,2,3,128]{3,0,2,1:T(8,128)(2,1)}, u32[]{:S(2)}, u32[]{:S(2)}) collective-permute-start(bf16[1536,2,3,128]{3,0,2,1:T(8,128)(2,1)} %all-gather.10.cloned.1.call-done), channel_id=1, source_target_pairs={{0,8},{8,0},{1,9},{9,1},{2,10},{10,2},{3,11},{11,3},{4,12},{12,4},... | collective-permute-start | bytes 7077896 | tf_op jit(solution)/shard_map/ppermute | solution.py:119
  227.6 6.3 %copy-start.1 = (bf16[1536,2,3,128]{3,0,2,1:T(8,128)(2,1)S(1)}, bf16[1536,2,3,128]{3,0,2,1:T(8,128)(2,1)}, u32[]{:S(2)}) copy-start(bf16[1536,2,3,128]{3,0,2,1:T(8,128)(2,1)} %all-gather.10.cloned.1.call-done) | copy-start | bytes 7077892
  236.1 2.5 copy-start.6
  238.6 27.7 %copy-start.5 = (f32[8,640]{1,0:T(8,128)S(1)}, f32[8,640]{1,0:T(8,128)}, u32[]{:S(2)}) copy-start(f32[8,640]{1,0:T(8,128)} %mul.177) | copy-start | bytes 61444
  274.2 1.0 copy-start.2
  275.3 8.4 %collective-permute-start = (bf16[192,640]{1,0:T(8,128)(2,1)S(1)}, bf16[192,640]{1,0:T(8,128)(2,1)S(1)}, u32[]{:S(2)}, u32[]{:S(2)}) collective-permute-start(bf16[192,640]{1,0:T(8,128)(2,1)S(1)} %dynamic-slice_bitcast_fusion), channel_id=1, source_target_pairs={{0,64},{64,0},{1,65},{65,1},{2,66},{66,2},{3,67},{67,3},{4,68},{68... | collective-permute-start | bytes 737288 | tf_op jit(solution)/shard_map/ppermute | solution.py:73
Sparse Core Ops, SparseCore 0:
  9.0 71.0 all-gather.7
  82.4 68.2 all-gather.11
  152.3 38.7 all-gather.5
  192.6 32.2 all-gather.9
  274.4 99.1 reduce-scatter.1

commit v2 on v1

--- a/solution.py
+++ b/solution.py
@@ -62,8 +62,10 @@
     cfg = lax.axis_index("cfg")
     core = lax.axis_index("core")
     seq = lax.axis_index("x") * 2 + core
+    blk = lax.axis_index("zhi") * lax.axis_size("y") + lax.axis_index("y")
     states = hidden[0]
     tok_count = states.shape[0]
+    feat_width = states.shape[1]
     half_rows = tok_count // 2
     n_blk = lax.axis_size(BLK)
     inner_width = in_projection.shape[2]
@@ -78,27 +80,23 @@
     scale = guidance[0]
     hidden_part = uncond_rows + scale * (cond_rows - uncond_rows)
 
-    full_states = lax.all_gather(states, BLK, axis=1, tiled=True)
-    modulated = (
-        layer_norm(full_states.astype(jnp.float32)) * (1.0 + modulation[1]) + modulation[0]
-    ).astype(jnp.bfloat16)
-
-    w_mine = lax.all_gather(in_projection, ("cfg", "x"), axis=0, tiled=True)
-    w_other = lax.ppermute(w_mine, "core", SWAP)
-    rows = in_projection.shape[0]
-    n_pairs = w_mine.shape[0] // rows
-    mod4 = modulated.reshape(tok_count, n_pairs, 2, rows)
-    mod_mine = lax.dynamic_index_in_dim(mod4, core, axis=2, keepdims=False)
-    mod_other = lax.dynamic_index_in_dim(mod4, 1 - core, axis=2, keepdims=False)
+    spread = jnp.broadcast_to(states[None], (n_blk,) + states.shape)
+    full_states = lax.all_to_all(spread, BLK, 0, 0, tiled=False)
+    full_states, hidden_part = lax.optimization_barrier((full_states, hidden_part))
+    inputs = full_states.astype(jnp.float32)
+    row_mean = jnp.mean(inputs, (0, 2), keepdims=True)
+    centered = inputs - row_mean
+    variance = jnp.mean(centered * centered, (0, 2), keepdims=True)
+    normed = centered * lax.rsqrt(variance + 1e-06)
+    mod_shift = modulation[0].reshape(n_blk, 1, feat_width)
+    mod_scale = modulation[1].reshape(n_blk, 1, feat_width)
+    modulated = (normed * (1.0 + mod_scale) + mod_shift).astype(jnp.bfloat16)
+
+    piece = lax.all_gather(in_projection, ("cfg",) + SEQ, axis=0, tiled=True)
     mixed = jnp.einsum(
-        "tjd,jdqe->tqe",
-        mod_mine,
-        w_mine.reshape(n_pairs, rows, 3, inner_width),
-        preferred_element_type=jnp.float32,
-    ) + jnp.einsum(
-        "tjd,jdqe->tqe",
-        mod_other,
-        w_other.reshape(n_pairs, rows, 3, inner_width),
+        "itf,ifqe->tqe",
+        modulated,
+        piece.reshape(n_blk, feat_width, 3, inner_width),
         preferred_element_type=jnp.float32,
     )
     mixed = mixed.reshape(tok_count, 3, head_count, HEAD_DIM)
@@ -165,32 +163,22 @@
         .reshape(tok_count, inner_width)
     )
 
-    wo_mine = lax.all_gather(out_projection, ("cfg", "x"), axis=1, tiled=True)
-    wo_other = lax.ppermute(wo_mine, "core", SWAP)
-    cols = out_projection.shape[1]
-    wo_mine = wo_mine.reshape(inner_width, n_blk, cols)
-    wo_other = wo_other.reshape(inner_width, n_blk, cols)
-    first_core = core == 0
-    wo_full = jnp.stack(
-        [jnp.where(first_core, wo_mine, wo_other), jnp.where(first_core, wo_other, wo_mine)], axis=2
-    ).reshape(inner_width, n_blk, 2 * cols)
-
-    weight = jnp.where(is_cond, scale, 1.0 - scale)
-    gate = modulation[2].reshape(n_blk, 2 * cols) * weight
+    out_piece = lax.all_gather(out_projection, ("cfg",) + SEQ, axis=1, tiled=True)
     partial = jnp.einsum(
         "rte,ebn->rbtn",
         attended.reshape(2, half_rows, inner_width),
-        wo_full,
+        out_piece.reshape(inner_width, n_blk, feat_width),
         preferred_element_type=jnp.float32,
-    ) * gate[None, :, None, :]
-    projected = lax.psum_scatter(
-        partial.reshape(2 * n_blk, half_rows, 2 * cols),
-        ("cfg",) + BLK,
-        scatter_dimension=0,
-        tiled=True,
-    )
-    guided = hidden_part + projected[0]
-    return guided.reshape(1, 1, half_rows, 2 * cols)
+    ).astype(jnp.bfloat16)
+    arrived = lax.all_to_all(
+        partial.reshape(2 * n_blk, half_rows, feat_width), ("cfg",) + BLK, 0, 0, tiled=False
+    ).astype(jnp.float32)
+    cond_sum = jnp.sum(arrived[:n_blk], 0)
+    uncond_sum = jnp.sum(arrived[n_blk:], 0)
+    gate = lax.dynamic_slice_in_dim(modulation[2], blk * feat_width, feat_width, 0)
+    projected = gate * (uncond_sum + scale * (cond_sum - uncond_sum))
+    guided = hidden_part + projected
+    return guided.reshape(1, 1, half_rows, feat_width)
 
 
 def solution(mesh):

time: 383 us -> 312 us (0.81)
  waiting for transfers between devices: 288 us -> 204 us
  starting transfers between devices: 1.81 us -> 16 us
  local copies, waits for them, and re-layouts: 20.7 us -> 27.7 us
  other arithmetic: 17.8 us -> 13.1 us
    all_gather x3 -> x2, waiting for transfers between devices: 158 us -> 47.7 us  [the longest x1 36.3 us: local(): piece = lax.all_gather(in_projection, ('cfg',) + SEQ, axis=0, tiled=True)]
    reduce_scatter x1 -> x0, waiting for transfers between devices: 89.8 us -> none  [local(): lax.psum_scatter(partial.reshape(2 * n_blk, half_rows, 2 * cols), ('cfg',...]
    all_to_all x0 -> x2, waiting for transfers between devices: none -> 60.2 us  [the longest x1 60.2 us: local(): lax.all_to_all(partial.reshape(2 * n_blk, half_rows, feat_width), ('cfg',...]
    ppermute x1, waiting for transfers between devices: 6.8 us -> 60.4 us  [local(): other_rows = lax.ppermute(sent_rows, 'cfg', SWAP)]
    reshape x0 -> x1, local copies, waits for them, and re-layouts: none -> 16.1 us  [local(): piece.reshape(n_blk, feat_width, 3, inner_width)]
    all_to_all x0 -> x2, starting transfers between devices: none -> 14.8 us  [the longest x1 8.04 us: local(): full_states = lax.all_to_all(spread, BLK, 0, 0, tiled=False)]
    dot_general x6, matrix products: 10.4 us -> 4.14 us  [key_step(): jnp.einsum('hqk,khd->qhd', weights.astype(jnp.bfloat16), value_slab, pref...]
    mul x2 -> x0, local copies, waits for them, and re-layouts: 4.19 us -> none  [the longest x1 3.59 us: local(): jnp.einsum('rte,ebn->rbtn', attended.reshape(2, half_rows, inner_width),...]
  transfers between devices with their start and end apart: 9 -> 7, of which waited for: 6 -> 5; matrix products, arithmetic and copies ran while one was open for 9% -> 12% of each run, Pallas kernels for 0% -> 0%
where the time goes in v2:
time: 312 us; the launch traced here: 311 us
  waiting for transfers between devices  204 us (65%)
  matrix products  36.1 us (12%)
  local copies, waits for them, and re-layouts  27.7 us (9%)
  starting transfers between devices  16 us (5%)
  between operations  14 us (4%)
  other arithmetic  13.1 us (4%)
    ppermute x1, waiting for transfers between devices, local(): other_rows = lax.ppermute(sent_rows, 'cfg', SWAP)  60.4 us
    all_to_all x1, waiting for transfers between devices, local(): lax.all_to_all(partial.reshape(2 * n_blk, half_rows, feat_width), ('cfg',...  60.2 us
    all_gather x1, waiting for transfers between devices, local(): piece = lax.all_gather(in_projection, ('cfg',) + SEQ, axis=0, tiled=True)  36.3 us
    all_gather x1, waiting for transfers between devices, local(): kv_mine = lax.all_gather(kv, 'x', axis=0, tiled=True)  34.6 us
    reshape x1, local copies, waits for them, and re-layouts, local(): piece.reshape(n_blk, feat_width, 3, inner_width)  16.1 us
    dot_general x6, matrix products, key_step(): jnp.einsum('qhd,khd->hqk', queries, key_slab, preferred_element_type=jnp....  11.6 us
    all_gather x1, waiting for transfers between devices, local(): lax.all_gather(out_projection, ('cfg',) + SEQ, axis=1, tiled=True)  11.5 us
    dot_general x1, matrix products, local(): jnp.einsum('itf,ifqe->tqe', modulated, piece.reshape(n_blk, feat_width, 3...  10.8 us
  transfers between devices with their start and end apart: 7, of which 5 were waited for; matrix products, arithmetic and copies ran while one was open for 12% of the time, Pallas kernels for 0%

profile of v2, /device:TPU:0, one launch (start us, length us, event | category | flops | bytes accessed | tf_op | source)
XLA Modules:
  0.0 310.9 jit_solution(8908683066597014462)
XLA Ops:
  6.5 0.7 all-gather.4.cloned.1.call-update
  7.3 3.3 %broadcast_in_dim.69 = bf16[8,384,640]{2,1,0:T(8,128)(2,1)} broadcast(bf16[384,640]{1,0:T(8,128)(2,1)} %bitcast.100), dimensions={1,2} | broadcast | bytes 4423680 | tf_op jit(solution)/shard_map/broadcast_in_dim | solution.py:83
  10.6 8.0 %all-to-all-start = ((bf16[8,384,640]{2,1,0:T(8,128)(2,1)}), bf16[8,384,640]{2,1,0:T(8,128)(2,1)}, u32[]{:S(2)}, u32[]{:S(2)}) async-start(bf16[8,384,640]{2,1,0:T(8,128)(2,1)} %broadcast_in_dim.69), calls=%async_computation | async-start | bytes 7864320 | tf_op jit(solution)/shard_map/all_to_all | solution.py:84
  18.7 1.1 collective-permute-start
  20.6 1.1 cosine_bitcast_fusion
  21.7 60.4 %collective-permute-done = bf16[192,640]{1,0:T(8,128)(2,1)S(1)} collective-permute-done((bf16[192,640]{1,0:T(8,128)(2,1)S(1)}, bf16[192,640]{1,0:T(8,128)(2,1)S(1)}, u32[]{:S(2)}, u32[]{:S(2)}) %collective-permute-start) | collective-permute-done | bytes 245792 | tf_op jit(solution)/shard_map/ppermute | solution.py:75
  82.1 0.1 convert_add_fusion
  82.3 2.7 convert_reduce_fusion
  85.0 3.4 %fusion.18 = f32[384]{0:T(512)S(1)} fusion(bf16[8,384,640]{2,1,0:T(8,128)(2,1)} %all-to-all-done, f32[384]{0:T(512)S(1)} %broadcast_multiply_fusion), kind=kLoop, calls=%fused_computation.23 | loop fusion | flops 7863936 | bytes 3935232 | tf_op jit(solution)/shard_map/reduce_sum | solution.py:89
  88.4 36.3 %all-gather.4.cloned.1.call-done = bf16[5120,3,384]{2,0,1:T(8,128)(2,1)} async-done(((bf16[320,3,384]{2,0,1:T(8,128)(2,1)}), bf16[5120,3,384]{2,0,1:T(8,128)(2,1)}) %all-gather.4.cloned.1.call-update) | async-done | bytes 11796496 | tf_op jit(solution)/shard_map/all_gather | solution.py:95
  124.7 16.1 %copy.49 = bf16[8,640,3,384]{1,0,3,2:T(8,128)(2,1)} copy(bf16[8,640,3,384]{3,1,0,2:T(8,128)(2,1)} %bitcast.97) | data formatting | bytes 23592960 | tf_op jit(solution)/shard_map/reshape | solution.py:99
  140.8 10.8 %fusion.28 = f32[384,3,3,128]{0,3,2,1:T(8,128)S(1)} fusion(bf16[3,3,128,640,8]{3,4,2,1,0:T(8,128)(2,1)} %bitcast.98, bf16[8,384,640]{2,1,0:T(8,128)(2,1)} %all-to-all-done, f32[8,640]{1,0:T(8,128)S(1)} %add.177, f32[8,640]{1,0:T(8,128)S(1)} %add.176, f32[384]{0:T(512)S(1)} %add_rsqrt_fusion.2, f32[384]{0:T(512)S(1)} %broadcast_multiply_fusion), kind=kOutput, calls=%fused_computation.37 | convolution fusion | flops 4541644800 | bytes 17542144 | tf_op jit(solution)/shard_map/itf,ifqe->tqe/dot_general | solution.py:96
  151.8 0.7 fusion.37
  152.5 0.9 pad_maximum_fusion
  153.4 34.6 %all-gather.6.cloned.1.call-done = bf16[1536,2,3,128]{0,3,2,1:T(8,128)(2,1)} async-done(((bf16[384,2,3,128]{0,3,2,1:T(8,128)(2,1)}), bf16[1536,2,3,128]{0,3,2,1:T(8,128)(2,1)}) %all-gather.6.cloned.1.call-update) | async-done | bytes 2359312 | tf_op jit(solution)/shard_map/all_gather | solution.py:116
  188.1 0.2 reduce-window.8
  188.5 1.4 fusion.36
  189.9 1.9 copy.37
  191.7 2.0 constant_dynamic-update-slice_fusion.1
  193.7 2.0 constant_dynamic-update-slice_fusion
  195.7 1.7 slice_bitcast_fusion
  197.5 17.6 %while.16 = (s32[]{:T(128)}, f32[384,3,128]{0,2,1:T(8,128)S(1)}, f32[3,384]{1,0:T(4,128)S(1)}, bf16[3072,3,128]{0,2,1:T(8,128)(2,1)S(1)}, s32[384]{0:T(512)S(1)}...) while((s32[]{:T(128)}, f32[384,3,128]{0,2,1:T(8,128)S(1)}, ...), condition=%wide.region_9.10_spmd.clone, body=%wide.region_7.9_spmd.clone.sunk | while | flops 306021504 | bytes 7595714 | solution.py:159
  197.5 0.2 broadcast_compare_fusion.2
  197.7 1.9 fusion.74
  199.7 0.7 fusion.75
  200.5 0.2 broadcast_compare_fusion.2
  200.6 1.9 fusion.74
  202.6 0.7 fusion.75
  203.4 0.2 broadcast_compare_fusion.2
  203.6 2.0 fusion.74
  205.5 0.7 fusion.75
  206.3 0.2 broadcast_compare_fusion.2
  206.5 1.9 fusion.74
  208.5 0.7 fusion.75
  209.3 0.2 broadcast_compare_fusion.2
  209.5 1.9 fusion.74
  211.4 0.7 fusion.75
  212.2 0.2 broadcast_compare_fusion.2
  212.4 1.9 fusion.74
  214.3 0.7 fusion.75
  215.1 0.2 reshape.159
  215.3 11.5 %all-gather.8.cloned.1.call-done = bf16[384,5120]{0,1:T(8,128)(2,1)} async-done(((bf16[384,320]{0,1:T(8,128)(2,1)}), bf16[384,5120]{0,1:T(8,128)(2,1)}) %all-gather.8.cloned.1.call-update) | async-done | bytes 3932176 | tf_op jit(solution)/shard_map/all_gather | solution.py:166
  226.8 6.3 %convolution_convert_fusion = bf16[2,192,8,640]{3,1,2,0:T(8,128)(2,1)} fusion(bf16[384,8,640,1]{0,2,1,3:T(8,128)(2,1)} %bitcast.99, bf16[2,192,384,1]{1,0,2,3:T(2,128)(2,1)S(1)} %bitcast.101), kind=kOutput, calls=%fused_computation.34 | convolution fusion | flops 1511915520 | bytes 8159232 | tf_op jit(solution)/shard_map/rte,ebn->rbtn/dot_general | solution.py:167
  233.1 6.7 %all-to-all-start.1 = ((bf16[16,192,640]{2,1,0:T(8,128)(2,1)}), bf16[16,192,640]{2,1,0:T(8,128)(2,1)}, u32[]{:S(2)}, u32[]{:S(2)}) async-start(bf16[16,192,640]{2,1,0:T(8,128)(2,1)} %bitcast.96), calls=%async_computation.1 | async-start | bytes 7864320 | tf_op jit(solution)/shard_map/all_to_all | solution.py:173
  239.9 60.2 %all-to-all-done.1 = bf16[16,192,640]{2,1,0:T(8,128)(2,1)} async-done(((bf16[16,192,640]{2,1,0:T(8,128)(2,1)}), bf16[16,192,640]{2,1,0:T(8,128)(2,1)}, u32[]{:S(2)}, u32[]{:S(2)}) %all-to-all-start.1) | async-done | bytes 3932192 | tf_op jit(solution)/shard_map/all_to_all | solution.py:173
  300.1 2.9 convert_element_type.60
  303.0 0.4 slice_reduce_fusion
  303.4 0.9 add_bitcast_fusion
  (49 shorter events, 1.3 us)
Async XLA Ops:
  6.5 118.2 %all-gather.4.cloned.1.call-start = ((), (), s32[]{:S(2)}) async-start(), calls=%async_computation.2 | async-start | bytes 12533760 | tf_op jit(solution)/shard_map/all_gather | solution.py:95
  10.6 8.1 %copy-start = (bf16[1,384,640]{2,1,0:T(8,128)(2,1)S(1)}, bf16[1,384,640]{2,1,0:T(8,128)(2,1)}, u32[]{:S(2)}) copy-start(bf16[1,384,640]{2,1,0:T(8,128)(2,1)} %param.11) | copy-start | bytes 1474564
  10.6 9.2 %copy-start.2 = (f32[3,5120]{1,0:T(4,128)S(1)}, f32[3,5120]{1,0:T(4,128)}, u32[]{:S(2)}) copy-start(f32[3,5120]{1,0:T(4,128)} %param.12) | copy-start | bytes 184324
  10.6 10.1 %copy-start.3 = (s32[3,384]{1,0:T(4,128)S(1)}, s32[3,384]{1,0:T(4,128)}, u32[]{:S(2)}) copy-start(s32[3,384]{1,0:T(4,128)} %param.16) | copy-start | bytes 13828
  10.6 10.1 %copy-start.4 = (f32[3,128]{1,0:T(4,128)S(1)}, f32[3,128]{1,0:T(4,128)}, u32[]{:S(2)}) copy-start(f32[3,128]{1,0:T(4,128)} %constant.131.clone) | copy-start | bytes 4612
  10.6 71.7 %all-to-all-start = ((bf16[8,384,640]{2,1,0:T(8,128)(2,1)}), bf16[8,384,640]{2,1,0:T(8,128)(2,1)}, u32[]{:S(2)}, u32[]{:S(2)}) async-start(bf16[8,384,640]{2,1,0:T(8,128)(2,1)} %broadcast_in_dim.69), calls=%async_computation | async-start | bytes 7864320 | tf_op jit(solution)/shard_map/all_to_all | solution.py:84
  18.6 169.4 %all-gather.6.cloned.1.call-start = ((), (), s32[]{:S(2)}) async-start(), calls=%async_computation.3 | async-start | bytes 2949120 | tf_op jit(solution)/shard_map/all_gather | solution.py:116
  18.7 63.4 %collective-permute-start = (bf16[192,640]{1,0:T(8,128)(2,1)S(1)}, bf16[192,640]{1,0:T(8,128)(2,1)S(1)}, u32[]{:S(2)}, u32[]{:S(2)}) collective-permute-start(bf16[192,640]{1,0:T(8,128)(2,1)S(1)} %dynamic-slice_bitcast_fusion), channel_id=1, source_target_pairs={{0,64},{64,0},{1,65},{65,1},{2,66},{66,2},{3,67},{67,3},{4,68},{68... | collective-permute-start | bytes 737288 | tf_op jit(solution)/shard_map/ppermute | solution.py:75
  140.7 11.0 %copy-start.1 = (f32[128,128,1]{1,0,2:T(8,128)S(1)}, f32[128,128,1]{1,0,2:T(8,128)}, u32[]{:S(2)}) copy-start(f32[128,128,1]{1,0,2:T(8,128)} %constant.134) | copy-start | bytes 196612
  151.6 36.5 %copy-start.5 = (s32[5]{0:T(128)S(1)}, s32[5]{0:T(128)}, u32[]{:S(2)}) copy-start(s32[5]{0:T(128)} %param.15) | copy-start | bytes 64
  153.4 73.4 %all-gather.8.cloned.1.call-start = ((), (), s32[]{:S(2)}) async-start(), calls=%async_computation.4 | async-start | bytes 4177920 | tf_op jit(solution)/shard_map/all_gather | solution.py:166
  188.0 5.7 %collective-permute-start.1 = (bf16[1536,2,3,128]{0,3,2,1:T(8,128)(2,1)}, bf16[1536,2,3,128]{0,3,2,1:T(8,128)(2,1)}, u32[]{:S(2)}, u32[]{:S(2)}) collective-permute-start(bf16[1536,2,3,128]{0,3,2,1:T(8,128)(2,1)} %all-gather.6.cloned.1.call-done), channel_id=1, source_target_pairs={{0,8},{8,0},{1,9},{9,1},{2,10},{10,2},{3,11},{11,3},{4,12},{12,4},... | collective-permute-start | bytes 7077896 | tf_op jit(solution)/shard_map/ppermute | solution.py:117
  233.1 67.0 %all-to-all-start.1 = ((bf16[16,192,640]{2,1,0:T(8,128)(2,1)}), bf16[16,192,640]{2,1,0:T(8,128)(2,1)}, u32[]{:S(2)}, u32[]{:S(2)}) async-start(bf16[16,192,640]{2,1,0:T(8,128)(2,1)} %bitcast.96), calls=%async_computation.1 | async-start | bytes 7864320 | tf_op jit(solution)/shard_map/all_to_all | solution.py:173
Sparse Core Ops, SparseCore 0:
  9.0 115.6 all-gather.3
  153.5 34.4 all-gather.5
  189.7 37.0 all-gather.7

commit v3 on v2

--- a/solution.py
+++ b/solution.py
@@ -2,6 +2,7 @@
 import jax.numpy as jnp
 import numpy as np
 from jax import lax
+from jax.experimental.layout import Layout, with_layout_constraint
 from jax.sharding import Mesh, PartitionSpec as P
 
 HEAD_DIM = 128
@@ -99,6 +100,7 @@
         piece.reshape(n_blk, feat_width, 3, inner_width),
         preferred_element_type=jnp.float32,
     )
+    mixed = with_layout_constraint(mixed, Layout((0, 1, 2)))
     mixed = mixed.reshape(tok_count, 3, head_count, HEAD_DIM)
 
     angle_table = jnp.asarray(rotary_angles(HEAD_DIM))
@@ -163,20 +165,20 @@
         .reshape(tok_count, inner_width)
     )
 
-    out_piece = lax.all_gather(out_projection, ("cfg",) + SEQ, axis=1, tiled=True)
-    partial = jnp.einsum(
-        "rte,ebn->rbtn",
-        attended.reshape(2, half_rows, inner_width),
-        out_piece.reshape(inner_width, n_blk, feat_width),
-        preferred_element_type=jnp.float32,
-    ).astype(jnp.bfloat16)
-    arrived = lax.all_to_all(
-        partial.reshape(2 * n_blk, half_rows, feat_width), ("cfg",) + BLK, 0, 0, tiled=False
-    ).astype(jnp.float32)
-    cond_sum = jnp.sum(arrived[:n_blk], 0)
-    uncond_sum = jnp.sum(arrived[n_blk:], 0)
+    sent_att = lax.dynamic_slice_in_dim(attended, (1 - cfg) * half_rows, half_rows, 0)
+    other_att = lax.ppermute(sent_att, "cfg", SWAP)
+    mine_att = lax.dynamic_slice_in_dim(attended, cfg * half_rows, half_rows, 0)
+    cond_att = jnp.where(is_cond, mine_att, other_att)
+    uncond_att = jnp.where(is_cond, other_att, mine_att)
+    out_piece = lax.all_gather(out_projection, ("cfg",) + SEQ, axis=1, tiled=True).reshape(
+        inner_width, n_blk, feat_width
+    )
+    cond_part = jnp.einsum("te,ebn->btn", cond_att, out_piece, preferred_element_type=jnp.float32)
+    uncond_part = jnp.einsum("te,ebn->btn", uncond_att, out_piece, preferred_element_type=jnp.float32)
+    partial = (uncond_part + scale * (cond_part - uncond_part)).astype(jnp.bfloat16)
+    arrived = lax.all_to_all(partial, BLK, 0, 0, tiled=False).astype(jnp.float32)
     gate = lax.dynamic_slice_in_dim(modulation[2], blk * feat_width, feat_width, 0)
-    projected = gate * (uncond_sum + scale * (cond_sum - uncond_sum))
+    projected = gate * jnp.sum(arrived, 0)
     guided = hidden_part + projected
     return guided.reshape(1, 1, half_rows, feat_width)
 

time: 312 us -> 266 us (0.85)
  waiting for transfers between devices: 204 us -> 161 us
  local copies, waits for them, and re-layouts: 27.7 us -> 16.5 us
  matrix products: 36.1 us -> 42.6 us
    all_to_all x1, waiting for transfers between devices: 60.2 us -> 26.1 us  [local(): lax.all_to_all(partial, BLK, 0, 0, tiled=False).astype(jnp.float32)]
    reshape x1 -> x0, local copies, waits for them, and re-layouts: 16.1 us -> none  [local(): piece.reshape(n_blk, feat_width, 3, inner_width)]
    all_gather x1, waiting for transfers between devices: 11.5 us -> 0.19 us  [local(): lax.all_gather(out_projection, ('cfg',) + SEQ, axis=1, tiled=True)]
    dot_general x6, matrix products: 4.14 us -> 10.4 us  [key_step(): jnp.einsum('hqk,khd->qhd', weights.astype(jnp.bfloat16), value_slab, pref...]
    ppermute x0 -> x1, waiting for transfers between devices: none -> 4.31 us  [local(): other_att = lax.ppermute(sent_att, 'cfg', SWAP)]
    dynamic_slice x6, local copies, waits for them, and re-layouts: 0.46 us -> 4.52 us  [key_step(): lax.dynamic_slice_in_dim(key_clip_all, block_index * key_block_size, key_...]
    dot_general x1 -> x2, matrix products: 6.3 us -> 6.68 us  [the longest x1 3.78 us: local(): jnp.einsum('te,ebn->btn', uncond_att, out_piece, preferred_element_type=j...]
  transfers between devices with their start and end apart: 7 -> 8, of which waited for: 5 -> 6; matrix products, arithmetic and copies ran while one was open for 12% -> 19% of each run, Pallas kernels for 0% -> 0%
where the time goes in v3:
time: 266 us; the launch traced here: 265 us
  waiting for transfers between devices  161 us (61%)
  matrix products  42.6 us (16%)
  starting transfers between devices  17.8 us (7%)
  local copies, waits for them, and re-layouts  16.5 us (6%)
  between operations  14.1 us (5%)
  other arithmetic  12.4 us (5%)
    ppermute x1, waiting for transfers between devices, local(): other_rows = lax.ppermute(sent_rows, 'cfg', SWAP)  59.5 us
    all_gather x1, waiting for transfers between devices, local(): piece = lax.all_gather(in_projection, ('cfg',) + SEQ, axis=0, tiled=True)  35.6 us
    all_gather x1, waiting for transfers between devices, local(): kv_mine = lax.all_gather(kv, 'x', axis=0, tiled=True)  34.6 us
    all_to_all x1, waiting for transfers between devices, local(): lax.all_to_all(partial, BLK, 0, 0, tiled=False).astype(jnp.float32)  26.1 us
    dot_general x1, matrix products, local(): jnp.einsum('itf,ifqe->tqe', modulated, piece.reshape(n_blk, feat_width, 3...  10.9 us
    dot_general x6, matrix products, key_step(): jnp.einsum('qhd,khd->hqk', queries, key_slab, preferred_element_type=jnp....  10.5 us
    dot_general x6, matrix products, key_step(): jnp.einsum('hqk,khd->qhd', weights.astype(jnp.bfloat16), value_slab, pref...  10.4 us
    all_to_all x1, starting transfers between devices, local(): full_states = lax.all_to_all(spread, BLK, 0, 0, tiled=False)  8.04 us
  transfers between devices with their start and end apart: 8, of which 6 were waited for; matrix products, arithmetic and copies ran while one was open for 19% of the time, Pallas kernels for 0%

profile of v3, /device:TPU:0, one launch (start us, length us, event | category | flops | bytes accessed | tf_op | source)
XLA Modules:
  0.0 264.7 jit_solution(9140397845163269127)
XLA Ops:
  6.5 0.7 all-gather.4.cloned.1.call-update
  7.3 3.2 %broadcast_in_dim.69 = bf16[8,384,640]{2,1,0:T(8,128)(2,1)} broadcast(bf16[384,640]{1,0:T(8,128)(2,1)} %bitcast.102), dimensions={1,2} | broadcast | bytes 4423680 | tf_op jit(solution)/shard_map/broadcast_in_dim | solution.py:84
  10.5 8.0 %all-to-all-start = ((bf16[8,384,640]{2,1,0:T(8,128)(2,1)}), bf16[8,384,640]{2,1,0:T(8,128)(2,1)}, u32[]{:S(2)}, u32[]{:S(2)}) async-start(bf16[8,384,640]{2,1,0:T(8,128)(2,1)} %broadcast_in_dim.69), calls=%async_computation | async-start | bytes 7864320 | tf_op jit(solution)/shard_map/all_to_all | solution.py:85
  18.6 1.1 collective-permute-start
  19.7 0.6 add_reduce_fusion
  21.1 1.1 cosine_bitcast_fusion
  22.4 59.5 %collective-permute-done = bf16[192,640]{1,0:T(8,128)(2,1)S(1)} collective-permute-done((bf16[192,640]{1,0:T(8,128)(2,1)S(1)}, bf16[192,640]{1,0:T(8,128)(2,1)S(1)}, u32[]{:S(2)}, u32[]{:S(2)}) %collective-permute-start) | collective-permute-done | bytes 245792 | tf_op jit(solution)/shard_map/ppermute | solution.py:76
  81.9 0.9 convert_add_fusion
  82.8 2.8 %convert_reduce_fusion = f32[384]{0:T(512)S(1)} fusion(bf16[8,384,640]{2,1,0:T(8,128)(2,1)} %all-to-all-done), kind=kLoop, calls=%fused_computation.18 | loop fusion | flops 3931776 | bytes 3933696 | tf_op jit(solution)/shard_map/reduce_sum | solution.py:88
  85.6 3.4 %fusion.16 = f32[384]{0:T(512)S(1)} fusion(bf16[8,384,640]{2,1,0:T(8,128)(2,1)} %all-to-all-done, f32[384]{0:T(512)S(1)} %broadcast_multiply_fusion), kind=kLoop, calls=%fused_computation.21 | loop fusion | flops 7863936 | bytes 3935232 | tf_op jit(solution)/shard_map/reduce_sum | solution.py:90
  89.1 35.6 %all-gather.4.cloned.1.call-done = bf16[5120,3,384]{2,0,1:T(8,128)(2,1)} async-done(((bf16[320,3,384]{2,0,1:T(8,128)(2,1)}), bf16[5120,3,384]{2,0,1:T(8,128)(2,1)}) %all-gather.4.cloned.1.call-update) | async-done | bytes 11796496 | tf_op jit(solution)/shard_map/all_gather | solution.py:96
  124.6 10.9 %fusion.21 = f32[384,3,384,1]{0,2,3,1:T(8,128)S(1)} fusion(bf16[8,640,3,384]{3,1,0,2:T(8,128)(2,1)} %bitcast.109, bf16[8,384,640]{2,1,0:T(8,128)(2,1)} %all-to-all-done, f32[8,640]{1,0:T(8,128)S(1)} %add.179, f32[8,640]{1,0:T(8,128)S(1)} %add.178, f32[384]{0:T(512)S(1)} %add_rsqrt_fusion.2, f32[384]{0:T(512)S(1)} %broadcast_multiply_fusion), kind=kOutput, calls=%fused_computation.26 | convolution fusion | flops 4541644800 | bytes 17542144 | tf_op jit(solution)/shard_map/itf,ifqe->tqe/dot_general | solution.py:97
  135.5 0.9 fusion.62
  137.2 0.7 fusion.34
  137.9 0.9 pad_maximum_fusion
  138.9 34.6 %all-gather.6.cloned.1.call-done = bf16[1536,2,3,128]{3,0,2,1:T(8,128)(2,1)} async-done(((bf16[384,2,3,128]{3,0,2,1:T(8,128)(2,1)}), bf16[1536,2,3,128]{3,0,2,1:T(8,128)(2,1)}) %all-gather.6.cloned.1.call-update) | async-done | bytes 2359312 | tf_op jit(solution)/shard_map/all_gather | solution.py:118
  173.8 0.7 convert_reduce_fusion.2
  174.5 1.3 copy.56
  176.1 2.5 fusion.33
  178.7 2.0 constant_dynamic-update-slice_fusion
  180.7 2.4 slice_bitcast_fusion
  183.1 26.8 %while.16 = (s32[]{:T(128)}, f32[384,3,128]{0,2,1:T(8,128)S(1)}, f32[3,384]{1,0:T(4,128)S(1)}, bf16[3072,3,128]{2,0,1:T(8,128)(2,1)}, s32[384]{0:T(512)S(1)}, /*...) while((s32[]{:T(128)}, f32[384,3,128]{0,2,1:T(8,128)S(1)}, ...), condition=%wide.region_9.10_spmd.clone, body=%wide.region_7.9_spmd.clone.sunk | while | flops 306021504 | bytes 7595706 | solution.py:161
  183.1 0.7 dynamic_slice.66
  184.0 1.7 fusion.80
  185.8 1.7 fusion.81
  187.6 0.7 dynamic_slice.66
  188.5 1.8 fusion.80
  190.2 1.7 fusion.81
  192.0 0.8 dynamic_slice.66
  193.0 1.8 fusion.80
  194.7 1.7 fusion.81
  196.5 0.8 dynamic_slice.66
  197.4 1.8 fusion.80
  199.2 1.7 fusion.81
  201.0 0.8 dynamic_slice.66
  201.9 1.7 fusion.80
  203.6 1.7 fusion.81
  205.4 0.8 dynamic_slice.66
  206.4 1.7 fusion.80
  208.1 1.7 fusion.81
  210.3 1.6 collective-permute-start.2
  212.2 4.3 %collective-permute-done.2 = bf16[192,384]{1,0:T(8,128)(2,1)S(1)} collective-permute-done((bf16[192,384]{1,0:T(8,128)(2,1)S(1)}, bf16[192,384]{1,0:T(8,128)(2,1)S(1)}, u32[]{:S(2)}, u32[]{:S(2)}) %collective-permute-start.2) | collective-permute-done | bytes 147488 | tf_op jit(solution)/shard_map/ppermute | solution.py:169
  216.6 3.8 %fusion.41 = f32[192,8,640]{2,0,1:T(8,128)S(1)} fusion(bf16[384,8,640]{0,2,1:T(8,128)(2,1)} %bitcast.100, bf16[192,384]{1,0:T(8,128)(2,1)S(1)} %collective-permute-done.2, bf16[192,384]{1,0:T(8,128)(2,1)S(1)} %copy.53, pred[]{:T(512)S(6)} %eq.39), kind=kOutput, calls=%fused_computation.65 | convolution fusion | flops 755048448 | bytes 8159233 | tf_op jit(solution)/shard_map/te,ebn->btn/dot_general | solution.py:177
  220.3 2.9 %fusion.25 = bf16[8,192,640]{2,1,0:T(8,128)(2,1)} fusion(f32[192,8,640]{2,0,1:T(8,128)S(1)} %fusion.41, bf16[384,8,640]{0,2,1:T(8,128)(2,1)S(1)} %bitcast.101, f32[]{:T(128)} %bitcast.99, bf16[192,384]{1,0:T(8,128)(2,1)S(1)} %copy.53, bf16[192,384]{1,0:T(8,128)(2,1)S(1)} %collective-permute-done.2, pred[]{:T(512)S(6)} %eq.39), kind=kOutput, calls=%fused_computation.30 | convolution fusion | flops 758980608 | bytes 10125317 | tf_op jit(solution)/shard_map/te,ebn->btn/dot_general | solution.py:176
  223.3 7.0 %all-to-all-start.1 = ((bf16[8,192,640]{2,1,0:T(8,128)(2,1)}), bf16[8,192,640]{2,1,0:T(8,128)(2,1)S(1)}, u32[]{:S(2)}, u32[]{:S(2)}) async-start(bf16[8,192,640]{2,1,0:T(8,128)(2,1)} %fusion.25), calls=%async_computation.1 | async-start | bytes 3932160 | tf_op jit(solution)/shard_map/all_to_all | solution.py:179
  230.2 0.7 dynamic-slice_reduce_fusion
  230.9 26.1 %all-to-all-done.1 = bf16[8,192,640]{2,1,0:T(8,128)(2,1)S(1)} async-done(((bf16[8,192,640]{2,1,0:T(8,128)(2,1)}), bf16[8,192,640]{2,1,0:T(8,128)(2,1)S(1)}, u32[]{:S(2)}, u32[]{:S(2)}) %all-to-all-start.1) | async-done | bytes 1966112 | tf_op jit(solution)/shard_map/all_to_all | solution.py:179
  257.3 0.9 add_bitcast_fusion
  (71 shorter events, 4.0 us)
Async XLA Ops:
  6.5 118.1 %all-gather.4.cloned.1.call-start = ((), (), s32[]{:S(2)}) async-start(), calls=%async_computation.2 | async-start | bytes 12533760 | tf_op jit(solution)/shard_map/all_gather | solution.py:96
  10.5 8.1 %copy-start.2 = (bf16[1,384,640]{2,1,0:T(8,128)(2,1)S(1)}, bf16[1,384,640]{2,1,0:T(8,128)(2,1)}, u32[]{:S(2)}) copy-start(bf16[1,384,640]{2,1,0:T(8,128)(2,1)} %param.11) | copy-start | bytes 1474564
  10.5 9.2 %copy-start.8 = (f32[3,5120]{1,0:T(4,128)S(1)}, f32[3,5120]{1,0:T(4,128)}, u32[]{:S(2)}) copy-start(f32[3,5120]{1,0:T(4,128)} %param.12) | copy-start | bytes 184324
  10.5 10.6 %copy-start.9 = (s32[3,384]{1,0:T(4,128)S(1)}, s32[3,384]{1,0:T(4,128)}, u32[]{:S(2)}) copy-start(s32[3,384]{1,0:T(4,128)} %param.16) | copy-start | bytes 13828
  10.5 10.6 %copy-start.10 = (f32[3,128]{1,0:T(4,128)S(1)}, f32[3,128]{1,0:T(4,128)}, u32[]{:S(2)}) copy-start(f32[3,128]{1,0:T(4,128)} %constant.131.clone) | copy-start | bytes 4612
  10.5 72.3 %all-to-all-start = ((bf16[8,384,640]{2,1,0:T(8,128)(2,1)}), bf16[8,384,640]{2,1,0:T(8,128)(2,1)}, u32[]{:S(2)}, u32[]{:S(2)}) async-start(bf16[8,384,640]{2,1,0:T(8,128)(2,1)} %broadcast_in_dim.69), calls=%async_computation | async-start | bytes 7864320 | tf_op jit(solution)/shard_map/all_to_all | solution.py:85
  18.5 154.9 %all-gather.6.cloned.1.call-start = ((), (), s32[]{:S(2)}) async-start(), calls=%async_computation.3 | async-start | bytes 2949120 | tf_op jit(solution)/shard_map/all_gather | solution.py:118
  18.6 63.3 %collective-permute-start = (bf16[192,640]{1,0:T(8,128)(2,1)S(1)}, bf16[192,640]{1,0:T(8,128)(2,1)S(1)}, u32[]{:S(2)}, u32[]{:S(2)}) collective-permute-start(bf16[192,640]{1,0:T(8,128)(2,1)S(1)} %dynamic-slice_bitcast_fusion), channel_id=1, source_target_pairs={{0,64},{64,0},{1,65},{65,1},{2,66},{66,2},{3,67},{67,3},{4,68},{68... | collective-permute-start | bytes 737288 | tf_op jit(solution)/shard_map/ppermute | solution.py:76
  22.3 114.9 %copy-start.4 = (f32[384,128]{1,0:T(8,128)}, f32[384,128]{1,0:T(8,128)S(1)}, u32[]{:S(2)}) copy-start(f32[384,128]{1,0:T(8,128)S(1)} %copy.37) | copy-start | bytes 589828
  22.4 114.8 %copy-start.5 = (f32[384,128]{1,0:T(8,128)}, f32[384,128]{1,0:T(8,128)S(1)}, u32[]{:S(2)}) copy-start(f32[384,128]{1,0:T(8,128)S(1)} %copy.38) | copy-start | bytes 589828
  135.5 1.7 copy-start.7
  135.5 38.0 %copy-start.11 = (s32[5]{0:T(128)S(1)}, s32[5]{0:T(128)}, u32[]{:S(2)}) copy-start(s32[5]{0:T(128)} %param.15) | copy-start | bytes 64
  138.8 73.4 %all-gather.8.cloned.1.call-start = ((), (), s32[]{:S(2)}) async-start(), calls=%async_computation.4 | async-start | bytes 4177920 | tf_op jit(solution)/shard_map/all_gather | solution.py:173
  173.5 5.1 %copy-start.1 = (bf16[1536,2,3,128]{3,0,2,1:T(8,128)(2,1)S(1)}, bf16[1536,2,3,128]{3,0,2,1:T(8,128)(2,1)}, u32[]{:S(2)}) copy-start(bf16[1536,2,3,128]{3,0,2,1:T(8,128)(2,1)} %all-gather.6.cloned.1.call-done) | copy-start | bytes 7077892
  173.5 5.2 %collective-permute-start.1 = (bf16[1536,2,3,128]{3,0,2,1:T(8,128)(2,1)}, bf16[1536,2,3,128]{3,0,2,1:T(8,128)(2,1)}, u32[]{:S(2)}, u32[]{:S(2)}) collective-permute-start(bf16[1536,2,3,128]{3,0,2,1:T(8,128)(2,1)} %all-gather.6.cloned.1.call-done), channel_id=1, source_target_pairs={{0,8},{8,0},{1,9},{9,1},{2,10},{10,2},{3,11},{11,3},{4,12},{12,4},... | collective-permute-start | bytes 7077896 | tf_op jit(solution)/shard_map/ppermute | solution.py:119
  180.7 2.4 copy-start.6
  210.3 6.3 %collective-permute-start.2 = (bf16[192,384]{1,0:T(8,128)(2,1)S(1)}, bf16[192,384]{1,0:T(8,128)(2,1)S(1)}, u32[]{:S(2)}, u32[]{:S(2)}) collective-permute-start(bf16[192,384]{1,0:T(8,128)(2,1)S(1)} %copy.52), channel_id=1, source_target_pairs={{0,64},{64,0},{1,65},{65,1},{2,66},{66,2},{3,67},{67,3},{4,68},{68... | collective-permute-start | bytes 442376 | tf_op jit(solution)/shard_map/ppermute | solution.py:169
  216.5 3.8 %copy-start = (bf16[384,5120]{0,1:T(8,128)(2,1)S(1)}, bf16[384,5120]{0,1:T(8,128)(2,1)}, u32[]{:S(2)}) copy-start(bf16[384,5120]{0,1:T(8,128)(2,1)} %all-gather.8.cloned.1.call-done) | copy-start | bytes 11796484
  223.2 34.1 %copy-start.3 = (f32[192,640]{1,0:T(8,128)S(1)}, f32[192,640]{1,0:T(8,128)}, u32[]{:S(2)}) copy-start(f32[192,640]{1,0:T(8,128)} %convert_add_fusion) | copy-start | bytes 1474564
  223.3 33.8 %all-to-all-start.1 = ((bf16[8,192,640]{2,1,0:T(8,128)(2,1)}), bf16[8,192,640]{2,1,0:T(8,128)(2,1)S(1)}, u32[]{:S(2)}, u32[]{:S(2)}) async-start(bf16[8,192,640]{2,1,0:T(8,128)(2,1)} %fusion.25), calls=%async_computation.1 | async-start | bytes 3932160 | tf_op jit(solution)/shard_map/all_to_all | solution.py:179
Sparse Core Ops, SparseCore 0:
  9.0 115.5 all-gather.3
  138.9 34.4 all-gather.5
  175.2 37.0 all-gather.7

commit v4 on v3

--- a/solution.py
+++ b/solution.py
@@ -93,11 +93,23 @@
     mod_scale = modulation[1].reshape(n_blk, 1, feat_width)
     modulated = (normed * (1.0 + mod_scale) + mod_shift).astype(jnp.bfloat16)
 
-    piece = lax.all_gather(in_projection, ("cfg",) + SEQ, axis=0, tiled=True)
+    shard_other = lax.ppermute(in_projection, "cfg", SWAP)
+    stacked = jnp.stack(
+        [
+            jnp.where(is_cond, in_projection, shard_other),
+            jnp.where(is_cond, shard_other, in_projection),
+        ]
+    )
+    piece = lax.all_gather(stacked, SEQ, axis=0, tiled=False)
+    n_seq = piece.shape[0]
+    rows = in_projection.shape[0]
+    per_blk = feat_width // rows
+    mod_perm = modulated.reshape(2, n_blk // 2, tok_count, per_blk, rows).transpose(2, 1, 3, 0, 4)
+    mod_perm = mod_perm.reshape(tok_count, n_seq, 2, rows)
     mixed = jnp.einsum(
-        "itf,ifqe->tqe",
-        modulated,
-        piece.reshape(n_blk, feat_width, 3, inner_width),
+        "tabi,abiqe->tqe",
+        mod_perm,
+        piece,
         preferred_element_type=jnp.float32,
     )
     mixed = with_layout_constraint(mixed, Layout((0, 1, 2)))

time: 266 us -> 247 us (0.929)
  waiting for transfers between devices: 161 us -> 131 us
  other arithmetic: 12.4 us -> 20.6 us
    all_gather x1, waiting for transfers between devices: 35.6 us -> 0.01 us  [local(): piece = lax.all_gather(stacked, SEQ, axis=0, tiled=False)]
    ppermute x0 -> x1, waiting for transfers between devices: none -> 16.7 us  [local(): shard_other = lax.ppermute(in_projection, 'cfg', SWAP)]
    ppermute x1, waiting for transfers between devices: 59.5 us -> 44.3 us  [local(): other_rows = lax.ppermute(sent_rows, 'cfg', SWAP)]
    convert_element_type x0 -> x1, other arithmetic: none -> 5.83 us  [local(): modulated = (normed * (1.0 + mod_scale) + mod_shift).astype(jnp.bfloat16)]
    all_gather x1, waiting for transfers between devices: 34.6 us -> 39.3 us  [local(): kv_mine = lax.all_gather(kv, 'x', axis=0, tiled=True)]
  transfers between devices with their start and end apart: 8 -> 9, of which waited for: 6 -> 5; matrix products, arithmetic and copies ran while one was open for 19% -> 22% of each run, Pallas kernels for 0% -> 0%
where the time goes in v4:
time: 247 us; the launch traced here: 245 us
  waiting for transfers between devices  131 us (53%)
  matrix products  41.7 us (17%)
  other arithmetic  20.6 us (8%)
  starting transfers between devices  19.6 us (8%)
  local copies, waits for them, and re-layouts  15.9 us (6%)
  between operations  15.8 us (6%)
    ppermute x1, waiting for transfers between devices, local(): other_rows = lax.ppermute(sent_rows, 'cfg', SWAP)  44.3 us
    all_gather x1, waiting for transfers between devices, local(): kv_mine = lax.all_gather(kv, 'x', axis=0, tiled=True)  39.3 us
    all_to_all x1, waiting for transfers between devices, local(): lax.all_to_all(partial, BLK, 0, 0, tiled=False).astype(jnp.float32)  26.2 us
    ppermute x1, waiting for transfers between devices, local(): shard_other = lax.ppermute(in_projection, 'cfg', SWAP)  16.7 us
    dot_general x6, matrix products, key_step(): jnp.einsum('hqk,khd->qhd', weights.astype(jnp.bfloat16), value_slab, pref...  10.4 us
    dot_general x6, matrix products, key_step(): jnp.einsum('qhd,khd->hqk', queries, key_slab, preferred_element_type=jnp....  10.4 us
    dot_general x1, matrix products, local(): jnp.einsum('tabi,abiqe->tqe', mod_perm, piece, preferred_element_type=jnp...  10.1 us
    all_to_all x1, starting transfers between devices, local(): full_states = lax.all_to_all(spread, BLK, 0, 0, tiled=False)  7.74 us
  transfers between devices with their start and end apart: 9, of which 5 were waited for; matrix products, arithmetic and copies ran while one was open for 22% of the time, Pallas kernels for 0%

profile of v4, /device:TPU:0, one launch (start us, length us, event | category | flops | bytes accessed | tf_op | source)
XLA Modules:
  0.0 245.1 jit_solution(10611775338479566306)
XLA Ops:
  7.4 2.0 collective-permute-start.1
  9.4 16.7 %collective-permute-done.1 = bf16[320,3,384]{2,0,1:T(8,128)(2,1)S(1)} collective-permute-done((bf16[320,3,384]{2,0,1:T(8,128)(2,1)}, bf16[320,3,384]{2,0,1:T(8,128)(2,1)S(1)}, u32[]{:S(2)}, u32[]{:S(2)}) %collective-permute-start.1) | collective-permute-done | bytes 737312 | tf_op jit(solution)/shard_map/ppermute | solution.py:96
  26.1 1.3 select_bitcast_fusion.1
  27.4 1.3 pad_maximum_fusion
  29.0 2.2 broadcast_in_dim.69
  31.2 7.7 %all-to-all-start = ((bf16[8,384,640]{1,2,0:T(8,128)(2,1)}), bf16[8,384,640]{1,2,0:T(8,128)(2,1)}, u32[]{:S(2)}, u32[]{:S(2)}) async-start(bf16[8,384,640]{1,2,0:T(8,128)(2,1)} %broadcast_in_dim.69), calls=%async_computation | async-start | bytes 7864320 | tf_op jit(solution)/shard_map/all_to_all | solution.py:85
  39.0 1.1 collective-permute-start
  41.5 1.1 cosine_bitcast_fusion
  42.8 44.3 %collective-permute-done = bf16[192,640]{1,0:T(8,128)(2,1)S(1)} collective-permute-done((bf16[192,640]{1,0:T(8,128)(2,1)S(1)}, bf16[192,640]{1,0:T(8,128)(2,1)S(1)}, u32[]{:S(2)}, u32[]{:S(2)}) %collective-permute-start) | collective-permute-done | bytes 245792 | tf_op jit(solution)/shard_map/ppermute | solution.py:76
  87.1 0.9 convert_add_fusion
  88.0 2.8 %convert_reduce_fusion = f32[384]{0:T(512)S(1)} fusion(bf16[8,384,640]{1,2,0:T(8,128)(2,1)} %all-to-all-done), kind=kLoop, calls=%fused_computation.20 | loop fusion | flops 3931776 | bytes 3933696 | tf_op jit(solution)/shard_map/reduce_sum | solution.py:88
  90.9 3.2 %fusion.18 = f32[384]{0:T(512)S(1)} fusion(bf16[8,384,640]{1,2,0:T(8,128)(2,1)} %all-to-all-done, f32[384]{0:T(512)S(1)} %broadcast_multiply_fusion), kind=kLoop, calls=%fused_computation.23 | loop fusion | flops 7863936 | bytes 3935232 | tf_op jit(solution)/shard_map/reduce_sum | solution.py:90
  94.1 5.8 %fusion.21 = bf16[8,384,640]{1,2,0:T(8,128)(2,1)} fusion(bf16[8,384,640]{1,2,0:T(8,128)(2,1)} %all-to-all-done, f32[8,640]{1,0:T(8,128)S(1)} %add.179, f32[8,640]{1,0:T(8,128)S(1)} %add.178, f32[384]{0:T(512)S(1)} %add_rsqrt_fusion.2, f32[384]{0:T(512)S(1)} %broadcast_multiply_fusion), kind=kLoop, calls=%fused_computation.26 | loop fusion | flops 11796480 | bytes 7908352 | tf_op jit(solution)/shard_map/convert_element_type | solution.py:94
  99.9 10.1 %fusion.14 = f32[384,3,384,1,1]{0,2,3,1,4:T(8,128)S(1)} fusion(bf16[384,8,2,320,1]{0,3,1,4,2:T(8,128)(2,1)} %bitcast.113, bf16[8,2,320,3,384]{4,2,3,1,0:T(8,128)(2,1)} %bitcast.121), kind=kOutput, calls=%fused_computation.17 | convolution fusion | flops 4529848320 | bytes 17498112 | tf_op jit(solution)/shard_map/tabi,abiqe->tqe/dot_general | solution.py:109
  110.0 1.0 fusion.57
  112.4 0.9 pad_maximum_fusion.1
  113.4 39.3 %all-gather.5.cloned.1.call-done = bf16[1536,2,3,128]{3,0,2,1:T(8,128)(2,1)} async-done(((bf16[384,2,3,128]{3,0,2,1:T(8,128)(2,1)}), bf16[1536,2,3,128]{3,0,2,1:T(8,128)(2,1)}) %all-gather.5.cloned.1.call-update) | async-done | bytes 2359312 | tf_op jit(solution)/shard_map/all_gather | solution.py:130
  153.0 0.7 convert_reduce_fusion.2
  153.7 1.3 copy.92
  155.3 2.5 %fusion.28 = bf16[384,3,128]{2,0,1:T(8,128)(2,1)} fusion(f32[128,128,1]{1,0,2:T(8,128)} %constant.134, f32[384,1,3,128]{3,0,2,1:T(8,128)S(1)} %copy.92, f32[384,3]{0,1:T(4,128)S(1)} %add_rsqrt_fusion, f32[384,128]{1,0:T(8,128)} %copy-done.5, f32[384,128]{1,0:T(8,128)} %copy-done.4), kind=kOutput, calls=%fused_computation.40 | convolution fusion | flops 227377152 | bytes 1348096 | tf_op jit(solution)/shard_map/thd,de->the/dot_general | solution.py:54
  157.9 2.0 constant_dynamic-update-slice_fusion
  159.9 2.5 %slice_bitcast_fusion = (bf16[3072,3,128]{2,0,1:T(8,128)(2,1)}, bf16[3072,3,128]{2,0,1:T(8,128)(2,1)}) fusion(bf16[3072,2,3,128]{3,0,2,1:T(8,128)(2,1)S(1)} %constant_dynamic-update-slice_fusion), kind=kLoop, calls=%fused_computation.32 | loop fusion | bytes 9437184 | tf_op jit(solution)/shard_map/squeeze | solution.py:133
  162.4 26.7 %while.16 = (s32[]{:T(128)}, f32[384,3,128]{0,2,1:T(8,128)S(1)}, f32[3,384]{1,0:T(4,128)S(1)}, bf16[3072,3,128]{2,0,1:T(8,128)(2,1)}, s32[384]{0:T(512)S(1)}, /*...) while((s32[]{:T(128)}, f32[384,3,128]{0,2,1:T(8,128)S(1)}, ...), condition=%wide.region_9.10_spmd.clone, body=%wide.region_7.9_spmd.clone.sunk | while | flops 306021504 | bytes 7595706 | solution.py:173
  162.4 0.8 dynamic_slice.66
  163.4 1.7 fusion.75
  165.1 1.7 fusion.76
  166.9 0.8 dynamic_slice.66
  167.8 1.7 fusion.75
  169.5 1.7 fusion.76
  171.3 0.8 dynamic_slice.66
  172.3 1.7 fusion.75
  174.0 1.7 fusion.76
  175.8 0.8 dynamic_slice.66
  176.7 1.7 fusion.75
  178.4 1.8 fusion.76
  180.2 0.8 dynamic_slice.66
  181.2 1.7 fusion.75
  182.9 1.7 fusion.76
  184.7 0.8 dynamic_slice.66
  185.6 1.7 fusion.75
  187.4 1.7 fusion.76
  189.5 1.7 collective-permute-start.3
  191.4 4.5 %collective-permute-done.3 = bf16[192,384]{1,0:T(8,128)(2,1)S(1)} collective-permute-done((bf16[192,384]{1,0:T(8,128)(2,1)S(1)}, bf16[192,384]{1,0:T(8,128)(2,1)S(1)}, u32[]{:S(2)}, u32[]{:S(2)}) %collective-permute-start.3) | collective-permute-done | bytes 147488 | tf_op jit(solution)/shard_map/ppermute | solution.py:181
  195.9 3.8 %fusion.36 = f32[192,8,640]{2,0,1:T(8,128)S(1)} fusion(bf16[384,8,640]{0,2,1:T(8,128)(2,1)} %bitcast.111, bf16[192,384]{1,0:T(8,128)(2,1)S(1)} %collective-permute-done.3, bf16[192,384]{1,0:T(8,128)(2,1)S(1)} %copy.89, pred[]{:T(512)S(6)} %eq.39), kind=kOutput, calls=%fused_computation.64 | convolution fusion | flops 755048448 | bytes 8159233 | tf_op jit(solution)/shard_map/te,ebn->btn/dot_general | solution.py:189
  199.7 2.9 %fusion.24 = bf16[8,192,640]{2,1,0:T(8,128)(2,1)} fusion(f32[192,8,640]{2,0,1:T(8,128)S(1)} %fusion.36, bf16[384,8,640]{0,2,1:T(8,128)(2,1)S(1)} %bitcast.112, f32[]{:T(128)} %bitcast.110, bf16[192,384]{1,0:T(8,128)(2,1)S(1)} %copy.89, bf16[192,384]{1,0:T(8,128)(2,1)S(1)} %collective-permute-done.3, pred[]{:T(512)S(6)} %eq.39), kind=kOutput, calls=%fused_computation.30 | convolution fusion | flops 758980608 | bytes 10125317 | tf_op jit(solution)/shard_map/te,ebn->btn/dot_general | solution.py:188
  202.6 7.0 %all-to-all-start.1 = ((bf16[8,192,640]{2,1,0:T(8,128)(2,1)}), bf16[8,192,640]{2,1,0:T(8,128)(2,1)S(1)}, u32[]{:S(2)}, u32[]{:S(2)}) async-start(bf16[8,192,640]{2,1,0:T(8,128)(2,1)} %fusion.24), calls=%async_computation.1 | async-start | bytes 3932160 | tf_op jit(solution)/shard_map/all_to_all | solution.py:191
  210.3 26.2 %all-to-all-done.1 = bf16[8,192,640]{2,1,0:T(8,128)(2,1)S(1)} async-done(((bf16[8,192,640]{2,1,0:T(8,128)(2,1)}), bf16[8,192,640]{2,1,0:T(8,128)(2,1)S(1)}, u32[]{:S(2)}, u32[]{:S(2)}) %all-to-all-start.1) | async-done | bytes 1966112 | tf_op jit(solution)/shard_map/all_to_all | solution.py:191
  236.8 0.9 add_bitcast_fusion
  (77 shorter events, 6.1 us)
Async XLA Ops:
  7.4 21.3 %copy-start.2 = (bf16[1,384,640]{2,1,0:T(8,128)(2,1)S(1)}, bf16[1,384,640]{2,1,0:T(8,128)(2,1)}, u32[]{:S(2)}) copy-start(bf16[1,384,640]{2,1,0:T(8,128)(2,1)} %param.11) | copy-start | bytes 1474564
  7.4 92.5 %all-gather.9.cloned.1.call-start = ((), (), s32[]{:S(2)}) async-start(), calls=%async_computation.4 | async-start | bytes 13271040 | tf_op jit(solution)/shard_map/all_gather | solution.py:103
  7.4 18.7 %collective-permute-start.1 = (bf16[320,3,384]{2,0,1:T(8,128)(2,1)}, bf16[320,3,384]{2,0,1:T(8,128)(2,1)S(1)}, u32[]{:S(2)}, u32[]{:S(2)}) collective-permute-start(bf16[320,3,384]{2,0,1:T(8,128)(2,1)} %param.13), channel_id=1, source_target_pairs={{0,64},{64,0},{1,65},{65,1},{2,66},{66,2},{3,67},{67,3},{4,68},{68... | collective-permute-start | bytes 2211848 | tf_op jit(solution)/shard_map/ppermute | solution.py:96
  31.2 8.9 %copy-start.8 = (f32[3,5120]{1,0:T(4,128)S(1)}, f32[3,5120]{1,0:T(4,128)}, u32[]{:S(2)}) copy-start(f32[3,5120]{1,0:T(4,128)} %param.12) | copy-start | bytes 184324
  31.2 10.3 %copy-start.9 = (s32[3,384]{1,0:T(4,128)S(1)}, s32[3,384]{1,0:T(4,128)}, u32[]{:S(2)}) copy-start(s32[3,384]{1,0:T(4,128)} %param.16) | copy-start | bytes 13828
  31.2 10.3 %copy-start.10 = (f32[3,128]{1,0:T(4,128)S(1)}, f32[3,128]{1,0:T(4,128)}, u32[]{:S(2)}) copy-start(f32[3,128]{1,0:T(4,128)} %constant.131.clone) | copy-start | bytes 4612
  31.2 56.8 %all-to-all-start = ((bf16[8,384,640]{1,2,0:T(8,128)(2,1)}), bf16[8,384,640]{1,2,0:T(8,128)(2,1)}, u32[]{:S(2)}, u32[]{:S(2)}) async-start(bf16[8,384,640]{1,2,0:T(8,128)(2,1)} %broadcast_in_dim.69), calls=%async_computation | async-start | bytes 7864320 | tf_op jit(solution)/shard_map/all_to_all | solution.py:85
  39.0 113.7 %all-gather.5.cloned.1.call-start = ((), (), s32[]{:S(2)}) async-start(), calls=%async_computation.2 | async-start | bytes 2949120 | tf_op jit(solution)/shard_map/all_gather | solution.py:130
  39.0 48.1 %collective-permute-start = (bf16[192,640]{1,0:T(8,128)(2,1)S(1)}, bf16[192,640]{1,0:T(8,128)(2,1)S(1)}, u32[]{:S(2)}, u32[]{:S(2)}) collective-permute-start(bf16[192,640]{1,0:T(8,128)(2,1)S(1)} %dynamic-slice_bitcast_fusion), channel_id=1, source_target_pairs={{0,64},{64,0},{1,65},{65,1},{2,66},{66,2},{3,67},{67,3},{4,68},{68... | collective-permute-start | bytes 737288 | tf_op jit(solution)/shard_map/ppermute | solution.py:76
  42.7 69.0 %copy-start.4 = (f32[384,128]{1,0:T(8,128)}, f32[384,128]{1,0:T(8,128)S(1)}, u32[]{:S(2)}) copy-start(f32[384,128]{1,0:T(8,128)S(1)} %copy.72) | copy-start | bytes 589828
  42.8 68.9 %copy-start.5 = (f32[384,128]{1,0:T(8,128)}, f32[384,128]{1,0:T(8,128)S(1)}, u32[]{:S(2)}) copy-start(f32[384,128]{1,0:T(8,128)S(1)} %copy.73) | copy-start | bytes 589828
  110.0 1.8 copy-start.7
  110.0 42.7 %copy-start.11 = (s32[5]{0:T(128)S(1)}, s32[5]{0:T(128)}, u32[]{:S(2)}) copy-start(s32[5]{0:T(128)} %param.15) | copy-start | bytes 64
  113.3 78.0 %all-gather.7.cloned.1.call-start = ((), (), s32[]{:S(2)}) async-start(), calls=%async_computation.3 | async-start | bytes 4177920 | tf_op jit(solution)/shard_map/all_gather | solution.py:185
  152.7 5.1 %copy-start.1 = (bf16[1536,2,3,128]{3,0,2,1:T(8,128)(2,1)S(1)}, bf16[1536,2,3,128]{3,0,2,1:T(8,128)(2,1)}, u32[]{:S(2)}) copy-start(bf16[1536,2,3,128]{3,0,2,1:T(8,128)(2,1)} %all-gather.5.cloned.1.call-done) | copy-start | bytes 7077892
  152.7 5.2 %collective-permute-start.2 = (bf16[1536,2,3,128]{3,0,2,1:T(8,128)(2,1)}, bf16[1536,2,3,128]{3,0,2,1:T(8,128)(2,1)}, u32[]{:S(2)}, u32[]{:S(2)}) collective-permute-start(bf16[1536,2,3,128]{3,0,2,1:T(8,128)(2,1)} %all-gather.5.cloned.1.call-done), channel_id=1, source_target_pairs={{0,8},{8,0},{1,9},{9,1},{2,10},{10,2},{3,11},{11,3},{4,12},{12,4},... | collective-permute-start | bytes 7077896 | tf_op jit(solution)/shard_map/ppermute | solution.py:131
  159.9 2.5 %copy-start.6 = (bf16[384,3,128]{2,0,1:T(8,128)(2,1)S(1)}, bf16[384,3,128]{2,0,1:T(8,128)(2,1)}, u32[]{:S(2)}) copy-start(bf16[384,3,128]{2,0,1:T(8,128)(2,1)} %fusion.28) | copy-start | bytes 884740
  189.5 6.3 %collective-permute-start.3 = (bf16[192,384]{1,0:T(8,128)(2,1)S(1)}, bf16[192,384]{1,0:T(8,128)(2,1)S(1)}, u32[]{:S(2)}, u32[]{:S(2)}) collective-permute-start(bf16[192,384]{1,0:T(8,128)(2,1)S(1)} %copy.88), channel_id=1, source_target_pairs={{0,64},{64,0},{1,65},{65,1},{2,66},{66,2},{3,67},{67,3},{4,68},{68... | collective-permute-start | bytes 442376 | tf_op jit(solution)/shard_map/ppermute | solution.py:181
  195.9 3.8 %copy-start = (bf16[384,5120]{0,1:T(8,128)(2,1)S(1)}, bf16[384,5120]{0,1:T(8,128)(2,1)}, u32[]{:S(2)}) copy-start(bf16[384,5120]{0,1:T(8,128)(2,1)} %all-gather.7.cloned.1.call-done) | copy-start | bytes 11796484
  202.6 34.2 %copy-start.3 = (f32[192,640]{1,0:T(8,128)S(1)}, f32[192,640]{1,0:T(8,128)}, u32[]{:S(2)}) copy-start(f32[192,640]{1,0:T(8,128)} %convert_add_fusion) | copy-start | bytes 1474564
  202.6 34.0 %all-to-all-start.1 = ((bf16[8,192,640]{2,1,0:T(8,128)(2,1)}), bf16[8,192,640]{2,1,0:T(8,128)(2,1)S(1)}, u32[]{:S(2)}, u32[]{:S(2)}) async-start(bf16[8,192,640]{2,1,0:T(8,128)(2,1)} %fusion.24), calls=%async_computation.1 | async-start | bytes 3932160 | tf_op jit(solution)/shard_map/all_to_all | solution.py:191
Sparse Core Ops, SparseCore 0:
  28.8 66.1 all-gather.8
  113.5 39.1 all-gather.4
Sparse Core Ops, SparseCore 1:
  152.8 37.1 all-gather.6

commit v5 on v3

--- a/solution.py
+++ b/solution.py
@@ -93,13 +93,19 @@
     mod_scale = modulation[1].reshape(n_blk, 1, feat_width)
     modulated = (normed * (1.0 + mod_scale) + mod_shift).astype(jnp.bfloat16)
 
-    piece = lax.all_gather(in_projection, ("cfg",) + SEQ, axis=0, tiled=True)
+    piece_own = lax.all_gather(in_projection, SEQ, axis=0, tiled=False)
+    shard_other = lax.ppermute(in_projection, "cfg", SWAP)
+    piece_other = lax.all_gather(shard_other, SEQ, axis=0, tiled=False)
+    n_seq = piece_own.shape[0]
+    rows = in_projection.shape[0]
+    per_blk = feat_width // rows
+    mod_perm = modulated.reshape(2, n_blk // 2, tok_count, per_blk, rows).transpose(0, 2, 1, 3, 4)
+    mod_perm = mod_perm.reshape(2, tok_count, n_seq, rows)
+    mod_own = lax.dynamic_index_in_dim(mod_perm, cfg, axis=0, keepdims=False)
+    mod_other = lax.dynamic_index_in_dim(mod_perm, 1 - cfg, axis=0, keepdims=False)
     mixed = jnp.einsum(
-        "itf,ifqe->tqe",
-        modulated,
-        piece.reshape(n_blk, feat_width, 3, inner_width),
-        preferred_element_type=jnp.float32,
-    )
+        "tai,aiqe->tqe", mod_own, piece_own, preferred_element_type=jnp.float32
+    ) + jnp.einsum("tai,aiqe->tqe", mod_other, piece_other, preferred_element_type=jnp.float32)
     mixed = with_layout_constraint(mixed, Layout((0, 1, 2)))
     mixed = mixed.reshape(tok_count, 3, head_count, HEAD_DIM)
 

time: 266 us -> 251 us (0.944)
  waiting for transfers between devices: 161 us -> 131 us
  other arithmetic: 12.4 us -> 18.1 us
  local copies, waits for them, and re-layouts: 16.5 us -> 20.4 us
    all_gather x1 -> x2, waiting for transfers between devices: 35.6 us -> 0.02 us  [the longest x1 0.02 us: local(): piece_other = lax.all_gather(shard_other, SEQ, axis=0, tiled=False)]
    ppermute x0 -> x1, waiting for transfers between devices: none -> 16.7 us  [local(): shard_other = lax.ppermute(in_projection, 'cfg', SWAP)]
    ppermute x1, waiting for transfers between devices: 59.5 us -> 43 us  [local(): other_rows = lax.ppermute(sent_rows, 'cfg', SWAP)]
    convert_element_type x0 -> x1, other arithmetic: none -> 5.81 us  [local(): modulated = (normed * (1.0 + mod_scale) + mod_shift).astype(jnp.bfloat16)]
    all_gather x1, waiting for transfers between devices: 34.6 us -> 39.7 us  [local(): kv_mine = lax.all_gather(kv, 'x', axis=0, tiled=True)]
    dot_general x1 -> x2, matrix products: 10.9 us -> 12.1 us  [the longest x1 6.03 us: local(): jnp.einsum('tai,aiqe->tqe', mod_own, piece_own, preferred_element_type=jn...]
  transfers between devices with their start and end apart: 8 -> 10, of which waited for: 6 -> 5; matrix products, arithmetic and copies ran while one was open for 19% -> 25% of each run, Pallas kernels for 0% -> 0%
where the time goes in v5:
time: 251 us; the launch traced here: 249 us
  waiting for transfers between devices  131 us (52%)
  matrix products  43.8 us (17%)
  local copies, waits for them, and re-layouts  20.4 us (8%)
  starting transfers between devices  19.8 us (8%)
  other arithmetic  18.1 us (7%)
  between operations  15.5 us (6%)
    ppermute x1, waiting for transfers between devices, local(): other_rows = lax.ppermute(sent_rows, 'cfg', SWAP)  43 us
    all_gather x1, waiting for transfers between devices, local(): kv_mine = lax.all_gather(kv, 'x', axis=0, tiled=True)  39.7 us
    all_to_all x1, waiting for transfers between devices, local(): lax.all_to_all(partial, BLK, 0, 0, tiled=False).astype(jnp.float32)  26.2 us
    ppermute x1, waiting for transfers between devices, local(): shard_other = lax.ppermute(in_projection, 'cfg', SWAP)  16.7 us
    dot_general x6, matrix products, key_step(): jnp.einsum('hqk,khd->qhd', weights.astype(jnp.bfloat16), value_slab, pref...  10.4 us
    dot_general x6, matrix products, key_step(): jnp.einsum('qhd,khd->hqk', queries, key_slab, preferred_element_type=jnp....  10.4 us
    all_to_all x1, starting transfers between devices, local(): full_states = lax.all_to_all(spread, BLK, 0, 0, tiled=False)  7.75 us
    all_to_all x1, starting transfers between devices, local(): lax.all_to_all(partial, BLK, 0, 0, tiled=False).astype(jnp.float32)  7.03 us
  transfers between devices with their start and end apart: 10, of which 5 were waited for; matrix products, arithmetic and copies ran while one was open for 25% of the time, Pallas kernels for 0%

profile of v5, /device:TPU:0, one launch (start us, length us, event | category | flops | bytes accessed | tf_op | source)
XLA Modules:
  0.0 248.8 jit_solution(12702032913325883505)
XLA Ops:
  8.1 2.1 collective-permute-start.1
  10.2 16.7 %collective-permute-done.1 = bf16[320,3,384]{2,0,1:T(8,128)(2,1)S(1)} collective-permute-done((bf16[320,3,384]{2,0,1:T(8,128)(2,1)}, bf16[320,3,384]{2,0,1:T(8,128)(2,1)S(1)}, u32[]{:S(2)}, u32[]{:S(2)}) %collective-permute-start.1) | collective-permute-done | bytes 737312 | tf_op jit(solution)/shard_map/ppermute | solution.py:97
  26.9 0.9 copy-done.6
  27.8 1.3 copy.53
  29.1 2.2 broadcast_in_dim.69
  31.4 7.8 %all-to-all-start = ((bf16[8,384,640]{1,2,0:T(8,128)(2,1)}), bf16[8,384,640]{1,2,0:T(8,128)(2,1)}, u32[]{:S(2)}, u32[]{:S(2)}) async-start(bf16[8,384,640]{1,2,0:T(8,128)(2,1)} %broadcast_in_dim.69), calls=%async_computation | async-start | bytes 7864320 | tf_op jit(solution)/shard_map/all_to_all | solution.py:85
  39.2 1.1 collective-permute-start
  41.7 1.1 cosine_bitcast_fusion
  42.8 0.8 copy.57
  43.6 0.8 copy.58
  44.4 43.0 %collective-permute-done = bf16[192,640]{1,0:T(8,128)(2,1)S(1)} collective-permute-done((bf16[192,640]{1,0:T(8,128)(2,1)S(1)}, bf16[192,640]{1,0:T(8,128)(2,1)S(1)}, u32[]{:S(2)}, u32[]{:S(2)}) %collective-permute-start) | collective-permute-done | bytes 245792 | tf_op jit(solution)/shard_map/ppermute | solution.py:76
  87.4 0.9 convert_add_fusion
  88.3 2.8 %convert_reduce_fusion = f32[384]{0:T(512)S(1)} fusion(bf16[8,384,640]{1,2,0:T(8,128)(2,1)} %all-to-all-done), kind=kLoop, calls=%fused_computation.18 | loop fusion | flops 3931776 | bytes 3933696 | tf_op jit(solution)/shard_map/reduce_sum | solution.py:88
  91.1 3.3 %fusion.16 = f32[384]{0:T(512)S(1)} fusion(bf16[8,384,640]{1,2,0:T(8,128)(2,1)} %all-to-all-done, f32[384]{0:T(512)S(1)} %broadcast_multiply_fusion), kind=kLoop, calls=%fused_computation.21 | loop fusion | flops 7863936 | bytes 3935232 | tf_op jit(solution)/shard_map/reduce_sum | solution.py:90
  94.4 5.8 %fusion.19 = bf16[8,384,640]{1,2,0:T(8,128)(2,1)} fusion(bf16[8,384,640]{1,2,0:T(8,128)(2,1)} %all-to-all-done, f32[8,640]{1,0:T(8,128)S(1)} %add.190, f32[8,640]{1,0:T(8,128)S(1)} %add.189, f32[384]{0:T(512)S(1)} %add_rsqrt_fusion.2, f32[384]{0:T(512)S(1)} %broadcast_multiply_fusion), kind=kLoop, calls=%fused_computation.24 | loop fusion | flops 11796480 | bytes 7908352 | tf_op jit(solution)/shard_map/convert_element_type | solution.py:94
  100.2 6.0 %fusion.25 = f32[384,3,384,1]{2,0,3,1:T(8,128)S(1)} fusion(bf16[8,320,3,384]{3,1,0,2:T(8,128)(2,1)} %bitcast.120, bf16[2,384,8,320]{1,3,2,0:T(8,128)(2,1)} %bitcast.116, s32[]{:T(128)S(6)} %select_n.104), kind=kOutput, calls=%fused_computation.34 | convolution fusion | flops 2264924160 | bytes 9633796 | tf_op jit(solution)/shard_map/tai,aiqe->tqe/dot_general | solution.py:106
  106.3 6.0 %bitcast_add_fusion = f32[384,3,384]{2,0,1:T(8,128)S(1)} fusion(f32[384,3,384,1]{2,0,3,1:T(8,128)S(1)} %fusion.25, bf16[8,320,3,384]{3,1,0,2:T(8,128)(2,1)} %bitcast.121, bf16[2,384,8,320]{1,3,2,0:T(8,128)(2,1)} %bitcast.117, s32[]{:T(128)S(6)} %select_n.105), kind=kOutput, calls=%fused_computation.38 | convolution fusion | flops 2265366528 | bytes 11403268 | tf_op jit(solution)/shard_map/tai,aiqe->tqe/dot_general | solution.py:108
  112.3 1.2 copy.55
  113.6 1.0 fusion.65
  116.0 0.9 pad_maximum_fusion
  117.0 39.7 %all-gather.7.cloned.1.call-done = bf16[1536,2,3,128]{3,0,2,1:T(8,128)(2,1)} async-done(((bf16[384,2,3,128]{3,0,2,1:T(8,128)(2,1)}), bf16[1536,2,3,128]{3,0,2,1:T(8,128)(2,1)}) %all-gather.7.cloned.1.call-update) | async-done | bytes 2359312 | tf_op jit(solution)/shard_map/all_gather | solution.py:124
  157.8 1.3 copy.77
  159.3 2.5 fusion.34
  162.0 2.0 constant_dynamic-update-slice_fusion
  164.0 2.5 %slice_bitcast_fusion = (bf16[3072,3,128]{2,0,1:T(8,128)(2,1)}, bf16[3072,3,128]{2,0,1:T(8,128)(2,1)}) fusion(bf16[3072,2,3,128]{3,0,2,1:T(8,128)(2,1)S(1)} %constant_dynamic-update-slice_fusion), kind=kLoop, calls=%fused_computation.30 | loop fusion | bytes 9437184 | tf_op jit(solution)/shard_map/squeeze | solution.py:127
  166.5 26.7 %while.16 = (s32[]{:T(128)}, f32[384,3,128]{0,2,1:T(8,128)S(1)}, f32[3,384]{1,0:T(4,128)S(1)}, bf16[3072,3,128]{2,0,1:T(8,128)(2,1)}, s32[384]{0:T(512)S(1)}, /*...) while((s32[]{:T(128)}, f32[384,3,128]{0,2,1:T(8,128)S(1)}, ...), condition=%wide.region_9.10_spmd.clone, body=%wide.region_7.9_spmd.clone.sunk | while | flops 306021504 | bytes 7595706 | solution.py:167
  167.4 1.7 fusion.84
  169.1 1.7 fusion.85
  170.9 0.8 dynamic_slice.85
  171.8 1.7 fusion.84
  173.6 1.7 fusion.85
  175.4 0.8 dynamic_slice.85
  176.3 1.7 fusion.84
  178.0 1.7 fusion.85
  179.8 0.8 dynamic_slice.85
  180.8 1.7 fusion.84
  182.5 1.7 fusion.85
  185.2 1.7 fusion.84
  187.0 1.7 fusion.85
  189.7 1.7 fusion.84
  191.4 1.7 fusion.85
  193.6 1.6 collective-permute-start.3
  195.4 4.5 %collective-permute-done.3 = bf16[192,384]{1,0:T(8,128)(2,1)S(1)} collective-permute-done((bf16[192,384]{1,0:T(8,128)(2,1)S(1)}, bf16[192,384]{1,0:T(8,128)(2,1)S(1)}, u32[]{:S(2)}, u32[]{:S(2)}) %collective-permute-start.3) | collective-permute-done | bytes 147488 | tf_op jit(solution)/shard_map/ppermute | solution.py:175
  199.9 3.8 %fusion.42 = f32[192,8,640]{2,0,1:T(8,128)S(1)} fusion(bf16[384,8,640]{0,2,1:T(8,128)(2,1)} %bitcast.118, bf16[192,384]{1,0:T(8,128)(2,1)S(1)} %collective-permute-done.3, bf16[192,384]{1,0:T(8,128)(2,1)S(1)} %copy.74, pred[]{:T(512)S(6)} %eq.39), kind=kOutput, calls=%fused_computation.66 | convolution fusion | flops 755048448 | bytes 8159233 | tf_op jit(solution)/shard_map/te,ebn->btn/dot_general | solution.py:183
  203.7 2.9 %fusion.22 = bf16[8,192,640]{2,1,0:T(8,128)(2,1)} fusion(f32[192,8,640]{2,0,1:T(8,128)S(1)} %fusion.42, bf16[384,8,640]{0,2,1:T(8,128)(2,1)S(1)} %bitcast.119, f32[]{:T(128)} %bitcast.115, bf16[192,384]{1,0:T(8,128)(2,1)S(1)} %copy.74, bf16[192,384]{1,0:T(8,128)(2,1)S(1)} %collective-permute-done.3, pred[]{:T(512)S(6)} %eq.39), kind=kOutput, calls=%fused_computation.28 | convolution fusion | flops 758980608 | bytes 10125317 | tf_op jit(solution)/shard_map/te,ebn->btn/dot_general | solution.py:182
  206.6 7.0 %all-to-all-start.1 = ((bf16[8,192,640]{2,1,0:T(8,128)(2,1)}), bf16[8,192,640]{2,1,0:T(8,128)(2,1)S(1)}, u32[]{:S(2)}, u32[]{:S(2)}) async-start(bf16[8,192,640]{2,1,0:T(8,128)(2,1)} %fusion.22), calls=%async_computation.1 | async-start | bytes 3932160 | tf_op jit(solution)/shard_map/all_to_all | solution.py:185
  214.3 26.2 %all-to-all-done.1 = bf16[8,192,640]{2,1,0:T(8,128)(2,1)S(1)} async-done(((bf16[8,192,640]{2,1,0:T(8,128)(2,1)}), bf16[8,192,640]{2,1,0:T(8,128)(2,1)S(1)}, u32[]{:S(2)}, u32[]{:S(2)}) %all-to-all-start.1) | async-done | bytes 1966112 | tf_op jit(solution)/shard_map/all_to_all | solution.py:185
  240.8 0.9 add_bitcast_fusion
  (82 shorter events, 9.3 us)
Async XLA Ops:
  7.4 92.9 %all-gather.11.cloned.1.call-start = ((), (), s32[]{:S(2)}) async-start(), calls=%async_computation.4 | async-start | bytes 6635520 | tf_op jit(solution)/shard_map/all_gather | solution.py:96
  8.1 98.2 %all-gather.13.cloned.1.call-start = ((), (), s32[]{:S(2)}) async-start(), calls=%async_computation.5 | async-start | bytes 6635520 | tf_op jit(solution)/shard_map/all_gather | solution.py:98
  8.1 18.8 %collective-permute-start.1 = (bf16[320,3,384]{2,0,1:T(8,128)(2,1)}, bf16[320,3,384]{2,0,1:T(8,128)(2,1)S(1)}, u32[]{:S(2)}, u32[]{:S(2)}) collective-permute-start(bf16[320,3,384]{2,0,1:T(8,128)(2,1)} %param.13), channel_id=1, source_target_pairs={{0,64},{64,0},{1,65},{65,1},{2,66},{66,2},{3,67},{67,3},{4,68},{68... | collective-permute-start | bytes 2211848 | tf_op jit(solution)/shard_map/ppermute | solution.py:97
  26.9 0.9 copy-start.6
  31.4 7.8 %copy-start.2 = (bf16[1,384,640]{2,1,0:T(8,128)(2,1)S(1)}, bf16[1,384,640]{2,1,0:T(8,128)(2,1)}, u32[]{:S(2)}) copy-start(bf16[1,384,640]{2,1,0:T(8,128)(2,1)} %param.11) | copy-start | bytes 1474564
  31.4 9.0 %copy-start.9 = (f32[3,5120]{1,0:T(4,128)S(1)}, f32[3,5120]{1,0:T(4,128)}, u32[]{:S(2)}) copy-start(f32[3,5120]{1,0:T(4,128)} %param.12) | copy-start | bytes 184324
  31.4 10.3 %copy-start.10 = (s32[3,384]{1,0:T(4,128)S(1)}, s32[3,384]{1,0:T(4,128)}, u32[]{:S(2)}) copy-start(s32[3,384]{1,0:T(4,128)} %param.16) | copy-start | bytes 13828
  31.4 10.3 %copy-start.11 = (f32[3,128]{1,0:T(4,128)S(1)}, f32[3,128]{1,0:T(4,128)}, u32[]{:S(2)}) copy-start(f32[3,128]{1,0:T(4,128)} %constant.138.clone) | copy-start | bytes 4612
  31.4 56.9 %all-to-all-start = ((bf16[8,384,640]{1,2,0:T(8,128)(2,1)}), bf16[8,384,640]{1,2,0:T(8,128)(2,1)}, u32[]{:S(2)}, u32[]{:S(2)}) async-start(bf16[8,384,640]{1,2,0:T(8,128)(2,1)} %broadcast_in_dim.69), calls=%async_computation | async-start | bytes 7864320 | tf_op jit(solution)/shard_map/all_to_all | solution.py:85
  39.1 117.6 %all-gather.7.cloned.1.call-start = ((), (), s32[]{:S(2)}) async-start(), calls=%async_computation.2 | async-start | bytes 2949120 | tf_op jit(solution)/shard_map/all_gather | solution.py:124
  39.2 48.2 %collective-permute-start = (bf16[192,640]{1,0:T(8,128)(2,1)S(1)}, bf16[192,640]{1,0:T(8,128)(2,1)S(1)}, u32[]{:S(2)}, u32[]{:S(2)}) collective-permute-start(bf16[192,640]{1,0:T(8,128)(2,1)S(1)} %dynamic-slice_bitcast_fusion), channel_id=1, source_target_pairs={{0,64},{64,0},{1,65},{65,1},{2,66},{66,2},{3,67},{67,3},{4,68},{68... | collective-permute-start | bytes 737288 | tf_op jit(solution)/shard_map/ppermute | solution.py:76
  113.5 1.8 copy-start.4
  113.5 1.8 copy-start.5
  113.5 1.8 copy-start.8
  113.5 43.2 %copy-start.12 = (s32[5]{0:T(128)S(1)}, s32[5]{0:T(128)}, u32[]{:S(2)}) copy-start(s32[5]{0:T(128)} %param.15) | copy-start | bytes 64
  116.9 78.4 %all-gather.9.cloned.1.call-start = ((), (), s32[]{:S(2)}) async-start(), calls=%async_computation.3 | async-start | bytes 4177920 | tf_op jit(solution)/shard_map/all_gather | solution.py:179
  156.7 5.1 %copy-start.1 = (bf16[1536,2,3,128]{3,0,2,1:T(8,128)(2,1)S(1)}, bf16[1536,2,3,128]{3,0,2,1:T(8,128)(2,1)}, u32[]{:S(2)}) copy-start(bf16[1536,2,3,128]{3,0,2,1:T(8,128)(2,1)} %all-gather.7.cloned.1.call-done) | copy-start | bytes 7077892
  156.7 5.3 %collective-permute-start.2 = (bf16[1536,2,3,128]{3,0,2,1:T(8,128)(2,1)}, bf16[1536,2,3,128]{3,0,2,1:T(8,128)(2,1)}, u32[]{:S(2)}, u32[]{:S(2)}) collective-permute-start(bf16[1536,2,3,128]{3,0,2,1:T(8,128)(2,1)} %all-gather.7.cloned.1.call-done), channel_id=1, source_target_pairs={{0,8},{8,0},{1,9},{9,1},{2,10},{10,2},{3,11},{11,3},{4,12},{12,4},... | collective-permute-start | bytes 7077896 | tf_op jit(solution)/shard_map/ppermute | solution.py:125
  163.9 2.5 %copy-start.7 = (bf16[384,3,128]{2,0,1:T(8,128)(2,1)S(1)}, bf16[384,3,128]{2,0,1:T(8,128)(2,1)}, u32[]{:S(2)}) copy-start(bf16[384,3,128]{2,0,1:T(8,128)(2,1)} %fusion.34) | copy-start | bytes 884740
  193.6 6.3 %collective-permute-start.3 = (bf16[192,384]{1,0:T(8,128)(2,1)S(1)}, bf16[192,384]{1,0:T(8,128)(2,1)S(1)}, u32[]{:S(2)}, u32[]{:S(2)}) collective-permute-start(bf16[192,384]{1,0:T(8,128)(2,1)S(1)} %copy.73), channel_id=1, source_target_pairs={{0,64},{64,0},{1,65},{65,1},{2,66},{66,2},{3,67},{67,3},{4,68},{68... | collective-permute-start | bytes 442376 | tf_op jit(solution)/shard_map/ppermute | solution.py:175
  199.9 3.8 %copy-start = (bf16[384,5120]{0,1:T(8,128)(2,1)S(1)}, bf16[384,5120]{0,1:T(8,128)(2,1)}, u32[]{:S(2)}) copy-start(bf16[384,5120]{0,1:T(8,128)(2,1)} %all-gather.9.cloned.1.call-done) | copy-start | bytes 11796484
  206.6 34.2 %copy-start.3 = (f32[192,640]{1,0:T(8,128)S(1)}, f32[192,640]{1,0:T(8,128)}, u32[]{:S(2)}) copy-start(f32[192,640]{1,0:T(8,128)} %convert_add_fusion) | copy-start | bytes 1474564
  206.6 33.9 %all-to-all-start.1 = ((bf16[8,192,640]{2,1,0:T(8,128)(2,1)}), bf16[8,192,640]{2,1,0:T(8,128)(2,1)S(1)}, u32[]{:S(2)}, u32[]{:S(2)}) async-start(bf16[8,192,640]{2,1,0:T(8,128)(2,1)} %fusion.22), calls=%async_computation.1 | async-start | bytes 3932160 | tf_op jit(solution)/shard_map/all_to_all | solution.py:185
Sparse Core Ops, SparseCore 0:
  9.9 41.6 all-gather.10
  53.2 39.2 all-gather.12
  117.0 39.6 all-gather.6
Sparse Core Ops, SparseCore 1:
  156.8 37.1 all-gather.8

commit v6 on v4

--- a/solution.py
+++ b/solution.py
@@ -93,13 +93,7 @@
     mod_scale = modulation[1].reshape(n_blk, 1, feat_width)
     modulated = (normed * (1.0 + mod_scale) + mod_shift).astype(jnp.bfloat16)
 
-    shard_other = lax.ppermute(in_projection, "cfg", SWAP)
-    stacked = jnp.stack(
-        [
-            jnp.where(is_cond, in_projection, shard_other),
-            jnp.where(is_cond, shard_other, in_projection),
-        ]
-    )
+    stacked = lax.all_gather(in_projection, "cfg", axis=0, tiled=False)
     piece = lax.all_gather(stacked, SEQ, axis=0, tiled=False)
     n_seq = piece.shape[0]
     rows = in_projection.shape[0]
@@ -144,42 +138,39 @@
     key_clip_all = clip_of(clip_ends, key_token)
 
     score_scale = HEAD_DIM ** (-0.5)
-    start_state = (
-        jnp.zeros((tok_count, head_count, HEAD_DIM), jnp.float32),
-        jnp.zeros((head_count, tok_count), jnp.float32),
-    )
     key_block_size = 512 if row_count % 512 == 0 else row_count
 
-    def key_step(block_index, running):
-        numerator, denominator = running
-        key_slab = lax.dynamic_slice_in_dim(key_piece, block_index * key_block_size, key_block_size, 0)
-        value_slab = lax.dynamic_slice_in_dim(value_piece, block_index * key_block_size, key_block_size, 0)
-        key_clip = lax.dynamic_slice_in_dim(key_clip_all, block_index * key_block_size, key_block_size, 0)
-        scores = (
-            jnp.einsum("qhd,khd->hqk", queries, key_slab, preferred_element_type=jnp.float32)
-            * score_scale
+    def attend(first_query):
+        query_rows = lax.dynamic_slice_in_dim(queries, first_query, half_rows, 0)
+        clip_rows = lax.dynamic_slice_in_dim(query_clip, first_query, half_rows, 0)
+        numerator = jnp.zeros((half_rows, head_count, HEAD_DIM), jnp.float32)
+        denominator = jnp.zeros((head_count, half_rows), jnp.float32)
+        for start in range(0, row_count, key_block_size):
+            key_slab = key_piece[start:start + key_block_size]
+            value_slab = value_piece[start:start + key_block_size]
+            key_clip = key_clip_all[start:start + key_block_size]
+            scores = (
+                jnp.einsum("qhd,khd->hqk", query_rows, key_slab, preferred_element_type=jnp.float32)
+                * score_scale
+            )
+            same_clip = clip_rows[:, None] == key_clip[None, :]
+            weights = jnp.where(same_clip[None], jnp.exp(scores), 0.0)
+            numerator = numerator + jnp.einsum(
+                "hqk,khd->qhd",
+                weights.astype(jnp.bfloat16),
+                value_slab,
+                preferred_element_type=jnp.float32,
+            )
+            denominator = denominator + jnp.sum(weights, -1)
+        return (
+            (numerator / jnp.transpose(denominator)[:, :, None])
+            .astype(jnp.bfloat16)
+            .reshape(half_rows, inner_width)
         )
-        same_clip = query_clip[:, None] == key_clip[None, :]
-        weights = jnp.where(same_clip[None], jnp.exp(scores), 0.0)
-        numerator = numerator + jnp.einsum(
-            "hqk,khd->qhd",
-            weights.astype(jnp.bfloat16),
-            value_slab,
-            preferred_element_type=jnp.float32,
-        )
-        denominator = denominator + jnp.sum(weights, -1)
-        return (numerator, denominator)
-
-    numerator, denominator = lax.fori_loop(0, row_count // key_block_size, key_step, start_state)
-    attended = (
-        (numerator / jnp.transpose(denominator)[:, :, None])
-        .astype(jnp.bfloat16)
-        .reshape(tok_count, inner_width)
-    )
-
-    sent_att = lax.dynamic_slice_in_dim(attended, (1 - cfg) * half_rows, half_rows, 0)
+
+    sent_att = attend((1 - cfg) * half_rows)
     other_att = lax.ppermute(sent_att, "cfg", SWAP)
-    mine_att = lax.dynamic_slice_in_dim(attended, cfg * half_rows, half_rows, 0)
+    mine_att = attend(cfg * half_rows)
     cond_att = jnp.where(is_cond, mine_att, other_att)
     uncond_att = jnp.where(is_cond, other_att, mine_att)
     out_piece = lax.all_gather(out_projection, ("cfg",) + SEQ, axis=1, tiled=True).reshape(

time: 247 us -> 255 us (1.032)
  waiting for transfers between devices: 131 us -> 173 us
  local copies, waits for them, and re-layouts: 15.9 us -> 3.83 us
  matrix products: 41.7 us -> 31.8 us
  other arithmetic: 20.6 us -> 16.1 us
  starting transfers between devices: 19.6 us -> 15.4 us
    all_gather x0 -> x1, waiting for transfers between devices: none -> 32.9 us  [local(): stacked = lax.all_gather(in_projection, 'cfg', axis=0, tiled=False)]
    all_gather x1, waiting for transfers between devices: 0.03 us -> 25.6 us  [local(): lax.all_gather(out_projection, ('cfg',) + SEQ, axis=1, tiled=True)]
    ppermute x1 -> x0, waiting for transfers between devices: 16.7 us -> none  [local(): shard_other = lax.ppermute(in_projection, 'cfg', SWAP)]
    dot_general x12 -> x24, matrix products: 20.8 us -> 12.5 us  [the longest x12 8.74 us: attend(): jnp.einsum('qhd,khd->hqk', query_rows, key_slab, preferred_element_type=j...]
    dynamic_slice x7 -> x1, local copies, waits for them, and re-layouts: 4.72 us -> 0.08 us  [attend(): clip_rows = lax.dynamic_slice_in_dim(query_clip, first_query, half_rows, 0)]
    ppermute x1, waiting for transfers between devices: 4.51 us -> 0.01 us  [local(): other_att = lax.ppermute(sent_att, 'cfg', SWAP)]
    another operation x3 -> x1, other arithmetic: 2.73 us -> 0.18 us  [the longest x2 2.55 us: local(): jnp.stack([jnp.where(is_cond, in_projection, shard_other), jnp.where(is_c...]
  transfers between devices with their start and end apart: 9 -> 9, of which waited for: 5 -> 5; matrix products, arithmetic and copies ran while one was open for 22% -> 12% of each run, Pallas kernels for 0% -> 0%
where the time goes in v6:
time: 255 us; the launch traced here: 254 us
  waiting for transfers between devices  173 us (68%)
  matrix products  31.8 us (12%)
  other arithmetic  16.1 us (6%)
  starting transfers between devices  15.4 us (6%)
  between operations  14.1 us (6%)
  local copies, waits for them, and re-layouts  3.83 us (2%)
    ppermute x1, waiting for transfers between devices, local(): other_rows = lax.ppermute(sent_rows, 'cfg', SWAP)  45.5 us
    all_gather x1, waiting for transfers between devices, local(): kv_mine = lax.all_gather(kv, 'x', axis=0, tiled=True)  39.9 us
    all_gather x1, waiting for transfers between devices, local(): stacked = lax.all_gather(in_projection, 'cfg', axis=0, tiled=False)  32.9 us
    all_to_all x1, waiting for transfers between devices, local(): lax.all_to_all(partial, BLK, 0, 0, tiled=False).astype(jnp.float32)  27.4 us
    all_gather x1, waiting for transfers between devices, local(): lax.all_gather(out_projection, ('cfg',) + SEQ, axis=1, tiled=True)  25.6 us
    dot_general x1, matrix products, local(): jnp.einsum('tabi,abiqe->tqe', mod_perm, piece, preferred_element_type=jnp...  10.1 us
    dot_general x12, matrix products, attend(): jnp.einsum('qhd,khd->hqk', query_rows, key_slab, preferred_element_type=j...  8.74 us
    all_to_all x1, starting transfers between devices, local(): full_states = lax.all_to_all(spread, BLK, 0, 0, tiled=False)  6.71 us
  transfers between devices with their start and end apart: 9, of which 5 were waited for; matrix products, arithmetic and copies ran while one was open for 12% of the time, Pallas kernels for 0%

profile of v6, /device:TPU:0, one launch (start us, length us, event | category | flops | bytes accessed | tf_op | source)
XLA Modules:
  0.0 253.8 jit_solution(4082337486552064951)
XLA Ops:
  6.5 0.7 all-gather.11.cloned.1.call-update
  7.3 32.9 %all-gather.11.cloned.1.call-done = bf16[640,3,384]{2,0,1:T(8,128)(2,1)} async-done(((bf16[320,3,384]{2,0,1:T(8,128)(2,1)}), bf16[640,3,384]{2,0,1:T(8,128)(2,1)}) %all-gather.11.cloned.1.call-update) | async-done | bytes 1474576 | tf_op jit(solution)/shard_map/all_gather | solution.py:96
  40.2 0.3 copy.54
  40.5 2.3 broadcast_in_dim.143
  42.8 6.7 %all-to-all-start = ((bf16[8,384,640]{1,2,0:T(8,128)(2,1)}), bf16[8,384,640]{1,2,0:T(8,128)(2,1)}, u32[]{:S(2)}, u32[]{:S(2)}) async-start(bf16[8,384,640]{1,2,0:T(8,128)(2,1)} %broadcast_in_dim.143), calls=%async_computation | async-start | bytes 7864320 | tf_op jit(solution)/shard_map/all_to_all | solution.py:85
  50.7 1.1 cosine_bitcast_fusion
  52.0 45.5 %collective-permute-done = bf16[192,640]{1,0:T(8,128)(2,1)S(1)} collective-permute-done((bf16[192,640]{1,0:T(8,128)(2,1)S(1)}, bf16[192,640]{1,0:T(8,128)(2,1)S(1)}, u32[]{:S(2)}, u32[]{:S(2)}) %collective-permute-start) | collective-permute-done | bytes 245792 | tf_op jit(solution)/shard_map/ppermute | solution.py:76
  97.7 2.9 %convert_reduce_fusion = f32[384]{0:T(512)S(1)} fusion(bf16[8,384,640]{1,2,0:T(8,128)(2,1)} %all-to-all-done), kind=kLoop, calls=%fused_computation.3 | loop fusion | flops 3931776 | bytes 3933696 | tf_op jit(solution)/shard_map/reduce_sum | solution.py:88
  100.6 3.3 %fusion.4 = f32[384]{0:T(512)S(1)} fusion(bf16[8,384,640]{1,2,0:T(8,128)(2,1)} %all-to-all-done, f32[384]{0:T(512)S(1)} %broadcast_multiply_fusion), kind=kLoop, calls=%fused_computation.6 | loop fusion | flops 7863936 | bytes 3935232 | tf_op jit(solution)/shard_map/reduce_sum | solution.py:90
  104.0 5.8 %fusion.7 = bf16[8,384,640]{1,2,0:T(8,128)(2,1)} fusion(bf16[8,384,640]{1,2,0:T(8,128)(2,1)} %all-to-all-done, f32[8,640]{1,0:T(8,128)S(1)} %add.236, f32[8,640]{1,0:T(8,128)S(1)} %add.235, f32[384]{0:T(512)S(1)} %add_rsqrt_fusion.2, f32[384]{0:T(512)S(1)} %broadcast_multiply_fusion), kind=kLoop, calls=%fused_computation.9 | loop fusion | flops 11796480 | bytes 7908352 | tf_op jit(solution)/shard_map/convert_element_type | solution.py:94
  109.8 10.1 %fusion = f32[384,3,384,1,1]{0,2,3,1,4:T(8,128)S(1)} fusion(bf16[384,8,2,320,1]{0,3,1,4,2:T(8,128)(2,1)} %bitcast.204, bf16[8,2,320,3,384]{4,2,1,0,3:T(8,128)(2,1)} %bitcast.212), kind=kOutput, calls=%fused_computation | convolution fusion | flops 4529848320 | bytes 17498112 | tf_op jit(solution)/shard_map/tabi,abiqe->tqe/dot_general | solution.py:103
  120.7 0.7 fusion.47
  121.5 0.9 pad_maximum_fusion
  122.4 0.5 all-gather.9.cloned.1.call-update
  123.5 0.8 broadcast_compare_fusion
  124.8 0.7 fusion.38
  125.5 39.9 %all-gather.7.cloned.1.call-done = bf16[1536,2,3,128]{3,0,2,1:T(8,128)(2,1)} async-done(((bf16[384,2,3,128]{3,0,2,1:T(8,128)(2,1)}), bf16[1536,2,3,128]{3,0,2,1:T(8,128)(2,1)}) %all-gather.7.cloned.1.call-update) | async-done | bytes 2359312 | tf_op jit(solution)/shard_map/all_gather | solution.py:124
  165.4 1.7 fusion.135
  167.1 1.6 fusion.137
  168.7 0.6 fusion.136
  169.2 0.6 fusion.129
  169.8 0.6 fusion.131
  170.3 0.6 fusion.130
  170.9 0.3 fusion.61
  171.2 0.3 fusion.70
  171.5 0.3 convolution_add_fusion.2
  171.8 0.3 convolution_add_fusion.1
  172.1 0.3 convolution_add_fusion.5
  172.5 0.3 convolution_add_fusion.4
  172.8 0.6 fusion.128
  173.3 0.5 fusion.127
  173.9 0.5 fusion.126
  174.4 0.3 fusion.65
  174.7 0.3 fusion.63
  175.1 0.3 fusion.50
  175.4 1.6 collective-permute-start.2
  177.1 0.5 fusion.134
  177.6 0.5 fusion.133
  178.1 0.5 fusion.132
  178.7 0.3 fusion.56
  179.0 0.3 fusion.54
  179.4 0.3 fusion.51
  179.7 25.6 %all-gather.9.cloned.1.call-done = bf16[384,5120]{0,1:T(8,128)(2,1)} async-done(((bf16[384,320]{0,1:T(8,128)(2,1)}), bf16[384,5120]{0,1:T(8,128)(2,1)}) %all-gather.9.cloned.1.call-update) | async-done | bytes 3932176 | tf_op jit(solution)/shard_map/all_gather | solution.py:176
  205.3 3.8 %fusion.76 = f32[192,8,640]{2,0,1:T(8,128)S(1)} fusion(bf16[384,8,640]{0,2,1:T(8,128)(2,1)} %bitcast.202, bf16[192,384]{1,0:T(8,128)(2,1)S(1)} %collective-permute-done.2, pred[]{:T(512)S(6)} %eq.178, bf16[3,24,8,128]{3,2,1,0:T(8,128)(2,1)S(1)} %fusion.51), kind=kOutput, calls=%fused_computation.139 | convolution fusion | flops 755048448 | bytes 8159233 | tf_op jit(solution)/shard_map/te,ebn->btn/dot_general | solution.py:180
  209.1 2.9 %fusion.10 = bf16[8,192,640]{2,1,0:T(8,128)(2,1)} fusion(f32[192,8,640]{2,0,1:T(8,128)S(1)} %fusion.76, bf16[384,8,640]{0,2,1:T(8,128)(2,1)S(1)} %bitcast.203, f32[]{:T(128)} %bitcast.201, bf16[192,384]{1,0:T(8,128)(2,1)S(1)} %collective-permute-done.2, pred[]{:T(512)S(6)} %eq.178, bf16[3,24,8,128]{3,2,1,0:T(8,128)(2,1)S(1)} %fusion.51), kind=kOutput, calls=%fused_computation.13 | convolution fusion | flops 758980608 | bytes 10125317 | tf_op jit(solution)/shard_map/te,ebn->btn/dot_general | solution.py:179
  212.0 6.7 %all-to-all-start.1 = ((bf16[8,192,640]{2,1,0:T(8,128)(2,1)}), bf16[8,192,640]{2,1,0:T(8,128)(2,1)S(1)}, u32[]{:S(2)}, u32[]{:S(2)}) async-start(bf16[8,192,640]{2,1,0:T(8,128)(2,1)} %fusion.10), calls=%async_computation.1 | async-start | bytes 3932160 | tf_op jit(solution)/shard_map/all_to_all | solution.py:182
  218.7 27.4 %all-to-all-done.1 = bf16[8,192,640]{2,1,0:T(8,128)(2,1)S(1)} async-done(((bf16[8,192,640]{2,1,0:T(8,128)(2,1)}), bf16[8,192,640]{2,1,0:T(8,128)(2,1)S(1)}, u32[]{:S(2)}, u32[]{:S(2)}) %all-to-all-start.1) | async-done | bytes 1966112 | tf_op jit(solution)/shard_map/all_to_all | solution.py:182
  246.4 0.9 add_bitcast_fusion
  (58 shorter events, 3.1 us)
Async XLA Ops:
  6.5 33.7 %copy-start.2 = (bf16[1,384,640]{2,1,0:T(8,128)(2,1)S(1)}, bf16[1,384,640]{2,1,0:T(8,128)(2,1)}, u32[]{:S(2)}) copy-start(bf16[1,384,640]{2,1,0:T(8,128)(2,1)} %param.9) | copy-start | bytes 1474564
  6.5 33.6 %all-gather.11.cloned.1.call-start = ((), (), s32[]{:S(2)}) async-start(), calls=%async_computation.4 | async-start | bytes 2211840 | tf_op jit(solution)/shard_map/all_gather | solution.py:96
  7.3 102.5 %all-gather.13.cloned.1.call-start = ((), (), s32[]{:S(2)}) async-start(), calls=%async_computation.5 | async-start | bytes 13271040 | tf_op jit(solution)/shard_map/all_gather | solution.py:97
  42.8 7.1 %copy-start.4 = (f32[3,5120]{1,0:T(4,128)S(1)}, f32[3,5120]{1,0:T(4,128)}, u32[]{:S(2)}) copy-start(f32[3,5120]{1,0:T(4,128)} %param.10) | copy-start | bytes 184324
  42.8 7.9 %copy-start.5 = (s32[3,384]{1,0:T(4,128)S(1)}, s32[3,384]{1,0:T(4,128)}, u32[]{:S(2)}) copy-start(s32[3,384]{1,0:T(4,128)} %param.14) | copy-start | bytes 13828
  42.8 7.9 %copy-start.6 = (f32[3,128]{1,0:T(4,128)S(1)}, f32[3,128]{1,0:T(4,128)}, u32[]{:S(2)}) copy-start(f32[3,128]{1,0:T(4,128)} %constant.91.clone) | copy-start | bytes 4612
  42.8 54.8 %all-to-all-start = ((bf16[8,384,640]{1,2,0:T(8,128)(2,1)}), bf16[8,384,640]{1,2,0:T(8,128)(2,1)}, u32[]{:S(2)}, u32[]{:S(2)}) async-start(bf16[8,384,640]{1,2,0:T(8,128)(2,1)} %broadcast_in_dim.143), calls=%async_computation | async-start | bytes 7864320 | tf_op jit(solution)/shard_map/all_to_all | solution.py:85
  49.5 115.9 %all-gather.7.cloned.1.call-start = ((), (), s32[]{:S(2)}) async-start(), calls=%async_computation.2 | async-start | bytes 2949120 | tf_op jit(solution)/shard_map/all_gather | solution.py:124
  49.6 47.9 %collective-permute-start = (bf16[192,640]{1,0:T(8,128)(2,1)S(1)}, bf16[192,640]{1,0:T(8,128)(2,1)S(1)}, u32[]{:S(2)}, u32[]{:S(2)}) collective-permute-start(bf16[192,640]{1,0:T(8,128)(2,1)S(1)} %dynamic-slice_bitcast_fusion), channel_id=1, source_target_pairs={{0,64},{64,0},{1,65},{65,1},{2,66},{66,2},{3,67},{67,3},{4,68},{68... | collective-permute-start | bytes 737288 | tf_op jit(solution)/shard_map/ppermute | solution.py:76
  119.9 0.9 copy-start.3
  120.2 2.7 %copy-start.7 = (s32[5]{0:T(128)S(1)}, s32[5]{0:T(128)}, u32[]{:S(2)}) copy-start(s32[5]{0:T(128)} %param.13) | copy-start | bytes 64
  122.4 82.9 %all-gather.9.cloned.1.call-start = ((), (), s32[]{:S(2)}) async-start(), calls=%async_computation.3 | async-start | bytes 4177920 | tf_op jit(solution)/shard_map/all_gather | solution.py:176
  165.4 3.3 %copy-start.1 = (bf16[1536,2,3,128]{3,0,2,1:T(8,128)(2,1)S(1)}, bf16[1536,2,3,128]{3,0,2,1:T(8,128)(2,1)}, u32[]{:S(2)}) copy-start(bf16[1536,2,3,128]{3,0,2,1:T(8,128)(2,1)} %all-gather.7.cloned.1.call-done) | copy-start | bytes 7077892
  165.4 7.3 %collective-permute-start.1 = (bf16[1536,2,3,128]{3,0,2,1:T(8,128)(2,1)}, bf16[1536,2,3,128]{3,0,2,1:T(8,128)(2,1)S(1)}, u32[]{:S(2)}, u32[]{:S(2)}) collective-permute-start(bf16[1536,2,3,128]{3,0,2,1:T(8,128)(2,1)} %all-gather.7.cloned.1.call-done), channel_id=1, source_target_pairs={{0,8},{8,0},{1,9},{9,1},{2,10},{10,2},{3,11},{11,3},{4,12},{12,4},... | collective-permute-start | bytes 7077896 | tf_op jit(solution)/shard_map/ppermute | solution.py:125
  175.4 29.9 %collective-permute-start.2 = (bf16[192,384]{1,0:T(8,128)(2,1)S(1)}, bf16[192,384]{1,0:T(8,128)(2,1)S(1)}, u32[]{:S(2)}, u32[]{:S(2)}) collective-permute-start(bf16[192,384]{1,0:T(8,128)(2,1)S(1)} %bitcast.209), channel_id=1, source_target_pairs={{0,64},{64,0},{1,65},{65,1},{2,66},{66,2},{3,67},{67,3},{4,68},{68... | collective-permute-start | bytes 442376 | tf_op jit(solution)/shard_map/ppermute | solution.py:172
  205.3 3.8 %copy-start = (bf16[384,5120]{0,1:T(8,128)(2,1)S(1)}, bf16[384,5120]{0,1:T(8,128)(2,1)}, u32[]{:S(2)}) copy-start(bf16[384,5120]{0,1:T(8,128)(2,1)} %all-gather.9.cloned.1.call-done) | copy-start | bytes 11796484
  212.0 34.1 %all-to-all-start.1 = ((bf16[8,192,640]{2,1,0:T(8,128)(2,1)}), bf16[8,192,640]{2,1,0:T(8,128)(2,1)S(1)}, u32[]{:S(2)}, u32[]{:S(2)}) async-start(bf16[8,192,640]{2,1,0:T(8,128)(2,1)} %fusion.10), calls=%async_computation.1 | async-start | bytes 3932160 | tf_op jit(solution)/shard_map/all_to_all | solution.py:182
Sparse Core Ops, SparseCore 0:
  9.0 31.1 all-gather.10
  41.9 64.8 all-gather.12
  122.5 42.8 all-gather.6
  167.0 38.2 all-gather.8

commit v7 on v6

--- a/solution.py
+++ b/solution.py
@@ -93,7 +93,13 @@
     mod_scale = modulation[1].reshape(n_blk, 1, feat_width)
     modulated = (normed * (1.0 + mod_scale) + mod_shift).astype(jnp.bfloat16)
 
-    stacked = lax.all_gather(in_projection, "cfg", axis=0, tiled=False)
+    shard_other = lax.ppermute(in_projection, "cfg", SWAP)
+    stacked = jnp.stack(
+        [
+            jnp.where(is_cond, in_projection, shard_other),
+            jnp.where(is_cond, shard_other, in_projection),
+        ]
+    )
     piece = lax.all_gather(stacked, SEQ, axis=0, tiled=False)
     n_seq = piece.shape[0]
     rows = in_projection.shape[0]
@@ -121,20 +127,25 @@
     value_rows = mixed[:, 2].astype(jnp.bfloat16)
 
     kv = jnp.stack([key_rows, value_rows], axis=1)
-    kv_mine = lax.all_gather(kv, "x", axis=0, tiled=True)
+    n_x = lax.axis_size("x")
+    x_index = lax.axis_index("x")
+    kv_mine = jnp.concatenate(
+        [kv] + [lax.ppermute(kv, "x", [(i, (i + j) % n_x) for i in range(n_x)]) for j in range(1, n_x)],
+        axis=0,
+    )
     kv_other = lax.ppermute(kv_mine, "core", SWAP)
     kv_all = jnp.concatenate([kv_mine, kv_other], axis=0)
     key_piece = kv_all[:, 0]
     value_piece = kv_all[:, 1]
     row_count = key_piece.shape[0]
-    n_x = kv_mine.shape[0] // tok_count
 
     clip_ends = jnp.cumsum(lengths)
     query_clip = clip_of(clip_ends, seq * tok_count + jnp.arange(tok_count, dtype=jnp.int32))
     key_row = jnp.arange(row_count, dtype=jnp.int32)
     key_block = key_row // tok_count
     key_core = jnp.where(key_block < n_x, core, 1 - core)
-    key_token = ((key_block % n_x) * 2 + key_core) * tok_count + key_row % tok_count
+    key_x = (x_index - key_block % n_x + n_x) % n_x
+    key_token = (key_x * 2 + key_core) * tok_count + key_row % tok_count
     key_clip_all = clip_of(clip_ends, key_token)
 
     score_scale = HEAD_DIM ** (-0.5)

time: 255 us -> 222 us (0.87)
  waiting for transfers between devices: 173 us -> 119 us
  starting transfers between devices: 15.4 us -> 26.1 us
  other arithmetic: 16.1 us -> 21.3 us
  local copies, waits for them, and re-layouts: 3.83 us -> 9.03 us
    all_gather x2 -> x0, waiting for transfers between devices: 72.8 us -> none  [the longest x1 39.9 us: local(): kv_mine = lax.all_gather(kv, 'x', axis=0, tiled=True)]
    ppermute x0 -> x4, waiting for transfers between devices: none -> 48.9 us  [the longest x3 32.2 us: local(): lax.ppermute(kv, 'x', [(i, (i + j) % n_x) for i in range(n_x)])]
    all_gather x1, waiting for transfers between devices: 25.6 us -> 0.02 us  [local(): lax.all_gather(out_projection, ('cfg',) + SEQ, axis=1, tiled=True)]
    ppermute x0 -> x4, starting transfers between devices: none -> 7.68 us  [the longest x3 5.66 us: local(): lax.ppermute(kv, 'x', [(i, (i + j) % n_x) for i in range(n_x)])]
    unnamed x19 -> x48, local copies, waits for them, and re-layouts: 0.7 us -> 4.98 us
    ppermute x1, waiting for transfers between devices: 45.5 us -> 42.1 us  [local(): other_rows = lax.ppermute(sent_rows, 'cfg', SWAP)]
  transfers between devices with their start and end apart: 9 -> 11, of which waited for: 5 -> 6; matrix products, arithmetic and copies ran while one was open for 12% -> 21% of each run, Pallas kernels for 0% -> 0%
where the time goes in v7:
time: 222 us; the launch traced here: 220 us
  waiting for transfers between devices  119 us (54%)
  matrix products  30.4 us (14%)
  starting transfers between devices  26.1 us (12%)
  other arithmetic  21.3 us (10%)
  between operations  14.6 us (7%)
  local copies, waits for them, and re-layouts  9.03 us (4%)
    ppermute x1, waiting for transfers between devices, local(): other_rows = lax.ppermute(sent_rows, 'cfg', SWAP)  42.1 us
    ppermute x3, waiting for transfers between devices, local(): lax.ppermute(kv, 'x', [(i, (i + j) % n_x) for i in range(n_x)])  32.2 us
    all_to_all x1, waiting for transfers between devices, local(): lax.all_to_all(partial, BLK, 0, 0, tiled=False).astype(jnp.float32)  26.2 us
    ppermute x1, waiting for transfers between devices, local(): shard_other = lax.ppermute(in_projection, 'cfg', SWAP)  16.7 us
    dot_general x1, matrix products, local(): jnp.einsum('tabi,abiqe->tqe', mod_perm, piece, preferred_element_type=jnp...  10.1 us
    all_to_all x1, starting transfers between devices, local(): full_states = lax.all_to_all(spread, BLK, 0, 0, tiled=False)  7.74 us
    all_to_all x1, starting transfers between devices, local(): lax.all_to_all(partial, BLK, 0, 0, tiled=False).astype(jnp.float32)  7.51 us
    dot_general x12, matrix products, attend(): jnp.einsum('qhd,khd->hqk', query_rows, key_slab, preferred_element_type=j...  6.49 us
  transfers between devices with their start and end apart: 11, of which 6 were waited for; matrix products, arithmetic and copies ran while one was open for 21% of the time, Pallas kernels for 0%

profile of v7, /device:TPU:0, one launch (start us, length us, event | category | flops | bytes accessed | tf_op | source)
XLA Modules:
  0.0 220.0 jit_solution(7316797946096431515)
XLA Ops:
  6.5 2.0 collective-permute-start.1
  8.6 16.7 %collective-permute-done.1 = bf16[320,3,384]{2,0,1:T(8,128)(2,1)S(1)} collective-permute-done((bf16[320,3,384]{2,0,1:T(8,128)(2,1)}, bf16[320,3,384]{2,0,1:T(8,128)(2,1)S(1)}, u32[]{:S(2)}, u32[]{:S(2)}) %collective-permute-start.1) | collective-permute-done | bytes 737312 | tf_op jit(solution)/shard_map/ppermute | solution.py:96
  25.3 1.3 select_bitcast_fusion.1
  26.5 1.3 pad_maximum_fusion.1
  27.8 1.0 copy-done.1
  29.1 2.3 %broadcast_in_dim.143 = bf16[8,384,640]{1,2,0:T(8,128)(2,1)} broadcast(bf16[384,640]{0,1:T(8,128)(2,1)S(1)} %copy.56), dimensions={1,2} | broadcast | bytes 4423680 | tf_op jit(solution)/shard_map/broadcast_in_dim | solution.py:84
  31.4 7.7 %all-to-all-start = ((bf16[8,384,640]{1,2,0:T(8,128)(2,1)}), bf16[8,384,640]{1,2,0:T(8,128)(2,1)}, u32[]{:S(2)}, u32[]{:S(2)}) async-start(bf16[8,384,640]{1,2,0:T(8,128)(2,1)} %broadcast_in_dim.143), calls=%async_computation | async-start | bytes 7864320 | tf_op jit(solution)/shard_map/all_to_all | solution.py:85
  39.2 1.1 collective-permute-start
  41.0 0.7 add_reduce_fusion
  41.7 1.1 cosine_bitcast_fusion
  43.6 1.6 broadcast_compare_fusion
  45.1 42.1 %collective-permute-done = bf16[192,640]{1,0:T(8,128)(2,1)S(1)} collective-permute-done((bf16[192,640]{1,0:T(8,128)(2,1)S(1)}, bf16[192,640]{1,0:T(8,128)(2,1)S(1)}, u32[]{:S(2)}, u32[]{:S(2)}) %collective-permute-start) | collective-permute-done | bytes 245792 | tf_op jit(solution)/shard_map/ppermute | solution.py:76
  87.3 0.9 convert_add_fusion
  88.2 2.9 %convert_reduce_fusion = f32[384]{0:T(512)S(1)} fusion(bf16[8,384,640]{1,2,0:T(8,128)(2,1)} %all-to-all-done), kind=kLoop, calls=%fused_computation.3 | loop fusion | flops 3931776 | bytes 3933696 | tf_op jit(solution)/shard_map/reduce_sum | solution.py:88
  91.1 3.2 %fusion.4 = f32[384]{0:T(512)S(1)} fusion(bf16[8,384,640]{1,2,0:T(8,128)(2,1)} %all-to-all-done, f32[384]{0:T(512)S(1)} %broadcast_multiply_fusion), kind=kLoop, calls=%fused_computation.6 | loop fusion | flops 7863936 | bytes 3935232 | tf_op jit(solution)/shard_map/reduce_sum | solution.py:90
  94.4 5.8 %fusion.7 = bf16[8,384,640]{1,2,0:T(8,128)(2,1)} fusion(bf16[8,384,640]{1,2,0:T(8,128)(2,1)} %all-to-all-done, f32[8,640]{1,0:T(8,128)S(1)} %add.251, f32[8,640]{1,0:T(8,128)S(1)} %add.250, f32[384]{0:T(512)S(1)} %add_rsqrt_fusion.2, f32[384]{0:T(512)S(1)} %broadcast_multiply_fusion), kind=kLoop, calls=%fused_computation.9 | loop fusion | flops 11796480 | bytes 7908352 | tf_op jit(solution)/shard_map/convert_element_type | solution.py:94
  100.2 10.1 %fusion = f32[384,3,384,1,1]{0,2,3,1,4:T(8,128)S(1)} fusion(bf16[384,8,2,320,1]{0,3,1,4,2:T(8,128)(2,1)} %bitcast.207, bf16[8,2,320,3,384]{4,2,3,1,0:T(8,128)(2,1)} %bitcast.214), kind=kOutput, calls=%fused_computation | convolution fusion | flops 4529848320 | bytes 17498112 | tf_op jit(solution)/shard_map/tabi,abiqe->tqe/dot_general | solution.py:109
  111.3 0.7 fusion.51
  112.0 0.9 pad_maximum_fusion.2
  112.8 1.4 collective-permute-start.2
  114.3 2.7 %collective-permute-start.3 = (bf16[384,2,3,128]{3,0,2,1:T(8,128)(2,1)}, bf16[384,2,3,128]{3,0,2,1:T(8,128)(2,1)S(1)}, u32[]{:S(2)}, u32[]{:S(2)}) collective-permute-start(bf16[384,2,3,128]{3,0,2,1:T(8,128)(2,1)} %pad_maximum_fusion.2), channel_id=1, source_target_pairs={{0,32},{16,48},{32,0},{48,16},{1,33},{17,49},{33,1},{49,17},{2,34}... | collective-permute-start | bytes 1769480 | tf_op jit(solution)/shard_map/ppermute | solution.py:133
  117.0 1.5 collective-permute-start.4
  119.0 1.7 fusion.38
  120.7 17.3 %collective-permute-done.2 = bf16[384,2,3,128]{3,0,2,1:T(8,128)(2,1)S(1)} collective-permute-done((bf16[384,2,3,128]{3,0,2,1:T(8,128)(2,1)}, bf16[384,2,3,128]{3,0,2,1:T(8,128)(2,1)S(1)}, u32[]{:S(2)}, u32[]{:S(2)}) %collective-permute-start.2) | collective-permute-done | bytes 589856 | tf_op jit(solution)/shard_map/ppermute | solution.py:133
  138.1 14.9 %collective-permute-done.3 = bf16[384,2,3,128]{3,0,2,1:T(8,128)(2,1)S(1)} collective-permute-done((bf16[384,2,3,128]{3,0,2,1:T(8,128)(2,1)}, bf16[384,2,3,128]{3,0,2,1:T(8,128)(2,1)S(1)}, u32[]{:S(2)}, u32[]{:S(2)}) %collective-permute-start.3) | collective-permute-done | bytes 589856 | tf_op jit(solution)/shard_map/ppermute | solution.py:133
  152.9 0.7 pad_maximum_fusion
  154.1 0.6 copy-done.17
  154.7 0.5 fusion.150
  155.3 0.8 copy-done.16
  156.1 0.5 fusion.144
  157.0 0.5 fusion.151
  157.6 0.5 fusion.145
  158.5 0.5 fusion.149
  159.1 0.5 fusion.143
  161.1 0.5 fusion.142
  161.7 0.5 fusion.141
  162.6 0.5 fusion.140
  164.4 1.9 collective-permute-start.6
  166.3 0.5 fusion.148
  166.9 0.5 fusion.147
  167.8 0.5 fusion.146
  169.6 1.4 collective-permute-done.6
  171.0 3.8 %fusion.85 = f32[192,8,640]{2,0,1:T(8,128)S(1)} fusion(bf16[384,8,640]{0,2,1:T(8,128)(2,1)} %bitcast.205, bf16[192,384]{1,0:T(8,128)(2,1)S(1)} %collective-permute-done.6, pred[]{:T(512)S(6)} %eq.179, bf16[3,24,8,128]{3,2,1,0:T(8,128)(2,1)S(1)} %fusion.55), kind=kOutput, calls=%fused_computation.149 | convolution fusion | flops 755048448 | bytes 8159233 | tf_op jit(solution)/shard_map/te,ebn->btn/dot_general | solution.py:191
  174.8 2.9 %fusion.10 = bf16[8,192,640]{2,1,0:T(8,128)(2,1)} fusion(f32[192,8,640]{2,0,1:T(8,128)S(1)} %fusion.85, bf16[384,8,640]{0,2,1:T(8,128)(2,1)S(1)} %bitcast.206, f32[]{:T(128)} %bitcast.204, bf16[192,384]{1,0:T(8,128)(2,1)S(1)} %collective-permute-done.6, pred[]{:T(512)S(6)} %eq.179, bf16[3,24,8,128]{3,2,1,0:T(8,128)(2,1)S(1)} %fusion.55), kind=kOutput, calls=%fused_computation.13 | convolution fusion | flops 758980608 | bytes 10125317 | tf_op jit(solution)/shard_map/te,ebn->btn/dot_general | solution.py:190
  177.6 7.5 %all-to-all-start.1 = ((bf16[8,192,640]{2,1,0:T(8,128)(2,1)}), bf16[8,192,640]{2,1,0:T(8,128)(2,1)S(1)}, u32[]{:S(2)}, u32[]{:S(2)}) async-start(bf16[8,192,640]{2,1,0:T(8,128)(2,1)} %fusion.10), calls=%async_computation.1 | async-start | bytes 3932160 | tf_op jit(solution)/shard_map/all_to_all | solution.py:193
  185.2 0.7 dynamic-slice_reduce_fusion
  185.9 26.2 %all-to-all-done.1 = bf16[8,192,640]{2,1,0:T(8,128)(2,1)S(1)} async-done(((bf16[8,192,640]{2,1,0:T(8,128)(2,1)}), bf16[8,192,640]{2,1,0:T(8,128)(2,1)S(1)}, u32[]{:S(2)}, u32[]{:S(2)}) %all-to-all-start.1) | async-done | bytes 1966112 | tf_op jit(solution)/shard_map/all_to_all | solution.py:193
  212.3 0.9 add_bitcast_fusion
  (94 shorter events, 8.7 us)
Async XLA Ops:
  6.5 93.6 %all-gather.6.cloned.1.call-start = ((), (), s32[]{:S(2)}) async-start(), calls=%async_computation.3 | async-start | bytes 13271040 | tf_op jit(solution)/shard_map/all_gather | solution.py:103
  6.5 18.7 %collective-permute-start.1 = (bf16[320,3,384]{2,0,1:T(8,128)(2,1)}, bf16[320,3,384]{2,0,1:T(8,128)(2,1)S(1)}, u32[]{:S(2)}, u32[]{:S(2)}) collective-permute-start(bf16[320,3,384]{2,0,1:T(8,128)(2,1)} %param.11), channel_id=1, source_target_pairs={{0,64},{64,0},{1,65},{65,1},{2,66},{66,2},{3,67},{67,3},{4,68},{68... | collective-permute-start | bytes 2211848 | tf_op jit(solution)/shard_map/ppermute | solution.py:96
  27.8 1.0 copy-start.1
  31.4 9.6 %copy-start.18 = (f32[3,5120]{1,0:T(4,128)S(1)}, f32[3,5120]{1,0:T(4,128)}, u32[]{:S(2)}) copy-start(f32[3,5120]{1,0:T(4,128)} %param.10) | copy-start | bytes 184324
  31.4 10.3 %copy-start.19 = (s32[3,384]{1,0:T(4,128)S(1)}, s32[3,384]{1,0:T(4,128)}, u32[]{:S(2)}) copy-start(s32[3,384]{1,0:T(4,128)} %param.14) | copy-start | bytes 13828
  31.4 10.3 %copy-start.20 = (f32[3,128]{1,0:T(4,128)S(1)}, f32[3,128]{1,0:T(4,128)}, u32[]{:S(2)}) copy-start(f32[3,128]{1,0:T(4,128)} %constant.96.clone) | copy-start | bytes 4612
  31.4 56.8 %all-to-all-start = ((bf16[8,384,640]{1,2,0:T(8,128)(2,1)}), bf16[8,384,640]{1,2,0:T(8,128)(2,1)}, u32[]{:S(2)}, u32[]{:S(2)}) async-start(bf16[8,384,640]{1,2,0:T(8,128)(2,1)} %broadcast_in_dim.143), calls=%async_computation | async-start | bytes 7864320 | tf_op jit(solution)/shard_map/all_to_all | solution.py:85
  39.1 3.9 %copy-start.21 = (s32[5]{0:T(128)S(1)}, s32[5]{0:T(128)}, u32[]{:S(2)}) copy-start(s32[5]{0:T(128)} %param.13) | copy-start | bytes 64
  39.1 130.5 %all-gather.4.cloned.1.call-start = ((), (), s32[]{:S(2)}) async-start(), calls=%async_computation.2 | async-start | bytes 4177920 | tf_op jit(solution)/shard_map/all_gather | solution.py:187
  39.2 48.1 %collective-permute-start = (bf16[192,640]{1,0:T(8,128)(2,1)S(1)}, bf16[192,640]{1,0:T(8,128)(2,1)S(1)}, u32[]{:S(2)}, u32[]{:S(2)}) collective-permute-start(bf16[192,640]{1,0:T(8,128)(2,1)S(1)} %dynamic-slice_bitcast_fusion), channel_id=1, source_target_pairs={{0,64},{64,0},{1,65},{65,1},{2,66},{66,2},{3,67},{67,3},{4,68},{68... | collective-permute-start | bytes 737288 | tf_op jit(solution)/shard_map/ppermute | solution.py:76
  42.9 68.3 %copy-start.3 = (f32[384,128]{1,0:T(8,128)}, f32[384,128]{1,0:T(8,128)S(1)}, u32[]{:S(2)}) copy-start(f32[384,128]{1,0:T(8,128)S(1)} %copy.61) | copy-start | bytes 589828
  43.0 68.1 %copy-start.4 = (f32[384,128]{1,0:T(8,128)}, f32[384,128]{1,0:T(8,128)S(1)}, u32[]{:S(2)}) copy-start(f32[384,128]{1,0:T(8,128)S(1)} %copy.62) | copy-start | bytes 589828
  110.4 0.8 copy-start.5
  112.8 25.2 %collective-permute-start.2 = (bf16[384,2,3,128]{3,0,2,1:T(8,128)(2,1)}, bf16[384,2,3,128]{3,0,2,1:T(8,128)(2,1)S(1)}, u32[]{:S(2)}, u32[]{:S(2)}) collective-permute-start(bf16[384,2,3,128]{3,0,2,1:T(8,128)(2,1)} %pad_maximum_fusion.2), channel_id=1, source_target_pairs={{0,16},{16,32},{32,48},{48,0},{1,17},{17,33},{33,49},{49,1},{2,18}... | collective-permute-start | bytes 1769480 | tf_op jit(solution)/shard_map/ppermute | solution.py:133
  114.3 38.6 %collective-permute-start.3 = (bf16[384,2,3,128]{3,0,2,1:T(8,128)(2,1)}, bf16[384,2,3,128]{3,0,2,1:T(8,128)(2,1)S(1)}, u32[]{:S(2)}, u32[]{:S(2)}) collective-permute-start(bf16[384,2,3,128]{3,0,2,1:T(8,128)(2,1)} %pad_maximum_fusion.2), channel_id=1, source_target_pairs={{0,32},{16,48},{32,0},{48,16},{1,33},{17,49},{33,1},{49,17},{2,34}... | collective-permute-start | bytes 1769480 | tf_op jit(solution)/shard_map/ppermute | solution.py:133
  117.0 35.9 %collective-permute-start.4 = (bf16[384,2,3,128]{3,0,2,1:T(8,128)(2,1)}, bf16[384,2,3,128]{3,0,2,1:T(8,128)(2,1)S(1)}, u32[]{:S(2)}, u32[]{:S(2)}) collective-permute-start(bf16[384,2,3,128]{3,0,2,1:T(8,128)(2,1)} %pad_maximum_fusion.2), channel_id=1, source_target_pairs={{0,48},{16,0},{32,16},{48,32},{1,49},{17,1},{33,17},{49,33},{2,50}... | collective-permute-start | bytes 1769480 | tf_op jit(solution)/shard_map/ppermute | solution.py:133
  153.7 7.2 %collective-permute-start.5 = (bf16[1536,2,3,128]{3,0,2,1:T(8,128)(2,1)S(1)}, bf16[1536,2,3,128]{3,0,2,1:T(8,128)(2,1)S(1)}, u32[]{:S(2)}, u32[]{:S(2)}) collective-permute-start(bf16[1536,2,3,128]{3,0,2,1:T(8,128)(2,1)S(1)} %pad_maximum_fusion), channel_id=1, source_target_pairs={{0,8},{8,0},{1,9},{9,1},{2,10},{10,2},{3,11},{11,3},{4,12},{12,4},... | collective-permute-start | bytes 7077896 | tf_op jit(solution)/shard_map/ppermute | solution.py:136
  153.8 0.9 copy-start.17
  155.2 0.9 copy-start.16
  156.1 0.9 copy-start.15
  156.7 0.9 copy-start.14
  157.6 0.9 copy-start.13
  158.1 0.9 copy-start.12
  160.2 0.9 copy-start.11
  160.8 0.9 copy-start.10
  161.6 0.9 copy-start.9
  164.0 2.3 %copy-start.8 = (pred[192,512]{1,0:T(8,128)(4,1)S(1)}, pred[192,512]{1,0:T(8,128)(4,1)}, u32[]{:S(2)}) copy-start(pred[192,512]{1,0:T(8,128)(4,1)} %get-tuple-element.58) | copy-start | bytes 294916
  164.4 2.5 %copy-start.7 = (pred[192,512]{1,0:T(8,128)(4,1)S(1)}, pred[192,512]{1,0:T(8,128)(4,1)}, u32[]{:S(2)}) copy-start(pred[192,512]{1,0:T(8,128)(4,1)} %get-tuple-element.67) | copy-start | bytes 294916
  164.4 6.5 %collective-permute-start.6 = (bf16[192,384]{1,0:T(8,128)(2,1)S(1)}, bf16[192,384]{1,0:T(8,128)(2,1)S(1)}, u32[]{:S(2)}, u32[]{:S(2)}) collective-permute-start(bf16[192,384]{1,0:T(8,128)(2,1)S(1)} %bitcast.211), channel_id=1, source_target_pairs={{0,64},{64,0},{1,65},{65,1},{2,66},{66,2},{3,67},{67,3},{4,68},{68... | collective-permute-start | bytes 442376 | tf_op jit(solution)/shard_map/ppermute | solution.py:183
  166.9 0.9 copy-start.6
  171.0 3.8 %copy-start = (bf16[384,5120]{0,1:T(8,128)(2,1)S(1)}, bf16[384,5120]{0,1:T(8,128)(2,1)}, u32[]{:S(2)}) copy-start(bf16[384,5120]{0,1:T(8,128)(2,1)} %all-gather.4.cloned.1.call-done) | copy-start | bytes 11796484
  177.6 34.4 %all-to-all-start.1 = ((bf16[8,192,640]{2,1,0:T(8,128)(2,1)}), bf16[8,192,640]{2,1,0:T(8,128)(2,1)S(1)}, u32[]{:S(2)}, u32[]{:S(2)}) async-start(bf16[8,192,640]{2,1,0:T(8,128)(2,1)} %fusion.10), calls=%async_computation.1 | async-start | bytes 3932160 | tf_op jit(solution)/shard_map/all_to_all | solution.py:193
  185.8 26.5 %copy-start.2 = (f32[192,640]{1,0:T(8,128)S(1)}, f32[192,640]{1,0:T(8,128)}, u32[]{:S(2)}) copy-start(f32[192,640]{1,0:T(8,128)} %convert_add_fusion) | copy-start | bytes 1474564
Sparse Core Ops, SparseCore 0:
  27.9 66.1 all-gather.5
  95.8 57.4 all-gather.3

commit v8 on v4

--- a/solution.py
+++ b/solution.py
@@ -127,59 +127,70 @@
     value_rows = mixed[:, 2].astype(jnp.bfloat16)
 
     kv = jnp.stack([key_rows, value_rows], axis=1)
-    kv_mine = lax.all_gather(kv, "x", axis=0, tiled=True)
-    kv_other = lax.ppermute(kv_mine, "core", SWAP)
-    kv_all = jnp.concatenate([kv_mine, kv_other], axis=0)
-    key_piece = kv_all[:, 0]
-    value_piece = kv_all[:, 1]
-    row_count = key_piece.shape[0]
-    n_x = kv_mine.shape[0] // tok_count
-
+    n_x = lax.axis_size("x")
+    x_index = lax.axis_index("x")
     clip_ends = jnp.cumsum(lengths)
-    query_clip = clip_of(clip_ends, seq * tok_count + jnp.arange(tok_count, dtype=jnp.int32))
-    key_row = jnp.arange(row_count, dtype=jnp.int32)
-    key_block = key_row // tok_count
-    key_core = jnp.where(key_block < n_x, core, 1 - core)
-    key_token = ((key_block % n_x) * 2 + key_core) * tok_count + key_row % tok_count
-    key_clip_all = clip_of(clip_ends, key_token)
+    local_rows = jnp.arange(tok_count, dtype=jnp.int32)
+    query_clip = clip_of(clip_ends, seq * tok_count + local_rows)
+
+    blocks = []
+    for j in range(n_x):
+        if j == 0:
+            kv_x = kv
+        else:
+            kv_x = lax.ppermute(kv, "x", [(i, (i + j) % n_x) for i in range(n_x)])
+        x_src = (x_index - j + n_x) % n_x
+        blocks.append((kv_x, x_src * 2 + core))
+        blocks.append((lax.ppermute(kv_x, "core", SWAP), x_src * 2 + 1 - core))
 
     score_scale = HEAD_DIM ** (-0.5)
-    start_state = (
-        jnp.zeros((tok_count, head_count, HEAD_DIM), jnp.float32),
-        jnp.zeros((head_count, tok_count), jnp.float32),
-    )
-    key_block_size = 512 if row_count % 512 == 0 else row_count
-
-    def key_step(block_index, running):
+
+    def update(running, query_rows, clip_rows, block):
         numerator, denominator = running
-        key_slab = lax.dynamic_slice_in_dim(key_piece, block_index * key_block_size, key_block_size, 0)
-        value_slab = lax.dynamic_slice_in_dim(value_piece, block_index * key_block_size, key_block_size, 0)
-        key_clip = lax.dynamic_slice_in_dim(key_clip_all, block_index * key_block_size, key_block_size, 0)
+        kv_block, source = block
+        key_clip = clip_of(clip_ends, source * tok_count + local_rows)
         scores = (
-            jnp.einsum("qhd,khd->hqk", queries, key_slab, preferred_element_type=jnp.float32)
+            jnp.einsum("qhd,khd->hqk", query_rows, kv_block[:, 0], preferred_element_type=jnp.float32)
             * score_scale
         )
-        same_clip = query_clip[:, None] == key_clip[None, :]
+        same_clip = clip_rows[:, None] == key_clip[None, :]
         weights = jnp.where(same_clip[None], jnp.exp(scores), 0.0)
         numerator = numerator + jnp.einsum(
             "hqk,khd->qhd",
             weights.astype(jnp.bfloat16),
-            value_slab,
+            kv_block[:, 1],
             preferred_element_type=jnp.float32,
         )
         denominator = denominator + jnp.sum(weights, -1)
         return (numerator, denominator)
 
-    numerator, denominator = lax.fori_loop(0, row_count // key_block_size, key_step, start_state)
-    attended = (
-        (numerator / jnp.transpose(denominator)[:, :, None])
-        .astype(jnp.bfloat16)
-        .reshape(tok_count, inner_width)
-    )
-
-    sent_att = lax.dynamic_slice_in_dim(attended, (1 - cfg) * half_rows, half_rows, 0)
+    running = (
+        jnp.zeros((tok_count, head_count, HEAD_DIM), jnp.float32),
+        jnp.zeros((head_count, tok_count), jnp.float32),
+    )
+    for block in blocks[:-1]:
+        running = update(running, queries, query_clip, block)
+
+    def attend(first_query):
+        part = (
+            lax.dynamic_slice_in_dim(running[0], first_query, half_rows, 0),
+            lax.dynamic_slice_in_dim(running[1], first_query, half_rows, 1),
+        )
+        numerator, denominator = update(
+            part,
+            lax.dynamic_slice_in_dim(queries, first_query, half_rows, 0),
+            lax.dynamic_slice_in_dim(query_clip, first_query, half_rows, 0),
+            blocks[-1],
+        )
+        return (
+            (numerator / jnp.transpose(denominator)[:, :, None])
+            .astype(jnp.bfloat16)
+            .reshape(half_rows, inner_width)
+        )
+
+    sent_att = attend((1 - cfg) * half_rows)
     other_att = lax.ppermute(sent_att, "cfg", SWAP)
-    mine_att = lax.dynamic_slice_in_dim(attended, cfg * half_rows, half_rows, 0)
+    mine_att = attend(cfg * half_rows)
     cond_att = jnp.where(is_cond, mine_att, other_att)
     uncond_att = jnp.where(is_cond, other_att, mine_att)
     out_piece = lax.all_gather(out_projection, ("cfg",) + SEQ, axis=1, tiled=True).reshape(

time: 247 us -> 225 us (0.911)
  waiting for transfers between devices: 131 us -> 119 us
  local copies, waits for them, and re-layouts: 15.9 us -> 4.97 us
  starting transfers between devices: 19.6 us -> 26.7 us
  matrix products: 41.7 us -> 38.7 us
    all_gather x1 -> x0, waiting for transfers between devices: 39.3 us -> none  [local(): kv_mine = lax.all_gather(kv, 'x', axis=0, tiled=True)]
    ppermute x1 -> x7, waiting for transfers between devices: 0.01 us -> 31.5 us  [the longest x3 31.5 us: local(): kv_x = lax.ppermute(kv, 'x', [(i, (i + j) % n_x) for i in range(n_x)])]
    ppermute x1 -> x7, starting transfers between devices: 0.01 us -> 6.35 us  [the longest x3 6.34 us: local(): kv_x = lax.ppermute(kv, 'x', [(i, (i + j) % n_x) for i in range(n_x)])]
    dynamic_slice x7 -> x1, local copies, waits for them, and re-layouts: 4.72 us -> 0.08 us  [attend(): lax.dynamic_slice_in_dim(query_clip, first_query, half_rows, 0)]
    ppermute x1, waiting for transfers between devices: 44.3 us -> 41.5 us  [local(): other_rows = lax.ppermute(sent_rows, 'cfg', SWAP)]
    squeeze x1 -> x0, local copies, waits for them, and re-layouts: 2.51 us -> none  [local(): key_piece = kv_all[:, 0]]
    dot_general x12 -> x18, matrix products: 20.8 us -> 18.7 us  [the longest x9 10.2 us: update(): jnp.einsum('qhd,khd->hqk', query_rows, kv_block[:, 0], preferred_element_...]
  transfers between devices with their start and end apart: 9 -> 14, of which waited for: 5 -> 7; matrix products, arithmetic and copies ran while one was open for 22% -> 24% of each run, Pallas kernels for 0% -> 0%
where the time goes in v8:
time: 225 us; the launch traced here: 224 us
  waiting for transfers between devices  119 us (53%)
  matrix products  38.7 us (17%)
  starting transfers between devices  26.7 us (12%)
  other arithmetic  19.7 us (9%)
  between operations  14.6 us (6%)
  local copies, waits for them, and re-layouts  4.97 us (2%)
    ppermute x1, waiting for transfers between devices, local(): other_rows = lax.ppermute(sent_rows, 'cfg', SWAP)  41.5 us
    ppermute x3, waiting for transfers between devices, local(): kv_x = lax.ppermute(kv, 'x', [(i, (i + j) % n_x) for i in range(n_x)])  31.5 us
    all_to_all x1, waiting for transfers between devices, local(): lax.all_to_all(partial, BLK, 0, 0, tiled=False).astype(jnp.float32)  26.2 us
    ppermute x1, waiting for transfers between devices, local(): shard_other = lax.ppermute(in_projection, 'cfg', SWAP)  16.7 us
    dot_general x9, matrix products, update(): jnp.einsum('qhd,khd->hqk', query_rows, kv_block[:, 0], preferred_element_...  10.2 us
    dot_general x1, matrix products, local(): jnp.einsum('tabi,abiqe->tqe', mod_perm, piece, preferred_element_type=jnp...  10.1 us
    dot_general x9, matrix products, update(): jnp.einsum('hqk,khd->qhd', weights.astype(jnp.bfloat16), kv_block[:, 1],...  8.47 us
    all_to_all x1, starting transfers between devices, local(): full_states = lax.all_to_all(spread, BLK, 0, 0, tiled=False)  7.75 us
  transfers between devices with their start and end apart: 14, of which 7 were waited for; matrix products, arithmetic and copies ran while one was open for 24% of the time, Pallas kernels for 0%

profile of v8, /device:TPU:0, one launch (start us, length us, event | category | flops | bytes accessed | tf_op | source)
XLA Modules:
  0.0 223.8 jit_solution(5010842769755727170)
XLA Ops:
  6.5 2.0 collective-permute-start.1
  8.6 16.7 %collective-permute-done.1 = bf16[320,3,384]{2,0,1:T(8,128)(2,1)S(1)} collective-permute-done((bf16[320,3,384]{2,0,1:T(8,128)(2,1)}, bf16[320,3,384]{2,0,1:T(8,128)(2,1)S(1)}, u32[]{:S(2)}, u32[]{:S(2)}) %collective-permute-start.1) | collective-permute-done | bytes 737312 | tf_op jit(solution)/shard_map/ppermute | solution.py:96
  25.3 1.3 select_bitcast_fusion.1
  26.5 1.3 pad_maximum_fusion
  28.1 2.3 %broadcast_in_dim.71 = bf16[8,384,640]{1,2,0:T(8,128)(2,1)} broadcast(bf16[384,640]{0,1:T(8,128)(2,1)S(1)} %copy.126), dimensions={1,2} | broadcast | bytes 4423680 | tf_op jit(solution)/shard_map/broadcast_in_dim | solution.py:84
  30.4 7.8 %all-to-all-start = ((bf16[8,384,640]{1,2,0:T(8,128)(2,1)}), bf16[8,384,640]{1,2,0:T(8,128)(2,1)}, u32[]{:S(2)}, u32[]{:S(2)}) async-start(bf16[8,384,640]{1,2,0:T(8,128)(2,1)} %broadcast_in_dim.71), calls=%async_computation | async-start | bytes 7864320 | tf_op jit(solution)/shard_map/all_to_all | solution.py:85
  38.2 1.1 collective-permute-start
  39.8 0.6 add_reduce_fusion
  40.4 1.1 cosine_bitcast_fusion
  41.5 1.5 broadcast_compare_fusion.1
  44.0 0.8 broadcast_compare_fusion.7
  44.8 41.5 %collective-permute-done = bf16[192,640]{1,0:T(8,128)(2,1)S(1)} collective-permute-done((bf16[192,640]{1,0:T(8,128)(2,1)S(1)}, bf16[192,640]{1,0:T(8,128)(2,1)S(1)}, u32[]{:S(2)}, u32[]{:S(2)}) %collective-permute-start) | collective-permute-done | bytes 245792 | tf_op jit(solution)/shard_map/ppermute | solution.py:76
  86.5 2.8 %convert_reduce_fusion = f32[384]{0:T(512)S(1)} fusion(bf16[8,384,640]{1,2,0:T(8,128)(2,1)} %all-to-all-done), kind=kLoop, calls=%fused_computation.3 | loop fusion | flops 3931776 | bytes 3933696 | tf_op jit(solution)/shard_map/reduce_sum | solution.py:88
  89.3 3.2 %fusion.4 = f32[384]{0:T(512)S(1)} fusion(bf16[8,384,640]{1,2,0:T(8,128)(2,1)} %all-to-all-done, f32[384]{0:T(512)S(1)} %broadcast_multiply_fusion), kind=kLoop, calls=%fused_computation.6 | loop fusion | flops 7863936 | bytes 3935232 | tf_op jit(solution)/shard_map/reduce_sum | solution.py:90
  92.5 5.9 %fusion.7 = bf16[8,384,640]{1,2,0:T(8,128)(2,1)} fusion(bf16[8,384,640]{1,2,0:T(8,128)(2,1)} %all-to-all-done, f32[8,640]{1,0:T(8,128)S(1)} %add.303, f32[8,640]{1,0:T(8,128)S(1)} %add.302, f32[384]{0:T(512)S(1)} %add_rsqrt_fusion.2, f32[384]{0:T(512)S(1)} %broadcast_multiply_fusion), kind=kLoop, calls=%fused_computation.9 | loop fusion | flops 11796480 | bytes 7908352 | tf_op jit(solution)/shard_map/convert_element_type | solution.py:94
  98.5 10.1 %fusion = f32[384,3,384,1,1]{0,2,3,1,4:T(8,128)S(1)} fusion(bf16[384,8,2,320,1]{0,3,1,4,2:T(8,128)(2,1)} %bitcast.184, bf16[8,2,320,3,384]{4,2,3,1,0:T(8,128)(2,1)} %bitcast.192), kind=kOutput, calls=%fused_computation | convolution fusion | flops 4529848320 | bytes 17498112 | tf_op jit(solution)/shard_map/tabi,abiqe->tqe/dot_general | solution.py:109
  109.5 0.7 fusion.20
  110.2 3.1 %collective-permute-start.5 = (bf16[384,2,3,128]{3,0,2,1:T(8,128)(2,1)S(1)}, bf16[384,2,3,128]{3,0,2,1:T(8,128)(2,1)}, u32[]{:S(2)}, u32[]{:S(2)}) collective-permute-start(bf16[384,2,3,128]{3,0,2,1:T(8,128)(2,1)S(1)} %pad_maximum_fusion.1), channel_id=1, source_target_pairs={{0,32},{16,48},{32,0},{48,16},{1,33},{17,49},{33,1},{49,17},{2,34}... | collective-permute-start | bytes 1769480 | tf_op jit(solution)/shard_map/ppermute | solution.py:141
  113.3 0.6 collective-permute-start.3
  113.9 2.6 %collective-permute-start.7 = (bf16[384,2,3,128]{3,0,2,1:T(8,128)(2,1)S(1)}, bf16[384,2,3,128]{3,0,2,1:T(8,128)(2,1)}, u32[]{:S(2)}, u32[]{:S(2)}) collective-permute-start(bf16[384,2,3,128]{3,0,2,1:T(8,128)(2,1)S(1)} %pad_maximum_fusion.1), channel_id=1, source_target_pairs={{0,48},{16,0},{32,16},{48,32},{1,49},{17,1},{33,17},{49,33},{2,50}... | collective-permute-start | bytes 1769480 | tf_op jit(solution)/shard_map/ppermute | solution.py:141
  117.1 1.5 fusion.19
  118.6 1.6 fusion.68
  120.6 15.1 %collective-permute-done.5 = bf16[384,2,3,128]{3,0,2,1:T(8,128)(2,1)} collective-permute-done((bf16[384,2,3,128]{3,0,2,1:T(8,128)(2,1)S(1)}, bf16[384,2,3,128]{3,0,2,1:T(8,128)(2,1)}, u32[]{:S(2)}, u32[]{:S(2)}) %collective-permute-start.5) | collective-permute-done | bytes 589856 | tf_op jit(solution)/shard_map/ppermute | solution.py:141
  135.8 14.4 %collective-permute-done.3 = bf16[384,2,3,128]{3,0,2,1:T(8,128)(2,1)} collective-permute-done((bf16[384,2,3,128]{3,0,2,1:T(8,128)(2,1)S(1)}, bf16[384,2,3,128]{3,0,2,1:T(8,128)(2,1)}, u32[]{:S(2)}, u32[]{:S(2)}) %collective-permute-start.3) | collective-permute-done | bytes 589856 | tf_op jit(solution)/shard_map/ppermute | solution.py:141
  150.2 1.9 collective-permute-done.7
  152.1 1.6 fusion.65
  153.7 1.6 fusion.63
  155.4 1.6 fusion.69
  157.0 1.4 fusion.24
  158.4 1.4 convolution_add_fusion.3
  159.8 1.4 fusion.21
  161.2 1.6 fusion.67
  162.8 1.4 convolution_add_fusion.2
  164.2 0.6 fusion.64
  165.1 0.6 fusion.66
  165.8 0.5 fusion.62
  166.3 0.5 fusion.70
  166.8 0.4 fusion.15
  167.2 0.4 fusion.16
  168.2 1.9 collective-permute-start.9
  170.1 1.3 fusion.38
  171.6 3.2 %collective-permute-done.9 = bf16[192,384]{1,0:T(8,128)(2,1)S(1)} collective-permute-done((bf16[192,384]{1,0:T(8,128)(2,1)S(1)}, bf16[192,384]{1,0:T(8,128)(2,1)S(1)}, u32[]{:S(2)}, u32[]{:S(2)}) %collective-permute-start.9) | collective-permute-done | bytes 147488 | tf_op jit(solution)/shard_map/ppermute | solution.py:192
  174.8 3.8 %fusion.48 = f32[192,8,640]{2,0,1:T(8,128)S(1)} fusion(bf16[384,8,640]{0,2,1:T(8,128)(2,1)} %bitcast.182, bf16[192,384]{1,0:T(8,128)(2,1)S(1)} %collective-permute-done.9, bf16[192,384]{1,0:T(8,128)(2,1)S(1)} %copy.152, pred[]{:T(512)S(6)} %eq.147), kind=kOutput, calls=%fused_computation.102 | convolution fusion | flops 755048448 | bytes 8159233 | tf_op jit(solution)/shard_map/te,ebn->btn/dot_general | solution.py:200
  178.5 2.9 %fusion.10 = bf16[8,192,640]{2,1,0:T(8,128)(2,1)} fusion(f32[192,8,640]{2,0,1:T(8,128)S(1)} %fusion.48, bf16[384,8,640]{0,2,1:T(8,128)(2,1)S(1)} %bitcast.183, f32[]{:T(128)} %bitcast.181, bf16[192,384]{1,0:T(8,128)(2,1)S(1)} %copy.152, bf16[192,384]{1,0:T(8,128)(2,1)S(1)} %collective-permute-done.9, pred[]{:T(512)S(6)} %eq.147), kind=kOutput, calls=%fused_computation.13 | convolution fusion | flops 758980608 | bytes 10125317 | tf_op jit(solution)/shard_map/te,ebn->btn/dot_general | solution.py:199
  181.4 7.5 %all-to-all-start.1 = ((bf16[8,192,640]{2,1,0:T(8,128)(2,1)}), bf16[8,192,640]{2,1,0:T(8,128)(2,1)S(1)}, u32[]{:S(2)}, u32[]{:S(2)}) async-start(bf16[8,192,640]{2,1,0:T(8,128)(2,1)} %fusion.10), calls=%async_computation.1 | async-start | bytes 3932160 | tf_op jit(solution)/shard_map/all_to_all | solution.py:202
  189.0 0.7 dynamic-slice_reduce_fusion
  189.7 26.2 %all-to-all-done.1 = bf16[8,192,640]{2,1,0:T(8,128)(2,1)S(1)} async-done(((bf16[8,192,640]{2,1,0:T(8,128)(2,1)}), bf16[8,192,640]{2,1,0:T(8,128)(2,1)S(1)}, u32[]{:S(2)}, u32[]{:S(2)}) %all-to-all-start.1) | async-done | bytes 1966112 | tf_op jit(solution)/shard_map/all_to_all | solution.py:202
  216.1 0.9 add_bitcast_fusion
  (81 shorter events, 4.3 us)
Async XLA Ops:
  6.5 91.9 %all-gather.6.cloned.1.call-start = ((), (), s32[]{:S(2)}) async-start(), calls=%async_computation.3 | async-start | bytes 13271040 | tf_op jit(solution)/shard_map/all_gather | solution.py:103
  6.5 18.7 %collective-permute-start.1 = (bf16[320,3,384]{2,0,1:T(8,128)(2,1)}, bf16[320,3,384]{2,0,1:T(8,128)(2,1)S(1)}, u32[]{:S(2)}, u32[]{:S(2)}) collective-permute-start(bf16[320,3,384]{2,0,1:T(8,128)(2,1)} %param.11), channel_id=1, source_target_pairs={{0,64},{64,0},{1,65},{65,1},{2,66},{66,2},{3,67},{67,3},{4,68},{68... | collective-permute-start | bytes 2211848 | tf_op jit(solution)/shard_map/ppermute | solution.py:96
  26.5 1.3 copy-start.1
  30.4 9.0 %copy-start.15 = (s32[5]{0:T(128)S(1)}, s32[5]{0:T(128)}, u32[]{:S(2)}) copy-start(s32[5]{0:T(128)} %param.13) | copy-start | bytes 64
  30.4 9.4 %copy-start.11 = (f32[3,5120]{1,0:T(4,128)S(1)}, f32[3,5120]{1,0:T(4,128)}, u32[]{:S(2)}) copy-start(f32[3,5120]{1,0:T(4,128)} %param.10) | copy-start | bytes 184324
  30.4 10.0 %copy-start.12 = (s32[3,384]{1,0:T(4,128)S(1)}, s32[3,384]{1,0:T(4,128)}, u32[]{:S(2)}) copy-start(s32[3,384]{1,0:T(4,128)} %param.14) | copy-start | bytes 13828
  30.4 10.0 %copy-start.13 = (f32[3,128]{1,0:T(4,128)S(1)}, f32[3,128]{1,0:T(4,128)}, u32[]{:S(2)}) copy-start(f32[3,128]{1,0:T(4,128)} %constant.93.clone) | copy-start | bytes 4612
  30.4 56.1 %all-to-all-start = ((bf16[8,384,640]{1,2,0:T(8,128)(2,1)}), bf16[8,384,640]{1,2,0:T(8,128)(2,1)}, u32[]{:S(2)}, u32[]{:S(2)}) async-start(bf16[8,384,640]{1,2,0:T(8,128)(2,1)} %broadcast_in_dim.71), calls=%async_computation | async-start | bytes 7864320 | tf_op jit(solution)/shard_map/all_to_all | solution.py:85
  38.2 133.4 %all-gather.4.cloned.1.call-start = ((), (), s32[]{:S(2)}) async-start(), calls=%async_computation.2 | async-start | bytes 4177920 | tf_op jit(solution)/shard_map/all_gather | solution.py:196
  38.2 48.1 %collective-permute-start = (bf16[192,640]{1,0:T(8,128)(2,1)S(1)}, bf16[192,640]{1,0:T(8,128)(2,1)S(1)}, u32[]{:S(2)}, u32[]{:S(2)}) collective-permute-start(bf16[192,640]{1,0:T(8,128)(2,1)S(1)} %dynamic-slice_bitcast_fusion), channel_id=1, source_target_pairs={{0,64},{64,0},{1,65},{65,1},{2,66},{66,2},{3,67},{67,3},{4,68},{68... | collective-permute-start | bytes 737288 | tf_op jit(solution)/shard_map/ppermute | solution.py:76
  108.6 0.8 copy-start.2
  110.2 25.5 %collective-permute-start.5 = (bf16[384,2,3,128]{3,0,2,1:T(8,128)(2,1)S(1)}, bf16[384,2,3,128]{3,0,2,1:T(8,128)(2,1)}, u32[]{:S(2)}, u32[]{:S(2)}) collective-permute-start(bf16[384,2,3,128]{3,0,2,1:T(8,128)(2,1)S(1)} %pad_maximum_fusion.1), channel_id=1, source_target_pairs={{0,32},{16,48},{32,0},{48,16},{1,33},{17,49},{33,1},{49,17},{2,34}... | collective-permute-start | bytes 1769480 | tf_op jit(solution)/shard_map/ppermute | solution.py:141
  113.3 36.8 %collective-permute-start.3 = (bf16[384,2,3,128]{3,0,2,1:T(8,128)(2,1)S(1)}, bf16[384,2,3,128]{3,0,2,1:T(8,128)(2,1)}, u32[]{:S(2)}, u32[]{:S(2)}) collective-permute-start(bf16[384,2,3,128]{3,0,2,1:T(8,128)(2,1)S(1)} %pad_maximum_fusion.1), channel_id=1, source_target_pairs={{0,16},{16,32},{32,48},{48,0},{1,17},{17,33},{33,49},{49,1},{2,18}... | collective-permute-start | bytes 1769480 | tf_op jit(solution)/shard_map/ppermute | solution.py:141
  113.9 41.4 %collective-permute-start.2 = (bf16[384,2,3,128]{3,0,2,1:T(8,128)(2,1)S(1)}, bf16[384,2,3,128]{3,0,2,1:T(8,128)(2,1)}, u32[]{:S(2)}, u32[]{:S(2)}) collective-permute-start(bf16[384,2,3,128]{3,0,2,1:T(8,128)(2,1)S(1)} %pad_maximum_fusion.1), channel_id=1, source_target_pairs={{0,8},{8,0},{1,9},{9,1},{2,10},{10,2},{3,11},{11,3},{4,12},{12,4},... | collective-permute-start | bytes 1769480 | tf_op jit(solution)/shard_map/ppermute | solution.py:144
  113.9 38.2 %collective-permute-start.7 = (bf16[384,2,3,128]{3,0,2,1:T(8,128)(2,1)S(1)}, bf16[384,2,3,128]{3,0,2,1:T(8,128)(2,1)}, u32[]{:S(2)}, u32[]{:S(2)}) collective-permute-start(bf16[384,2,3,128]{3,0,2,1:T(8,128)(2,1)S(1)} %pad_maximum_fusion.1), channel_id=1, source_target_pairs={{0,48},{16,0},{32,16},{48,32},{1,49},{17,1},{33,17},{49,33},{2,50}... | collective-permute-start | bytes 1769480 | tf_op jit(solution)/shard_map/ppermute | solution.py:141
  118.6 33.5 %copy-start.8 = (pred[384,384]{0,1:T(8,128)(4,1)S(1)}, pred[384,384]{0,1:T(8,128)(4,1)}, u32[]{:S(2)}) copy-start(pred[384,384]{0,1:T(8,128)(4,1)} %get-tuple-element.37) | copy-start | bytes 442372
  120.6 33.1 %copy-start.7 = (pred[384,384]{0,1:T(8,128)(4,1)S(1)}, pred[384,384]{0,1:T(8,128)(4,1)}, u32[]{:S(2)}) copy-start(pred[384,384]{0,1:T(8,128)(4,1)} %get-tuple-element.38) | copy-start | bytes 442372
  135.8 28.4 %collective-permute-start.6 = (bf16[384,2,3,128]{3,0,2,1:T(8,128)(2,1)}, bf16[384,2,3,128]{3,0,2,1:T(8,128)(2,1)S(1)}, u32[]{:S(2)}, u32[]{:S(2)}) collective-permute-start(bf16[384,2,3,128]{3,0,2,1:T(8,128)(2,1)} %collective-permute-done.5), channel_id=1, source_target_pairs={{0,8},{8,0},{1,9},{9,1},{2,10},{10,2},{3,11},{11,3},{4,12},{12,4},... | collective-permute-start | bytes 1769480 | tf_op jit(solution)/shard_map/ppermute | solution.py:144
  150.2 14.7 %collective-permute-start.4 = (bf16[384,2,3,128]{3,0,2,1:T(8,128)(2,1)}, bf16[384,2,3,128]{3,0,2,1:T(8,128)(2,1)S(1)}, u32[]{:S(2)}, u32[]{:S(2)}) collective-permute-start(bf16[384,2,3,128]{3,0,2,1:T(8,128)(2,1)} %collective-permute-done.3), channel_id=1, source_target_pairs={{0,8},{8,0},{1,9},{9,1},{2,10},{10,2},{3,11},{11,3},{4,12},{12,4},... | collective-permute-start | bytes 1769480 | tf_op jit(solution)/shard_map/ppermute | solution.py:144
  152.1 13.6 %collective-permute-start.8 = (bf16[384,2,3,128]{3,0,2,1:T(8,128)(2,1)}, bf16[384,2,3,128]{3,0,2,1:T(8,128)(2,1)S(1)}, u32[]{:S(2)}, u32[]{:S(2)}) collective-permute-start(bf16[384,2,3,128]{3,0,2,1:T(8,128)(2,1)} %collective-permute-done.7), channel_id=1, source_target_pairs={{0,8},{8,0},{1,9},{9,1},{2,10},{10,2},{3,11},{11,3},{4,12},{12,4},... | collective-permute-start | bytes 1769480 | tf_op jit(solution)/shard_map/ppermute | solution.py:144
  153.7 1.7 copy-start.6
  158.4 2.8 %copy-start.5 = (pred[384,384]{0,1:T(8,128)(4,1)S(1)}, pred[384,384]{0,1:T(8,128)(4,1)}, u32[]{:S(2)}) copy-start(pred[384,384]{0,1:T(8,128)(4,1)} %get-tuple-element.35) | copy-start | bytes 442372
  162.8 1.4 copy-start.4
  164.2 0.9 copy-start.3
  164.9 0.9 copy-start.10
  165.1 1.2 copy-start.9
  165.8 1.9 copy-start.14
  168.2 6.6 %collective-permute-start.9 = (bf16[192,384]{1,0:T(8,128)(2,1)S(1)}, bf16[192,384]{1,0:T(8,128)(2,1)S(1)}, u32[]{:S(2)}, u32[]{:S(2)}) collective-permute-start(bf16[192,384]{1,0:T(8,128)(2,1)S(1)} %copy.150), channel_id=1, source_target_pairs={{0,64},{64,0},{1,65},{65,1},{2,66},{66,2},{3,67},{67,3},{4,68},{68... | collective-permute-start | bytes 442376 | tf_op jit(solution)/shard_map/ppermute | solution.py:192
  174.8 3.8 %copy-start = (bf16[384,5120]{0,1:T(8,128)(2,1)S(1)}, bf16[384,5120]{0,1:T(8,128)(2,1)}, u32[]{:S(2)}) copy-start(bf16[384,5120]{0,1:T(8,128)(2,1)} %all-gather.4.cloned.1.call-done) | copy-start | bytes 11796484
  181.4 34.4 %all-to-all-start.1 = ((bf16[8,192,640]{2,1,0:T(8,128)(2,1)}), bf16[8,192,640]{2,1,0:T(8,128)(2,1)S(1)}, u32[]{:S(2)}, u32[]{:S(2)}) async-start(bf16[8,192,640]{2,1,0:T(8,128)(2,1)} %fusion.10), calls=%async_computation.1 | async-start | bytes 3932160 | tf_op jit(solution)/shard_map/all_to_all | solution.py:202
Sparse Core Ops, SparseCore 0:
  28.0 66.1 all-gather.5
  95.8 57.5 all-gather.3

commit v9 on v7

--- a/solution.py
+++ b/solution.py
@@ -129,10 +129,13 @@
     kv = jnp.stack([key_rows, value_rows], axis=1)
     n_x = lax.axis_size("x")
     x_index = lax.axis_index("x")
-    kv_mine = jnp.concatenate(
-        [kv] + [lax.ppermute(kv, "x", [(i, (i + j) % n_x) for i in range(n_x)]) for j in range(1, n_x)],
-        axis=0,
-    )
+    from_behind = lax.ppermute(kv, "x", [(i, (i + 1) % n_x) for i in range(n_x)])
+    from_ahead = lax.ppermute(kv, "x", [(i, (i - 1) % n_x) for i in range(n_x)])
+    relayed = jnp.where(core == 0, from_behind, from_ahead)
+    relay_pairs = [(i * 2, ((i + 1) % n_x) * 2) for i in range(n_x)]
+    relay_pairs += [(i * 2 + 1, ((i - 1) % n_x) * 2 + 1) for i in range(n_x)]
+    from_far = lax.ppermute(relayed, SEQ, relay_pairs)
+    kv_mine = jnp.concatenate([kv, from_behind, from_far, from_ahead], axis=0)
     kv_other = lax.ppermute(kv_mine, "core", SWAP)
     kv_all = jnp.concatenate([kv_mine, kv_other], axis=0)
     key_piece = kv_all[:, 0]

time: 222 us -> 218 us (0.982)
    ppermute x1, waiting for transfers between devices: 42.1 us -> 44.4 us  [local(): other_rows = lax.ppermute(sent_rows, 'cfg', SWAP)]
    unnamed x48 -> x49, local copies, waits for them, and re-layouts: 4.98 us -> 3.68 us
  transfers between devices with their start and end apart: 11 -> 11, of which waited for: 6 -> 7; matrix products, arithmetic and copies ran while one was open for 21% -> 20% of each run, Pallas kernels for 0% -> 0%
where the time goes in v9:
time: 218 us; the launch traced here: 217 us
  waiting for transfers between devices  120 us (55%)
  matrix products  29.4 us (13%)
  starting transfers between devices  25.3 us (12%)
  other arithmetic  20.1 us (9%)
  between operations  14.6 us (7%)
  local copies, waits for them, and re-layouts  7.06 us (3%)
    ppermute x1, waiting for transfers between devices, local(): other_rows = lax.ppermute(sent_rows, 'cfg', SWAP)  44.4 us
    all_to_all x1, waiting for transfers between devices, local(): lax.all_to_all(partial, BLK, 0, 0, tiled=False).astype(jnp.float32)  26.8 us
    ppermute x1, waiting for transfers between devices, local(): lax.ppermute(kv, 'x', [(i, (i + 1) % n_x) for i in range(n_x)])  20.5 us
    ppermute x1, waiting for transfers between devices, local(): shard_other = lax.ppermute(in_projection, 'cfg', SWAP)  16.7 us
    dot_general x1, matrix products, local(): jnp.einsum('tabi,abiqe->tqe', mod_perm, piece, preferred_element_type=jnp...  10.1 us
    ppermute x1, waiting for transfers between devices, local(): from_far = lax.ppermute(relayed, SEQ, relay_pairs)  8.23 us
    all_to_all x1, starting transfers between devices, local(): full_states = lax.all_to_all(spread, BLK, 0, 0, tiled=False)  7.75 us
    all_to_all x1, starting transfers between devices, local(): lax.all_to_all(partial, BLK, 0, 0, tiled=False).astype(jnp.float32)  7.63 us
  transfers between devices with their start and end apart: 11, of which 7 were waited for; matrix products, arithmetic and copies ran while one was open for 20% of the time, Pallas kernels for 0%

profile of v9, /device:TPU:0, one launch (start us, length us, event | category | flops | bytes accessed | tf_op | source)
XLA Modules:
  0.0 216.7 jit_solution(874652224137909095)
XLA Ops:
  6.5 2.0 collective-permute-start.1
  8.6 16.7 %collective-permute-done.1 = bf16[320,3,384]{2,0,1:T(8,128)(2,1)S(1)} collective-permute-done((bf16[320,3,384]{2,0,1:T(8,128)(2,1)}, bf16[320,3,384]{2,0,1:T(8,128)(2,1)S(1)}, u32[]{:S(2)}, u32[]{:S(2)}) %collective-permute-start.1) | collective-permute-done | bytes 737312 | tf_op jit(solution)/shard_map/ppermute | solution.py:96
  25.3 1.3 select_bitcast_fusion.1
  26.5 1.3 pad_maximum_fusion.1
  27.8 1.0 copy-done.1
  29.1 2.3 %broadcast_in_dim.143 = bf16[8,384,640]{1,2,0:T(8,128)(2,1)} broadcast(bf16[384,640]{0,1:T(8,128)(2,1)S(1)} %copy.56), dimensions={1,2} | broadcast | bytes 4423680 | tf_op jit(solution)/shard_map/broadcast_in_dim | solution.py:84
  31.4 7.8 %all-to-all-start = ((bf16[8,384,640]{1,2,0:T(8,128)(2,1)}), bf16[8,384,640]{1,2,0:T(8,128)(2,1)}, u32[]{:S(2)}, u32[]{:S(2)}) async-start(bf16[8,384,640]{1,2,0:T(8,128)(2,1)} %broadcast_in_dim.143), calls=%async_computation | async-start | bytes 7864320 | tf_op jit(solution)/shard_map/all_to_all | solution.py:85
  39.2 1.1 collective-permute-start
  40.8 1.1 cosine_bitcast_fusion
  42.9 44.4 %collective-permute-done = bf16[192,640]{1,0:T(8,128)(2,1)S(1)} collective-permute-done((bf16[192,640]{1,0:T(8,128)(2,1)S(1)}, bf16[192,640]{1,0:T(8,128)(2,1)S(1)}, u32[]{:S(2)}, u32[]{:S(2)}) %collective-permute-start) | collective-permute-done | bytes 245792 | tf_op jit(solution)/shard_map/ppermute | solution.py:76
  87.4 2.8 %convert_reduce_fusion = f32[384]{0:T(512)S(1)} fusion(bf16[8,384,640]{1,2,0:T(8,128)(2,1)} %all-to-all-done), kind=kLoop, calls=%fused_computation.3 | loop fusion | flops 3931776 | bytes 3933696 | tf_op jit(solution)/shard_map/reduce_sum | solution.py:88
  90.3 3.2 %fusion.4 = f32[384]{0:T(512)S(1)} fusion(bf16[8,384,640]{1,2,0:T(8,128)(2,1)} %all-to-all-done, f32[384]{0:T(512)S(1)} %broadcast_multiply_fusion), kind=kLoop, calls=%fused_computation.6 | loop fusion | flops 7863936 | bytes 3935232 | tf_op jit(solution)/shard_map/reduce_sum | solution.py:90
  93.5 5.8 %fusion.7 = bf16[8,384,640]{1,2,0:T(8,128)(2,1)} fusion(bf16[8,384,640]{1,2,0:T(8,128)(2,1)} %all-to-all-done, f32[8,640]{1,0:T(8,128)S(1)} %add.251, f32[8,640]{1,0:T(8,128)S(1)} %add.250, f32[384]{0:T(512)S(1)} %add_rsqrt_fusion.2, f32[384]{0:T(512)S(1)} %broadcast_multiply_fusion), kind=kLoop, calls=%fused_computation.9 | loop fusion | flops 11796480 | bytes 7908352 | tf_op jit(solution)/shard_map/convert_element_type | solution.py:94
  99.3 10.1 %fusion = f32[384,3,384,1,1]{0,2,3,1,4:T(8,128)S(1)} fusion(bf16[384,8,2,320,1]{0,3,1,4,2:T(8,128)(2,1)} %bitcast.207, bf16[8,2,320,3,384]{4,2,3,1,0:T(8,128)(2,1)} %bitcast.214), kind=kOutput, calls=%fused_computation | convolution fusion | flops 4529848320 | bytes 17498112 | tf_op jit(solution)/shard_map/tabi,abiqe->tqe/dot_general | solution.py:109
  110.4 0.7 fusion.51
  111.1 0.9 pad_maximum_fusion.2
  112.0 1.5 collective-permute-start.2
  113.5 1.7 collective-permute-start.3
  115.4 1.5 broadcast_compare_fusion
  117.4 20.5 %collective-permute-done.2 = bf16[384,2,3,128]{3,0,2,1:T(8,128)(2,1)S(1)} collective-permute-done((bf16[384,2,3,128]{3,0,2,1:T(8,128)(2,1)}, bf16[384,2,3,128]{3,0,2,1:T(8,128)(2,1)S(1)}, u32[]{:S(2)}, u32[]{:S(2)}) %collective-permute-start.2) | collective-permute-done | bytes 589856 | tf_op jit(solution)/shard_map/ppermute | solution.py:132
  137.9 1.9 collective-permute-done.3
  140.0 1.8 collective-permute-start.4
  141.9 0.7 fusion.38
  142.6 0.6 fusion.150
  143.1 8.2 %collective-permute-done.4 = bf16[384,2,3,128]{3,0,2,1:T(8,128)(2,1)S(1)} collective-permute-done((bf16[384,2,3,128]{3,0,2,1:T(8,128)(2,1)S(1)}, bf16[384,2,3,128]{3,0,2,1:T(8,128)(2,1)S(1)}, u32[]{:S(2)}, u32[]{:S(2)}) %collective-permute-start.4) | collective-permute-done | bytes 589856 | tf_op jit(solution)/shard_map/ppermute | solution.py:137
  151.4 0.7 pad_maximum_fusion
  152.2 0.6 fusion.144
  153.1 0.5 copy-done.16
  153.7 0.5 fusion.151
  154.2 0.5 fusion.145
  154.8 0.3 copy-done.14
  155.1 0.5 fusion.149
  155.7 0.5 fusion.143
  157.7 0.5 fusion.142
  158.4 0.5 fusion.141
  159.2 0.5 fusion.140
  161.1 1.6 collective-permute-start.6
  162.7 0.5 fusion.148
  163.2 0.6 fusion.147
  163.8 0.3 copy-done.7
  164.1 0.5 fusion.146
  165.6 0.3 fusion.55
  165.9 1.7 collective-permute-done.6
  167.6 3.8 %fusion.85 = f32[192,8,640]{2,0,1:T(8,128)S(1)} fusion(bf16[384,8,640]{0,2,1:T(8,128)(2,1)} %bitcast.205, bf16[192,384]{1,0:T(8,128)(2,1)S(1)} %collective-permute-done.6, pred[]{:T(512)S(6)} %eq.182, bf16[3,24,8,128]{3,2,1,0:T(8,128)(2,1)S(1)} %fusion.55), kind=kOutput, calls=%fused_computation.150 | convolution fusion | flops 755048448 | bytes 8159233 | tf_op jit(solution)/shard_map/te,ebn->btn/dot_general | solution.py:194
  171.4 2.9 %fusion.10 = bf16[8,192,640]{2,1,0:T(8,128)(2,1)} fusion(f32[192,8,640]{2,0,1:T(8,128)S(1)} %fusion.85, bf16[384,8,640]{0,2,1:T(8,128)(2,1)S(1)} %bitcast.206, f32[]{:T(128)} %bitcast.204, bf16[192,384]{1,0:T(8,128)(2,1)S(1)} %collective-permute-done.6, pred[]{:T(512)S(6)} %eq.182, bf16[3,24,8,128]{3,2,1,0:T(8,128)(2,1)S(1)} %fusion.55), kind=kOutput, calls=%fused_computation.13 | convolution fusion | flops 758980608 | bytes 10125317 | tf_op jit(solution)/shard_map/te,ebn->btn/dot_general | solution.py:193
  174.3 7.6 %all-to-all-start.1 = ((bf16[8,192,640]{2,1,0:T(8,128)(2,1)}), bf16[8,192,640]{2,1,0:T(8,128)(2,1)S(1)}, u32[]{:S(2)}, u32[]{:S(2)}) async-start(bf16[8,192,640]{2,1,0:T(8,128)(2,1)} %fusion.10), calls=%async_computation.1 | async-start | bytes 3932160 | tf_op jit(solution)/shard_map/all_to_all | solution.py:196
  181.9 26.8 %all-to-all-done.1 = bf16[8,192,640]{2,1,0:T(8,128)(2,1)S(1)} async-done(((bf16[8,192,640]{2,1,0:T(8,128)(2,1)}), bf16[8,192,640]{2,1,0:T(8,128)(2,1)S(1)}, u32[]{:S(2)}, u32[]{:S(2)}) %all-to-all-start.1) | async-done | bytes 1966112 | tf_op jit(solution)/shard_map/all_to_all | solution.py:196
  209.0 0.9 add_bitcast_fusion
  (96 shorter events, 7.8 us)
Async XLA Ops:
  6.5 92.8 %all-gather.6.cloned.1.call-start = ((), (), s32[]{:S(2)}) async-start(), calls=%async_computation.3 | async-start | bytes 13271040 | tf_op jit(solution)/shard_map/all_gather | solution.py:103
  6.5 18.7 %collective-permute-start.1 = (bf16[320,3,384]{2,0,1:T(8,128)(2,1)}, bf16[320,3,384]{2,0,1:T(8,128)(2,1)S(1)}, u32[]{:S(2)}, u32[]{:S(2)}) collective-permute-start(bf16[320,3,384]{2,0,1:T(8,128)(2,1)} %param.11), channel_id=1, source_target_pairs={{0,64},{64,0},{1,65},{65,1},{2,66},{66,2},{3,67},{67,3},{4,68},{68... | collective-permute-start | bytes 2211848 | tf_op jit(solution)/shard_map/ppermute | solution.py:96
  27.8 1.0 copy-start.1
  31.4 9.0 %copy-start.22 = (s32[5]{0:T(128)S(1)}, s32[5]{0:T(128)}, u32[]{:S(2)}) copy-start(s32[5]{0:T(128)} %param.13) | copy-start | bytes 64
  31.4 9.3 %copy-start.19 = (f32[3,5120]{1,0:T(4,128)S(1)}, f32[3,5120]{1,0:T(4,128)}, u32[]{:S(2)}) copy-start(f32[3,5120]{1,0:T(4,128)} %param.10) | copy-start | bytes 184324
  31.4 9.4 %copy-start.20 = (s32[3,384]{1,0:T(4,128)S(1)}, s32[3,384]{1,0:T(4,128)}, u32[]{:S(2)}) copy-start(s32[3,384]{1,0:T(4,128)} %param.14) | copy-start | bytes 13828
  31.4 9.5 %copy-start.21 = (f32[3,128]{1,0:T(4,128)S(1)}, f32[3,128]{1,0:T(4,128)}, u32[]{:S(2)}) copy-start(f32[3,128]{1,0:T(4,128)} %constant.96.clone) | copy-start | bytes 4612
  31.4 56.1 %all-to-all-start = ((bf16[8,384,640]{1,2,0:T(8,128)(2,1)}), bf16[8,384,640]{1,2,0:T(8,128)(2,1)}, u32[]{:S(2)}, u32[]{:S(2)}) async-start(bf16[8,384,640]{1,2,0:T(8,128)(2,1)} %broadcast_in_dim.143), calls=%async_computation | async-start | bytes 7864320 | tf_op jit(solution)/shard_map/all_to_all | solution.py:85
  39.1 126.8 %all-gather.4.cloned.1.call-start = ((), (), s32[]{:S(2)}) async-start(), calls=%async_computation.2 | async-start | bytes 4177920 | tf_op jit(solution)/shard_map/all_gather | solution.py:190
  39.2 48.1 %collective-permute-start = (bf16[192,640]{1,0:T(8,128)(2,1)S(1)}, bf16[192,640]{1,0:T(8,128)(2,1)S(1)}, u32[]{:S(2)}, u32[]{:S(2)}) collective-permute-start(bf16[192,640]{1,0:T(8,128)(2,1)S(1)} %dynamic-slice_bitcast_fusion), channel_id=1, source_target_pairs={{0,64},{64,0},{1,65},{65,1},{2,66},{66,2},{3,67},{67,3},{4,68},{68... | collective-permute-start | bytes 737288 | tf_op jit(solution)/shard_map/ppermute | solution.py:76
  42.8 67.5 %copy-start.2 = (f32[384,128]{1,0:T(8,128)}, f32[384,128]{1,0:T(8,128)S(1)}, u32[]{:S(2)}) copy-start(f32[384,128]{1,0:T(8,128)S(1)} %copy.61) | copy-start | bytes 589828
  42.9 67.4 %copy-start.4 = (f32[384,128]{1,0:T(8,128)}, f32[384,128]{1,0:T(8,128)S(1)}, u32[]{:S(2)}) copy-start(f32[384,128]{1,0:T(8,128)S(1)} %copy.62) | copy-start | bytes 589828
  109.6 0.8 copy-start.6
  112.0 25.9 %collective-permute-start.2 = (bf16[384,2,3,128]{3,0,2,1:T(8,128)(2,1)}, bf16[384,2,3,128]{3,0,2,1:T(8,128)(2,1)S(1)}, u32[]{:S(2)}, u32[]{:S(2)}) collective-permute-start(bf16[384,2,3,128]{3,0,2,1:T(8,128)(2,1)} %pad_maximum_fusion.2), channel_id=1, source_target_pairs={{0,16},{16,32},{32,48},{48,0},{1,17},{17,33},{33,49},{49,1},{2,18}... | collective-permute-start | bytes 1769480 | tf_op jit(solution)/shard_map/ppermute | solution.py:132
  113.5 26.3 %collective-permute-start.3 = (bf16[384,2,3,128]{3,0,2,1:T(8,128)(2,1)}, bf16[384,2,3,128]{3,0,2,1:T(8,128)(2,1)S(1)}, u32[]{:S(2)}, u32[]{:S(2)}) collective-permute-start(bf16[384,2,3,128]{3,0,2,1:T(8,128)(2,1)} %pad_maximum_fusion.2), channel_id=1, source_target_pairs={{0,48},{16,0},{32,16},{48,32},{1,49},{17,1},{33,17},{49,33},{2,50}... | collective-permute-start | bytes 1769480 | tf_op jit(solution)/shard_map/ppermute | solution.py:133
  117.4 24.5 %copy-start.3 = (f32[384,128]{1,0:T(8,128)S(1)}, f32[384,128]{1,0:T(8,128)}, u32[]{:S(2)}) copy-start(f32[384,128]{1,0:T(8,128)} %copy-done.2) | copy-start | bytes 589828
  117.4 24.5 %copy-start.5 = (f32[384,128]{1,0:T(8,128)S(1)}, f32[384,128]{1,0:T(8,128)}, u32[]{:S(2)}) copy-start(f32[384,128]{1,0:T(8,128)} %copy-done.4) | copy-start | bytes 589828
  140.0 2.6 %copy-start.18 = (pred[192,512]{1,0:T(8,128)(4,1)S(1)}, pred[192,512]{1,0:T(8,128)(4,1)}, u32[]{:S(2)}) copy-start(pred[192,512]{1,0:T(8,128)(4,1)} %get-tuple-element.65) | copy-start | bytes 294916
  140.0 11.3 %collective-permute-start.4 = (bf16[384,2,3,128]{3,0,2,1:T(8,128)(2,1)S(1)}, bf16[384,2,3,128]{3,0,2,1:T(8,128)(2,1)S(1)}, u32[]{:S(2)}, u32[]{:S(2)}) collective-permute-start(bf16[384,2,3,128]{3,0,2,1:T(8,128)(2,1)S(1)} %get-tuple-element.18), channel_id=1, source_target_pairs={{0,16},{16,32},{32,48},{48,0},{8,56},{24,8},{40,24},{56,40},{1,17}... | collective-permute-start | bytes 1769480 | tf_op jit(solution)/shard_map/ppermute | solution.py:137
  143.1 9.1 %copy-start.17 = (pred[192,512]{1,0:T(8,128)(4,1)S(1)}, pred[192,512]{1,0:T(8,128)(4,1)}, u32[]{:S(2)}) copy-start(pred[192,512]{1,0:T(8,128)(4,1)} %get-tuple-element.64) | copy-start | bytes 294916
  152.1 5.4 %collective-permute-start.5 = (bf16[1536,2,3,128]{3,0,2,1:T(8,128)(2,1)S(1)}, bf16[1536,2,3,128]{3,0,2,1:T(8,128)(2,1)S(1)}, u32[]{:S(2)}, u32[]{:S(2)}) collective-permute-start(bf16[1536,2,3,128]{3,0,2,1:T(8,128)(2,1)S(1)} %pad_maximum_fusion), channel_id=1, source_target_pairs={{0,8},{8,0},{1,9},{9,1},{2,10},{10,2},{3,11},{11,3},{4,12},{12,4},... | collective-permute-start | bytes 7077896 | tf_op jit(solution)/shard_map/ppermute | solution.py:139
  152.8 0.9 copy-start.16
  153.1 1.1 copy-start.15
  154.2 0.9 copy-start.14
  154.8 0.9 copy-start.13
  156.9 0.9 copy-start.12
  157.5 0.9 copy-start.11
  158.3 0.9 copy-start.10
  160.7 2.0 copy-start.9
  161.1 2.2 %copy-start.8 = (pred[192,512]{1,0:T(8,128)(4,1)S(1)}, pred[192,512]{1,0:T(8,128)(4,1)}, u32[]{:S(2)}) copy-start(pred[192,512]{1,0:T(8,128)(4,1)} %get-tuple-element.69) | copy-start | bytes 294916
  161.1 6.5 %collective-permute-start.6 = (bf16[192,384]{1,0:T(8,128)(2,1)S(1)}, bf16[192,384]{1,0:T(8,128)(2,1)S(1)}, u32[]{:S(2)}, u32[]{:S(2)}) collective-permute-start(bf16[192,384]{1,0:T(8,128)(2,1)S(1)} %bitcast.211), channel_id=1, source_target_pairs={{0,64},{64,0},{1,65},{65,1},{2,66},{66,2},{3,67},{67,3},{4,68},{68... | collective-permute-start | bytes 442376 | tf_op jit(solution)/shard_map/ppermute | solution.py:186
  163.2 0.9 copy-start.7
  167.6 3.8 %copy-start = (bf16[384,5120]{0,1:T(8,128)(2,1)S(1)}, bf16[384,5120]{0,1:T(8,128)(2,1)}, u32[]{:S(2)}) copy-start(bf16[384,5120]{0,1:T(8,128)(2,1)} %all-gather.4.cloned.1.call-done) | copy-start | bytes 11796484
  174.3 34.5 %all-to-all-start.1 = ((bf16[8,192,640]{2,1,0:T(8,128)(2,1)}), bf16[8,192,640]{2,1,0:T(8,128)(2,1)S(1)}, u32[]{:S(2)}, u32[]{:S(2)}) async-start(bf16[8,192,640]{2,1,0:T(8,128)(2,1)} %fusion.10), calls=%async_computation.1 | async-start | bytes 3932160 | tf_op jit(solution)/shard_map/all_to_all | solution.py:196
Sparse Core Ops, SparseCore 0:
  27.9 66.1 all-gather.5
  95.8 45.1 all-gather.3

commit v10 on v9

--- a/solution.py
+++ b/solution.py
@@ -136,7 +136,9 @@
     relay_pairs += [(i * 2 + 1, ((i - 1) % n_x) * 2 + 1) for i in range(n_x)]
     from_far = lax.ppermute(relayed, SEQ, relay_pairs)
     kv_mine = jnp.concatenate([kv, from_behind, from_far, from_ahead], axis=0)
-    kv_other = lax.ppermute(kv_mine, "core", SWAP)
+    kv_other = jnp.concatenate(
+        [lax.ppermute(block, "core", SWAP) for block in (kv, from_behind, from_far, from_ahead)], axis=0
+    )
     kv_all = jnp.concatenate([kv_mine, kv_other], axis=0)
     key_piece = kv_all[:, 0]
     value_piece = kv_all[:, 1]

time: 218 us -> 219 us (level)
    unnamed x49 -> x46, local copies, waits for them, and re-layouts: 3.68 us -> 5.05 us
  transfers between devices with their start and end apart: 11 -> 14, of which waited for: 7 -> 7; matrix products, arithmetic and copies ran while one was open for 20% -> 21% of each run, Pallas kernels for 0% -> 0%
where the time goes in v10:
time: 219 us; the launch traced here: 218 us
  waiting for transfers between devices  118 us (54%)
  matrix products  30.4 us (14%)
  starting transfers between devices  25.9 us (12%)
  other arithmetic  19.3 us (9%)
  between operations  14.6 us (7%)
  local copies, waits for them, and re-layouts  8.99 us (4%)
    ppermute x1, waiting for transfers between devices, local(): other_rows = lax.ppermute(sent_rows, 'cfg', SWAP)  42.7 us
    all_to_all x1, waiting for transfers between devices, local(): lax.all_to_all(partial, BLK, 0, 0, tiled=False).astype(jnp.float32)  26.8 us
    ppermute x1, waiting for transfers between devices, local(): lax.ppermute(kv, 'x', [(i, (i + 1) % n_x) for i in range(n_x)])  21.2 us
    ppermute x1, waiting for transfers between devices, local(): shard_other = lax.ppermute(in_projection, 'cfg', SWAP)  16.7 us
    dot_general x1, matrix products, local(): jnp.einsum('tabi,abiqe->tqe', mod_perm, piece, preferred_element_type=jnp...  10.1 us
    all_to_all x1, starting transfers between devices, local(): lax.all_to_all(partial, BLK, 0, 0, tiled=False).astype(jnp.float32)  7.78 us
    all_to_all x1, starting transfers between devices, local(): full_states = lax.all_to_all(spread, BLK, 0, 0, tiled=False)  7.74 us
    ppermute x1, waiting for transfers between devices, local(): from_far = lax.ppermute(relayed, SEQ, relay_pairs)  6.76 us
  transfers between devices with their start and end apart: 14, of which 7 were waited for; matrix products, arithmetic and copies ran while one was open for 21% of the time, Pallas kernels for 0%

profile of v10, /device:TPU:0, one launch (start us, length us, event | category | flops | bytes accessed | tf_op | source)
XLA Modules:
  0.0 217.6 jit_solution(14018708545466097000)
XLA Ops:
  6.5 2.0 collective-permute-start.1
  8.6 16.7 %collective-permute-done.1 = bf16[320,3,384]{2,0,1:T(8,128)(2,1)S(1)} collective-permute-done((bf16[320,3,384]{2,0,1:T(8,128)(2,1)}, bf16[320,3,384]{2,0,1:T(8,128)(2,1)S(1)}, u32[]{:S(2)}, u32[]{:S(2)}) %collective-permute-start.1) | collective-permute-done | bytes 737312 | tf_op jit(solution)/shard_map/ppermute | solution.py:96
  25.3 1.3 select_bitcast_fusion.1
  26.5 1.3 pad_maximum_fusion
  27.8 1.0 copy-done.1
  29.1 2.3 %broadcast_in_dim.143 = bf16[8,384,640]{1,2,0:T(8,128)(2,1)} broadcast(bf16[384,640]{0,1:T(8,128)(2,1)S(1)} %copy.56), dimensions={1,2} | broadcast | bytes 4423680 | tf_op jit(solution)/shard_map/broadcast_in_dim | solution.py:84
  31.4 7.7 %all-to-all-start = ((bf16[8,384,640]{1,2,0:T(8,128)(2,1)}), bf16[8,384,640]{1,2,0:T(8,128)(2,1)}, u32[]{:S(2)}, u32[]{:S(2)}) async-start(bf16[8,384,640]{1,2,0:T(8,128)(2,1)} %broadcast_in_dim.143), calls=%async_computation | async-start | bytes 7864320 | tf_op jit(solution)/shard_map/all_to_all | solution.py:85
  39.2 1.1 collective-permute-start
  41.2 1.1 cosine_bitcast_fusion
  43.1 1.5 broadcast_compare_fusion
  44.6 42.7 %collective-permute-done = bf16[192,640]{1,0:T(8,128)(2,1)S(1)} collective-permute-done((bf16[192,640]{1,0:T(8,128)(2,1)S(1)}, bf16[192,640]{1,0:T(8,128)(2,1)S(1)}, u32[]{:S(2)}, u32[]{:S(2)}) %collective-permute-start) | collective-permute-done | bytes 245792 | tf_op jit(solution)/shard_map/ppermute | solution.py:76
  87.4 2.8 %convert_reduce_fusion = f32[384]{0:T(512)S(1)} fusion(bf16[8,384,640]{1,2,0:T(8,128)(2,1)} %all-to-all-done), kind=kLoop, calls=%fused_computation.3 | loop fusion | flops 3931776 | bytes 3933696 | tf_op jit(solution)/shard_map/reduce_sum | solution.py:88
  90.3 3.2 %fusion.4 = f32[384]{0:T(512)S(1)} fusion(bf16[8,384,640]{1,2,0:T(8,128)(2,1)} %all-to-all-done, f32[384]{0:T(512)S(1)} %broadcast_multiply_fusion), kind=kLoop, calls=%fused_computation.6 | loop fusion | flops 7863936 | bytes 3935232 | tf_op jit(solution)/shard_map/reduce_sum | solution.py:90
  93.5 5.8 %fusion.7 = bf16[8,384,640]{1,2,0:T(8,128)(2,1)} fusion(bf16[8,384,640]{1,2,0:T(8,128)(2,1)} %all-to-all-done, f32[8,640]{1,0:T(8,128)S(1)} %add.251, f32[8,640]{1,0:T(8,128)S(1)} %add.250, f32[384]{0:T(512)S(1)} %add_rsqrt_fusion.2, f32[384]{0:T(512)S(1)} %broadcast_multiply_fusion), kind=kLoop, calls=%fused_computation.9 | loop fusion | flops 11796480 | bytes 7908352 | tf_op jit(solution)/shard_map/convert_element_type | solution.py:94
  99.3 10.1 %fusion = f32[384,3,384,1,1]{0,2,3,1,4:T(8,128)S(1)} fusion(bf16[384,8,2,320,1]{0,3,1,4,2:T(8,128)(2,1)} %bitcast.207, bf16[8,2,320,3,384]{4,2,3,1,0:T(8,128)(2,1)} %bitcast.214), kind=kOutput, calls=%fused_computation | convolution fusion | flops 4529848320 | bytes 17498112 | tf_op jit(solution)/shard_map/tabi,abiqe->tqe/dot_general | solution.py:109
  110.4 0.7 fusion.49
  111.1 0.9 pad_maximum_fusion.1
  111.9 1.6 collective-permute-start.2
  113.5 1.7 collective-permute-start.3
  115.7 1.7 fusion.38
  117.4 21.2 %collective-permute-done.2 = bf16[384,2,3,128]{3,0,2,1:T(8,128)(2,1)S(1)} collective-permute-done((bf16[384,2,3,128]{3,0,2,1:T(8,128)(2,1)}, bf16[384,2,3,128]{3,0,2,1:T(8,128)(2,1)S(1)}, u32[]{:S(2)}, u32[]{:S(2)}) %collective-permute-start.2) | collective-permute-done | bytes 589856 | tf_op jit(solution)/shard_map/ppermute | solution.py:132
  138.6 1.5 collective-permute-done.3
  140.3 1.6 collective-permute-start.4
  141.9 0.5 collective-permute-start.8
  142.4 0.5 fusion.146
  143.0 1.1 constant_dynamic-update-slice_fusion.5
  144.1 0.5 fusion.140
  144.7 6.8 %collective-permute-done.4 = bf16[384,2,3,128]{3,0,2,1:T(8,128)(2,1)S(1)} collective-permute-done((bf16[384,2,3,128]{3,0,2,1:T(8,128)(2,1)S(1)}, bf16[384,2,3,128]{3,0,2,1:T(8,128)(2,1)S(1)}, u32[]{:S(2)}, u32[]{:S(2)}) %collective-permute-start.4) | collective-permute-done | bytes 589856 | tf_op jit(solution)/shard_map/ppermute | solution.py:137
  152.0 0.6 copy-done.14
  152.7 0.5 fusion.147
  153.2 0.5 fusion.141
  154.1 0.5 fusion.145
  154.7 0.5 fusion.139
  156.8 0.6 copy-done.10
  157.4 0.5 fusion.144
  157.9 0.5 fusion.138
  159.1 0.5 copy-done.8
  159.7 0.5 fusion.137
  160.2 0.5 fusion.136
  161.8 1.9 collective-permute-start.9
  163.6 0.5 fusion.143
  164.2 0.5 fusion.142
  165.7 2.6 %collective-permute-done.9 = bf16[192,384]{1,0:T(8,128)(2,1)S(1)} collective-permute-done((bf16[192,384]{1,0:T(8,128)(2,1)S(1)}, bf16[192,384]{1,0:T(8,128)(2,1)S(1)}, u32[]{:S(2)}, u32[]{:S(2)}) %collective-permute-start.9) | collective-permute-done | bytes 147488 | tf_op jit(solution)/shard_map/ppermute | solution.py:188
  168.3 3.8 %fusion.81 = f32[192,8,640]{2,0,1:T(8,128)S(1)} fusion(bf16[384,8,640]{0,2,1:T(8,128)(2,1)} %bitcast.205, bf16[192,384]{1,0:T(8,128)(2,1)S(1)} %collective-permute-done.9, pred[]{:T(512)S(6)} %eq.182, bf16[3,24,8,128]{3,2,1,0:T(8,128)(2,1)S(1)} %fusion.53), kind=kOutput, calls=%fused_computation.147 | convolution fusion | flops 755048448 | bytes 8159233 | tf_op jit(solution)/shard_map/te,ebn->btn/dot_general | solution.py:196
  172.1 2.9 %fusion.10 = bf16[8,192,640]{2,1,0:T(8,128)(2,1)} fusion(f32[192,8,640]{2,0,1:T(8,128)S(1)} %fusion.81, bf16[384,8,640]{0,2,1:T(8,128)(2,1)S(1)} %bitcast.206, f32[]{:T(128)} %bitcast.204, bf16[192,384]{1,0:T(8,128)(2,1)S(1)} %collective-permute-done.9, pred[]{:T(512)S(6)} %eq.182, bf16[3,24,8,128]{3,2,1,0:T(8,128)(2,1)S(1)} %fusion.53), kind=kOutput, calls=%fused_computation.13 | convolution fusion | flops 758980608 | bytes 10125317 | tf_op jit(solution)/shard_map/te,ebn->btn/dot_general | solution.py:195
  175.0 7.8 %all-to-all-start.1 = ((bf16[8,192,640]{2,1,0:T(8,128)(2,1)}), bf16[8,192,640]{2,1,0:T(8,128)(2,1)S(1)}, u32[]{:S(2)}, u32[]{:S(2)}) async-start(bf16[8,192,640]{2,1,0:T(8,128)(2,1)} %fusion.10), calls=%async_computation.1 | async-start | bytes 3932160 | tf_op jit(solution)/shard_map/all_to_all | solution.py:198
  182.8 26.8 %all-to-all-done.1 = bf16[8,192,640]{2,1,0:T(8,128)(2,1)S(1)} async-done(((bf16[8,192,640]{2,1,0:T(8,128)(2,1)}), bf16[8,192,640]{2,1,0:T(8,128)(2,1)S(1)}, u32[]{:S(2)}, u32[]{:S(2)}) %all-to-all-start.1) | async-done | bytes 1966112 | tf_op jit(solution)/shard_map/all_to_all | solution.py:198
  209.9 0.9 add_bitcast_fusion
  (101 shorter events, 8.3 us)
Async XLA Ops:
  6.5 92.8 %all-gather.6.cloned.1.call-start = ((), (), s32[]{:S(2)}) async-start(), calls=%async_computation.3 | async-start | bytes 13271040 | tf_op jit(solution)/shard_map/all_gather | solution.py:103
  6.5 18.7 %collective-permute-start.1 = (bf16[320,3,384]{2,0,1:T(8,128)(2,1)}, bf16[320,3,384]{2,0,1:T(8,128)(2,1)S(1)}, u32[]{:S(2)}, u32[]{:S(2)}) collective-permute-start(bf16[320,3,384]{2,0,1:T(8,128)(2,1)} %param.11), channel_id=1, source_target_pairs={{0,64},{64,0},{1,65},{65,1},{2,66},{66,2},{3,67},{67,3},{4,68},{68... | collective-permute-start | bytes 2211848 | tf_op jit(solution)/shard_map/ppermute | solution.py:96
  27.8 1.0 copy-start.1
  31.4 9.6 %copy-start.17 = (f32[3,5120]{1,0:T(4,128)S(1)}, f32[3,5120]{1,0:T(4,128)}, u32[]{:S(2)}) copy-start(f32[3,5120]{1,0:T(4,128)} %param.10) | copy-start | bytes 184324
  31.4 9.8 %copy-start.18 = (s32[3,384]{1,0:T(4,128)S(1)}, s32[3,384]{1,0:T(4,128)}, u32[]{:S(2)}) copy-start(s32[3,384]{1,0:T(4,128)} %param.14) | copy-start | bytes 13828
  31.4 9.8 %copy-start.19 = (f32[3,128]{1,0:T(4,128)S(1)}, f32[3,128]{1,0:T(4,128)}, u32[]{:S(2)}) copy-start(f32[3,128]{1,0:T(4,128)} %constant.96.clone) | copy-start | bytes 4612
  31.4 56.0 %all-to-all-start = ((bf16[8,384,640]{1,2,0:T(8,128)(2,1)}), bf16[8,384,640]{1,2,0:T(8,128)(2,1)}, u32[]{:S(2)}, u32[]{:S(2)}) async-start(bf16[8,384,640]{1,2,0:T(8,128)(2,1)} %broadcast_in_dim.143), calls=%async_computation | async-start | bytes 7864320 | tf_op jit(solution)/shard_map/all_to_all | solution.py:85
  39.1 3.4 %copy-start.20 = (s32[5]{0:T(128)S(1)}, s32[5]{0:T(128)}, u32[]{:S(2)}) copy-start(s32[5]{0:T(128)} %param.13) | copy-start | bytes 64
  39.1 126.6 %all-gather.4.cloned.1.call-start = ((), (), s32[]{:S(2)}) async-start(), calls=%async_computation.2 | async-start | bytes 4177920 | tf_op jit(solution)/shard_map/all_gather | solution.py:192
  39.2 48.1 %collective-permute-start = (bf16[192,640]{1,0:T(8,128)(2,1)S(1)}, bf16[192,640]{1,0:T(8,128)(2,1)S(1)}, u32[]{:S(2)}, u32[]{:S(2)}) collective-permute-start(bf16[192,640]{1,0:T(8,128)(2,1)S(1)} %dynamic-slice_bitcast_fusion), channel_id=1, source_target_pairs={{0,64},{64,0},{1,65},{65,1},{2,66},{66,2},{3,67},{67,3},{4,68},{68... | collective-permute-start | bytes 737288 | tf_op jit(solution)/shard_map/ppermute | solution.py:76
  42.4 67.9 %copy-start.2 = (f32[384,128]{1,0:T(8,128)}, f32[384,128]{1,0:T(8,128)S(1)}, u32[]{:S(2)}) copy-start(f32[384,128]{1,0:T(8,128)S(1)} %copy.61) | copy-start | bytes 589828
  42.5 67.7 %copy-start.3 = (f32[384,128]{1,0:T(8,128)}, f32[384,128]{1,0:T(8,128)S(1)}, u32[]{:S(2)}) copy-start(f32[384,128]{1,0:T(8,128)S(1)} %copy.62) | copy-start | bytes 589828
  109.5 0.8 copy-start.4
  111.9 31.0 %collective-permute-start.5 = (bf16[384,2,3,128]{3,0,2,1:T(8,128)(2,1)}, bf16[384,2,3,128]{3,0,2,1:T(8,128)(2,1)}, u32[]{:S(2)}, u32[]{:S(2)}) collective-permute-start(bf16[384,2,3,128]{3,0,2,1:T(8,128)(2,1)} %pad_maximum_fusion.1), channel_id=1, source_target_pairs={{0,8},{8,0},{1,9},{9,1},{2,10},{10,2},{3,11},{11,3},{4,12},{12,4},... | collective-permute-start | bytes 1769480 | tf_op jit(solution)/shard_map/ppermute | solution.py:140
  111.9 26.6 %collective-permute-start.2 = (bf16[384,2,3,128]{3,0,2,1:T(8,128)(2,1)}, bf16[384,2,3,128]{3,0,2,1:T(8,128)(2,1)S(1)}, u32[]{:S(2)}, u32[]{:S(2)}) collective-permute-start(bf16[384,2,3,128]{3,0,2,1:T(8,128)(2,1)} %pad_maximum_fusion.1), channel_id=1, source_target_pairs={{0,16},{16,32},{32,48},{48,0},{1,17},{17,33},{33,49},{49,1},{2,18}... | collective-permute-start | bytes 1769480 | tf_op jit(solution)/shard_map/ppermute | solution.py:132
  113.5 26.5 %collective-permute-start.3 = (bf16[384,2,3,128]{3,0,2,1:T(8,128)(2,1)}, bf16[384,2,3,128]{3,0,2,1:T(8,128)(2,1)S(1)}, u32[]{:S(2)}, u32[]{:S(2)}) collective-permute-start(bf16[384,2,3,128]{3,0,2,1:T(8,128)(2,1)} %pad_maximum_fusion.1), channel_id=1, source_target_pairs={{0,48},{16,0},{32,16},{48,32},{1,49},{17,1},{33,17},{49,33},{2,50}... | collective-permute-start | bytes 1769480 | tf_op jit(solution)/shard_map/ppermute | solution.py:133
  117.4 25.0 %copy-start.16 = (pred[192,512]{1,0:T(8,128)(4,1)S(1)}, pred[192,512]{1,0:T(8,128)(4,1)}, u32[]{:S(2)}) copy-start(pred[192,512]{1,0:T(8,128)(4,1)} %get-tuple-element.66) | copy-start | bytes 294916
  140.3 11.2 %collective-permute-start.4 = (bf16[384,2,3,128]{3,0,2,1:T(8,128)(2,1)S(1)}, bf16[384,2,3,128]{3,0,2,1:T(8,128)(2,1)S(1)}, u32[]{:S(2)}, u32[]{:S(2)}) collective-permute-start(bf16[384,2,3,128]{3,0,2,1:T(8,128)(2,1)S(1)} %get-tuple-element.20), channel_id=1, source_target_pairs={{0,16},{16,32},{32,48},{48,0},{8,56},{24,8},{40,24},{56,40},{1,17}... | collective-permute-start | bytes 1769480 | tf_op jit(solution)/shard_map/ppermute | solution.py:137
  141.9 9.9 %collective-permute-start.6 = (bf16[384,2,3,128]{3,0,2,1:T(8,128)(2,1)S(1)}, bf16[384,2,3,128]{3,0,2,1:T(8,128)(2,1)S(1)}, u32[]{:S(2)}, u32[]{:S(2)}) collective-permute-start(bf16[384,2,3,128]{3,0,2,1:T(8,128)(2,1)S(1)} %collective-permute-done.2), channel_id=1, source_target_pairs={{0,8},{8,0},{1,9},{9,1},{2,10},{10,2},{3,11},{11,3},{4,12},{12,4},... | collective-permute-start | bytes 1769480 | tf_op jit(solution)/shard_map/ppermute | solution.py:140
  141.9 17.1 %collective-permute-start.8 = (bf16[384,2,3,128]{3,0,2,1:T(8,128)(2,1)S(1)}, bf16[384,2,3,128]{3,0,2,1:T(8,128)(2,1)S(1)}, u32[]{:S(2)}, u32[]{:S(2)}) collective-permute-start(bf16[384,2,3,128]{3,0,2,1:T(8,128)(2,1)S(1)} %collective-permute-done.3), channel_id=1, source_target_pairs={{0,8},{8,0},{1,9},{9,1},{2,10},{10,2},{3,11},{11,3},{4,12},{12,4},... | collective-permute-start | bytes 1769480 | tf_op jit(solution)/shard_map/ppermute | solution.py:140
  143.0 1.2 copy-start.15
  151.4 7.3 %collective-permute-start.7 = (bf16[384,2,3,128]{3,0,2,1:T(8,128)(2,1)S(1)}, bf16[384,2,3,128]{3,0,2,1:T(8,128)(2,1)S(1)}, u32[]{:S(2)}, u32[]{:S(2)}) collective-permute-start(bf16[384,2,3,128]{3,0,2,1:T(8,128)(2,1)S(1)} %collective-permute-done.4), channel_id=1, source_target_pairs={{0,8},{8,0},{1,9},{9,1},{2,10},{10,2},{3,11},{11,3},{4,12},{12,4},... | collective-permute-start | bytes 1769480 | tf_op jit(solution)/shard_map/ppermute | solution.py:140
  151.8 0.9 copy-start.14
  152.0 1.2 copy-start.13
  153.2 0.9 copy-start.12
  153.8 0.9 copy-start.11
  156.5 0.9 copy-start.10
  156.8 1.1 copy-start.9
  158.8 0.9 copy-start.8
  159.1 1.1 copy-start.7
  161.4 2.2 %copy-start.6 = (pred[192,512]{1,0:T(8,128)(4,1)S(1)}, pred[192,512]{1,0:T(8,128)(4,1)}, u32[]{:S(2)}) copy-start(pred[192,512]{1,0:T(8,128)(4,1)} %get-tuple-element.73) | copy-start | bytes 294916
  161.8 2.4 %copy-start.5 = (pred[192,512]{1,0:T(8,128)(4,1)S(1)}, pred[192,512]{1,0:T(8,128)(4,1)}, u32[]{:S(2)}) copy-start(pred[192,512]{1,0:T(8,128)(4,1)} %get-tuple-element.62) | copy-start | bytes 294916
  161.8 6.6 %collective-permute-start.9 = (bf16[192,384]{1,0:T(8,128)(2,1)S(1)}, bf16[192,384]{1,0:T(8,128)(2,1)S(1)}, u32[]{:S(2)}, u32[]{:S(2)}) collective-permute-start(bf16[192,384]{1,0:T(8,128)(2,1)S(1)} %bitcast.211), channel_id=1, source_target_pairs={{0,64},{64,0},{1,65},{65,1},{2,66},{66,2},{3,67},{67,3},{4,68},{68... | collective-permute-start | bytes 442376 | tf_op jit(solution)/shard_map/ppermute | solution.py:188
  168.3 3.8 %copy-start = (bf16[384,5120]{0,1:T(8,128)(2,1)S(1)}, bf16[384,5120]{0,1:T(8,128)(2,1)}, u32[]{:S(2)}) copy-start(bf16[384,5120]{0,1:T(8,128)(2,1)} %all-gather.4.cloned.1.call-done) | copy-start | bytes 11796484
  175.0 34.6 %all-to-all-start.1 = ((bf16[8,192,640]{2,1,0:T(8,128)(2,1)}), bf16[8,192,640]{2,1,0:T(8,128)(2,1)S(1)}, u32[]{:S(2)}, u32[]{:S(2)}) async-start(bf16[8,192,640]{2,1,0:T(8,128)(2,1)} %fusion.10), calls=%async_computation.1 | async-start | bytes 3932160 | tf_op jit(solution)/shard_map/all_to_all | solution.py:198
Sparse Core Ops, SparseCore 0:
  27.9 66.1 all-gather.5
  95.8 45.0 all-gather.3

commit v11 on v9

--- a/solution.py
+++ b/solution.py
@@ -192,8 +192,22 @@
     )
     cond_part = jnp.einsum("te,ebn->btn", cond_att, out_piece, preferred_element_type=jnp.float32)
     uncond_part = jnp.einsum("te,ebn->btn", uncond_att, out_piece, preferred_element_type=jnp.float32)
-    partial = (uncond_part + scale * (cond_part - uncond_part)).astype(jnp.bfloat16)
-    arrived = lax.all_to_all(partial, BLK, 0, 0, tiled=False).astype(jnp.float32)
+    partial = (uncond_part + scale * (cond_part - uncond_part)).reshape(
+        2, n_blk // 2, half_rows, feat_width
+    )
+    zhi = lax.axis_index("zhi")
+    own_plane = lax.dynamic_index_in_dim(partial, zhi, axis=0, keepdims=False)
+    sent_plane = lax.dynamic_index_in_dim(partial, 1 - zhi, axis=0, keepdims=False).astype(jnp.bfloat16)
+    quarter = half_rows // 2
+    flip_both = [(0, 3), (3, 0), (1, 2), (2, 1)]
+    via_cfg = lax.ppermute(
+        lax.ppermute(sent_plane[:, :quarter], "cfg", SWAP), ("cfg", "zhi"), flip_both
+    )
+    via_diagonal = lax.ppermute(
+        lax.ppermute(sent_plane[:, quarter:], ("cfg", "zhi"), flip_both), "cfg", SWAP
+    )
+    plane_sum = own_plane + jnp.concatenate([via_cfg, via_diagonal], axis=1).astype(jnp.float32)
+    arrived = lax.all_to_all(plane_sum.astype(jnp.bfloat16), "y", 0, 0, tiled=False).astype(jnp.float32)
     gate = lax.dynamic_slice_in_dim(modulation[2], blk * feat_width, feat_width, 0)
     projected = gate * jnp.sum(arrived, 0)
     guided = hidden_part + projected

time: 218 us -> 231 us (1.060)
  waiting for transfers between devices: 120 us -> 129 us
  other arithmetic: 20.1 us -> 22.6 us
    ppermute x0 -> x4, waiting for transfers between devices: none -> 23 us  [the longest x1 10.9 us: local(): lax.ppermute(sent_plane[:, quarter:], ('cfg', 'zhi'), flip_both)]
    all_to_all x1, waiting for transfers between devices: 26.8 us -> 12.2 us  [local(): lax.all_to_all(plane_sum.astype(jnp.bfloat16), 'y', 0, 0, tiled=False)]
    ppermute x0 -> x4, starting transfers between devices: none -> 4.76 us  [the longest x1 2.45 us: local(): lax.ppermute(sent_plane[:, quarter:], ('cfg', 'zhi'), flip_both)]
    convert_element_type x0 -> x1, other arithmetic: none -> 2.7 us  [local(): plane_sum.astype(jnp.bfloat16)]
    all_to_all x1, starting transfers between devices: 7.63 us -> 5 us  [local(): lax.all_to_all(plane_sum.astype(jnp.bfloat16), 'y', 0, 0, tiled=False)]
    unnamed x49 -> x51, local copies, waits for them, and re-layouts: 3.68 us -> 5.26 us
  transfers between devices with their start and end apart: 11 -> 15, of which waited for: 7 -> 11; matrix products, arithmetic and copies ran while one was open for 20% -> 19% of each run, Pallas kernels for 0% -> 0%
where the time goes in v11:
time: 231 us; the launch traced here: 230 us
  waiting for transfers between devices  129 us (56%)
  matrix products  28.1 us (12%)
  starting transfers between devices  27.4 us (12%)
  other arithmetic  22.6 us (10%)
  between operations  14.7 us (6%)
  local copies, waits for them, and re-layouts  8.84 us (4%)
    ppermute x1, waiting for transfers between devices, local(): other_rows = lax.ppermute(sent_rows, 'cfg', SWAP)  44.4 us
    ppermute x1, waiting for transfers between devices, local(): lax.ppermute(kv, 'x', [(i, (i + 1) % n_x) for i in range(n_x)])  20.5 us
    ppermute x1, waiting for transfers between devices, local(): shard_other = lax.ppermute(in_projection, 'cfg', SWAP)  16.7 us
    all_to_all x1, waiting for transfers between devices, local(): lax.all_to_all(plane_sum.astype(jnp.bfloat16), 'y', 0, 0, tiled=False)  12.2 us
    ppermute x1, waiting for transfers between devices, local(): lax.ppermute(sent_plane[:, quarter:], ('cfg', 'zhi'), flip_both)  10.9 us
    dot_general x1, matrix products, local(): jnp.einsum('tabi,abiqe->tqe', mod_perm, piece, preferred_element_type=jnp...  10.1 us
    ppermute x1, waiting for transfers between devices, local(): lax.ppermute(lax.ppermute(sent_plane[:, quarter:], ('cfg', 'zhi'), flip_b...  9.4 us
    ppermute x1, waiting for transfers between devices, local(): from_far = lax.ppermute(relayed, SEQ, relay_pairs)  8.21 us
  transfers between devices with their start and end apart: 15, of which 11 were waited for; matrix products, arithmetic and copies ran while one was open for 19% of the time, Pallas kernels for 0%

profile of v11, /device:TPU:0, one launch (start us, length us, event | category | flops | bytes accessed | tf_op | source)
XLA Modules:
  0.0 230.3 jit_solution(12667212168638162531)
XLA Ops:
  6.5 2.0 collective-permute-start.1
  8.6 16.7 %collective-permute-done.1 = bf16[320,3,384]{2,0,1:T(8,128)(2,1)S(1)} collective-permute-done((bf16[320,3,384]{2,0,1:T(8,128)(2,1)}, bf16[320,3,384]{2,0,1:T(8,128)(2,1)S(1)}, u32[]{:S(2)}, u32[]{:S(2)}) %collective-permute-start.1) | collective-permute-done | bytes 737312 | tf_op jit(solution)/shard_map/ppermute | solution.py:96
  25.3 1.3 select_bitcast_fusion.1
  26.5 1.3 pad_maximum_fusion.1
  27.8 1.0 copy-done.2
  29.1 2.3 broadcast_in_dim.143
  31.4 7.8 %all-to-all-start = ((bf16[8,384,640]{1,2,0:T(8,128)(2,1)}), bf16[8,384,640]{1,2,0:T(8,128)(2,1)}, u32[]{:S(2)}, u32[]{:S(2)}) async-start(bf16[8,384,640]{1,2,0:T(8,128)(2,1)} %broadcast_in_dim.143), calls=%async_computation | async-start | bytes 7864320 | tf_op jit(solution)/shard_map/all_to_all | solution.py:85
  39.2 1.1 collective-permute-start
  40.8 1.1 cosine_bitcast_fusion
  42.9 44.4 %collective-permute-done = bf16[192,640]{1,0:T(8,128)(2,1)S(1)} collective-permute-done((bf16[192,640]{1,0:T(8,128)(2,1)S(1)}, bf16[192,640]{1,0:T(8,128)(2,1)S(1)}, u32[]{:S(2)}, u32[]{:S(2)}) %collective-permute-start) | collective-permute-done | bytes 245792 | tf_op jit(solution)/shard_map/ppermute | solution.py:76
  87.4 2.8 %convert_reduce_fusion = f32[384]{0:T(512)S(1)} fusion(bf16[8,384,640]{1,2,0:T(8,128)(2,1)} %all-to-all-done), kind=kLoop, calls=%fused_computation.3 | loop fusion | flops 3931776 | bytes 3933696 | tf_op jit(solution)/shard_map/reduce_sum | solution.py:88
  90.3 3.2 %fusion.4 = f32[384]{0:T(512)S(1)} fusion(bf16[8,384,640]{1,2,0:T(8,128)(2,1)} %all-to-all-done, f32[384]{0:T(512)S(1)} %broadcast_multiply_fusion), kind=kLoop, calls=%fused_computation.6 | loop fusion | flops 7863936 | bytes 3935232 | tf_op jit(solution)/shard_map/reduce_sum | solution.py:90
  93.5 5.8 %fusion.7 = bf16[8,384,640]{1,2,0:T(8,128)(2,1)} fusion(bf16[8,384,640]{1,2,0:T(8,128)(2,1)} %all-to-all-done, f32[8,640]{1,0:T(8,128)S(1)} %add.262, f32[8,640]{1,0:T(8,128)S(1)} %add.261, f32[384]{0:T(512)S(1)} %add_rsqrt_fusion.2, f32[384]{0:T(512)S(1)} %broadcast_multiply_fusion), kind=kLoop, calls=%fused_computation.9 | loop fusion | flops 11796480 | bytes 7908352 | tf_op jit(solution)/shard_map/convert_element_type | solution.py:94
  99.3 10.1 %fusion = f32[384,3,384,1,1]{0,2,3,1,4:T(8,128)S(1)} fusion(bf16[384,8,2,320,1]{0,3,1,4,2:T(8,128)(2,1)} %bitcast.214, bf16[8,2,320,3,384]{4,2,3,1,0:T(8,128)(2,1)} %bitcast.221), kind=kOutput, calls=%fused_computation | convolution fusion | flops 4529848320 | bytes 17498112 | tf_op jit(solution)/shard_map/tabi,abiqe->tqe/dot_general | solution.py:109
  110.4 0.7 fusion.51
  111.0 0.9 pad_maximum_fusion.2
  111.9 1.5 collective-permute-start.2
  113.5 1.7 collective-permute-start.3
  115.3 1.5 broadcast_compare_fusion
  117.3 20.5 %collective-permute-done.2 = bf16[384,2,3,128]{3,0,2,1:T(8,128)(2,1)S(1)} collective-permute-done((bf16[384,2,3,128]{3,0,2,1:T(8,128)(2,1)}, bf16[384,2,3,128]{3,0,2,1:T(8,128)(2,1)S(1)}, u32[]{:S(2)}, u32[]{:S(2)}) %collective-permute-start.2) | collective-permute-done | bytes 589856 | tf_op jit(solution)/shard_map/ppermute | solution.py:132
  137.8 2.0 collective-permute-done.3
  140.0 1.9 collective-permute-start.4
  141.9 0.7 fusion.38
  142.6 0.6 fusion.152
  143.2 8.2 %collective-permute-done.4 = bf16[384,2,3,128]{3,0,2,1:T(8,128)(2,1)S(1)} collective-permute-done((bf16[384,2,3,128]{3,0,2,1:T(8,128)(2,1)S(1)}, bf16[384,2,3,128]{3,0,2,1:T(8,128)(2,1)S(1)}, u32[]{:S(2)}, u32[]{:S(2)}) %collective-permute-start.4) | collective-permute-done | bytes 589856 | tf_op jit(solution)/shard_map/ppermute | solution.py:137
  151.4 0.7 pad_maximum_fusion
  152.2 0.6 fusion.146
  153.1 0.5 copy-done.17
  155.1 0.5 fusion.151
  158.3 0.6 fusion.143
  161.1 1.5 collective-permute-start.6
  163.2 0.6 fusion.149
  164.0 0.5 fusion.148
  165.9 1.7 collective-permute-done.6
  167.6 3.8 %fusion.86 = f32[192,8,640]{2,0,1:T(8,128)S(1)} fusion(bf16[384,8,640]{0,2,1:T(8,128)(2,1)} %bitcast.210, bf16[192,384]{1,0:T(8,128)(2,1)S(1)} %collective-permute-done.6, pred[]{:T(512)S(6)} %eq.182, bf16[3,24,8,128]{3,2,1,0:T(8,128)(2,1)S(1)} %fusion.55), kind=kOutput, calls=%fused_computation.153 | convolution fusion | flops 755048448 | bytes 8159233 | tf_op jit(solution)/shard_map/te,ebn->btn/dot_general | solution.py:194
  171.4 1.6 fusion.9
  173.2 1.7 copy-done.1
  174.9 2.5 %collective-permute-start.9 = (bf16[4,96,640]{2,1,0:T(8,128)(2,1)S(1)}, bf16[4,96,640]{2,1,0:T(8,128)(2,1)S(1)}, u32[]{:S(2)}, u32[]{:S(2)}) collective-permute-start(bf16[4,96,640]{2,1,0:T(8,128)(2,1)S(1)} %get-tuple-element.16), channel_id=1, source_target_pairs={{0,68},{68,0},{4,64},{64,4},{1,69},{69,1},{5,65},{65,5},{2,70},{70... | collective-permute-start | bytes 1474568 | tf_op jit(solution)/shard_map/ppermute | solution.py:207
  177.3 0.6 collective-permute-start.7
  177.9 10.9 %collective-permute-done.9 = bf16[4,96,640]{2,1,0:T(8,128)(2,1)S(1)} collective-permute-done((bf16[4,96,640]{2,1,0:T(8,128)(2,1)S(1)}, bf16[4,96,640]{2,1,0:T(8,128)(2,1)S(1)}, u32[]{:S(2)}, u32[]{:S(2)}) %collective-permute-start.9) | collective-permute-done | bytes 491552 | tf_op jit(solution)/shard_map/ppermute | solution.py:207
  189.0 0.8 collective-permute-done.7
  189.8 1.5 collective-permute-start.8
  191.3 9.4 %collective-permute-done.10 = bf16[4,96,640]{2,1,0:T(8,128)(2,1)S(1)} collective-permute-done((bf16[4,96,640]{2,1,0:T(8,128)(2,1)S(1)}, bf16[4,96,640]{2,1,0:T(8,128)(2,1)S(1)}, u32[]{:S(2)}, u32[]{:S(2)}) %collective-permute-start.10) | collective-permute-done | bytes 491552 | tf_op jit(solution)/shard_map/ppermute | solution.py:206
  200.7 1.9 collective-permute-done.8
  202.6 2.7 %fusion.10 = bf16[4,192,640]{2,1,0:T(8,128)(2,1)} fusion(f32[2,4,192,640]{3,2,1,0:T(8,128)} %bitcast.213, s32[]{:T(128)S(6)} %select_n.178, bf16[4,96,640]{2,1,0:T(8,128)(2,1)S(1)} %collective-permute-done.10, bf16[4,96,640]{2,1,0:T(8,128)(2,1)S(1)} %collective-permute-done.8), kind=kLoop, calls=%fused_computation.15 | loop fusion | flops 2949120 | bytes 3932164 | tf_op jit(solution)/shard_map/convert_element_type | solution.py:210
  205.3 5.0 %all-to-all-start.1 = ((bf16[4,192,640]{2,1,0:T(8,128)(2,1)}), bf16[4,192,640]{2,1,0:T(8,128)(2,1)S(1)}, u32[]{:S(2)}, u32[]{:S(2)}) async-start(bf16[4,192,640]{2,1,0:T(8,128)(2,1)} %fusion.10), calls=%async_computation.1 | async-start | bytes 1966080 | tf_op jit(solution)/shard_map/all_to_all | solution.py:210
  210.3 12.2 %all-to-all-done.1 = bf16[4,192,640]{2,1,0:T(8,128)(2,1)S(1)} async-done(((bf16[4,192,640]{2,1,0:T(8,128)(2,1)}), bf16[4,192,640]{2,1,0:T(8,128)(2,1)S(1)}, u32[]{:S(2)}, u32[]{:S(2)}) %all-to-all-start.1) | async-done | bytes 983072 | tf_op jit(solution)/shard_map/all_to_all | solution.py:210
  222.7 0.8 add_bitcast_fusion
  (109 shorter events, 12.2 us)
Async XLA Ops:
  6.5 92.8 %all-gather.6.cloned.1.call-start = ((), (), s32[]{:S(2)}) async-start(), calls=%async_computation.3 | async-start | bytes 13271040 | tf_op jit(solution)/shard_map/all_gather | solution.py:103
  6.5 18.7 %collective-permute-start.1 = (bf16[320,3,384]{2,0,1:T(8,128)(2,1)}, bf16[320,3,384]{2,0,1:T(8,128)(2,1)S(1)}, u32[]{:S(2)}, u32[]{:S(2)}) collective-permute-start(bf16[320,3,384]{2,0,1:T(8,128)(2,1)} %param.11), channel_id=1, source_target_pairs={{0,64},{64,0},{1,65},{65,1},{2,66},{66,2},{3,67},{67,3},{4,68},{68... | collective-permute-start | bytes 2211848 | tf_op jit(solution)/shard_map/ppermute | solution.py:96
  27.8 1.0 copy-start.2
  31.4 9.0 %copy-start.23 = (s32[5]{0:T(128)S(1)}, s32[5]{0:T(128)}, u32[]{:S(2)}) copy-start(s32[5]{0:T(128)} %param.13) | copy-start | bytes 64
  31.4 9.3 %copy-start.20 = (f32[3,5120]{1,0:T(4,128)S(1)}, f32[3,5120]{1,0:T(4,128)}, u32[]{:S(2)}) copy-start(f32[3,5120]{1,0:T(4,128)} %param.10) | copy-start | bytes 184324
  31.4 9.4 %copy-start.21 = (s32[3,384]{1,0:T(4,128)S(1)}, s32[3,384]{1,0:T(4,128)}, u32[]{:S(2)}) copy-start(s32[3,384]{1,0:T(4,128)} %param.14) | copy-start | bytes 13828
  31.4 9.5 %copy-start.22 = (f32[3,128]{1,0:T(4,128)S(1)}, f32[3,128]{1,0:T(4,128)}, u32[]{:S(2)}) copy-start(f32[3,128]{1,0:T(4,128)} %constant.103.clone) | copy-start | bytes 4612
  31.4 56.1 %all-to-all-start = ((bf16[8,384,640]{1,2,0:T(8,128)(2,1)}), bf16[8,384,640]{1,2,0:T(8,128)(2,1)}, u32[]{:S(2)}, u32[]{:S(2)}) async-start(bf16[8,384,640]{1,2,0:T(8,128)(2,1)} %broadcast_in_dim.143), calls=%async_computation | async-start | bytes 7864320 | tf_op jit(solution)/shard_map/all_to_all | solution.py:85
  39.1 126.7 %all-gather.4.cloned.1.call-start = ((), (), s32[]{:S(2)}) async-start(), calls=%async_computation.2 | async-start | bytes 4177920 | tf_op jit(solution)/shard_map/all_gather | solution.py:190
  39.2 48.1 %collective-permute-start = (bf16[192,640]{1,0:T(8,128)(2,1)S(1)}, bf16[192,640]{1,0:T(8,128)(2,1)S(1)}, u32[]{:S(2)}, u32[]{:S(2)}) collective-permute-start(bf16[192,640]{1,0:T(8,128)(2,1)S(1)} %dynamic-slice_bitcast_fusion), channel_id=1, source_target_pairs={{0,64},{64,0},{1,65},{65,1},{2,66},{66,2},{3,67},{67,3},{4,68},{68... | collective-permute-start | bytes 737288 | tf_op jit(solution)/shard_map/ppermute | solution.py:76
  42.8 67.5 %copy-start.3 = (f32[384,128]{1,0:T(8,128)}, f32[384,128]{1,0:T(8,128)S(1)}, u32[]{:S(2)}) copy-start(f32[384,128]{1,0:T(8,128)S(1)} %copy.61) | copy-start | bytes 589828
  42.9 67.4 %copy-start.5 = (f32[384,128]{1,0:T(8,128)}, f32[384,128]{1,0:T(8,128)S(1)}, u32[]{:S(2)}) copy-start(f32[384,128]{1,0:T(8,128)S(1)} %copy.62) | copy-start | bytes 589828
  109.5 0.8 copy-start.7
  111.9 25.9 %collective-permute-start.2 = (bf16[384,2,3,128]{3,0,2,1:T(8,128)(2,1)}, bf16[384,2,3,128]{3,0,2,1:T(8,128)(2,1)S(1)}, u32[]{:S(2)}, u32[]{:S(2)}) collective-permute-start(bf16[384,2,3,128]{3,0,2,1:T(8,128)(2,1)} %pad_maximum_fusion.2), channel_id=1, source_target_pairs={{0,16},{16,32},{32,48},{48,0},{1,17},{17,33},{33,49},{49,1},{2,18}... | collective-permute-start | bytes 1769480 | tf_op jit(solution)/shard_map/ppermute | solution.py:132
  113.5 26.3 %collective-permute-start.3 = (bf16[384,2,3,128]{3,0,2,1:T(8,128)(2,1)}, bf16[384,2,3,128]{3,0,2,1:T(8,128)(2,1)S(1)}, u32[]{:S(2)}, u32[]{:S(2)}) collective-permute-start(bf16[384,2,3,128]{3,0,2,1:T(8,128)(2,1)} %pad_maximum_fusion.2), channel_id=1, source_target_pairs={{0,48},{16,0},{32,16},{48,32},{1,49},{17,1},{33,17},{49,33},{2,50}... | collective-permute-start | bytes 1769480 | tf_op jit(solution)/shard_map/ppermute | solution.py:133
  117.1 24.8 %copy-start.4 = (f32[384,128]{1,0:T(8,128)S(1)}, f32[384,128]{1,0:T(8,128)}, u32[]{:S(2)}) copy-start(f32[384,128]{1,0:T(8,128)} %copy-done.3) | copy-start | bytes 589828
  117.1 24.8 %copy-start.6 = (f32[384,128]{1,0:T(8,128)S(1)}, f32[384,128]{1,0:T(8,128)}, u32[]{:S(2)}) copy-start(f32[384,128]{1,0:T(8,128)} %copy-done.5) | copy-start | bytes 589828
  117.3 25.3 %copy-start.19 = (pred[192,512]{1,0:T(8,128)(4,1)S(1)}, pred[192,512]{1,0:T(8,128)(4,1)}, u32[]{:S(2)}) copy-start(pred[192,512]{1,0:T(8,128)(4,1)} %get-tuple-element.67) | copy-start | bytes 294916
  140.0 11.3 %collective-permute-start.4 = (bf16[384,2,3,128]{3,0,2,1:T(8,128)(2,1)S(1)}, bf16[384,2,3,128]{3,0,2,1:T(8,128)(2,1)S(1)}, u32[]{:S(2)}, u32[]{:S(2)}) collective-permute-start(bf16[384,2,3,128]{3,0,2,1:T(8,128)(2,1)S(1)} %get-tuple-element.20), channel_id=1, source_target_pairs={{0,16},{16,32},{32,48},{48,0},{8,56},{24,8},{40,24},{56,40},{1,17}... | collective-permute-start | bytes 1769480 | tf_op jit(solution)/shard_map/ppermute | solution.py:137
  143.2 9.1 %copy-start.18 = (pred[192,512]{1,0:T(8,128)(4,1)S(1)}, pred[192,512]{1,0:T(8,128)(4,1)}, u32[]{:S(2)}) copy-start(pred[192,512]{1,0:T(8,128)(4,1)} %get-tuple-element.66) | copy-start | bytes 294916
  152.1 5.4 %collective-permute-start.5 = (bf16[1536,2,3,128]{3,0,2,1:T(8,128)(2,1)S(1)}, bf16[1536,2,3,128]{3,0,2,1:T(8,128)(2,1)S(1)}, u32[]{:S(2)}, u32[]{:S(2)}) collective-permute-start(bf16[1536,2,3,128]{3,0,2,1:T(8,128)(2,1)S(1)} %pad_maximum_fusion), channel_id=1, source_target_pairs={{0,8},{8,0},{1,9},{9,1},{2,10},{10,2},{3,11},{11,3},{4,12},{12,4},... | collective-permute-start | bytes 7077896 | tf_op jit(solution)/shard_map/ppermute | solution.py:139
  152.8 0.9 copy-start.17
  153.0 1.2 copy-start.16
  154.2 0.9 copy-start.15
  154.8 0.9 copy-start.14
  156.9 0.9 copy-start.13
  157.2 1.1 copy-start.12
  158.3 0.9 copy-start.11
  160.7 1.9 copy-start.10
  161.0 2.1 copy-start.9
  161.1 6.5 %collective-permute-start.6 = (bf16[192,384]{1,0:T(8,128)(2,1)S(1)}, bf16[192,384]{1,0:T(8,128)(2,1)S(1)}, u32[]{:S(2)}, u32[]{:S(2)}) collective-permute-start(bf16[192,384]{1,0:T(8,128)(2,1)S(1)} %bitcast.218), channel_id=1, source_target_pairs={{0,64},{64,0},{1,65},{65,1},{2,66},{66,2},{3,67},{67,3},{4,68},{68... | collective-permute-start | bytes 442376 | tf_op jit(solution)/shard_map/ppermute | solution.py:186
  163.1 0.9 copy-start.8
  167.6 3.8 %copy-start = (bf16[384,5120]{0,1:T(8,128)(2,1)S(1)}, bf16[384,5120]{0,1:T(8,128)(2,1)}, u32[]{:S(2)}) copy-start(bf16[384,5120]{0,1:T(8,128)(2,1)} %all-gather.4.cloned.1.call-done) | copy-start | bytes 11796484
  173.0 1.9 copy-start.1
  174.9 14.0 %collective-permute-start.9 = (bf16[4,96,640]{2,1,0:T(8,128)(2,1)S(1)}, bf16[4,96,640]{2,1,0:T(8,128)(2,1)S(1)}, u32[]{:S(2)}, u32[]{:S(2)}) collective-permute-start(bf16[4,96,640]{2,1,0:T(8,128)(2,1)S(1)} %get-tuple-element.16), channel_id=1, source_target_pairs={{0,68},{68,0},{4,64},{64,4},{1,69},{69,1},{5,65},{65,5},{2,70},{70... | collective-permute-start | bytes 1474568 | tf_op jit(solution)/shard_map/ppermute | solution.py:207
  177.3 12.5 %collective-permute-start.7 = (bf16[4,96,640]{2,1,0:T(8,128)(2,1)S(1)}, bf16[4,96,640]{2,1,0:T(8,128)(2,1)S(1)}, u32[]{:S(2)}, u32[]{:S(2)}) collective-permute-start(bf16[4,96,640]{2,1,0:T(8,128)(2,1)S(1)} %get-tuple-element.15), channel_id=1, source_target_pairs={{0,64},{64,0},{1,65},{65,1},{2,66},{66,2},{3,67},{67,3},{4,68},{68... | collective-permute-start | bytes 1474568 | tf_op jit(solution)/shard_map/ppermute | solution.py:204
  188.8 11.9 %collective-permute-start.10 = (bf16[4,96,640]{2,1,0:T(8,128)(2,1)S(1)}, bf16[4,96,640]{2,1,0:T(8,128)(2,1)S(1)}, u32[]{:S(2)}, u32[]{:S(2)}) collective-permute-start(bf16[4,96,640]{2,1,0:T(8,128)(2,1)S(1)} %collective-permute-done.9), channel_id=1, source_target_pairs={{0,64},{64,0},{1,65},{65,1},{2,66},{66,2},{3,67},{67,3},{4,68},{68... | collective-permute-start | bytes 1474568 | tf_op jit(solution)/shard_map/ppermute | solution.py:206
  189.8 12.8 %collective-permute-start.8 = (bf16[4,96,640]{2,1,0:T(8,128)(2,1)S(1)}, bf16[4,96,640]{2,1,0:T(8,128)(2,1)S(1)}, u32[]{:S(2)}, u32[]{:S(2)}) collective-permute-start(bf16[4,96,640]{2,1,0:T(8,128)(2,1)S(1)} %collective-permute-done.7), channel_id=1, source_target_pairs={{0,68},{68,0},{4,64},{64,4},{1,69},{69,1},{5,65},{65,5},{2,70},{70... | collective-permute-start | bytes 1474568 | tf_op jit(solution)/shard_map/ppermute | solution.py:203
  205.3 17.2 %all-to-all-start.1 = ((bf16[4,192,640]{2,1,0:T(8,128)(2,1)}), bf16[4,192,640]{2,1,0:T(8,128)(2,1)S(1)}, u32[]{:S(2)}, u32[]{:S(2)}) async-start(bf16[4,192,640]{2,1,0:T(8,128)(2,1)} %fusion.10), calls=%async_computation.1 | async-start | bytes 1966080 | tf_op jit(solution)/shard_map/all_to_all | solution.py:210
Sparse Core Ops, SparseCore 0:
  27.9 66.1 all-gather.5
  95.8 45.1 all-gather.3

commit v12 on v9

--- a/solution.py
+++ b/solution.py
@@ -81,17 +81,23 @@
     scale = guidance[0]
     hidden_part = uncond_rows + scale * (cond_rows - uncond_rows)
 
-    spread = jnp.broadcast_to(states[None], (n_blk,) + states.shape)
-    full_states = lax.all_to_all(spread, BLK, 0, 0, tiled=False)
-    full_states, hidden_part = lax.optimization_barrier((full_states, hidden_part))
-    inputs = full_states.astype(jnp.float32)
-    row_mean = jnp.mean(inputs, (0, 2), keepdims=True)
-    centered = inputs - row_mean
-    variance = jnp.mean(centered * centered, (0, 2), keepdims=True)
-    normed = centered * lax.rsqrt(variance + 1e-06)
     mod_shift = modulation[0].reshape(n_blk, 1, feat_width)
     mod_scale = modulation[1].reshape(n_blk, 1, feat_width)
-    modulated = (normed * (1.0 + mod_scale) + mod_shift).astype(jnp.bfloat16)
+    pieces = []
+    for first in (0, half_rows):
+        rows_here = states[first:first + half_rows]
+        spread = jnp.broadcast_to(rows_here[None], (n_blk,) + rows_here.shape)
+        pieces.append(lax.all_to_all(spread, BLK, 0, 0, tiled=False))
+    pieces[1], hidden_part = lax.optimization_barrier((pieces[1], hidden_part))
+    normed_pieces = []
+    for full_states in pieces:
+        inputs = full_states.astype(jnp.float32)
+        row_mean = jnp.mean(inputs, (0, 2), keepdims=True)
+        centered = inputs - row_mean
+        variance = jnp.mean(centered * centered, (0, 2), keepdims=True)
+        normed = centered * lax.rsqrt(variance + 1e-06)
+        normed_pieces.append((normed * (1.0 + mod_scale) + mod_shift).astype(jnp.bfloat16))
+    modulated = jnp.concatenate(normed_pieces, axis=1)
 
     shard_other = lax.ppermute(in_projection, "cfg", SWAP)
     stacked = jnp.stack(

time: 218 us -> 218 us (level)
  local copies, waits for them, and re-layouts: 7.06 us -> 16.6 us
  waiting for transfers between devices: 120 us -> 112 us
  other arithmetic: 20.1 us -> 17.7 us
    ppermute x1, waiting for transfers between devices: 44.4 us -> 0.01 us  [local(): other_rows = lax.ppermute(sent_rows, 'cfg', SWAP)]
    all_to_all x1 -> x2, waiting for transfers between devices: 0.01 us -> 42.7 us  [local(): pieces.append(lax.all_to_all(spread, BLK, 0, 0, tiled=False))]
    ppermute x1, waiting for transfers between devices: 20.5 us -> 11.6 us  [local(): lax.ppermute(kv, 'x', [(i, (i + 1) % n_x) for i in range(n_x)])]
    all_to_all x1 -> x2, starting transfers between devices: 7.75 us -> 12.3 us  [local(): pieces.append(lax.all_to_all(spread, BLK, 0, 0, tiled=False))]
    all_to_all x0 -> x1, local copies, waits for them, and re-layouts: none -> 4.28 us  [local(): pieces.append(lax.all_to_all(spread, BLK, 0, 0, tiled=False))]
    convert_element_type x1, other arithmetic: 5.8 us -> 2.14 us  [local(): (normed * (1.0 + mod_scale) + mod_shift).astype(jnp.bfloat16)]
    optimization_barrier x0 -> x1, local copies, waits for them, and re-layouts: none -> 2.85 us  [local(): pieces[1], hidden_part = lax.optimization_barrier((pieces[1], hidden_part))]
    transpose x0 -> x1, local copies, waits for them, and re-layouts: none -> 2.32 us  [local(): modulated.reshape(2, n_blk // 2, tok_count, per_blk, rows)]
  transfers between devices with their start and end apart: 11 -> 12, of which waited for: 7 -> 8; matrix products, arithmetic and copies ran while one was open for 20% -> 24% of each run, Pallas kernels for 0% -> 0%
where the time goes in v12:
time: 218 us; the launch traced here: 217 us
  waiting for transfers between devices  112 us (51%)
  matrix products  29.5 us (14%)
  starting transfers between devices  26.4 us (12%)
  other arithmetic  17.7 us (8%)
  local copies, waits for them, and re-layouts  16.6 us (8%)
  between operations  14.7 us (7%)
    all_to_all x2, waiting for transfers between devices, local(): pieces.append(lax.all_to_all(spread, BLK, 0, 0, tiled=False))  42.7 us
    all_to_all x1, waiting for transfers between devices, local(): lax.all_to_all(partial, BLK, 0, 0, tiled=False).astype(jnp.float32)  26.8 us
    ppermute x1, waiting for transfers between devices, local(): shard_other = lax.ppermute(in_projection, 'cfg', SWAP)  16.7 us
    all_to_all x2, starting transfers between devices, local(): pieces.append(lax.all_to_all(spread, BLK, 0, 0, tiled=False))  12.3 us
    ppermute x1, waiting for transfers between devices, local(): lax.ppermute(kv, 'x', [(i, (i + 1) % n_x) for i in range(n_x)])  11.6 us
    dot_general x1, matrix products, local(): jnp.einsum('tabi,abiqe->tqe', mod_perm, piece, preferred_element_type=jnp...  10.1 us
    ppermute x1, waiting for transfers between devices, local(): from_far = lax.ppermute(relayed, SEQ, relay_pairs)  8.95 us
    dot_general x12, matrix products, attend(): jnp.einsum('qhd,khd->hqk', query_rows, key_slab, preferred_element_type=j...  6.59 us
  transfers between devices with their start and end apart: 12, of which 8 were waited for; matrix products, arithmetic and copies ran while one was open for 24% of the time, Pallas kernels for 0%

profile of v12, /device:TPU:0, one launch (start us, length us, event | category | flops | bytes accessed | tf_op | source)
XLA Modules:
  0.0 216.6 jit_solution(6667746958920760270)
XLA Ops:
  6.5 2.0 collective-permute-start.1
  8.6 16.7 %collective-permute-done.1 = bf16[320,3,384]{2,0,1:T(8,128)(2,1)S(1)} collective-permute-done((bf16[320,3,384]{2,0,1:T(8,128)(2,1)}, bf16[320,3,384]{2,0,1:T(8,128)(2,1)S(1)}, u32[]{:S(2)}, u32[]{:S(2)}) %collective-permute-start.1) | collective-permute-done | bytes 737312 | tf_op jit(solution)/shard_map/ppermute | solution.py:102
  25.3 1.3 select_bitcast_fusion.1
  26.5 1.3 pad_maximum_fusion.2
  27.9 1.5 broadcast_in_dim.154
  29.4 7.7 %all-to-all-start = ((bf16[8,192,640]{2,1,0:T(8,128)(2,1)}), bf16[8,192,640]{2,1,0:T(8,128)(2,1)S(1)}, u32[]{:S(2)}, u32[]{:S(2)}) async-start(bf16[8,192,640]{2,1,0:T(8,128)(2,1)} %broadcast_in_dim.154), calls=%async_computation | async-start | bytes 3932160 | tf_op jit(solution)/shard_map/all_to_all | solution.py:90
  37.2 1.1 collective-permute-start
  38.5 1.1 cosine_bitcast_fusion
  39.5 23.9 %all-to-all-done = bf16[8,192,640]{2,1,0:T(8,128)(2,1)S(1)} async-done(((bf16[8,192,640]{2,1,0:T(8,128)(2,1)}), bf16[8,192,640]{2,1,0:T(8,128)(2,1)S(1)}, u32[]{:S(2)}, u32[]{:S(2)}) %all-to-all-start) | async-done | bytes 1966112 | tf_op jit(solution)/shard_map/all_to_all | solution.py:90
  63.5 1.6 broadcast_in_dim.156
  65.4 4.5 %all-to-all-start.1 = ((bf16[8,192,640]{2,1,0:T(8,128)(2,1)}), bf16[8,192,640]{2,1,0:T(8,128)(2,1)}, u32[]{:S(2)}, u32[]{:S(2)}) async-start(bf16[8,192,640]{2,1,0:T(8,128)(2,1)} %broadcast_in_dim.156), calls=%async_computation.1 | async-start | bytes 3932160 | tf_op jit(solution)/shard_map/all_to_all | solution.py:90
  70.9 0.8 copy.68
  71.7 0.8 copy.69
  72.6 1.1 convert_add_fusion
  73.6 2.9 %copy.62 = bf16[8,192,640]{1,2,0:T(8,128)(2,1)S(1)} copy(bf16[8,192,640]{2,1,0:T(8,128)(2,1)} %copy-done.2) | data formatting | bytes 3932160 | tf_op jit(solution)/shard_map/optimization_barrier | solution.py:91
  76.5 0.7 convert_reduce_fusion
  77.2 0.8 fusion.4
  78.1 18.8 %all-to-all-done.1 = bf16[8,192,640]{2,1,0:T(8,128)(2,1)} async-done(((bf16[8,192,640]{2,1,0:T(8,128)(2,1)}), bf16[8,192,640]{2,1,0:T(8,128)(2,1)}, u32[]{:S(2)}, u32[]{:S(2)}) %all-to-all-start.1) | async-done | bytes 1966112 | tf_op jit(solution)/shard_map/all_to_all | solution.py:90
  96.8 4.3 %copy.61 = bf16[8,192,640]{1,2,0:T(8,128)(2,1)} copy(bf16[8,192,640]{2,1,0:T(8,128)(2,1)} %all-to-all-done.1) | data formatting | bytes 3932160 | tf_op jit(solution)/shard_map/all_to_all | solution.py:90
  101.1 2.6 %convert_reduce_fusion.1 = f32[192]{0:T(256)S(1)} fusion(bf16[8,192,640]{1,2,0:T(8,128)(2,1)} %copy.61), kind=kLoop, calls=%fused_computation.3 | loop fusion | flops 1965888 | bytes 1966848 | tf_op jit(solution)/shard_map/reduce_sum | solution.py:95
  103.7 0.8 fusion.8
  104.5 2.1 fusion.11
  106.7 1.4 pad_maximum_fusion
  108.1 2.3 %copy.63 = bf16[384,4,2,2,320]{0,4,3,2,1:T(8,128)(2,1)} copy(bf16[384,4,2,2,320]{0,4,2,1,3:T(8,128)(2,1)S(1)} %bitcast.212) | data formatting | bytes 7864320 | tf_op jit(solution)/shard_map/transpose | solution.py:113
  110.4 10.1 %fusion.158 = f32[384,3,384,1,1]{0,2,1,4,3:T(8,128)S(1)} fusion(bf16[384,8,2,320,1]{0,3,4,2,1:T(8,128)(2,1)} %bitcast.215, bf16[8,2,320,3,384]{4,2,3,1,0:T(8,128)(2,1)} %bitcast.221), kind=kOutput, calls=%fused_computation.251 | convolution fusion | flops 4529848320 | bytes 17498112 | tf_op jit(solution)/shard_map/tabi,abiqe->tqe/dot_general | solution.py:115
  121.7 0.7 fusion.55
  122.3 0.9 pad_maximum_fusion.3
  123.2 1.6 collective-permute-start.2
  124.8 1.7 collective-permute-start.3
  126.6 1.6 broadcast_compare_fusion
  128.7 11.6 %collective-permute-done.2 = bf16[384,2,3,128]{3,0,2,1:T(8,128)(2,1)S(1)} collective-permute-done((bf16[384,2,3,128]{3,0,2,1:T(8,128)(2,1)}, bf16[384,2,3,128]{3,0,2,1:T(8,128)(2,1)S(1)}, u32[]{:S(2)}, u32[]{:S(2)}) %collective-permute-start.2) | collective-permute-done | bytes 589856 | tf_op jit(solution)/shard_map/ppermute | solution.py:138
  140.3 1.9 collective-permute-done.3
  142.4 1.1 collective-permute-start.4
  143.6 0.7 fusion.42
  144.3 0.6 fusion.154
  144.9 9.0 %collective-permute-done.4 = bf16[384,2,3,128]{3,0,2,1:T(8,128)(2,1)S(1)} collective-permute-done((bf16[384,2,3,128]{3,0,2,1:T(8,128)(2,1)S(1)}, bf16[384,2,3,128]{3,0,2,1:T(8,128)(2,1)S(1)}, u32[]{:S(2)}, u32[]{:S(2)}) %collective-permute-start.4) | collective-permute-done | bytes 589856 | tf_op jit(solution)/shard_map/ppermute | solution.py:143
  153.8 0.7 pad_maximum_fusion.1
  154.7 0.6 fusion.148
  157.2 0.6 fusion.153
  160.8 0.6 fusion.144
  162.6 0.6 collective-permute-start.6
  164.3 0.6 fusion.150
  166.2 3.0 %collective-permute-done.6 = bf16[192,384]{1,0:T(8,128)(2,1)S(1)} collective-permute-done((bf16[192,384]{1,0:T(8,128)(2,1)S(1)}, bf16[192,384]{1,0:T(8,128)(2,1)S(1)}, u32[]{:S(2)}, u32[]{:S(2)}) %collective-permute-start.6) | collective-permute-done | bytes 147488 | tf_op jit(solution)/shard_map/ppermute | solution.py:192
  169.2 3.8 %fusion.89 = f32[192,8,640]{2,0,1:T(8,128)S(1)} fusion(bf16[384,8,640]{0,2,1:T(8,128)(2,1)} %bitcast.213, bf16[192,384]{1,0:T(8,128)(2,1)S(1)} %collective-permute-done.6, pred[]{:T(512)S(6)} %eq.182, bf16[3,24,8,128]{3,2,1,0:T(8,128)(2,1)S(1)} %fusion.59), kind=kOutput, calls=%fused_computation.159 | convolution fusion | flops 755048448 | bytes 8159233 | tf_op jit(solution)/shard_map/te,ebn->btn/dot_general | solution.py:200
  173.0 2.9 %fusion.14 = bf16[8,192,640]{2,1,0:T(8,128)(2,1)} fusion(f32[192,8,640]{2,0,1:T(8,128)S(1)} %fusion.89, bf16[384,8,640]{0,2,1:T(8,128)(2,1)S(1)} %bitcast.214, f32[]{:T(128)} %bitcast.211, bf16[192,384]{1,0:T(8,128)(2,1)S(1)} %collective-permute-done.6, pred[]{:T(512)S(6)} %eq.182, bf16[3,24,8,128]{3,2,1,0:T(8,128)(2,1)S(1)} %fusion.59), kind=kOutput, calls=%fused_computation.20 | convolution fusion | flops 758980608 | bytes 10125317 | tf_op jit(solution)/shard_map/te,ebn->btn/dot_general | solution.py:199
  175.9 5.9 %all-to-all-start.2 = ((bf16[8,192,640]{2,1,0:T(8,128)(2,1)}), bf16[8,192,640]{2,1,0:T(8,128)(2,1)S(1)}, u32[]{:S(2)}, u32[]{:S(2)}) async-start(bf16[8,192,640]{2,1,0:T(8,128)(2,1)} %fusion.14), calls=%async_computation.2 | async-start | bytes 3932160 | tf_op jit(solution)/shard_map/all_to_all | solution.py:202
  181.8 26.8 %all-to-all-done.2 = bf16[8,192,640]{2,1,0:T(8,128)(2,1)S(1)} async-done(((bf16[8,192,640]{2,1,0:T(8,128)(2,1)}), bf16[8,192,640]{2,1,0:T(8,128)(2,1)S(1)}, u32[]{:S(2)}, u32[]{:S(2)}) %all-to-all-start.2) | async-done | bytes 1966112 | tf_op jit(solution)/shard_map/all_to_all | solution.py:202
  208.9 0.9 add_bitcast_fusion
  (114 shorter events, 11.7 us)
Async XLA Ops:
  6.5 103.9 %all-gather.6.cloned.1.call-start = ((), (), s32[]{:S(2)}) async-start(), calls=%async_computation.4 | async-start | bytes 13271040 | tf_op jit(solution)/shard_map/all_gather | solution.py:109
  6.5 18.7 %collective-permute-start.1 = (bf16[320,3,384]{2,0,1:T(8,128)(2,1)}, bf16[320,3,384]{2,0,1:T(8,128)(2,1)S(1)}, u32[]{:S(2)}, u32[]{:S(2)}) collective-permute-start(bf16[320,3,384]{2,0,1:T(8,128)(2,1)} %param.11), channel_id=1, source_target_pairs={{0,64},{64,0},{1,65},{65,1},{2,66},{66,2},{3,67},{67,3},{4,68},{68... | collective-permute-start | bytes 2211848 | tf_op jit(solution)/shard_map/ppermute | solution.py:102
  26.5 1.3 copy-start.3
  29.4 8.9 %copy-start.21 = (f32[3,5120]{1,0:T(4,128)S(1)}, f32[3,5120]{1,0:T(4,128)}, u32[]{:S(2)}) copy-start(f32[3,5120]{1,0:T(4,128)} %param.10) | copy-start | bytes 184324
  29.4 9.1 %copy-start.22 = (s32[3,384]{1,0:T(4,128)S(1)}, s32[3,384]{1,0:T(4,128)}, u32[]{:S(2)}) copy-start(s32[3,384]{1,0:T(4,128)} %param.14) | copy-start | bytes 13828
  29.4 9.1 %copy-start.23 = (f32[3,128]{1,0:T(4,128)S(1)}, f32[3,128]{1,0:T(4,128)}, u32[]{:S(2)}) copy-start(f32[3,128]{1,0:T(4,128)} %constant.98.clone) | copy-start | bytes 4612
  29.4 34.1 %all-to-all-start = ((bf16[8,192,640]{2,1,0:T(8,128)(2,1)}), bf16[8,192,640]{2,1,0:T(8,128)(2,1)S(1)}, u32[]{:S(2)}, u32[]{:S(2)}) async-start(bf16[8,192,640]{2,1,0:T(8,128)(2,1)} %broadcast_in_dim.154), calls=%async_computation | async-start | bytes 3932160 | tf_op jit(solution)/shard_map/all_to_all | solution.py:90
  37.1 129.1 %all-gather.4.cloned.1.call-start = ((), (), s32[]{:S(2)}) async-start(), calls=%async_computation.3 | async-start | bytes 4177920 | tf_op jit(solution)/shard_map/all_gather | solution.py:196
  37.2 35.4 %collective-permute-start = (bf16[192,640]{1,0:T(8,128)(2,1)S(1)}, bf16[192,640]{1,0:T(8,128)(2,1)}, u32[]{:S(2)}, u32[]{:S(2)}) collective-permute-start(bf16[192,640]{1,0:T(8,128)(2,1)S(1)} %get-tuple-element.20), channel_id=1, source_target_pairs={{0,64},{64,0},{1,65},{65,1},{2,66},{66,2},{3,67},{67,3},{4,68},{68... | collective-permute-start | bytes 737288 | tf_op jit(solution)/shard_map/ppermute | solution.py:76
  63.5 1.9 copy-start.2
  65.1 4.9 %copy-start.26 = (s32[5]{0:T(128)S(1)}, s32[5]{0:T(128)}, u32[]{:S(2)}) copy-start(s32[5]{0:T(128)} %param.13) | copy-start | bytes 64
  65.4 31.4 %all-to-all-start.1 = ((bf16[8,192,640]{2,1,0:T(8,128)(2,1)}), bf16[8,192,640]{2,1,0:T(8,128)(2,1)}, u32[]{:S(2)}, u32[]{:S(2)}) async-start(bf16[8,192,640]{2,1,0:T(8,128)(2,1)} %broadcast_in_dim.156), calls=%async_computation.1 | async-start | bytes 3932160 | tf_op jit(solution)/shard_map/all_to_all | solution.py:90
  70.1 6.4 %copy-start.24 = (s32[5,1]{0,1:T(1,128)}, s32[5,1]{0,1:T(1,128)S(1)}, u32[]{:S(2)}) copy-start(s32[5,1]{0,1:T(1,128)S(1)} %reduce-window.8) | copy-start | bytes 64
  101.1 2.6 %copy-start = (bf16[8,192,640]{1,2,0:T(8,128)(2,1)S(1)}, bf16[8,192,640]{1,2,0:T(8,128)(2,1)}, u32[]{:S(2)}) copy-start(bf16[8,192,640]{1,2,0:T(8,128)(2,1)} %copy.61) | copy-start | bytes 5898244
  120.6 0.9 copy-start.4
  120.6 1.0 copy-start.6
  120.7 1.0 copy-start.8
  120.9 5.5 %copy-start.25 = (s32[5,1]{0,1:T(1,128)S(1)}, s32[5,1]{0,1:T(1,128)}, u32[]{:S(2)}) copy-start(s32[5,1]{0,1:T(1,128)} %copy-done.24) | copy-start | bytes 64
  123.2 17.1 %collective-permute-start.2 = (bf16[384,2,3,128]{3,0,2,1:T(8,128)(2,1)}, bf16[384,2,3,128]{3,0,2,1:T(8,128)(2,1)S(1)}, u32[]{:S(2)}, u32[]{:S(2)}) collective-permute-start(bf16[384,2,3,128]{3,0,2,1:T(8,128)(2,1)} %pad_maximum_fusion.3), channel_id=1, source_target_pairs={{0,16},{16,32},{32,48},{48,0},{1,17},{17,33},{33,49},{49,1},{2,18}... | collective-permute-start | bytes 1769480 | tf_op jit(solution)/shard_map/ppermute | solution.py:138
  124.8 17.4 %collective-permute-start.3 = (bf16[384,2,3,128]{3,0,2,1:T(8,128)(2,1)}, bf16[384,2,3,128]{3,0,2,1:T(8,128)(2,1)S(1)}, u32[]{:S(2)}, u32[]{:S(2)}) collective-permute-start(bf16[384,2,3,128]{3,0,2,1:T(8,128)(2,1)} %pad_maximum_fusion.3), channel_id=1, source_target_pairs={{0,48},{16,0},{32,16},{48,32},{1,49},{17,1},{33,17},{49,33},{2,50}... | collective-permute-start | bytes 1769480 | tf_op jit(solution)/shard_map/ppermute | solution.py:139
  128.4 15.2 %copy-start.5 = (f32[384,128]{1,0:T(8,128)S(1)}, f32[384,128]{1,0:T(8,128)}, u32[]{:S(2)}) copy-start(f32[384,128]{1,0:T(8,128)} %copy.68) | copy-start | bytes 589828
  128.4 15.2 %copy-start.7 = (f32[384,128]{1,0:T(8,128)S(1)}, f32[384,128]{1,0:T(8,128)}, u32[]{:S(2)}) copy-start(f32[384,128]{1,0:T(8,128)} %copy.69) | copy-start | bytes 589828
  128.7 15.6 %copy-start.20 = (pred[192,512]{1,0:T(8,128)(4,1)S(1)}, pred[192,512]{1,0:T(8,128)(4,1)}, u32[]{:S(2)}) copy-start(pred[192,512]{1,0:T(8,128)(4,1)} %get-tuple-element.70) | copy-start | bytes 294916
  142.4 11.4 %collective-permute-start.4 = (bf16[384,2,3,128]{3,0,2,1:T(8,128)(2,1)S(1)}, bf16[384,2,3,128]{3,0,2,1:T(8,128)(2,1)S(1)}, u32[]{:S(2)}, u32[]{:S(2)}) collective-permute-start(bf16[384,2,3,128]{3,0,2,1:T(8,128)(2,1)S(1)} %get-tuple-element.18), channel_id=1, source_target_pairs={{0,16},{16,32},{32,48},{48,0},{8,56},{24,8},{40,24},{56,40},{1,17}... | collective-permute-start | bytes 1769480 | tf_op jit(solution)/shard_map/ppermute | solution.py:143
  144.9 9.8 %copy-start.19 = (pred[192,512]{1,0:T(8,128)(4,1)S(1)}, pred[192,512]{1,0:T(8,128)(4,1)}, u32[]{:S(2)}) copy-start(pred[192,512]{1,0:T(8,128)(4,1)} %get-tuple-element.69) | copy-start | bytes 294916
  154.6 5.0 %collective-permute-start.5 = (bf16[1536,2,3,128]{3,0,2,1:T(8,128)(2,1)S(1)}, bf16[1536,2,3,128]{3,0,2,1:T(8,128)(2,1)S(1)}, u32[]{:S(2)}, u32[]{:S(2)}) collective-permute-start(bf16[1536,2,3,128]{3,0,2,1:T(8,128)(2,1)S(1)} %pad_maximum_fusion.1), channel_id=1, source_target_pairs={{0,8},{8,0},{1,9},{9,1},{2,10},{10,2},{3,11},{11,3},{4,12},{12,4},... | collective-permute-start | bytes 7077896 | tf_op jit(solution)/shard_map/ppermute | solution.py:145
  155.2 0.9 copy-start.18
  155.5 1.2 copy-start.17
  156.1 1.1 copy-start.16
  156.7 1.1 copy-start.15
  158.7 1.0 copy-start.14
  159.3 0.9 copy-start.13
  159.6 1.1 copy-start.12
  162.3 1.0 copy-start.11
  162.6 1.2 copy-start.10
  162.6 6.6 %collective-permute-start.6 = (bf16[192,384]{1,0:T(8,128)(2,1)S(1)}, bf16[192,384]{1,0:T(8,128)(2,1)S(1)}, u32[]{:S(2)}, u32[]{:S(2)}) collective-permute-start(bf16[192,384]{1,0:T(8,128)(2,1)S(1)} %bitcast.218), channel_id=1, source_target_pairs={{0,64},{64,0},{1,65},{65,1},{2,66},{66,2},{3,67},{67,3},{4,68},{68... | collective-permute-start | bytes 442376 | tf_op jit(solution)/shard_map/ppermute | solution.py:192
  163.2 1.1 copy-start.9
  169.2 3.8 %copy-start.1 = (bf16[384,5120]{0,1:T(8,128)(2,1)S(1)}, bf16[384,5120]{0,1:T(8,128)(2,1)}, u32[]{:S(2)}) copy-start(bf16[384,5120]{0,1:T(8,128)(2,1)} %all-gather.4.cloned.1.call-done) | copy-start | bytes 11796484
  175.9 32.7 %all-to-all-start.2 = ((bf16[8,192,640]{2,1,0:T(8,128)(2,1)}), bf16[8,192,640]{2,1,0:T(8,128)(2,1)S(1)}, u32[]{:S(2)}, u32[]{:S(2)}) async-start(bf16[8,192,640]{2,1,0:T(8,128)(2,1)} %fusion.14), calls=%async_computation.2 | async-start | bytes 3932160 | tf_op jit(solution)/shard_map/all_to_all | solution.py:202
Sparse Core Ops, SparseCore 0:
  27.9 66.1 all-gather.5
  95.8 39.2 all-gather.3

commit v13 on v7

--- a/solution.py
+++ b/solution.py
@@ -100,18 +100,44 @@
             jnp.where(is_cond, shard_other, in_projection),
         ]
     )
-    piece = lax.all_gather(stacked, SEQ, axis=0, tiled=False)
+    n_x = lax.axis_size("x")
+    x_index = lax.axis_index("x")
+
+    def around_x(block):
+        from_behind = lax.ppermute(block, "x", [(i, (i + 1) % n_x) for i in range(n_x)])
+        from_ahead = lax.ppermute(block, "x", [(i, (i - 1) % n_x) for i in range(n_x)])
+        relayed = jnp.where(core == 0, from_behind, from_ahead)
+        relay_pairs = [(i * 2, ((i + 1) % n_x) * 2) for i in range(n_x)]
+        relay_pairs += [(i * 2 + 1, ((i - 1) % n_x) * 2 + 1) for i in range(n_x)]
+        from_far = lax.ppermute(relayed, SEQ, relay_pairs)
+        mine = jnp.stack([block, from_behind, from_far, from_ahead])
+        return mine, lax.ppermute(mine, "core", SWAP)
+
+    piece = lax.all_gather(stacked[:, :, :2], SEQ, axis=0, tiled=False)
     n_seq = piece.shape[0]
     rows = in_projection.shape[0]
     per_blk = feat_width // rows
     mod_perm = modulated.reshape(2, n_blk // 2, tok_count, per_blk, rows).transpose(2, 1, 3, 0, 4)
     mod_perm = mod_perm.reshape(tok_count, n_seq, 2, rows)
-    mixed = jnp.einsum(
+    mixed_qk = jnp.einsum(
         "tabi,abiqe->tqe",
         mod_perm,
         piece,
         preferred_element_type=jnp.float32,
     )
+    value_mine, value_other = around_x(stacked[:, :, 2])
+    value_piece = jnp.concatenate([value_mine, value_other], axis=0)
+    back = jnp.arange(n_x, dtype=jnp.int32)
+    source_x = (x_index - back + n_x) % n_x
+    order = jnp.concatenate([source_x * 2 + core, source_x * 2 + 1 - core])
+    mod_value = jnp.take(mod_perm, order, axis=1)
+    mixed_v = jnp.einsum(
+        "tabi,abie->te",
+        mod_value,
+        value_piece,
+        preferred_element_type=jnp.float32,
+    )
+    mixed = jnp.concatenate([mixed_qk, mixed_v[:, None]], axis=1)
     mixed = with_layout_constraint(mixed, Layout((0, 1, 2)))
     mixed = mixed.reshape(tok_count, 3, head_count, HEAD_DIM)
 
@@ -127,14 +153,10 @@
     value_rows = mixed[:, 2].astype(jnp.bfloat16)
 
     kv = jnp.stack([key_rows, value_rows], axis=1)
-    n_x = lax.axis_size("x")
-    x_index = lax.axis_index("x")
-    kv_mine = jnp.concatenate(
-        [kv] + [lax.ppermute(kv, "x", [(i, (i + j) % n_x) for i in range(n_x)]) for j in range(1, n_x)],
-        axis=0,
-    )
-    kv_other = lax.ppermute(kv_mine, "core", SWAP)
-    kv_all = jnp.concatenate([kv_mine, kv_other], axis=0)
+    kv_mine, kv_other = around_x(kv)
+    kv_all = jnp.concatenate(
+        [kv_mine.reshape((-1,) + kv.shape[1:]), kv_other.reshape((-1,) + kv.shape[1:])], axis=0
+    )
     key_piece = kv_all[:, 0]
     value_piece = kv_all[:, 1]
     row_count = key_piece.shape[0]

time: 222 us -> 228 us (1.027)
  waiting for transfers between devices: 119 us -> 103 us
  local copies, waits for them, and re-layouts: 9.03 us -> 23.6 us
  starting transfers between devices: 26.1 us -> 29.7 us
  other arithmetic: 21.3 us -> 24.4 us
    ppermute x1, waiting for transfers between devices: 42.1 us -> 18.1 us  [local(): other_rows = lax.ppermute(sent_rows, 'cfg', SWAP)]
    ppermute x4 -> x8, waiting for transfers between devices: 32.2 us -> 39.7 us  [the longest x2 30.4 us: around_x(): lax.ppermute(block, 'x', [(i, (i + 1) % n_x) for i in range(n_x)])]
    gather x0 -> x1, local copies, waits for them, and re-layouts: none -> 5.34 us  [local(): mod_value = jnp.take(mod_perm, order, axis=1)]
    dot_general x0 -> x1, matrix products: none -> 4.53 us  [local(): jnp.einsum('tabi,abie->te', mod_value, value_piece, preferred_element_typ...]
    ppermute x4 -> x8, starting transfers between devices: 5.74 us -> 9.86 us  [the longest x2 3.55 us: around_x(): lax.ppermute(block, 'x', [(i, (i - 1) % n_x) for i in range(n_x)])]
    another operation x0 -> x2, local copies, waits for them, and re-layouts: none -> 2.61 us  [the longest x1 2.38 us: local(): mixed = with_layout_constraint(mixed, Layout((0, 1, 2)))]
    unnamed x48 -> x54, local copies, waits for them, and re-layouts: 4.98 us -> 5.75 us
  transfers between devices with their start and end apart: 11 -> 15, of which waited for: 6 -> 9; matrix products, arithmetic and copies ran while one was open for 21% -> 30% of each run, Pallas kernels for 0% -> 0%
where the time goes in v13:
time: 228 us; the launch traced here: 227 us
  waiting for transfers between devices  103 us (45%)
  matrix products  31.8 us (14%)
  starting transfers between devices  29.7 us (13%)
  other arithmetic  24.4 us (11%)
  local copies, waits for them, and re-layouts  23.6 us (10%)
  between operations  14.6 us (6%)
    ppermute x2, waiting for transfers between devices, around_x(): lax.ppermute(block, 'x', [(i, (i + 1) % n_x) for i in range(n_x)])  30.4 us
    all_to_all x1, waiting for transfers between devices, local(): lax.all_to_all(partial, BLK, 0, 0, tiled=False).astype(jnp.float32)  26.3 us
    ppermute x1, waiting for transfers between devices, local(): other_rows = lax.ppermute(sent_rows, 'cfg', SWAP)  18.1 us
    ppermute x1, waiting for transfers between devices, local(): shard_other = lax.ppermute(in_projection, 'cfg', SWAP)  16.7 us
    ppermute x2, waiting for transfers between devices, around_x(): from_far = lax.ppermute(relayed, SEQ, relay_pairs)  8.68 us
    dot_general x1, matrix products, local(): jnp.einsum('tabi,abiqe->tqe', mod_perm, piece, preferred_element_type=jnp...  7.86 us
    all_to_all x1, starting transfers between devices, local(): full_states = lax.all_to_all(spread, BLK, 0, 0, tiled=False)  7.74 us
    all_to_all x1, starting transfers between devices, local(): lax.all_to_all(partial, BLK, 0, 0, tiled=False).astype(jnp.float32)  7.44 us
  transfers between devices with their start and end apart: 15, of which 9 were waited for; matrix products, arithmetic and copies ran while one was open for 30% of the time, Pallas kernels for 0%

profile of v13, /device:TPU:0, one launch (start us, length us, event | category | flops | bytes accessed | tf_op | source)
XLA Modules:
  0.0 227.0 jit_solution(5720683262410240799)
XLA Ops:
  6.5 2.0 collective-permute-start.1
  8.6 16.7 %collective-permute-done.1 = bf16[320,3,384]{2,0,1:T(8,128)(2,1)S(1)} collective-permute-done((bf16[320,3,384]{2,0,1:T(8,128)(2,1)}, bf16[320,3,384]{2,0,1:T(8,128)(2,1)S(1)}, u32[]{:S(2)}, u32[]{:S(2)}) %collective-permute-start.1) | collective-permute-done | bytes 737312 | tf_op jit(solution)/shard_map/ppermute | solution.py:96
  25.3 1.3 select_bitcast_fusion.1
  26.5 1.1 fusion.59
  28.0 2.2 broadcast_in_dim.156
  30.2 7.7 %all-to-all-start = ((bf16[8,384,640]{1,2,0:T(8,128)(2,1)}), bf16[8,384,640]{1,2,0:T(8,128)(2,1)}, u32[]{:S(2)}, u32[]{:S(2)}) async-start(bf16[8,384,640]{1,2,0:T(8,128)(2,1)} %broadcast_in_dim.156), calls=%async_computation | async-start | bytes 7864320 | tf_op jit(solution)/shard_map/all_to_all | solution.py:85
  38.1 1.1 collective-permute-start
  39.4 1.1 cosine_bitcast_fusion
  40.5 0.9 constant_dynamic-update-slice_fusion.4
  41.4 1.5 collective-permute-start.2
  42.9 1.7 collective-permute-start.3
  45.4 0.8 copy.55
  46.2 0.8 copy.56
  47.4 18.6 %collective-permute-done.2 = bf16[2,320,384]{2,1,0:T(8,128)(2,1)S(1)} collective-permute-done((bf16[2,320,384]{2,1,0:T(8,128)(2,1)S(1)}, bf16[2,320,384]{2,1,0:T(8,128)(2,1)S(1)}, u32[]{:S(2)}, u32[]{:S(2)}) %collective-permute-start.2) | collective-permute-done | bytes 491552 | tf_op jit(solution)/shard_map/ppermute | solution.py:107
  66.6 1.6 collective-permute-start.4
  68.2 18.1 %collective-permute-done = bf16[192,640]{1,0:T(8,128)(2,1)} collective-permute-done((bf16[192,640]{1,0:T(8,128)(2,1)S(1)}, bf16[192,640]{1,0:T(8,128)(2,1)}, u32[]{:S(2)}, u32[]{:S(2)}) %collective-permute-start) | collective-permute-done | bytes 245792 | tf_op jit(solution)/shard_map/ppermute | solution.py:76
  86.2 1.1 convert_add_fusion
  87.3 0.9 constant_dynamic-update-slice_fusion.3
  88.2 1.6 pad_maximum_fusion.2
  89.8 0.8 constant_dynamic-update-slice_fusion.2
  90.7 0.8 constant_dynamic-update-slice_fusion.1
  91.5 2.9 %convert_reduce_fusion = f32[384]{0:T(512)S(1)} fusion(bf16[8,384,640]{1,2,0:T(8,128)(2,1)} %all-to-all-done), kind=kLoop, calls=%fused_computation.2 | loop fusion | flops 3931776 | bytes 3933696 | tf_op jit(solution)/shard_map/reduce_sum | solution.py:88
  94.4 3.2 %fusion.2 = f32[384]{0:T(512)S(1)} fusion(bf16[8,384,640]{1,2,0:T(8,128)(2,1)} %all-to-all-done, f32[384]{0:T(512)S(1)} %broadcast_multiply_fusion), kind=kLoop, calls=%fused_computation.5 | loop fusion | flops 7863936 | bytes 3935232 | tf_op jit(solution)/shard_map/reduce_sum | solution.py:90
  97.6 6.0 %fusion.5 = bf16[8,384,640]{1,2,0:T(8,128)(2,1)} fusion(bf16[8,384,640]{1,2,0:T(8,128)(2,1)} %all-to-all-done, f32[8,640]{1,0:T(8,128)S(1)} %add.356, f32[8,640]{1,0:T(8,128)S(1)} %add.355, f32[384]{0:T(512)S(1)} %add_rsqrt_fusion.2, f32[384]{0:T(512)S(1)} %broadcast_multiply_fusion), kind=kLoop, calls=%fused_computation.8 | loop fusion | flops 11796480 | bytes 7908352 | tf_op jit(solution)/shard_map/convert_element_type | solution.py:94
  103.6 5.3 %gather_fusion = bf16[8,384,2,320]{1,3,2,0:T(8,128)(2,1)} fusion(bf16[384,8,2,320]{0,3,1,2:T(8,128)(2,1)} %bitcast.236, s32[1024]{0:T(1024)S(1)} %pad_clamp_fusion), kind=kCustom, calls=%fused_computation | custom fusion | bytes 7864352 | tf_op jit(solution)/shard_map/jit(_take)/gather | solution.py:133
  109.0 1.5 constant_dynamic-update-slice_fusion
  110.5 1.3 copy-done.1
  111.8 4.5 %fusion.43 = f32[384,384]{1,0:T(8,128)S(1)} fusion(bf16[8,2,320,384]{3,2,1,0:T(8,128)(2,1)} %constant_dynamic-update-slice_fusion, bf16[8,384,2,320]{1,3,2,0:T(8,128)(2,1)S(1)} %copy-done.1, pred[8]{0:T(512)(128)(4,1)S(1)} %compare_and_fusion), kind=kOutput, calls=%fused_computation.63 | convolution fusion | flops 1511915520 | bytes 8454152 | tf_op jit(solution)/shard_map/tabi,abie->te/dot_general | solution.py:134
  116.8 7.9 %fusion.40 = f32[384,2,384]{2,0,1:T(8,128)S(1)} fusion(bf16[384,8,2,320,1]{0,3,1,4,2:T(8,128)(2,1)} %bitcast.237, bf16[8,2,320,2,384]{4,2,1,0,3:T(8,128)(2,1)} %bitcast.281), kind=kOutput, calls=%fused_computation.62 | convolution fusion | flops 3019898880 | bytes 12976128 | tf_op jit(solution)/shard_map/tabi,abiqe->tqe/dot_general | solution.py:122
  124.7 0.9 copy.52
  125.6 1.1 pad_maximum_fusion
  126.7 2.4 %copy.53 = f32[384,3,384]{0,2,1:T(8,128)} copy(f32[384,3,384]{2,1,0:T(4,128)S(1)} %pad_maximum_fusion) | data formatting | bytes 3538944 | tf_op jit(solution)/shard_map/layout_constraint | solution.py:141
  129.1 1.4 fusion.135
  130.5 1.1 slice.204
  133.0 0.9 fusion.134
  133.9 1.4 collective-permute-start.6
  135.3 1.8 collective-permute-start.7
  137.2 1.6 broadcast_compare_fusion.10
  139.0 11.8 %collective-permute-done.6 = bf16[384,2,3,128]{3,0,2,1:T(8,128)(2,1)S(1)} collective-permute-done((bf16[384,2,3,128]{3,0,2,1:T(8,128)(2,1)}, bf16[384,2,3,128]{3,0,2,1:T(8,128)(2,1)S(1)}, u32[]{:S(2)}, u32[]{:S(2)}) %collective-permute-start.6) | collective-permute-done | bytes 589856 | tf_op jit(solution)/shard_map/ppermute | solution.py:107
  151.0 1.7 collective-permute-start.8
  153.7 8.7 %collective-permute-done.8 = bf16[384,2,3,128]{3,0,2,1:T(8,128)(2,1)S(1)} collective-permute-done((bf16[384,2,3,128]{3,0,2,1:T(8,128)(2,1)S(1)}, bf16[384,2,3,128]{3,0,2,1:T(8,128)(2,1)S(1)}, u32[]{:S(2)}, u32[]{:S(2)}) %collective-permute-start.8) | collective-permute-done | bytes 589856 | tf_op jit(solution)/shard_map/ppermute | solution.py:112
  172.5 1.5 collective-permute-start.10
  176.6 2.0 collective-permute-done.10
  178.5 3.8 %fusion.80 = f32[192,8,640]{2,0,1:T(8,128)S(1)} fusion(bf16[384,8,640]{0,2,1:T(8,128)(2,1)} %bitcast.238, bf16[192,384]{1,0:T(8,128)(2,1)S(1)} %collective-permute-done.10, pred[]{:T(512)S(6)} %eq.185, bf16[3,24,8,128]{3,2,1,0:T(8,128)(2,1)S(1)} %fusion.58), kind=kOutput, calls=%fused_computation.154 | convolution fusion | flops 755048448 | bytes 8159233 | tf_op jit(solution)/shard_map/te,ebn->btn/dot_general | solution.py:213
  182.3 2.9 %fusion.10 = bf16[8,192,640]{2,1,0:T(8,128)(2,1)} fusion(f32[192,8,640]{2,0,1:T(8,128)S(1)} %fusion.80, bf16[384,8,640]{0,2,1:T(8,128)(2,1)S(1)} %bitcast.239, f32[]{:T(128)} %bitcast.235, bf16[192,384]{1,0:T(8,128)(2,1)S(1)} %collective-permute-done.10, pred[]{:T(512)S(6)} %eq.185, bf16[3,24,8,128]{3,2,1,0:T(8,128)(2,1)S(1)} %fusion.58), kind=kOutput, calls=%fused_computation.14 | convolution fusion | flops 758980608 | bytes 10125317 | tf_op jit(solution)/shard_map/te,ebn->btn/dot_general | solution.py:212
  185.2 7.4 %all-to-all-start.1 = ((bf16[8,192,640]{2,1,0:T(8,128)(2,1)}), bf16[8,192,640]{2,1,0:T(8,128)(2,1)S(1)}, u32[]{:S(2)}, u32[]{:S(2)}) async-start(bf16[8,192,640]{2,1,0:T(8,128)(2,1)} %fusion.10), calls=%async_computation.1 | async-start | bytes 3932160 | tf_op jit(solution)/shard_map/all_to_all | solution.py:215
  192.7 26.3 %all-to-all-done.1 = bf16[8,192,640]{2,1,0:T(8,128)(2,1)S(1)} async-done(((bf16[8,192,640]{2,1,0:T(8,128)(2,1)}), bf16[8,192,640]{2,1,0:T(8,128)(2,1)S(1)}, u32[]{:S(2)}, u32[]{:S(2)}) %all-to-all-start.1) | async-done | bytes 1966112 | tf_op jit(solution)/shard_map/all_to_all | solution.py:215
  219.3 0.9 add_bitcast_fusion
  (123 shorter events, 17.6 us)
Async XLA Ops:
  6.5 110.3 %all-gather.6.cloned.1.call-start = ((), (), s32[]{:S(2)}) async-start(), calls=%async_computation.3 | async-start | bytes 8847360 | tf_op jit(solution)/shard_map/all_gather | solution.py:116
  6.5 18.7 %collective-permute-start.1 = (bf16[320,3,384]{2,0,1:T(8,128)(2,1)}, bf16[320,3,384]{2,0,1:T(8,128)(2,1)S(1)}, u32[]{:S(2)}, u32[]{:S(2)}) collective-permute-start(bf16[320,3,384]{2,0,1:T(8,128)(2,1)} %param.11), channel_id=1, source_target_pairs={{0,64},{64,0},{1,65},{65,1},{2,66},{66,2},{3,67},{67,3},{4,68},{68... | collective-permute-start | bytes 2211848 | tf_op jit(solution)/shard_map/ppermute | solution.py:96
  26.5 1.2 copy-start.2
  30.2 9.1 %copy-start.20 = (f32[3,5120]{1,0:T(4,128)S(1)}, f32[3,5120]{1,0:T(4,128)}, u32[]{:S(2)}) copy-start(f32[3,5120]{1,0:T(4,128)} %param.10) | copy-start | bytes 184324
  30.2 9.2 %copy-start.21 = (s32[3,384]{1,0:T(4,128)S(1)}, s32[3,384]{1,0:T(4,128)}, u32[]{:S(2)}) copy-start(s32[3,384]{1,0:T(4,128)} %param.14) | copy-start | bytes 13828
  30.2 9.2 %copy-start.22 = (f32[3,128]{1,0:T(4,128)S(1)}, f32[3,128]{1,0:T(4,128)}, u32[]{:S(2)}) copy-start(f32[3,128]{1,0:T(4,128)} %constant.122.clone) | copy-start | bytes 4612
  30.2 61.3 %all-to-all-start = ((bf16[8,384,640]{1,2,0:T(8,128)(2,1)}), bf16[8,384,640]{1,2,0:T(8,128)(2,1)}, u32[]{:S(2)}, u32[]{:S(2)}) async-start(bf16[8,384,640]{1,2,0:T(8,128)(2,1)} %broadcast_in_dim.156), calls=%async_computation | async-start | bytes 7864320 | tf_op jit(solution)/shard_map/all_to_all | solution.py:85
  38.0 9.1 %copy-start.23 = (s32[5]{0:T(128)S(1)}, s32[5]{0:T(128)}, u32[]{:S(2)}) copy-start(s32[5]{0:T(128)} %param.13) | copy-start | bytes 64
  38.0 138.6 %all-gather.4.cloned.1.call-start = ((), (), s32[]{:S(2)}) async-start(), calls=%async_computation.2 | async-start | bytes 4177920 | tf_op jit(solution)/shard_map/all_gather | solution.py:209
  38.1 48.2 %collective-permute-start = (bf16[192,640]{1,0:T(8,128)(2,1)S(1)}, bf16[192,640]{1,0:T(8,128)(2,1)}, u32[]{:S(2)}, u32[]{:S(2)}) collective-permute-start(bf16[192,640]{1,0:T(8,128)(2,1)S(1)} %dynamic-slice_bitcast_fusion), channel_id=1, source_target_pairs={{0,64},{64,0},{1,65},{65,1},{2,66},{66,2},{3,67},{67,3},{4,68},{68... | collective-permute-start | bytes 737288 | tf_op jit(solution)/shard_map/ppermute | solution.py:76
  41.4 24.6 %collective-permute-start.2 = (bf16[2,320,384]{2,1,0:T(8,128)(2,1)S(1)}, bf16[2,320,384]{2,1,0:T(8,128)(2,1)S(1)}, u32[]{:S(2)}, u32[]{:S(2)}) collective-permute-start(bf16[2,320,384]{2,1,0:T(8,128)(2,1)S(1)} %bitcast.270), channel_id=1, source_target_pairs={{0,16},{16,32},{32,48},{48,0},{1,17},{17,33},{33,49},{49,1},{2,18}... | collective-permute-start | bytes 1474568 | tf_op jit(solution)/shard_map/ppermute | solution.py:107
  42.9 23.6 %collective-permute-start.3 = (bf16[2,320,384]{2,1,0:T(8,128)(2,1)S(1)}, bf16[2,320,384]{2,1,0:T(8,128)(2,1)S(1)}, u32[]{:S(2)}, u32[]{:S(2)}) collective-permute-start(bf16[2,320,384]{2,1,0:T(8,128)(2,1)S(1)} %bitcast.271), channel_id=1, source_target_pairs={{0,48},{16,0},{32,16},{48,32},{1,49},{17,1},{33,17},{49,33},{2,50}... | collective-permute-start | bytes 1474568 | tf_op jit(solution)/shard_map/ppermute | solution.py:108
  66.6 21.6 %collective-permute-start.4 = (bf16[2,320,384]{2,1,0:T(8,128)(2,1)S(1)}, bf16[2,320,384]{2,1,0:T(8,128)(2,1)S(1)}, u32[]{:S(2)}, u32[]{:S(2)}) collective-permute-start(bf16[2,320,384]{2,1,0:T(8,128)(2,1)S(1)} %broadcast_select_fusion.1), channel_id=1, source_target_pairs={{0,16},{16,32},{32,48},{48,0},{8,56},{24,8},{40,24},{56,40},{1,17}... | collective-permute-start | bytes 1474568 | tf_op jit(solution)/shard_map/ppermute | solution.py:112
  89.8 19.2 %collective-permute-start.5 = (bf16[4,2,320,384]{3,2,1,0:T(8,128)(2,1)}, bf16[4,2,320,384]{3,2,1,0:T(8,128)(2,1)S(1)}, u32[]{:S(2)}, u32[]{:S(2)}) collective-permute-start(bf16[4,2,320,384]{3,2,1,0:T(8,128)(2,1)} %pad_maximum_fusion.2), channel_id=1, source_target_pairs={{0,8},{8,0},{1,9},{9,1},{2,10},{10,2},{3,11},{11,3},{4,12},{12,4},... | collective-permute-start | bytes 5898248 | tf_op jit(solution)/shard_map/ppermute | solution.py:114
  109.0 2.9 %copy-start.1 = (bf16[8,384,2,320]{1,3,2,0:T(8,128)(2,1)S(1)}, bf16[8,384,2,320]{1,3,2,0:T(8,128)(2,1)}, u32[]{:S(2)}) copy-start(bf16[8,384,2,320]{1,3,2,0:T(8,128)(2,1)} %gather_fusion) | copy-start | bytes 11796484
  129.1 3.2 %copy-start.3 = (f32[384,128]{1,0:T(8,128)S(1)}, f32[384,128]{1,0:T(8,128)}, u32[]{:S(2)}) copy-start(f32[384,128]{1,0:T(8,128)} %copy.55) | copy-start | bytes 589828
  129.1 3.2 %copy-start.5 = (f32[384,128]{1,0:T(8,128)S(1)}, f32[384,128]{1,0:T(8,128)}, u32[]{:S(2)}) copy-start(f32[384,128]{1,0:T(8,128)} %copy.56) | copy-start | bytes 589828
  129.1 3.2 %copy-start.7 = (f32[128,128,1]{1,0,2:T(8,128)S(1)}, f32[128,128,1]{1,0,2:T(8,128)}, u32[]{:S(2)}) copy-start(f32[128,128,1]{1,0,2:T(8,128)} %constant.125) | copy-start | bytes 196612
  133.9 17.0 %collective-permute-start.6 = (bf16[384,2,3,128]{3,0,2,1:T(8,128)(2,1)}, bf16[384,2,3,128]{3,0,2,1:T(8,128)(2,1)S(1)}, u32[]{:S(2)}, u32[]{:S(2)}) collective-permute-start(bf16[384,2,3,128]{3,0,2,1:T(8,128)(2,1)} %get-tuple-element.18), channel_id=1, source_target_pairs={{0,16},{16,32},{32,48},{48,0},{1,17},{17,33},{33,49},{49,1},{2,18}... | collective-permute-start | bytes 1769480 | tf_op jit(solution)/shard_map/ppermute | solution.py:107
  135.3 15.6 %collective-permute-start.7 = (bf16[384,2,3,128]{3,0,2,1:T(8,128)(2,1)}, bf16[384,2,3,128]{3,0,2,1:T(8,128)(2,1)S(1)}, u32[]{:S(2)}, u32[]{:S(2)}) collective-permute-start(bf16[384,2,3,128]{3,0,2,1:T(8,128)(2,1)} %get-tuple-element.18), channel_id=1, source_target_pairs={{0,48},{16,0},{32,16},{48,32},{1,49},{17,1},{33,17},{49,33},{2,50}... | collective-permute-start | bytes 1769480 | tf_op jit(solution)/shard_map/ppermute | solution.py:108
  139.0 14.0 %copy-start.4 = (f32[384,128]{1,0:T(8,128)S(1)}, f32[384,128]{1,0:T(8,128)}, u32[]{:S(2)}) copy-start(f32[384,128]{1,0:T(8,128)} %copy.55) | copy-start | bytes 589828
  139.0 14.0 %copy-start.6 = (f32[384,128]{1,0:T(8,128)S(1)}, f32[384,128]{1,0:T(8,128)}, u32[]{:S(2)}) copy-start(f32[384,128]{1,0:T(8,128)} %copy.56) | copy-start | bytes 589828
  151.0 11.4 %collective-permute-start.8 = (bf16[384,2,3,128]{3,0,2,1:T(8,128)(2,1)S(1)}, bf16[384,2,3,128]{3,0,2,1:T(8,128)(2,1)S(1)}, u32[]{:S(2)}, u32[]{:S(2)}) collective-permute-start(bf16[384,2,3,128]{3,0,2,1:T(8,128)(2,1)S(1)} %broadcast_select_fusion), channel_id=1, source_target_pairs={{0,16},{16,32},{32,48},{48,0},{8,56},{24,8},{40,24},{56,40},{1,17}... | collective-permute-start | bytes 1769480 | tf_op jit(solution)/shard_map/ppermute | solution.py:112
  162.7 0.9 copy-start.19
  162.7 1.4 copy-start.18
  162.7 6.2 %collective-permute-start.9 = (bf16[4,384,2,3,128]{4,1,3,2,0:T(8,128)(2,1)S(1)}, bf16[4,384,2,3,128]{4,1,3,2,0:T(8,128)(2,1)S(1)}, u32[]{:S(2)}, u32[]{:S(2)}) collective-permute-start(bf16[4,384,2,3,128]{4,1,3,2,0:T(8,128)(2,1)S(1)} %pad_maximum_fusion.1), channel_id=1, source_target_pairs={{0,8},{8,0},{1,9},{9,1},{2,10},{10,2},{3,11},{11,3},{4,12},{12,4},... | collective-permute-start | bytes 7077896 | tf_op jit(solution)/shard_map/ppermute | solution.py:114
  163.1 1.7 copy-start.17
  164.2 1.1 copy-start.16
  164.7 1.1 copy-start.15
  165.3 1.1 copy-start.14
  168.9 0.9 copy-start.13
  168.9 1.4 copy-start.12
  169.2 1.7 copy-start.11
  171.8 2.2 copy-start.10
  172.1 2.4 %copy-start.9 = (pred[192,512]{1,0:T(8,128)(4,1)S(1)}, pred[192,512]{1,0:T(8,128)(4,1)}, u32[]{:S(2)}) copy-start(pred[192,512]{1,0:T(8,128)(4,1)} %get-tuple-element.62) | copy-start | bytes 294916
  172.4 2.6 %copy-start.8 = (pred[192,512]{1,0:T(8,128)(4,1)S(1)}, pred[192,512]{1,0:T(8,128)(4,1)}, u32[]{:S(2)}) copy-start(pred[192,512]{1,0:T(8,128)(4,1)} %get-tuple-element.67) | copy-start | bytes 294916
  172.5 6.1 %collective-permute-start.10 = (bf16[192,384]{1,0:T(8,128)(2,1)S(1)}, bf16[192,384]{1,0:T(8,128)(2,1)S(1)}, u32[]{:S(2)}, u32[]{:S(2)}) collective-permute-start(bf16[192,384]{1,0:T(8,128)(2,1)S(1)} %bitcast.276), channel_id=1, source_target_pairs={{0,64},{64,0},{1,65},{65,1},{2,66},{66,2},{3,67},{67,3},{4,68},{68... | collective-permute-start | bytes 442376 | tf_op jit(solution)/shard_map/ppermute | solution.py:205
  178.5 3.8 %copy-start = (bf16[384,5120]{0,1:T(8,128)(2,1)S(1)}, bf16[384,5120]{0,1:T(8,128)(2,1)}, u32[]{:S(2)}) copy-start(bf16[384,5120]{0,1:T(8,128)(2,1)} %all-gather.4.cloned.1.call-done) | copy-start | bytes 11796484
  185.2 33.8 %all-to-all-start.1 = ((bf16[8,192,640]{2,1,0:T(8,128)(2,1)}), bf16[8,192,640]{2,1,0:T(8,128)(2,1)S(1)}, u32[]{:S(2)}, u32[]{:S(2)}) async-start(bf16[8,192,640]{2,1,0:T(8,128)(2,1)} %fusion.10), calls=%async_computation.1 | async-start | bytes 3932160 | tf_op jit(solution)/shard_map/all_to_all | solution.py:215
Sparse Core Ops, SparseCore 0:
  27.8 65.2 all-gather.5
  94.9 37.3 all-gather.3

commit v14 on v9

--- a/solution.py
+++ b/solution.py
@@ -104,14 +104,13 @@
     n_seq = piece.shape[0]
     rows = in_projection.shape[0]
     per_blk = feat_width // rows
-    mod_perm = modulated.reshape(2, n_blk // 2, tok_count, per_blk, rows).transpose(2, 1, 3, 0, 4)
-    mod_perm = mod_perm.reshape(tok_count, n_seq, 2, rows)
+    mod5 = modulated.reshape(2, n_blk // 2, tok_count, per_blk, rows)
     mixed = jnp.einsum(
-        "tabi,abiqe->tqe",
-        mod_perm,
-        piece,
+        "zythi,yhzin->tn",
+        mod5,
+        piece.reshape(n_blk // 2, per_blk, 2, rows, 3 * inner_width),
         preferred_element_type=jnp.float32,
-    )
+    ).reshape(tok_count, 3, inner_width)
     mixed = with_layout_constraint(mixed, Layout((0, 1, 2)))
     mixed = mixed.reshape(tok_count, 3, head_count, HEAD_DIM)
 

time: 218 us -> 218 us (level)
  no operation moved by 1% of the time
where the time goes in v14:
time: 218 us; the launch traced here: 217 us
  waiting for transfers between devices  120 us (55%)
  matrix products  29.4 us (13%)
  starting transfers between devices  25.3 us (12%)
  other arithmetic  20.1 us (9%)
  between operations  14.6 us (7%)
  local copies, waits for them, and re-layouts  7.06 us (3%)
    ppermute x1, waiting for transfers between devices, local(): other_rows = lax.ppermute(sent_rows, 'cfg', SWAP)  44.4 us
    all_to_all x1, waiting for transfers between devices, local(): lax.all_to_all(partial, BLK, 0, 0, tiled=False).astype(jnp.float32)  26.8 us
    ppermute x1, waiting for transfers between devices, local(): lax.ppermute(kv, 'x', [(i, (i + 1) % n_x) for i in range(n_x)])  20.5 us
    ppermute x1, waiting for transfers between devices, local(): shard_other = lax.ppermute(in_projection, 'cfg', SWAP)  16.7 us
    dot_general x1, matrix products, local(): jnp.einsum('zythi,yhzin->tn', mod5, piece.reshape(n_blk // 2, per_blk, 2,...  10.1 us
    ppermute x1, waiting for transfers between devices, local(): from_far = lax.ppermute(relayed, SEQ, relay_pairs)  8.23 us
    all_to_all x1, starting transfers between devices, local(): full_states = lax.all_to_all(spread, BLK, 0, 0, tiled=False)  7.75 us
    all_to_all x1, starting transfers between devices, local(): lax.all_to_all(partial, BLK, 0, 0, tiled=False).astype(jnp.float32)  7.63 us
  transfers between devices with their start and end apart: 11, of which 7 were waited for; matrix products, arithmetic and copies ran while one was open for 20% of the time, Pallas kernels for 0%

profile of v14, /device:TPU:0, one launch (start us, length us, event | category | flops | bytes accessed | tf_op | source)
XLA Modules:
  0.0 216.7 jit_solution(8154539508698325531)
XLA Ops:
  6.5 2.0 collective-permute-start.1
  8.6 16.7 %collective-permute-done.1 = bf16[320,3,384]{2,0,1:T(8,128)(2,1)S(1)} collective-permute-done((bf16[320,3,384]{2,0,1:T(8,128)(2,1)}, bf16[320,3,384]{2,0,1:T(8,128)(2,1)S(1)}, u32[]{:S(2)}, u32[]{:S(2)}) %collective-permute-start.1) | collective-permute-done | bytes 737312 | tf_op jit(solution)/shard_map/ppermute | solution.py:96
  25.3 1.3 select_bitcast_fusion.1
  26.5 1.3 pad_maximum_fusion.1
  27.8 1.0 copy-done.1
  29.1 2.3 %broadcast_in_dim.143 = bf16[8,384,640]{1,2,0:T(8,128)(2,1)} broadcast(bf16[384,640]{0,1:T(8,128)(2,1)S(1)} %copy.48), dimensions={1,2} | broadcast | bytes 4423680 | tf_op jit(solution)/shard_map/broadcast_in_dim | solution.py:84
  31.4 7.8 %all-to-all-start = ((bf16[8,384,640]{1,2,0:T(8,128)(2,1)}), bf16[8,384,640]{1,2,0:T(8,128)(2,1)}, u32[]{:S(2)}, u32[]{:S(2)}) async-start(bf16[8,384,640]{1,2,0:T(8,128)(2,1)} %broadcast_in_dim.143), calls=%async_computation | async-start | bytes 7864320 | tf_op jit(solution)/shard_map/all_to_all | solution.py:85
  39.2 1.1 collective-permute-start
  40.8 1.1 cosine_bitcast_fusion
  42.9 44.4 %collective-permute-done = bf16[192,640]{1,0:T(8,128)(2,1)S(1)} collective-permute-done((bf16[192,640]{1,0:T(8,128)(2,1)S(1)}, bf16[192,640]{1,0:T(8,128)(2,1)S(1)}, u32[]{:S(2)}, u32[]{:S(2)}) %collective-permute-start) | collective-permute-done | bytes 245792 | tf_op jit(solution)/shard_map/ppermute | solution.py:76
  87.4 2.8 %convert_reduce_fusion = f32[384]{0:T(512)S(1)} fusion(bf16[8,384,640]{1,2,0:T(8,128)(2,1)} %all-to-all-done), kind=kLoop, calls=%fused_computation.3 | loop fusion | flops 3931776 | bytes 3933696 | tf_op jit(solution)/shard_map/reduce_sum | solution.py:88
  90.3 3.2 %fusion.4 = f32[384]{0:T(512)S(1)} fusion(bf16[8,384,640]{1,2,0:T(8,128)(2,1)} %all-to-all-done, f32[384]{0:T(512)S(1)} %broadcast_multiply_fusion), kind=kLoop, calls=%fused_computation.6 | loop fusion | flops 7863936 | bytes 3935232 | tf_op jit(solution)/shard_map/reduce_sum | solution.py:90
  93.5 5.8 %fusion.7 = bf16[8,384,640]{1,2,0:T(8,128)(2,1)} fusion(bf16[8,384,640]{1,2,0:T(8,128)(2,1)} %all-to-all-done, f32[8,640]{1,0:T(8,128)S(1)} %add.251, f32[8,640]{1,0:T(8,128)S(1)} %add.250, f32[384]{0:T(512)S(1)} %add_rsqrt_fusion.2, f32[384]{0:T(512)S(1)} %broadcast_multiply_fusion), kind=kLoop, calls=%fused_computation.9 | loop fusion | flops 11796480 | bytes 7908352 | tf_op jit(solution)/shard_map/convert_element_type | solution.py:94
  99.3 10.1 %fusion = f32[384,3,384,1,1,1]{0,2,3,1,5,4:T(8,128)S(1)} fusion(bf16[3,384,2,320,4,2]{1,3,0,5,2,4:T(8,128)(2,1)} %bitcast.212, bf16[2,4,384,2,320,1]{2,4,3,1,0,5:T(8,128)(2,1)} %bitcast.205), kind=kOutput, calls=%fused_computation | convolution fusion | flops 4529848320 | bytes 17498112 | tf_op jit(solution)/shard_map/zythi,yhzin->tn/dot_general | solution.py:108
  110.4 0.7 fusion.52
  111.1 0.9 pad_maximum_fusion.2
  112.0 1.5 collective-permute-start.2
  113.5 1.7 collective-permute-start.3
  115.4 1.5 broadcast_compare_fusion
  117.4 20.5 %collective-permute-done.2 = bf16[384,2,3,128]{3,0,2,1:T(8,128)(2,1)S(1)} collective-permute-done((bf16[384,2,3,128]{3,0,2,1:T(8,128)(2,1)}, bf16[384,2,3,128]{3,0,2,1:T(8,128)(2,1)S(1)}, u32[]{:S(2)}, u32[]{:S(2)}) %collective-permute-start.2) | collective-permute-done | bytes 589856 | tf_op jit(solution)/shard_map/ppermute | solution.py:131
  137.9 1.9 collective-permute-done.3
  140.0 1.8 collective-permute-start.4
  141.9 0.7 fusion.39
  142.6 0.6 fusion.151
  143.1 8.2 %collective-permute-done.4 = bf16[384,2,3,128]{3,0,2,1:T(8,128)(2,1)S(1)} collective-permute-done((bf16[384,2,3,128]{3,0,2,1:T(8,128)(2,1)S(1)}, bf16[384,2,3,128]{3,0,2,1:T(8,128)(2,1)S(1)}, u32[]{:S(2)}, u32[]{:S(2)}) %collective-permute-start.4) | collective-permute-done | bytes 589856 | tf_op jit(solution)/shard_map/ppermute | solution.py:136
  151.4 0.7 pad_maximum_fusion
  152.2 0.6 fusion.145
  153.1 0.5 copy-done.16
  153.7 0.5 fusion.152
  154.2 0.5 fusion.146
  154.8 0.3 copy-done.14
  155.1 0.5 fusion.150
  155.7 0.5 fusion.144
  157.7 0.5 fusion.143
  158.4 0.5 fusion.142
  159.2 0.5 fusion.141
  161.1 1.6 collective-permute-start.6
  162.7 0.5 fusion.149
  163.2 0.6 fusion.148
  163.8 0.3 copy-done.7
  164.1 0.5 fusion.147
  165.6 0.3 fusion.56
  165.9 1.7 collective-permute-done.6
  167.6 3.8 %fusion.86 = f32[192,8,640]{2,0,1:T(8,128)S(1)} fusion(bf16[384,8,640]{0,2,1:T(8,128)(2,1)} %bitcast.203, bf16[192,384]{1,0:T(8,128)(2,1)S(1)} %collective-permute-done.6, pred[]{:T(512)S(6)} %eq.182, bf16[3,24,8,128]{3,2,1,0:T(8,128)(2,1)S(1)} %fusion.56), kind=kOutput, calls=%fused_computation.151 | convolution fusion | flops 755048448 | bytes 8159233 | tf_op jit(solution)/shard_map/te,ebn->btn/dot_general | solution.py:193
  171.4 2.9 %fusion.10 = bf16[8,192,640]{2,1,0:T(8,128)(2,1)} fusion(f32[192,8,640]{2,0,1:T(8,128)S(1)} %fusion.86, bf16[384,8,640]{0,2,1:T(8,128)(2,1)S(1)} %bitcast.204, f32[]{:T(128)} %bitcast.202, bf16[192,384]{1,0:T(8,128)(2,1)S(1)} %collective-permute-done.6, pred[]{:T(512)S(6)} %eq.182, bf16[3,24,8,128]{3,2,1,0:T(8,128)(2,1)S(1)} %fusion.56), kind=kOutput, calls=%fused_computation.13 | convolution fusion | flops 758980608 | bytes 10125317 | tf_op jit(solution)/shard_map/te,ebn->btn/dot_general | solution.py:192
  174.3 7.6 %all-to-all-start.1 = ((bf16[8,192,640]{2,1,0:T(8,128)(2,1)}), bf16[8,192,640]{2,1,0:T(8,128)(2,1)S(1)}, u32[]{:S(2)}, u32[]{:S(2)}) async-start(bf16[8,192,640]{2,1,0:T(8,128)(2,1)} %fusion.10), calls=%async_computation.1 | async-start | bytes 3932160 | tf_op jit(solution)/shard_map/all_to_all | solution.py:195
  181.9 26.8 %all-to-all-done.1 = bf16[8,192,640]{2,1,0:T(8,128)(2,1)S(1)} async-done(((bf16[8,192,640]{2,1,0:T(8,128)(2,1)}), bf16[8,192,640]{2,1,0:T(8,128)(2,1)S(1)}, u32[]{:S(2)}, u32[]{:S(2)}) %all-to-all-start.1) | async-done | bytes 1966112 | tf_op jit(solution)/shard_map/all_to_all | solution.py:195
  209.0 0.9 add_bitcast_fusion
  (96 shorter events, 7.8 us)
Async XLA Ops:
  6.5 92.8 %all-gather.6.cloned.1.call-start = ((), (), s32[]{:S(2)}) async-start(), calls=%async_computation.3 | async-start | bytes 13271040 | tf_op jit(solution)/shard_map/all_gather | solution.py:103
  6.5 18.7 %collective-permute-start.1 = (bf16[320,3,384]{2,0,1:T(8,128)(2,1)}, bf16[320,3,384]{2,0,1:T(8,128)(2,1)S(1)}, u32[]{:S(2)}, u32[]{:S(2)}) collective-permute-start(bf16[320,3,384]{2,0,1:T(8,128)(2,1)} %param.11), channel_id=1, source_target_pairs={{0,64},{64,0},{1,65},{65,1},{2,66},{66,2},{3,67},{67,3},{4,68},{68... | collective-permute-start | bytes 2211848 | tf_op jit(solution)/shard_map/ppermute | solution.py:96
  27.8 1.0 copy-start.1
  31.4 9.0 %copy-start.22 = (s32[5]{0:T(128)S(1)}, s32[5]{0:T(128)}, u32[]{:S(2)}) copy-start(s32[5]{0:T(128)} %param.13) | copy-start | bytes 64
  31.4 9.3 %copy-start.19 = (f32[3,5120]{1,0:T(4,128)S(1)}, f32[3,5120]{1,0:T(4,128)}, u32[]{:S(2)}) copy-start(f32[3,5120]{1,0:T(4,128)} %param.10) | copy-start | bytes 184324
  31.4 9.4 %copy-start.20 = (s32[3,384]{1,0:T(4,128)S(1)}, s32[3,384]{1,0:T(4,128)}, u32[]{:S(2)}) copy-start(s32[3,384]{1,0:T(4,128)} %param.14) | copy-start | bytes 13828
  31.4 9.5 %copy-start.21 = (f32[3,128]{1,0:T(4,128)S(1)}, f32[3,128]{1,0:T(4,128)}, u32[]{:S(2)}) copy-start(f32[3,128]{1,0:T(4,128)} %constant.96.clone) | copy-start | bytes 4612
  31.4 56.1 %all-to-all-start = ((bf16[8,384,640]{1,2,0:T(8,128)(2,1)}), bf16[8,384,640]{1,2,0:T(8,128)(2,1)}, u32[]{:S(2)}, u32[]{:S(2)}) async-start(bf16[8,384,640]{1,2,0:T(8,128)(2,1)} %broadcast_in_dim.143), calls=%async_computation | async-start | bytes 7864320 | tf_op jit(solution)/shard_map/all_to_all | solution.py:85
  39.1 126.8 %all-gather.4.cloned.1.call-start = ((), (), s32[]{:S(2)}) async-start(), calls=%async_computation.2 | async-start | bytes 4177920 | tf_op jit(solution)/shard_map/all_gather | solution.py:189
  39.2 48.1 %collective-permute-start = (bf16[192,640]{1,0:T(8,128)(2,1)S(1)}, bf16[192,640]{1,0:T(8,128)(2,1)S(1)}, u32[]{:S(2)}, u32[]{:S(2)}) collective-permute-start(bf16[192,640]{1,0:T(8,128)(2,1)S(1)} %dynamic-slice_bitcast_fusion), channel_id=1, source_target_pairs={{0,64},{64,0},{1,65},{65,1},{2,66},{66,2},{3,67},{67,3},{4,68},{68... | collective-permute-start | bytes 737288 | tf_op jit(solution)/shard_map/ppermute | solution.py:76
  42.8 67.5 %copy-start.2 = (f32[384,128]{1,0:T(8,128)}, f32[384,128]{1,0:T(8,128)S(1)}, u32[]{:S(2)}) copy-start(f32[384,128]{1,0:T(8,128)S(1)} %copy.56) | copy-start | bytes 589828
  42.9 67.4 %copy-start.4 = (f32[384,128]{1,0:T(8,128)}, f32[384,128]{1,0:T(8,128)S(1)}, u32[]{:S(2)}) copy-start(f32[384,128]{1,0:T(8,128)S(1)} %copy.57) | copy-start | bytes 589828
  109.6 0.8 copy-start.6
  112.0 25.9 %collective-permute-start.2 = (bf16[384,2,3,128]{3,0,2,1:T(8,128)(2,1)}, bf16[384,2,3,128]{3,0,2,1:T(8,128)(2,1)S(1)}, u32[]{:S(2)}, u32[]{:S(2)}) collective-permute-start(bf16[384,2,3,128]{3,0,2,1:T(8,128)(2,1)} %pad_maximum_fusion.2), channel_id=1, source_target_pairs={{0,16},{16,32},{32,48},{48,0},{1,17},{17,33},{33,49},{49,1},{2,18}... | collective-permute-start | bytes 1769480 | tf_op jit(solution)/shard_map/ppermute | solution.py:131
  113.5 26.3 %collective-permute-start.3 = (bf16[384,2,3,128]{3,0,2,1:T(8,128)(2,1)}, bf16[384,2,3,128]{3,0,2,1:T(8,128)(2,1)S(1)}, u32[]{:S(2)}, u32[]{:S(2)}) collective-permute-start(bf16[384,2,3,128]{3,0,2,1:T(8,128)(2,1)} %pad_maximum_fusion.2), channel_id=1, source_target_pairs={{0,48},{16,0},{32,16},{48,32},{1,49},{17,1},{33,17},{49,33},{2,50}... | collective-permute-start | bytes 1769480 | tf_op jit(solution)/shard_map/ppermute | solution.py:132
  117.4 24.5 %copy-start.3 = (f32[384,128]{1,0:T(8,128)S(1)}, f32[384,128]{1,0:T(8,128)}, u32[]{:S(2)}) copy-start(f32[384,128]{1,0:T(8,128)} %copy-done.2) | copy-start | bytes 589828
  117.4 24.5 %copy-start.5 = (f32[384,128]{1,0:T(8,128)S(1)}, f32[384,128]{1,0:T(8,128)}, u32[]{:S(2)}) copy-start(f32[384,128]{1,0:T(8,128)} %copy-done.4) | copy-start | bytes 589828
  140.0 2.6 %copy-start.18 = (pred[192,512]{1,0:T(8,128)(4,1)S(1)}, pred[192,512]{1,0:T(8,128)(4,1)}, u32[]{:S(2)}) copy-start(pred[192,512]{1,0:T(8,128)(4,1)} %get-tuple-element.65) | copy-start | bytes 294916
  140.0 11.3 %collective-permute-start.4 = (bf16[384,2,3,128]{3,0,2,1:T(8,128)(2,1)S(1)}, bf16[384,2,3,128]{3,0,2,1:T(8,128)(2,1)S(1)}, u32[]{:S(2)}, u32[]{:S(2)}) collective-permute-start(bf16[384,2,3,128]{3,0,2,1:T(8,128)(2,1)S(1)} %get-tuple-element.18), channel_id=1, source_target_pairs={{0,16},{16,32},{32,48},{48,0},{8,56},{24,8},{40,24},{56,40},{1,17}... | collective-permute-start | bytes 1769480 | tf_op jit(solution)/shard_map/ppermute | solution.py:136
  143.1 9.1 %copy-start.17 = (pred[192,512]{1,0:T(8,128)(4,1)S(1)}, pred[192,512]{1,0:T(8,128)(4,1)}, u32[]{:S(2)}) copy-start(pred[192,512]{1,0:T(8,128)(4,1)} %get-tuple-element.64) | copy-start | bytes 294916
  152.1 5.4 %collective-permute-start.5 = (bf16[1536,2,3,128]{3,0,2,1:T(8,128)(2,1)S(1)}, bf16[1536,2,3,128]{3,0,2,1:T(8,128)(2,1)S(1)}, u32[]{:S(2)}, u32[]{:S(2)}) collective-permute-start(bf16[1536,2,3,128]{3,0,2,1:T(8,128)(2,1)S(1)} %pad_maximum_fusion), channel_id=1, source_target_pairs={{0,8},{8,0},{1,9},{9,1},{2,10},{10,2},{3,11},{11,3},{4,12},{12,4},... | collective-permute-start | bytes 7077896 | tf_op jit(solution)/shard_map/ppermute | solution.py:138
  152.8 0.9 copy-start.16
  153.1 1.1 copy-start.15
  154.2 0.9 copy-start.14
  154.8 0.9 copy-start.13
  156.9 0.9 copy-start.12
  157.5 0.9 copy-start.11
  158.3 0.9 copy-start.10
  160.7 2.0 copy-start.9
  161.1 2.2 %copy-start.8 = (pred[192,512]{1,0:T(8,128)(4,1)S(1)}, pred[192,512]{1,0:T(8,128)(4,1)}, u32[]{:S(2)}) copy-start(pred[192,512]{1,0:T(8,128)(4,1)} %get-tuple-element.69) | copy-start | bytes 294916
  161.1 6.5 %collective-permute-start.6 = (bf16[192,384]{1,0:T(8,128)(2,1)S(1)}, bf16[192,384]{1,0:T(8,128)(2,1)S(1)}, u32[]{:S(2)}, u32[]{:S(2)}) collective-permute-start(bf16[192,384]{1,0:T(8,128)(2,1)S(1)} %bitcast.209), channel_id=1, source_target_pairs={{0,64},{64,0},{1,65},{65,1},{2,66},{66,2},{3,67},{67,3},{4,68},{68... | collective-permute-start | bytes 442376 | tf_op jit(solution)/shard_map/ppermute | solution.py:185
  163.2 0.9 copy-start.7
  167.6 3.8 %copy-start = (bf16[384,5120]{0,1:T(8,128)(2,1)S(1)}, bf16[384,5120]{0,1:T(8,128)(2,1)}, u32[]{:S(2)}) copy-start(bf16[384,5120]{0,1:T(8,128)(2,1)} %all-gather.4.cloned.1.call-done) | copy-start | bytes 11796484
  174.3 34.5 %all-to-all-start.1 = ((bf16[8,192,640]{2,1,0:T(8,128)(2,1)}), bf16[8,192,640]{2,1,0:T(8,128)(2,1)S(1)}, u32[]{:S(2)}, u32[]{:S(2)}) async-start(bf16[8,192,640]{2,1,0:T(8,128)(2,1)} %fusion.10), calls=%async_computation.1 | async-start | bytes 3932160 | tf_op jit(solution)/shard_map/all_to_all | solution.py:195
Sparse Core Ops, SparseCore 0:
  27.9 66.1 all-gather.5
  95.8 45.1 all-gather.3

commit v15 on v13

--- a/solution.py
+++ b/solution.py
@@ -113,31 +113,23 @@
         mine = jnp.stack([block, from_behind, from_far, from_ahead])
         return mine, lax.ppermute(mine, "core", SWAP)
 
-    piece = lax.all_gather(stacked[:, :, :2], SEQ, axis=0, tiled=False)
+    w_mine, w_other = around_x(stacked)
+    piece = jnp.concatenate([w_mine, w_other], axis=0)
     n_seq = piece.shape[0]
     rows = in_projection.shape[0]
+    back = jnp.arange(n_x, dtype=jnp.int32)
+    source_x = (x_index - back + n_x) % n_x
+    order = jnp.concatenate([source_x * 2 + core, source_x * 2 + 1 - core])
     per_blk = feat_width // rows
     mod_perm = modulated.reshape(2, n_blk // 2, tok_count, per_blk, rows).transpose(2, 1, 3, 0, 4)
     mod_perm = mod_perm.reshape(tok_count, n_seq, 2, rows)
-    mixed_qk = jnp.einsum(
+    mod_w = jnp.take(mod_perm, order, axis=1)
+    mixed = jnp.einsum(
         "tabi,abiqe->tqe",
-        mod_perm,
+        mod_w,
         piece,
         preferred_element_type=jnp.float32,
     )
-    value_mine, value_other = around_x(stacked[:, :, 2])
-    value_piece = jnp.concatenate([value_mine, value_other], axis=0)
-    back = jnp.arange(n_x, dtype=jnp.int32)
-    source_x = (x_index - back + n_x) % n_x
-    order = jnp.concatenate([source_x * 2 + core, source_x * 2 + 1 - core])
-    mod_value = jnp.take(mod_perm, order, axis=1)
-    mixed_v = jnp.einsum(
-        "tabi,abie->te",
-        mod_value,
-        value_piece,
-        preferred_element_type=jnp.float32,
-    )
-    mixed = jnp.concatenate([mixed_qk, mixed_v[:, None]], axis=1)
     mixed = with_layout_constraint(mixed, Layout((0, 1, 2)))
     mixed = mixed.reshape(tok_count, 3, head_count, HEAD_DIM)
 
@@ -206,9 +198,18 @@
     mine_att = attend(cfg * half_rows)
     cond_att = jnp.where(is_cond, mine_att, other_att)
     uncond_att = jnp.where(is_cond, other_att, mine_att)
-    out_piece = lax.all_gather(out_projection, ("cfg",) + SEQ, axis=1, tiled=True).reshape(
-        inner_width, n_blk, feat_width
-    )
+    out_other = lax.ppermute(out_projection, "cfg", SWAP)
+    out_stacked = jnp.stack(
+        [jnp.where(is_cond, out_projection, out_other), jnp.where(is_cond, out_other, out_projection)]
+    )
+    o_mine, o_other = around_x(out_stacked)
+    o_all = jnp.concatenate([o_mine, o_other], axis=0)
+    seq_ids = jnp.arange(n_seq, dtype=jnp.int32)
+    x_of, core_of = seq_ids // 2, seq_ids % 2
+    distance = (x_index - x_of + n_x) % n_x
+    position = jnp.where(core_of == core, distance, n_x + distance)
+    o_sorted = jnp.take(o_all, position, axis=0)
+    out_piece = o_sorted.transpose(2, 1, 0, 3).reshape(inner_width, n_blk, feat_width)
     cond_part = jnp.einsum("te,ebn->btn", cond_att, out_piece, preferred_element_type=jnp.float32)
     uncond_part = jnp.einsum("te,ebn->btn", uncond_att, out_piece, preferred_element_type=jnp.float32)
     partial = (uncond_part + scale * (cond_part - uncond_part)).astype(jnp.bfloat16)

time: 228 us -> 277 us (1.21)
  waiting for transfers between devices: 103 us -> 138 us
  local copies, waits for them, and re-layouts: 23.6 us -> 41.4 us
  between operations: 14.6 us -> 1.3 us
  other arithmetic: 24.4 us -> 34.3 us
  matrix products: 31.8 us -> 26.3 us
  starting transfers between devices: 29.7 us -> 34.7 us
    ppermute x0 -> x1, waiting for transfers between devices: none -> 32.8 us  [local(): out_other = lax.ppermute(out_projection, 'cfg', SWAP)]
    ppermute x1, waiting for transfers between devices: 18.1 us -> 0.01 us  [local(): other_rows = lax.ppermute(sent_rows, 'cfg', SWAP)]
    ppermute x2 -> x3, waiting for transfers between devices: 8.68 us -> 21.8 us  [around_x(): from_far = lax.ppermute(relayed, SEQ, relay_pairs)]
    concatenate x1 -> x2, local copies, waits for them, and re-layouts: 1.54 us -> 9.13 us  [the longest x1 6.11 us: local(): piece = jnp.concatenate([w_mine, w_other], axis=0)]
    another operation x3 -> x6, other arithmetic: 2.82 us -> 9.88 us  [around_x(): mine = jnp.stack([block, from_behind, from_far, from_ahead])]
    ppermute x2 -> x3, waiting for transfers between devices: 30.4 us -> 37.1 us  [around_x(): lax.ppermute(block, 'x', [(i, (i + 1) % n_x) for i in range(n_x)])]
    gather x1 -> x2, local copies, waits for them, and re-layouts: 5.34 us -> 10.2 us  [the longest x1 5.18 us: local(): mod_w = jnp.take(mod_perm, order, axis=1)]
    ppermute x2 -> x3, starting transfers between devices: 3.55 us -> 8.2 us  [around_x(): lax.ppermute(block, 'x', [(i, (i - 1) % n_x) for i in range(n_x)])]
  transfers between devices with their start and end apart: 15 -> 18, of which waited for: 9 -> 9; matrix products, arithmetic and copies ran while one was open for 30% -> 31% of each run, Pallas kernels for 0% -> 0%
where the time goes in v15:
time: 277 us; the launch traced here: 276 us
  waiting for transfers between devices  138 us (50%)
  local copies, waits for them, and re-layouts  41.4 us (15%)
  starting transfers between devices  34.7 us (13%)
  other arithmetic  34.3 us (12%)
  matrix products  26.3 us (9%)
    ppermute x3, waiting for transfers between devices, around_x(): lax.ppermute(block, 'x', [(i, (i + 1) % n_x) for i in range(n_x)])  37.1 us
    ppermute x1, waiting for transfers between devices, local(): out_other = lax.ppermute(out_projection, 'cfg', SWAP)  32.8 us
    all_to_all x1, waiting for transfers between devices, local(): lax.all_to_all(partial, BLK, 0, 0, tiled=False).astype(jnp.float32)  26.3 us
    ppermute x3, waiting for transfers between devices, around_x(): from_far = lax.ppermute(relayed, SEQ, relay_pairs)  21.8 us
    ppermute x1, waiting for transfers between devices, local(): shard_other = lax.ppermute(in_projection, 'cfg', SWAP)  16.7 us
    unnamed x67, local copies, waits for them, and re-layouts  10 us
    another operation x6, other arithmetic, around_x(): mine = jnp.stack([block, from_behind, from_far, from_ahead])  9.88 us
    all_to_all x1, starting transfers between devices, local(): lax.all_to_all(partial, BLK, 0, 0, tiled=False).astype(jnp.float32)  9.3 us
  transfers between devices with their start and end apart: 18, of which 9 were waited for; matrix products, arithmetic and copies ran while one was open for 31% of the time, Pallas kernels for 0%

profile of v15, /device:TPU:0, one launch (start us, length us, event | category | flops | bytes accessed | tf_op | source)
XLA Modules:
  0.0 275.7 jit_solution(10803277946622015504)
XLA Ops:
  0.0 2.0 collective-permute-start.6
  2.0 16.7 %collective-permute-done.6 = bf16[320,3,384]{2,0,1:T(8,128)(2,1)S(1)} collective-permute-done((bf16[320,3,384]{2,0,1:T(8,128)(2,1)}, bf16[320,3,384]{2,0,1:T(8,128)(2,1)S(1)}, u32[]{:S(2)}, u32[]{:S(2)}) %collective-permute-start.6) | collective-permute-done | bytes 737312 | tf_op jit(solution)/shard_map/ppermute | solution.py:96
  18.7 1.3 select_bitcast_fusion.2
  20.0 2.1 fusion.134
  22.1 1.5 collective-permute-start.7
  23.6 1.7 collective-permute-start.8
  25.3 31.6 %collective-permute-done.7 = bf16[2,320,3,384]{3,1,0,2:T(8,128)(2,1)S(1)} collective-permute-done((bf16[2,320,3,384]{3,1,0,2:T(8,128)(2,1)}, bf16[2,320,3,384]{3,1,0,2:T(8,128)(2,1)S(1)}, u32[]{:S(2)}, u32[]{:S(2)}) %collective-permute-start.7) | collective-permute-done | bytes 1474592 | tf_op jit(solution)/shard_map/ppermute | solution.py:107
  57.0 1.3 broadcast_select_fusion
  58.3 1.4 collective-permute-start.9
  60.4 1.6 collective-permute-start
  61.9 1.0 copy.62
  62.9 3.4 %broadcast_in_dim.163 = bf16[8,384,640]{1,2,0:T(8,128)(2,1)} broadcast(bf16[384,640]{0,1:T(8,128)(2,1)} %copy.62), dimensions={1,2} | broadcast | bytes 4423680 | tf_op jit(solution)/shard_map/broadcast_in_dim | solution.py:84
  66.3 7.6 %all-to-all-start = ((bf16[8,384,640]{1,2,0:T(8,128)(2,1)}), bf16[8,384,640]{1,2,0:T(8,128)(2,1)}, u32[]{:S(2)}, u32[]{:S(2)}) async-start(bf16[8,384,640]{1,2,0:T(8,128)(2,1)} %broadcast_in_dim.163), calls=%async_computation | async-start | bytes 7864320 | tf_op jit(solution)/shard_map/all_to_all | solution.py:85
  74.4 4.8 %collective-permute-done.9 = bf16[2,320,3,384]{3,1,0,2:T(8,128)(2,1)} collective-permute-done((bf16[2,320,3,384]{3,1,0,2:T(8,128)(2,1)}, bf16[2,320,3,384]{3,1,0,2:T(8,128)(2,1)}, u32[]{:S(2)}, u32[]{:S(2)}) %collective-permute-start.9) | collective-permute-done | bytes 1474592 | tf_op jit(solution)/shard_map/ppermute | solution.py:112
  79.2 5.0 %pad_maximum_fusion = bf16[4,2,320,3,384]{4,2,1,3,0:T(8,128)(2,1)} fusion(bf16[1,2,320,3,384]{4,2,1,3,0:T(8,128)(2,1)S(1)} %bitcast.249, bf16[1,2,320,3,384]{4,2,1,3,0:T(8,128)(2,1)} %bitcast.27, bf16[1,2,320,3,384]{4,2,1,3,0:T(8,128)(2,1)S(1)} %bitcast.250, bf16[1,2,320,3,384]{4,2,1,3,0:T(8,128)(2,1)} %get-tuple-element.13), kind=kLoop, calls=%fused_computation.10 | loop fusion | flops 8847360 | bytes 11796480 | tf_op jit(solution)/shard_map/stack | solution.py:113
  84.6 1.1 cosine_bitcast_fusion
  88.0 32.8 %collective-permute-done.1 = bf16[384,320]{0,1:T(8,128)(2,1)} collective-permute-done((bf16[384,320]{0,1:T(8,128)(2,1)}, bf16[384,320]{0,1:T(8,128)(2,1)}, u32[]{:S(2)}, u32[]{:S(2)}) %collective-permute-start.1) | collective-permute-done | bytes 245792 | tf_op jit(solution)/shard_map/ppermute | solution.py:201
  120.7 1.1 select_bitcast_fusion.4
  122.1 3.2 %collective-permute-start.3 = (bf16[2,384,320]{1,2,0:T(8,128)(2,1)S(1)}, bf16[2,384,320]{1,2,0:T(8,128)(2,1)S(1)}, u32[]{:S(2)}, u32[]{:S(2)}) collective-permute-start(bf16[2,384,320]{1,2,0:T(8,128)(2,1)S(1)} %get-tuple-element.20), channel_id=1, source_target_pairs={{0,48},{16,0},{32,16},{48,32},{1,49},{17,1},{33,17},{49,33},{2,50}... | collective-permute-start | bytes 1474568 | tf_op jit(solution)/shard_map/ppermute | solution.py:108
  125.3 1.6 broadcast_compare_fusion.10
  126.9 2.0 convert_add_fusion
  128.8 5.4 %collective-permute-done.2 = bf16[2,384,320]{1,2,0:T(8,128)(2,1)S(1)} collective-permute-done((bf16[2,384,320]{1,2,0:T(8,128)(2,1)S(1)}, bf16[2,384,320]{1,2,0:T(8,128)(2,1)S(1)}, u32[]{:S(2)}, u32[]{:S(2)}) %collective-permute-start.2) | collective-permute-done | bytes 491552 | tf_op jit(solution)/shard_map/ppermute | solution.py:107
  135.3 1.3 constant_dynamic-update-slice_fusion.9
  137.4 7.0 %collective-permute-done.4 = bf16[2,384,320]{1,2,0:T(8,128)(2,1)S(1)} collective-permute-done((bf16[2,384,320]{1,2,0:T(8,128)(2,1)S(1)}, bf16[2,384,320]{1,2,0:T(8,128)(2,1)S(1)}, u32[]{:S(2)}, u32[]{:S(2)}) %collective-permute-start.4) | collective-permute-done | bytes 491552 | tf_op jit(solution)/shard_map/ppermute | solution.py:112
  144.5 1.6 pad_maximum_fusion.2
  146.9 1.3 constant_dynamic-update-slice_fusion.8
  148.1 2.8 %convert_reduce_fusion = f32[384]{0:T(512)S(1)} fusion(bf16[8,384,640]{1,2,0:T(8,128)(2,1)} %all-to-all-done), kind=kLoop, calls=%fused_computation.3 | loop fusion | flops 3931776 | bytes 3933696 | tf_op jit(solution)/shard_map/reduce_sum | solution.py:88
  151.0 3.2 %fusion.2 = f32[384]{0:T(512)S(1)} fusion(bf16[8,384,640]{1,2,0:T(8,128)(2,1)} %all-to-all-done, f32[384]{0:T(512)S(1)} %broadcast_multiply_fusion), kind=kLoop, calls=%fused_computation.6 | loop fusion | flops 7863936 | bytes 3935232 | tf_op jit(solution)/shard_map/reduce_sum | solution.py:90
  154.2 3.8 %fusion.5 = bf16[8,384,640]{1,2,0:T(8,128)(2,1)S(1)} fusion(bf16[8,384,640]{1,2,0:T(8,128)(2,1)} %all-to-all-done, f32[8,640]{1,0:T(8,128)S(1)} %add.457, f32[8,640]{1,0:T(8,128)S(1)} %add.456, f32[384]{0:T(512)S(1)} %add_rsqrt_fusion.2, f32[384]{0:T(512)S(1)} %broadcast_multiply_fusion), kind=kLoop, calls=%fused_computation.9 | loop fusion | flops 11796480 | bytes 7908352 | tf_op jit(solution)/shard_map/convert_element_type | solution.py:94
  158.0 2.4 copy.64
  160.4 5.2 %gather_fusion.1 = bf16[8,384,2,320]{1,3,2,0:T(8,128)(2,1)} fusion(bf16[384,8,2,320]{0,3,2,1:T(8,128)(2,1)} %bitcast.247, s32[1024]{0:T(1024)S(1)} %pad_clamp_fusion), kind=kCustom, calls=%fused_computation.1 | custom fusion | bytes 7864352 | tf_op jit(solution)/shard_map/jit(_take)/gather | solution.py:126
  165.6 2.7 constant_dynamic-update-slice_fusion.7
  168.2 1.3 constant_dynamic-update-slice_fusion.6
  169.5 6.1 %constant_dynamic-update-slice_fusion.5 = bf16[8,2,320,3,384]{4,2,1,3,0:T(8,128)(2,1)} fusion(bf16[8,2,320,3,384]{4,2,1,3,0:T(8,128)(2,1)} %constant_dynamic-update-slice_fusion.6, bf16[4,2,320,3,384]{4,2,1,3,0:T(8,128)(2,1)} %collective-permute-done.10), kind=kLoop, calls=%fused_computation.185 | loop fusion | bytes 11796480 | tf_op jit(solution)/shard_map/concatenate | solution.py:117
  175.7 9.2 %fusion.6 = f32[384,3,384,1,1]{0,2,4,1,3:T(8,128)S(1)} fusion(bf16[8,2,320,3,384]{4,2,1,3,0:T(8,128)(2,1)} %constant_dynamic-update-slice_fusion.5, bf16[8,384,2,320]{1,3,2,0:T(8,128)(2,1)S(1)} %copy-done.5, pred[8]{0:T(512)(128)(4,1)S(1)} %compare_and_fusion), kind=kOutput, calls=%fused_computation.11 | convolution fusion | flops 4531814400 | bytes 17498120 | tf_op jit(solution)/shard_map/tabi,abiqe->tqe/dot_general | solution.py:127
  186.6 0.9 fusion.132
  187.5 3.2 %collective-permute-start.12 = (bf16[384,2,3,128]{3,0,2,1:T(8,128)(2,1)}, bf16[384,2,3,128]{3,0,2,1:T(8,128)(2,1)S(1)}, u32[]{:S(2)}, u32[]{:S(2)}) collective-permute-start(bf16[384,2,3,128]{3,0,2,1:T(8,128)(2,1)} %get-tuple-element.18), channel_id=1, source_target_pairs={{0,48},{16,0},{32,16},{48,32},{1,49},{17,1},{33,17},{49,33},{2,50}... | collective-permute-start | bytes 1769480 | tf_op jit(solution)/shard_map/ppermute | solution.py:108
  191.6 3.0 %constant_dynamic-update-slice_fusion = bf16[8,2,384,320]{2,3,1,0:T(8,128)(2,1)} fusion(bf16[8,2,384,320]{2,3,1,0:T(8,128)(2,1)} %constant_dynamic-update-slice_fusion.1, bf16[4,2,384,320]{2,3,1,0:T(8,128)(2,1)} %collective-permute-done.5), kind=kLoop, calls=%fused_computation.180 | loop fusion | bytes 3932160 | tf_op jit(solution)/shard_map/concatenate | solution.py:206
  194.6 5.1 %gather_fusion = bf16[8,2,384,320]{2,3,1,0:T(8,128)(2,1)} fusion(bf16[8,2,384,320]{2,3,1,0:T(8,128)(2,1)} %constant_dynamic-update-slice_fusion, s32[1024]{0:T(1024)S(1)} %pad_clamp_fusion.1), kind=kCustom, calls=%fused_computation | custom fusion | bytes 7864352 | tf_op jit(solution)/shard_map/jit(_take)/gather | solution.py:211
  199.7 2.6 select_bitcast_fusion
  202.3 2.3 copy.63
  206.3 10.0 %collective-permute-done.13 = bf16[384,2,3,128]{3,0,2,1:T(8,128)(2,1)S(1)} collective-permute-done((bf16[384,2,3,128]{3,0,2,1:T(8,128)(2,1)S(1)}, bf16[384,2,3,128]{3,0,2,1:T(8,128)(2,1)S(1)}, u32[]{:S(2)}, u32[]{:S(2)}) %collective-permute-start.13) | collective-permute-done | bytes 589856 | tf_op jit(solution)/shard_map/ppermute | solution.py:112
  228.0 2.6 collective-permute-start.15
  231.5 3.0 %collective-permute-done.15 = bf16[192,384]{1,0:T(8,128)(2,1)S(1)} collective-permute-done((bf16[192,384]{1,0:T(8,128)(2,1)S(1)}, bf16[192,384]{1,0:T(8,128)(2,1)S(1)}, u32[]{:S(2)}, u32[]{:S(2)}) %collective-permute-start.15) | collective-permute-done | bytes 147488 | tf_op jit(solution)/shard_map/ppermute | solution.py:197
  234.5 1.5 fusion.71
  236.0 2.9 %fusion.10 = bf16[8,192,640]{2,1,0:T(8,128)(2,1)} fusion(f32[8,640,192]{1,2,0:T(8,128)S(1)} %fusion.71, bf16[384,8,640]{0,2,1:T(8,128)(2,1)S(1)} %bitcast.246, f32[]{:T(128)} %bitcast.244, bf16[192,384]{1,0:T(8,128)(2,1)S(1)} %collective-permute-done.15, pred[]{:T(512)S(6)} %eq.208, bf16[3,24,8,128]{3,2,1,0:T(8,128)(2,1)S(1)} %fusion.50), kind=kOutput, calls=%fused_computation.16 | convolution fusion | flops 758980608 | bytes 10125317 | tf_op jit(solution)/shard_map/te,ebn->btn/dot_general | solution.py:213
  238.9 9.3 %all-to-all-start.1 = ((bf16[8,192,640]{2,1,0:T(8,128)(2,1)}), bf16[8,192,640]{2,1,0:T(8,128)(2,1)S(1)}, u32[]{:S(2)}, u32[]{:S(2)}) async-start(bf16[8,192,640]{2,1,0:T(8,128)(2,1)} %fusion.10), calls=%async_computation.1 | async-start | bytes 3932160 | tf_op jit(solution)/shard_map/all_to_all | solution.py:216
  248.3 26.3 %all-to-all-done.1 = bf16[8,192,640]{2,1,0:T(8,128)(2,1)S(1)} async-done(((bf16[8,192,640]{2,1,0:T(8,128)(2,1)}), bf16[8,192,640]{2,1,0:T(8,128)(2,1)S(1)}, u32[]{:S(2)}, u32[]{:S(2)}) %all-to-all-start.1) | async-done | bytes 1966112 | tf_op jit(solution)/shard_map/all_to_all | solution.py:216
  (148 shorter events, 23.9 us)
Async XLA Ops:
  0.0 18.7 %collective-permute-start.6 = (bf16[320,3,384]{2,0,1:T(8,128)(2,1)}, bf16[320,3,384]{2,0,1:T(8,128)(2,1)S(1)}, u32[]{:S(2)}, u32[]{:S(2)}) collective-permute-start(bf16[320,3,384]{2,0,1:T(8,128)(2,1)} %param.11), channel_id=1, source_target_pairs={{0,64},{64,0},{1,65},{65,1},{2,66},{66,2},{3,67},{67,3},{4,68},{68... | collective-permute-start | bytes 2211848 | tf_op jit(solution)/shard_map/ppermute | solution.py:96
  20.0 2.1 copy-start.1
  20.0 3.6 %copy-start.3 = (bf16[1,320,3,384]{3,1,0,2:T(8,128)(2,1)}, bf16[1,320,3,384]{3,1,0,2:T(8,128)(2,1)S(1)}, u32[]{:S(2)}) copy-start(bf16[1,320,3,384]{3,1,0,2:T(8,128)(2,1)S(1)} %get-tuple-element.16) | copy-start | bytes 2211844
  22.1 37.6 %copy-start.6 = (bf16[1,384,640]{2,1,0:T(8,128)(2,1)S(1)}, bf16[1,384,640]{2,1,0:T(8,128)(2,1)}, u32[]{:S(2)}) copy-start(bf16[1,384,640]{2,1,0:T(8,128)(2,1)} %param.9) | copy-start | bytes 1474564
  22.1 34.9 %collective-permute-start.7 = (bf16[2,320,3,384]{3,1,0,2:T(8,128)(2,1)}, bf16[2,320,3,384]{3,1,0,2:T(8,128)(2,1)S(1)}, u32[]{:S(2)}, u32[]{:S(2)}) collective-permute-start(bf16[2,320,3,384]{3,1,0,2:T(8,128)(2,1)} %get-tuple-element.14), channel_id=1, source_target_pairs={{0,16},{16,32},{32,48},{48,0},{1,17},{17,33},{33,49},{49,1},{2,18}... | collective-permute-start | bytes 4423688 | tf_op jit(solution)/shard_map/ppermute | solution.py:107
  23.6 33.4 %collective-permute-start.8 = (bf16[2,320,3,384]{3,1,0,2:T(8,128)(2,1)}, bf16[2,320,3,384]{3,1,0,2:T(8,128)(2,1)S(1)}, u32[]{:S(2)}, u32[]{:S(2)}) collective-permute-start(bf16[2,320,3,384]{3,1,0,2:T(8,128)(2,1)} %get-tuple-element.14), channel_id=1, source_target_pairs={{0,48},{16,0},{32,16},{48,32},{1,49},{17,1},{33,17},{49,33},{2,50}... | collective-permute-start | bytes 4423688 | tf_op jit(solution)/shard_map/ppermute | solution.py:108
  58.3 20.9 %collective-permute-start.9 = (bf16[2,320,3,384]{3,1,0,2:T(8,128)(2,1)}, bf16[2,320,3,384]{3,1,0,2:T(8,128)(2,1)}, u32[]{:S(2)}, u32[]{:S(2)}) collective-permute-start(bf16[2,320,3,384]{3,1,0,2:T(8,128)(2,1)} %broadcast_select_fusion), channel_id=1, source_target_pairs={{0,16},{16,32},{32,48},{48,0},{8,56},{24,8},{40,24},{56,40},{1,17}... | collective-permute-start | bytes 4423688 | tf_op jit(solution)/shard_map/ppermute | solution.py:112
  60.4 66.5 %collective-permute-start = (bf16[192,640]{1,0:T(8,128)(2,1)}, bf16[192,640]{1,0:T(8,128)(2,1)}, u32[]{:S(2)}, u32[]{:S(2)}) collective-permute-start(bf16[192,640]{1,0:T(8,128)(2,1)} %dynamic-slice_bitcast_fusion), channel_id=1, source_target_pairs={{0,64},{64,0},{1,65},{65,1},{2,66},{66,2},{3,67},{67,3},{4,68},{68... | collective-permute-start | bytes 737288 | tf_op jit(solution)/shard_map/ppermute | solution.py:76
  66.3 7.6 %copy-start.28 = (s32[5]{0:T(128)S(1)}, s32[5]{0:T(128)}, u32[]{:S(2)}) copy-start(s32[5]{0:T(128)} %param.13) | copy-start | bytes 64
  66.3 81.8 %all-to-all-start = ((bf16[8,384,640]{1,2,0:T(8,128)(2,1)}), bf16[8,384,640]{1,2,0:T(8,128)(2,1)}, u32[]{:S(2)}, u32[]{:S(2)}) async-start(bf16[8,384,640]{1,2,0:T(8,128)(2,1)} %broadcast_in_dim.163), calls=%async_computation | async-start | bytes 7864320 | tf_op jit(solution)/shard_map/all_to_all | solution.py:85
  73.9 46.8 %collective-permute-start.1 = (bf16[384,320]{0,1:T(8,128)(2,1)}, bf16[384,320]{0,1:T(8,128)(2,1)}, u32[]{:S(2)}, u32[]{:S(2)}) collective-permute-start(bf16[384,320]{0,1:T(8,128)(2,1)} %param.12), channel_id=1, source_target_pairs={{0,64},{64,0},{1,65},{65,1},{2,66},{66,2},{3,67},{67,3},{4,68},{68... | collective-permute-start | bytes 737288 | tf_op jit(solution)/shard_map/ppermute | solution.py:201
  79.2 5.3 %copy-start.25 = (f32[3,5120]{1,0:T(4,128)S(1)}, f32[3,5120]{1,0:T(4,128)}, u32[]{:S(2)}) copy-start(f32[3,5120]{1,0:T(4,128)} %param.10) | copy-start | bytes 184324
  79.2 5.4 %copy-start.26 = (s32[3,384]{1,0:T(4,128)S(1)}, s32[3,384]{1,0:T(4,128)}, u32[]{:S(2)}) copy-start(s32[3,384]{1,0:T(4,128)} %param.14) | copy-start | bytes 13828
  79.2 5.4 %copy-start.27 = (f32[3,128]{1,0:T(4,128)S(1)}, f32[3,128]{1,0:T(4,128)}, u32[]{:S(2)}) copy-start(f32[3,128]{1,0:T(4,128)} %constant.171.clone) | copy-start | bytes 4612
  84.1 85.4 %collective-permute-start.10 = (bf16[4,2,320,3,384]{4,2,1,3,0:T(8,128)(2,1)}, bf16[4,2,320,3,384]{4,2,1,3,0:T(8,128)(2,1)}, u32[]{:S(2)}, u32[]{:S(2)}) collective-permute-start(bf16[4,2,320,3,384]{4,2,1,3,0:T(8,128)(2,1)} %pad_maximum_fusion), channel_id=1, source_target_pairs={{0,8},{8,0},{1,9},{9,1},{2,10},{10,2},{3,11},{11,3},{4,12},{12,4},... | collective-permute-start | bytes 17694728 | tf_op jit(solution)/shard_map/ppermute | solution.py:114
  122.0 13.3 %copy-start.2 = (bf16[1,320,3,384]{3,1,0,2:T(8,128)(2,1)S(1)}, bf16[1,320,3,384]{3,1,0,2:T(8,128)(2,1)}, u32[]{:S(2)}) copy-start(bf16[1,320,3,384]{3,1,0,2:T(8,128)(2,1)} %copy-done.1) | copy-start | bytes 2211844
  122.0 13.3 %copy-start.4 = (bf16[1,320,3,384]{3,1,0,2:T(8,128)(2,1)S(1)}, bf16[1,320,3,384]{3,1,0,2:T(8,128)(2,1)}, u32[]{:S(2)}) copy-start(bf16[1,320,3,384]{3,1,0,2:T(8,128)(2,1)} %copy-done.3) | copy-start | bytes 2211844
  122.0 12.3 %collective-permute-start.2 = (bf16[2,384,320]{1,2,0:T(8,128)(2,1)S(1)}, bf16[2,384,320]{1,2,0:T(8,128)(2,1)S(1)}, u32[]{:S(2)}, u32[]{:S(2)}) collective-permute-start(bf16[2,384,320]{1,2,0:T(8,128)(2,1)S(1)} %get-tuple-element.20), channel_id=1, source_target_pairs={{0,16},{16,32},{32,48},{48,0},{1,17},{17,33},{33,49},{49,1},{2,18}... | collective-permute-start | bytes 1474568 | tf_op jit(solution)/shard_map/ppermute | solution.py:107
  122.1 12.2 %collective-permute-start.3 = (bf16[2,384,320]{1,2,0:T(8,128)(2,1)S(1)}, bf16[2,384,320]{1,2,0:T(8,128)(2,1)S(1)}, u32[]{:S(2)}, u32[]{:S(2)}) collective-permute-start(bf16[2,384,320]{1,2,0:T(8,128)(2,1)S(1)} %get-tuple-element.20), channel_id=1, source_target_pairs={{0,48},{16,0},{32,16},{48,32},{1,49},{17,1},{33,17},{49,33},{2,50}... | collective-permute-start | bytes 1474568 | tf_op jit(solution)/shard_map/ppermute | solution.py:108
  134.4 10.1 %collective-permute-start.4 = (bf16[2,384,320]{1,2,0:T(8,128)(2,1)S(1)}, bf16[2,384,320]{1,2,0:T(8,128)(2,1)S(1)}, u32[]{:S(2)}, u32[]{:S(2)}) collective-permute-start(bf16[2,384,320]{1,2,0:T(8,128)(2,1)S(1)} %broadcast_select_fusion.2), channel_id=1, source_target_pairs={{0,16},{16,32},{32,48},{48,0},{8,56},{24,8},{40,24},{56,40},{1,17}... | collective-permute-start | bytes 1474568 | tf_op jit(solution)/shard_map/ppermute | solution.py:112
  146.0 45.6 %collective-permute-start.5 = (bf16[4,2,384,320]{2,3,1,0:T(8,128)(2,1)}, bf16[4,2,384,320]{2,3,1,0:T(8,128)(2,1)}, u32[]{:S(2)}, u32[]{:S(2)}) collective-permute-start(bf16[4,2,384,320]{2,3,1,0:T(8,128)(2,1)} %pad_maximum_fusion.2), channel_id=1, source_target_pairs={{0,8},{8,0},{1,9},{9,1},{2,10},{10,2},{3,11},{11,3},{4,12},{12,4},... | collective-permute-start | bytes 5898248 | tf_op jit(solution)/shard_map/ppermute | solution.py:114
  169.5 6.1 %copy-start.5 = (bf16[8,384,2,320]{1,3,2,0:T(8,128)(2,1)S(1)}, bf16[8,384,2,320]{1,3,2,0:T(8,128)(2,1)}, u32[]{:S(2)}) copy-start(bf16[8,384,2,320]{1,3,2,0:T(8,128)(2,1)} %gather_fusion.1) | copy-start | bytes 11796484
  184.9 0.9 copy-start.8
  184.9 1.0 copy-start.10
  184.9 1.0 copy-start.12
  187.5 17.3 %collective-permute-start.11 = (bf16[384,2,3,128]{3,0,2,1:T(8,128)(2,1)}, bf16[384,2,3,128]{3,0,2,1:T(8,128)(2,1)S(1)}, u32[]{:S(2)}, u32[]{:S(2)}) collective-permute-start(bf16[384,2,3,128]{3,0,2,1:T(8,128)(2,1)} %get-tuple-element.18), channel_id=1, source_target_pairs={{0,16},{16,32},{32,48},{48,0},{1,17},{17,33},{33,49},{49,1},{2,18}... | collective-permute-start | bytes 1769480 | tf_op jit(solution)/shard_map/ppermute | solution.py:107
  187.5 17.3 %collective-permute-start.12 = (bf16[384,2,3,128]{3,0,2,1:T(8,128)(2,1)}, bf16[384,2,3,128]{3,0,2,1:T(8,128)(2,1)S(1)}, u32[]{:S(2)}, u32[]{:S(2)}) collective-permute-start(bf16[384,2,3,128]{3,0,2,1:T(8,128)(2,1)} %get-tuple-element.18), channel_id=1, source_target_pairs={{0,48},{16,0},{32,16},{48,32},{1,49},{17,1},{33,17},{49,33},{2,50}... | collective-permute-start | bytes 1769480 | tf_op jit(solution)/shard_map/ppermute | solution.py:108
  204.6 0.9 copy-start.9
  204.6 1.0 copy-start.11
  204.9 11.4 %collective-permute-start.13 = (bf16[384,2,3,128]{3,0,2,1:T(8,128)(2,1)S(1)}, bf16[384,2,3,128]{3,0,2,1:T(8,128)(2,1)S(1)}, u32[]{:S(2)}, u32[]{:S(2)}) collective-permute-start(bf16[384,2,3,128]{3,0,2,1:T(8,128)(2,1)S(1)} %broadcast_select_fusion.1), channel_id=1, source_target_pairs={{0,16},{16,32},{32,48},{48,0},{8,56},{24,8},{40,24},{56,40},{1,17}... | collective-permute-start | bytes 1769480 | tf_op jit(solution)/shard_map/ppermute | solution.py:112
  216.6 0.9 copy-start.24
  216.6 1.4 copy-start.23
  216.6 6.2 %collective-permute-start.14 = (bf16[4,384,2,3,128]{4,1,3,2,0:T(8,128)(2,1)S(1)}, bf16[4,384,2,3,128]{4,1,3,2,0:T(8,128)(2,1)S(1)}, u32[]{:S(2)}, u32[]{:S(2)}) collective-permute-start(bf16[4,384,2,3,128]{4,1,3,2,0:T(8,128)(2,1)S(1)} %pad_maximum_fusion.1), channel_id=1, source_target_pairs={{0,8},{8,0},{1,9},{9,1},{2,10},{10,2},{3,11},{11,3},{4,12},{12,4},... | collective-permute-start | bytes 7077896 | tf_op jit(solution)/shard_map/ppermute | solution.py:114
  216.9 1.7 copy-start.22
  218.0 1.1 copy-start.21
  218.6 1.1 copy-start.20
  219.1 1.1 copy-start.19
  222.7 0.9 copy-start.18
  222.8 1.4 copy-start.17
  223.0 1.7 copy-start.16
  224.2 1.1 copy-start.15
  224.7 1.1 copy-start.14
  225.3 1.1 copy-start.13
  228.0 6.5 %collective-permute-start.15 = (bf16[192,384]{1,0:T(8,128)(2,1)S(1)}, bf16[192,384]{1,0:T(8,128)(2,1)S(1)}, u32[]{:S(2)}, u32[]{:S(2)}) collective-permute-start(bf16[192,384]{1,0:T(8,128)(2,1)S(1)} %bitcast.284), channel_id=1, source_target_pairs={{0,64},{64,0},{1,65},{65,1},{2,66},{66,2},{3,67},{67,3},{4,68},{68... | collective-permute-start | bytes 442376 | tf_op jit(solution)/shard_map/ppermute | solution.py:197
  230.5 4.0 %copy-start = (bf16[384,2,8,320]{0,3,2,1:T(8,128)(2,1)S(1)}, bf16[384,2,8,320]{0,3,2,1:T(8,128)(2,1)}, u32[]{:S(2)}) copy-start(bf16[384,2,8,320]{0,3,2,1:T(8,128)(2,1)} %copy.63) | copy-start | bytes 11796484
  238.9 35.9 %copy-start.7 = (f32[192,640]{1,0:T(8,128)S(1)}, f32[192,640]{1,0:T(8,128)}, u32[]{:S(2)}) copy-start(f32[192,640]{1,0:T(8,128)} %convert_add_fusion) | copy-start | bytes 1474564
  238.9 35.6 %all-to-all-start.1 = ((bf16[8,192,640]{2,1,0:T(8,128)(2,1)}), bf16[8,192,640]{2,1,0:T(8,128)(2,1)S(1)}, u32[]{:S(2)}, u32[]{:S(2)}) async-start(bf16[8,192,640]{2,1,0:T(8,128)(2,1)} %fusion.10), calls=%async_computation.1 | async-start | bytes 3932160 | tf_op jit(solution)/shard_map/all_to_all | solution.py:216

commit v16 on v9

--- a/solution.py
+++ b/solution.py
@@ -73,17 +73,12 @@
     head_count = inner_width // HEAD_DIM
 
     sent_rows = lax.dynamic_slice_in_dim(states, (1 - cfg) * half_rows, half_rows, 0)
-    other_rows = lax.ppermute(sent_rows, "cfg", SWAP)
     mine_rows = lax.dynamic_slice_in_dim(states, cfg * half_rows, half_rows, 0)
     is_cond = cfg == 0
-    cond_rows = jnp.where(is_cond, mine_rows, other_rows).astype(jnp.float32)
-    uncond_rows = jnp.where(is_cond, other_rows, mine_rows).astype(jnp.float32)
     scale = guidance[0]
-    hidden_part = uncond_rows + scale * (cond_rows - uncond_rows)
 
     spread = jnp.broadcast_to(states[None], (n_blk,) + states.shape)
     full_states = lax.all_to_all(spread, BLK, 0, 0, tiled=False)
-    full_states, hidden_part = lax.optimization_barrier((full_states, hidden_part))
     inputs = full_states.astype(jnp.float32)
     row_mean = jnp.mean(inputs, (0, 2), keepdims=True)
     centered = inputs - row_mean
@@ -113,6 +108,11 @@
         preferred_element_type=jnp.float32,
     )
     mixed = with_layout_constraint(mixed, Layout((0, 1, 2)))
+    mixed, sent_rows = lax.optimization_barrier((mixed, sent_rows))
+    other_rows = lax.ppermute(sent_rows, "cfg", SWAP)
+    cond_rows = jnp.where(is_cond, mine_rows, other_rows).astype(jnp.float32)
+    uncond_rows = jnp.where(is_cond, other_rows, mine_rows).astype(jnp.float32)
+    hidden_part = uncond_rows + scale * (cond_rows - uncond_rows)
     mixed = mixed.reshape(tok_count, 3, head_count, HEAD_DIM)
 
     angle_table = jnp.asarray(rotary_angles(HEAD_DIM))
@@ -138,6 +138,7 @@
     kv_mine = jnp.concatenate([kv, from_behind, from_far, from_ahead], axis=0)
     kv_other = lax.ppermute(kv_mine, "core", SWAP)
     kv_all = jnp.concatenate([kv_mine, kv_other], axis=0)
+    kv_all, hidden_part = lax.optimization_barrier((kv_all, hidden_part))
     key_piece = kv_all[:, 0]
     value_piece = kv_all[:, 1]
     row_count = key_piece.shape[0]

time: 218 us -> 242 us (1.11)
  local copies, waits for them, and re-layouts: 7.06 us -> 17.3 us
  waiting for transfers between devices: 120 us -> 128 us
  matrix products: 29.4 us -> 33.6 us
    all_to_all x1, waiting for transfers between devices: 0.01 us -> 43.7 us  [local(): full_states = lax.all_to_all(spread, BLK, 0, 0, tiled=False)]
    ppermute x1, waiting for transfers between devices: 44.4 us -> 5.35 us  [local(): other_rows = lax.ppermute(sent_rows, 'cfg', SWAP)]
    all_gather x1, waiting for transfers between devices: 0.02 us -> 12.3 us  [local(): lax.all_gather(out_projection, ('cfg',) + SEQ, axis=1, tiled=True)]
    ppermute x1, waiting for transfers between devices: 20.5 us -> 12.9 us  [local(): lax.ppermute(kv, 'x', [(i, (i + 1) % n_x) for i in range(n_x)])]
    concatenate x2 -> x1, local copies, waits for them, and re-layouts: 0.32 us -> 3.7 us  [local(): kv_all = jnp.concatenate([kv_mine, kv_other], axis=0)]
    dot_general x12, matrix products: 6.57 us -> 9.77 us  [attend(): jnp.einsum('qhd,khd->hqk', query_rows, key_slab, preferred_element_type=j...]
  transfers between devices with their start and end apart: 11 -> 11, of which waited for: 7 -> 7; matrix products, arithmetic and copies ran while one was open for 20% -> 17% of each run, Pallas kernels for 0% -> 0%
where the time goes in v16:
time: 242 us; the launch traced here: 241 us
  waiting for transfers between devices  128 us (53%)
  matrix products  33.6 us (14%)
  starting transfers between devices  23.3 us (10%)
  other arithmetic  22.4 us (9%)
  local copies, waits for them, and re-layouts  17.3 us (7%)
  between operations  15.9 us (7%)
    all_to_all x1, waiting for transfers between devices, local(): full_states = lax.all_to_all(spread, BLK, 0, 0, tiled=False)  43.7 us
    all_to_all x1, waiting for transfers between devices, local(): lax.all_to_all(partial, BLK, 0, 0, tiled=False).astype(jnp.float32)  27.4 us
    ppermute x1, waiting for transfers between devices, local(): shard_other = lax.ppermute(in_projection, 'cfg', SWAP)  16.7 us
    ppermute x1, waiting for transfers between devices, local(): lax.ppermute(kv, 'x', [(i, (i + 1) % n_x) for i in range(n_x)])  12.9 us
    all_gather x1, waiting for transfers between devices, local(): lax.all_gather(out_projection, ('cfg',) + SEQ, axis=1, tiled=True)  12.3 us
    dot_general x1, matrix products, local(): jnp.einsum('tabi,abiqe->tqe', mod_perm, piece, preferred_element_type=jnp...  10 us
    dot_general x12, matrix products, attend(): jnp.einsum('qhd,khd->hqk', query_rows, key_slab, preferred_element_type=j...  9.77 us
    ppermute x1, waiting for transfers between devices, local(): from_far = lax.ppermute(relayed, SEQ, relay_pairs)  9.61 us
  transfers between devices with their start and end apart: 11, of which 7 were waited for; matrix products, arithmetic and copies ran while one was open for 17% of the time, Pallas kernels for 0%

profile of v16, /device:TPU:0, one launch (start us, length us, event | category | flops | bytes accessed | tf_op | source)
XLA Modules:
  0.0 240.6 jit_solution(3283192047246278729)
XLA Ops:
  7.4 2.0 collective-permute-start
  9.4 16.7 %collective-permute-done = bf16[320,3,384]{2,0,1:T(8,128)(2,1)S(1)} collective-permute-done((bf16[320,3,384]{2,0,1:T(8,128)(2,1)}, bf16[320,3,384]{2,0,1:T(8,128)(2,1)S(1)}, u32[]{:S(2)}, u32[]{:S(2)}) %collective-permute-start) | collective-permute-done | bytes 737312 | tf_op jit(solution)/shard_map/ppermute | solution.py:91
  26.1 1.3 select_bitcast_fusion.1
  27.4 1.3 pad_maximum_fusion.1
  29.0 2.2 broadcast_in_dim.143
  31.2 7.7 %all-to-all-start = ((bf16[8,384,640]{1,2,0:T(8,128)(2,1)}), bf16[8,384,640]{1,2,0:T(8,128)(2,1)}, u32[]{:S(2)}, u32[]{:S(2)}) async-start(bf16[8,384,640]{1,2,0:T(8,128)(2,1)} %broadcast_in_dim.143), calls=%async_computation | async-start | bytes 7864320 | tf_op jit(solution)/shard_map/all_to_all | solution.py:81
  39.2 1.1 cosine_bitcast_fusion
  40.2 0.8 copy.62
  41.1 0.8 copy.61
  41.9 0.7 dynamic-slice_bitcast_fusion
  42.6 43.7 %all-to-all-done = bf16[8,384,640]{1,2,0:T(8,128)(2,1)} async-done(((bf16[8,384,640]{1,2,0:T(8,128)(2,1)}), bf16[8,384,640]{1,2,0:T(8,128)(2,1)}, u32[]{:S(2)}, u32[]{:S(2)}) %all-to-all-start) | async-done | bytes 3932192 | tf_op jit(solution)/shard_map/all_to_all | solution.py:81
  86.3 2.8 %convert_reduce_fusion = f32[384]{0:T(512)S(1)} fusion(bf16[8,384,640]{1,2,0:T(8,128)(2,1)} %all-to-all-done), kind=kLoop, calls=%fused_computation.3 | loop fusion | flops 3931776 | bytes 3933696 | tf_op jit(solution)/shard_map/reduce_sum | solution.py:83
  89.1 3.3 %fusion.4 = f32[384]{0:T(512)S(1)} fusion(bf16[8,384,640]{1,2,0:T(8,128)(2,1)} %all-to-all-done, f32[384]{0:T(512)S(1)} %broadcast_multiply_fusion), kind=kLoop, calls=%fused_computation.6 | loop fusion | flops 7863936 | bytes 3935232 | tf_op jit(solution)/shard_map/reduce_sum | solution.py:85
  92.5 5.8 %fusion.7 = bf16[8,384,640]{1,2,0:T(8,128)(2,1)} fusion(bf16[8,384,640]{1,2,0:T(8,128)(2,1)} %all-to-all-done, f32[8,640]{1,0:T(8,128)S(1)} %add.246, f32[8,640]{1,0:T(8,128)S(1)} %add.245, f32[384]{0:T(512)S(1)} %add_rsqrt_fusion.2, f32[384]{0:T(512)S(1)} %broadcast_multiply_fusion), kind=kLoop, calls=%fused_computation.9 | loop fusion | flops 11796480 | bytes 7908352 | tf_op jit(solution)/shard_map/convert_element_type | solution.py:89
  98.3 10.0 %fusion.11 = f32[384,3,384]{2,0,1:T(8,128)S(1)} fusion(bf16[384,8,2,320,1]{0,3,1,4,2:T(8,128)(2,1)} %bitcast.220, bf16[8,2,320,3,384]{4,2,3,1,0:T(8,128)(2,1)} %bitcast.225), kind=kOutput, calls=%fused_computation.16 | convolution fusion | flops 4529848320 | bytes 17498112 | tf_op jit(solution)/shard_map/tabi,abiqe->tqe/dot_general | solution.py:104
  108.3 1.2 copy.58
  109.6 2.4 copy.59
  111.9 1.1 slice.178
  113.1 1.3 fusion.169
  115.2 0.7 fusion.46
  115.9 1.0 pad_maximum_fusion.2
  116.9 1.4 collective-permute-start.1
  118.3 1.8 collective-permute-start.2
  120.1 12.9 %collective-permute-done.1 = bf16[384,2,3,128]{3,0,2,1:T(8,128)(2,1)S(1)} collective-permute-done((bf16[384,2,3,128]{3,0,2,1:T(8,128)(2,1)S(1)}, bf16[384,2,3,128]{3,0,2,1:T(8,128)(2,1)S(1)}, u32[]{:S(2)}, u32[]{:S(2)}) %collective-permute-start.1) | collective-permute-done | bytes 589856 | tf_op jit(solution)/shard_map/ppermute | solution.py:132
  133.0 1.1 broadcast_select_fusion
  134.1 1.5 collective-permute-start.3
  135.6 9.6 %collective-permute-done.3 = bf16[384,2,3,128]{3,0,2,1:T(8,128)(2,1)S(1)} collective-permute-done((bf16[384,2,3,128]{3,0,2,1:T(8,128)(2,1)S(1)}, bf16[384,2,3,128]{3,0,2,1:T(8,128)(2,1)S(1)}, u32[]{:S(2)}, u32[]{:S(2)}) %collective-permute-start.3) | collective-permute-done | bytes 589856 | tf_op jit(solution)/shard_map/ppermute | solution.py:137
  145.2 1.8 pad_maximum_fusion
  148.2 1.6 broadcast_compare_fusion.10
  149.8 1.0 collective-permute-start.5
  151.3 1.7 fusion.41
  153.0 5.3 %collective-permute-done.5 = bf16[192,640]{1,0:T(8,128)(2,1)S(1)} collective-permute-done((bf16[192,640]{1,0:T(8,128)(2,1)}, bf16[192,640]{1,0:T(8,128)(2,1)S(1)}, u32[]{:S(2)}, u32[]{:S(2)}) %collective-permute-start.5) | collective-permute-done | bytes 245792 | tf_op jit(solution)/shard_map/ppermute | solution.py:112
  158.5 0.9 constant_dynamic-update-slice_fusion.2
  159.4 0.9 constant_dynamic-update-slice_fusion.1
  160.4 3.7 %constant_dynamic-update-slice_fusion = bf16[3072,2,3,128]{3,0,2,1:T(8,128)(2,1)} fusion(bf16[3072,2,3,128]{3,0,2,1:T(8,128)(2,1)} %constant_dynamic-update-slice_fusion.1, bf16[1536,2,3,128]{3,0,2,1:T(8,128)(2,1)} %collective-permute-done.4), kind=kLoop, calls=%fused_computation.226 | loop fusion | bytes 4718592 | tf_op jit(solution)/shard_map/concatenate | solution.py:140
  164.1 1.7 fusion.176
  165.8 1.6 fusion.177
  167.4 1.6 fusion.175
  169.6 0.5 fusion.173
  170.1 0.5 fusion.172
  172.6 1.2 collective-permute-start.6
  176.0 0.5 fusion.179
  179.0 12.3 %all-gather.4.cloned.1.call-done = bf16[384,5120]{0,1:T(8,128)(2,1)} async-done(((bf16[384,320]{0,1:T(8,128)(2,1)}), bf16[384,5120]{0,1:T(8,128)(2,1)}) %all-gather.4.cloned.1.call-update) | async-done | bytes 3932176 | tf_op jit(solution)/shard_map/all_gather | solution.py:191
  191.3 3.8 %fusion.119 = f32[192,8,640]{2,0,1:T(8,128)S(1)} fusion(bf16[384,8,640]{0,2,1:T(8,128)(2,1)} %bitcast.216, bf16[192,384]{1,0:T(8,128)(2,1)S(1)} %collective-permute-done.6, pred[]{:T(512)S(6)} %eq.182, bf16[3,24,8,128]{3,2,1,0:T(8,128)(2,1)S(1)} %fusion.50), kind=kOutput, calls=%fused_computation.177 | convolution fusion | flops 755048448 | bytes 8159233 | tf_op jit(solution)/shard_map/te,ebn->btn/dot_general | solution.py:195
  195.1 2.9 %fusion.10 = bf16[8,192,640]{2,1,0:T(8,128)(2,1)} fusion(f32[192,8,640]{2,0,1:T(8,128)S(1)} %fusion.119, bf16[384,8,640]{0,2,1:T(8,128)(2,1)S(1)} %bitcast.217, f32[]{:T(128)} %bitcast.215, bf16[192,384]{1,0:T(8,128)(2,1)S(1)} %collective-permute-done.6, pred[]{:T(512)S(6)} %eq.182, bf16[3,24,8,128]{3,2,1,0:T(8,128)(2,1)S(1)} %fusion.50), kind=kOutput, calls=%fused_computation.13 | convolution fusion | flops 758980608 | bytes 10125317 | tf_op jit(solution)/shard_map/te,ebn->btn/dot_general | solution.py:194
  198.0 6.5 %all-to-all-start.1 = ((bf16[8,192,640]{2,1,0:T(8,128)(2,1)}), bf16[8,192,640]{2,1,0:T(8,128)(2,1)S(1)}, u32[]{:S(2)}, u32[]{:S(2)}) async-start(bf16[8,192,640]{2,1,0:T(8,128)(2,1)} %fusion.10), calls=%async_computation.1 | async-start | bytes 3932160 | tf_op jit(solution)/shard_map/all_to_all | solution.py:197
  204.6 27.4 %all-to-all-done.1 = bf16[8,192,640]{2,1,0:T(8,128)(2,1)S(1)} async-done(((bf16[8,192,640]{2,1,0:T(8,128)(2,1)}), bf16[8,192,640]{2,1,0:T(8,128)(2,1)S(1)}, u32[]{:S(2)}, u32[]{:S(2)}) %all-to-all-start.1) | async-done | bytes 1966112 | tf_op jit(solution)/shard_map/all_to_all | solution.py:197
  232.3 0.9 add_bitcast_fusion
  (97 shorter events, 9.7 us)
Async XLA Ops:
  7.4 21.3 %copy-start.2 = (bf16[1,384,640]{2,1,0:T(8,128)(2,1)S(1)}, bf16[1,384,640]{2,1,0:T(8,128)(2,1)}, u32[]{:S(2)}) copy-start(bf16[1,384,640]{2,1,0:T(8,128)(2,1)} %param.9) | copy-start | bytes 1474564
  7.4 90.9 %all-gather.6.cloned.1.call-start = ((), (), s32[]{:S(2)}) async-start(), calls=%async_computation.3 | async-start | bytes 13271040 | tf_op jit(solution)/shard_map/all_gather | solution.py:98
  7.4 18.7 %collective-permute-start = (bf16[320,3,384]{2,0,1:T(8,128)(2,1)}, bf16[320,3,384]{2,0,1:T(8,128)(2,1)S(1)}, u32[]{:S(2)}, u32[]{:S(2)}) collective-permute-start(bf16[320,3,384]{2,0,1:T(8,128)(2,1)} %param.11), channel_id=1, source_target_pairs={{0,64},{64,0},{1,65},{65,1},{2,66},{66,2},{3,67},{67,3},{4,68},{68... | collective-permute-start | bytes 2211848 | tf_op jit(solution)/shard_map/ppermute | solution.py:91
  31.2 7.8 %copy-start.18 = (f32[3,5120]{1,0:T(4,128)S(1)}, f32[3,5120]{1,0:T(4,128)}, u32[]{:S(2)}) copy-start(f32[3,5120]{1,0:T(4,128)} %param.10) | copy-start | bytes 184324
  31.2 8.0 %copy-start.19 = (s32[3,384]{1,0:T(4,128)S(1)}, s32[3,384]{1,0:T(4,128)}, u32[]{:S(2)}) copy-start(s32[3,384]{1,0:T(4,128)} %param.14) | copy-start | bytes 13828
  31.2 8.0 %copy-start.20 = (f32[3,128]{1,0:T(4,128)S(1)}, f32[3,128]{1,0:T(4,128)}, u32[]{:S(2)}) copy-start(f32[3,128]{1,0:T(4,128)} %constant.96.clone) | copy-start | bytes 4612
  31.2 55.1 %all-to-all-start = ((bf16[8,384,640]{1,2,0:T(8,128)(2,1)}), bf16[8,384,640]{1,2,0:T(8,128)(2,1)}, u32[]{:S(2)}, u32[]{:S(2)}) async-start(bf16[8,384,640]{1,2,0:T(8,128)(2,1)} %broadcast_in_dim.143), calls=%async_computation | async-start | bytes 7864320 | tf_op jit(solution)/shard_map/all_to_all | solution.py:81
  38.9 152.4 %all-gather.4.cloned.1.call-start = ((), (), s32[]{:S(2)}) async-start(), calls=%async_computation.2 | async-start | bytes 4177920 | tf_op jit(solution)/shard_map/all_gather | solution.py:191
  109.5 5.6 %copy-start.5 = (f32[128,128,1]{1,0,2:T(8,128)S(1)}, f32[128,128,1]{1,0,2:T(8,128)}, u32[]{:S(2)}) copy-start(f32[128,128,1]{1,0,2:T(8,128)} %constant.99) | copy-start | bytes 196612
  111.9 3.2 %copy-start.3 = (f32[384,128]{1,0:T(8,128)S(1)}, f32[384,128]{1,0:T(8,128)}, u32[]{:S(2)}) copy-start(f32[384,128]{1,0:T(8,128)} %copy.62) | copy-start | bytes 589828
  111.9 3.2 %copy-start.4 = (f32[384,128]{1,0:T(8,128)S(1)}, f32[384,128]{1,0:T(8,128)}, u32[]{:S(2)}) copy-start(f32[384,128]{1,0:T(8,128)} %copy.61) | copy-start | bytes 589828
  116.9 30.8 %copy-start.21 = (s32[5]{0:T(128)S(1)}, s32[5]{0:T(128)}, u32[]{:S(2)}) copy-start(s32[5]{0:T(128)} %param.13) | copy-start | bytes 64
  116.9 16.2 %collective-permute-start.1 = (bf16[384,2,3,128]{3,0,2,1:T(8,128)(2,1)S(1)}, bf16[384,2,3,128]{3,0,2,1:T(8,128)(2,1)S(1)}, u32[]{:S(2)}, u32[]{:S(2)}) collective-permute-start(bf16[384,2,3,128]{3,0,2,1:T(8,128)(2,1)S(1)} %get-tuple-element.21), channel_id=1, source_target_pairs={{0,16},{16,32},{32,48},{48,0},{1,17},{17,33},{33,49},{49,1},{2,18}... | collective-permute-start | bytes 1769480 | tf_op jit(solution)/shard_map/ppermute | solution.py:132
  118.3 14.7 %collective-permute-start.2 = (bf16[384,2,3,128]{3,0,2,1:T(8,128)(2,1)S(1)}, bf16[384,2,3,128]{3,0,2,1:T(8,128)(2,1)S(1)}, u32[]{:S(2)}, u32[]{:S(2)}) collective-permute-start(bf16[384,2,3,128]{3,0,2,1:T(8,128)(2,1)S(1)} %get-tuple-element.21), channel_id=1, source_target_pairs={{0,48},{16,0},{32,16},{48,32},{1,49},{17,1},{33,17},{49,33},{2,50}... | collective-permute-start | bytes 1769480 | tf_op jit(solution)/shard_map/ppermute | solution.py:133
  134.1 11.1 %collective-permute-start.3 = (bf16[384,2,3,128]{3,0,2,1:T(8,128)(2,1)S(1)}, bf16[384,2,3,128]{3,0,2,1:T(8,128)(2,1)S(1)}, u32[]{:S(2)}, u32[]{:S(2)}) collective-permute-start(bf16[384,2,3,128]{3,0,2,1:T(8,128)(2,1)S(1)} %get-tuple-element.19), channel_id=1, source_target_pairs={{0,16},{16,32},{32,48},{48,0},{8,56},{24,8},{40,24},{56,40},{1,17}... | collective-permute-start | bytes 1769480 | tf_op jit(solution)/shard_map/ppermute | solution.py:137
  147.0 13.3 %collective-permute-start.4 = (bf16[1536,2,3,128]{3,0,2,1:T(8,128)(2,1)}, bf16[1536,2,3,128]{3,0,2,1:T(8,128)(2,1)}, u32[]{:S(2)}, u32[]{:S(2)}) collective-permute-start(bf16[1536,2,3,128]{3,0,2,1:T(8,128)(2,1)} %pad_maximum_fusion), channel_id=1, source_target_pairs={{0,8},{8,0},{1,9},{9,1},{2,10},{10,2},{3,11},{11,3},{4,12},{12,4},... | collective-permute-start | bytes 7077896 | tf_op jit(solution)/shard_map/ppermute | solution.py:139
  149.8 8.6 %collective-permute-start.5 = (bf16[192,640]{1,0:T(8,128)(2,1)}, bf16[192,640]{1,0:T(8,128)(2,1)S(1)}, u32[]{:S(2)}, u32[]{:S(2)}) collective-permute-start(bf16[192,640]{1,0:T(8,128)(2,1)} %dynamic-slice_bitcast_fusion), channel_id=1, source_target_pairs={{0,64},{64,0},{1,65},{65,1},{2,66},{66,2},{3,67},{67,3},{4,68},{68... | collective-permute-start | bytes 737288 | tf_op jit(solution)/shard_map/ppermute | solution.py:112
  158.4 5.7 %copy-start.17 = (pred[192,512]{1,0:T(8,128)(4,1)S(1)}, pred[192,512]{1,0:T(8,128)(4,1)}, u32[]{:S(2)}) copy-start(pred[192,512]{1,0:T(8,128)(4,1)} %get-tuple-element.63) | copy-start | bytes 294916
  159.4 6.3 %copy-start.16 = (pred[192,512]{1,0:T(8,128)(4,1)S(1)}, pred[192,512]{1,0:T(8,128)(4,1)}, u32[]{:S(2)}) copy-start(pred[192,512]{1,0:T(8,128)(4,1)} %get-tuple-element.72) | copy-start | bytes 294916
  160.4 7.0 %copy-start.15 = (pred[192,512]{1,0:T(8,128)(4,1)S(1)}, pred[192,512]{1,0:T(8,128)(4,1)}, u32[]{:S(2)}) copy-start(pred[192,512]{1,0:T(8,128)(4,1)} %get-tuple-element.65) | copy-start | bytes 294916
  164.1 4.9 %copy-start.1 = (bf16[3072,2,3,128]{3,0,2,1:T(8,128)(2,1)S(1)}, bf16[3072,2,3,128]{3,0,2,1:T(8,128)(2,1)}, u32[]{:S(2)}) copy-start(bf16[3072,2,3,128]{3,0,2,1:T(8,128)(2,1)} %constant_dynamic-update-slice_fusion) | copy-start | bytes 14155780
  164.1 4.9 %copy-start.14 = (pred[192,512]{1,0:T(8,128)(4,1)S(1)}, pred[192,512]{1,0:T(8,128)(4,1)}, u32[]{:S(2)}) copy-start(pred[192,512]{1,0:T(8,128)(4,1)} %get-tuple-element.70) | copy-start | bytes 294916
  165.8 3.8 %copy-start.13 = (pred[192,512]{1,0:T(8,128)(4,1)S(1)}, pred[192,512]{1,0:T(8,128)(4,1)}, u32[]{:S(2)}) copy-start(pred[192,512]{1,0:T(8,128)(4,1)} %get-tuple-element.67) | copy-start | bytes 294916
  167.4 2.7 %copy-start.12 = (pred[192,512]{1,0:T(8,128)(4,1)S(1)}, pred[192,512]{1,0:T(8,128)(4,1)}, u32[]{:S(2)}) copy-start(pred[192,512]{1,0:T(8,128)(4,1)} %get-tuple-element.68) | copy-start | bytes 294916
  171.3 2.5 %copy-start.11 = (pred[192,512]{1,0:T(8,128)(4,1)S(1)}, pred[192,512]{1,0:T(8,128)(4,1)}, u32[]{:S(2)}) copy-start(pred[192,512]{1,0:T(8,128)(4,1)} %get-tuple-element.62) | copy-start | bytes 294916
  171.6 2.7 %copy-start.10 = (pred[192,512]{1,0:T(8,128)(4,1)S(1)}, pred[192,512]{1,0:T(8,128)(4,1)}, u32[]{:S(2)}) copy-start(pred[192,512]{1,0:T(8,128)(4,1)} %get-tuple-element.73) | copy-start | bytes 294916
  171.9 3.0 %copy-start.9 = (pred[192,512]{1,0:T(8,128)(4,1)S(1)}, pred[192,512]{1,0:T(8,128)(4,1)}, u32[]{:S(2)}) copy-start(pred[192,512]{1,0:T(8,128)(4,1)} %get-tuple-element.64) | copy-start | bytes 294916
  172.6 2.9 %copy-start.8 = (pred[192,512]{1,0:T(8,128)(4,1)S(1)}, pred[192,512]{1,0:T(8,128)(4,1)}, u32[]{:S(2)}) copy-start(pred[192,512]{1,0:T(8,128)(4,1)} %get-tuple-element.71) | copy-start | bytes 294916
  172.6 18.7 %collective-permute-start.6 = (bf16[192,384]{1,0:T(8,128)(2,1)S(1)}, bf16[192,384]{1,0:T(8,128)(2,1)S(1)}, u32[]{:S(2)}, u32[]{:S(2)}) collective-permute-start(bf16[192,384]{1,0:T(8,128)(2,1)S(1)} %bitcast.222), channel_id=1, source_target_pairs={{0,64},{64,0},{1,65},{65,1},{2,66},{66,2},{3,67},{67,3},{4,68},{68... | collective-permute-start | bytes 442376 | tf_op jit(solution)/shard_map/ppermute | solution.py:187
  174.3 1.7 copy-start.7
  174.9 1.7 copy-start.6
  191.3 3.8 %copy-start = (bf16[384,5120]{0,1:T(8,128)(2,1)S(1)}, bf16[384,5120]{0,1:T(8,128)(2,1)}, u32[]{:S(2)}) copy-start(bf16[384,5120]{0,1:T(8,128)(2,1)} %all-gather.4.cloned.1.call-done) | copy-start | bytes 11796484
  198.0 34.0 %all-to-all-start.1 = ((bf16[8,192,640]{2,1,0:T(8,128)(2,1)}), bf16[8,192,640]{2,1,0:T(8,128)(2,1)S(1)}, u32[]{:S(2)}, u32[]{:S(2)}) async-start(bf16[8,192,640]{2,1,0:T(8,128)(2,1)} %fusion.10), calls=%async_computation.1 | async-start | bytes 3932160 | tf_op jit(solution)/shard_map/all_to_all | solution.py:197
Sparse Core Ops, SparseCore 0:
  28.8 66.1 all-gather.5
Sparse Core Ops, SparseCore 1:
  147.1 44.1 all-gather.3

commit v17 on v9

--- a/solution.py
+++ b/solution.py
@@ -85,10 +85,14 @@
     full_states = lax.all_to_all(spread, BLK, 0, 0, tiled=False)
     full_states, hidden_part = lax.optimization_barrier((full_states, hidden_part))
     inputs = full_states.astype(jnp.float32)
-    row_mean = jnp.mean(inputs, (0, 2), keepdims=True)
-    centered = inputs - row_mean
-    variance = jnp.mean(centered * centered, (0, 2), keepdims=True)
-    normed = centered * lax.rsqrt(variance + 1e-06)
+    block_mean = jnp.mean(inputs, 2, keepdims=True)
+    block_dev = inputs - block_mean
+    block_m2 = jnp.sum(block_dev * block_dev, 2, keepdims=True)
+    row_mean = jnp.mean(block_mean, 0, keepdims=True)
+    shift = block_mean - row_mean
+    total_m2 = jnp.sum(block_m2, 0, keepdims=True) + feat_width * jnp.sum(shift * shift, 0, keepdims=True)
+    variance = total_m2 / (n_blk * feat_width)
+    normed = (inputs - row_mean) * lax.rsqrt(variance + 1e-06)
     mod_shift = modulation[0].reshape(n_blk, 1, feat_width)
     mod_scale = modulation[1].reshape(n_blk, 1, feat_width)
     modulated = (normed * (1.0 + mod_scale) + mod_shift).astype(jnp.bfloat16)

time: 218 us -> 218 us (level)
    reduce_sum x2 -> x4, other arithmetic: 6.05 us -> 5.92 us  [the longest x1 3.24 us: local(): jnp.sum(block_m2, 0, keepdims=True)]
where the time goes in v17:
time: 218 us; the launch traced here: 217 us
  waiting for transfers between devices  121 us (56%)
  matrix products  29.4 us (13%)
  starting transfers between devices  25 us (11%)
  other arithmetic  19.9 us (9%)
  between operations  14.6 us (7%)
  local copies, waits for them, and re-layouts  7.06 us (3%)
    ppermute x1, waiting for transfers between devices, local(): other_rows = lax.ppermute(sent_rows, 'cfg', SWAP)  44.4 us
    all_to_all x1, waiting for transfers between devices, local(): lax.all_to_all(partial, BLK, 0, 0, tiled=False).astype(jnp.float32)  26.8 us
    ppermute x1, waiting for transfers between devices, local(): lax.ppermute(kv, 'x', [(i, (i + 1) % n_x) for i in range(n_x)])  20.5 us
    ppermute x1, waiting for transfers between devices, local(): shard_other = lax.ppermute(in_projection, 'cfg', SWAP)  16.7 us
    dot_general x1, matrix products, local(): jnp.einsum('tabi,abiqe->tqe', mod_perm, piece, preferred_element_type=jnp...  10.1 us
    ppermute x1, waiting for transfers between devices, local(): from_far = lax.ppermute(relayed, SEQ, relay_pairs)  8.31 us
    all_to_all x1, starting transfers between devices, local(): full_states = lax.all_to_all(spread, BLK, 0, 0, tiled=False)  7.75 us
    all_to_all x1, starting transfers between devices, local(): lax.all_to_all(partial, BLK, 0, 0, tiled=False).astype(jnp.float32)  7.6 us
  transfers between devices with their start and end apart: 11, of which 7 were waited for; matrix products, arithmetic and copies ran while one was open for 20% of the time, Pallas kernels for 0%

profile of v17, /device:TPU:0, one launch (start us, length us, event | category | flops | bytes accessed | tf_op | source)
XLA Modules:
  0.0 216.7 jit_solution(6792471928728811473)
XLA Ops:
  6.5 2.0 collective-permute-start.1
  8.6 16.7 %collective-permute-done.1 = bf16[320,3,384]{2,0,1:T(8,128)(2,1)S(1)} collective-permute-done((bf16[320,3,384]{2,0,1:T(8,128)(2,1)}, bf16[320,3,384]{2,0,1:T(8,128)(2,1)S(1)}, u32[]{:S(2)}, u32[]{:S(2)}) %collective-permute-start.1) | collective-permute-done | bytes 737312 | tf_op jit(solution)/shard_map/ppermute | solution.py:100
  25.3 1.3 select_bitcast_fusion.1
  26.5 1.3 pad_maximum_fusion.1
  27.8 1.0 copy-done.1
  29.1 2.3 %broadcast_in_dim.146 = bf16[8,384,640]{1,2,0:T(8,128)(2,1)} broadcast(bf16[384,640]{0,1:T(8,128)(2,1)S(1)} %copy.56), dimensions={1,2} | broadcast | bytes 4423680 | tf_op jit(solution)/shard_map/broadcast_in_dim | solution.py:84
  31.4 7.8 %all-to-all-start = ((bf16[8,384,640]{1,2,0:T(8,128)(2,1)}), bf16[8,384,640]{1,2,0:T(8,128)(2,1)}, u32[]{:S(2)}, u32[]{:S(2)}) async-start(bf16[8,384,640]{1,2,0:T(8,128)(2,1)} %broadcast_in_dim.146), calls=%async_computation | async-start | bytes 7864320 | tf_op jit(solution)/shard_map/all_to_all | solution.py:85
  39.2 1.1 collective-permute-start
  40.8 1.1 cosine_bitcast_fusion
  42.9 44.4 %collective-permute-done = bf16[192,640]{1,0:T(8,128)(2,1)S(1)} collective-permute-done((bf16[192,640]{1,0:T(8,128)(2,1)S(1)}, bf16[192,640]{1,0:T(8,128)(2,1)S(1)}, u32[]{:S(2)}, u32[]{:S(2)}) %collective-permute-start) | collective-permute-done | bytes 245792 | tf_op jit(solution)/shard_map/ppermute | solution.py:76
  87.4 2.6 %convert_reduce_fusion = f32[8,384]{1,0:T(8,128)S(1)} fusion(bf16[8,384,640]{1,2,0:T(8,128)(2,1)} %all-to-all-done), kind=kLoop, calls=%fused_computation.4 | loop fusion | flops 3929088 | bytes 3944448 | tf_op jit(solution)/shard_map/reduce_sum | solution.py:88
  90.1 3.2 %fusion.7 = f32[384]{0:T(512)S(1)} fusion(bf16[8,384,640]{1,2,0:T(8,128)(2,1)} %all-to-all-done, f32[8,384]{1,0:T(8,128)S(1)} %get-tuple-element.29), kind=kLoop, calls=%fused_computation.10 | loop fusion | flops 7863936 | bytes 3945984 | tf_op jit(solution)/shard_map/reduce_sum | solution.py:93
  93.4 5.8 %fusion.5 = bf16[8,384,640]{1,2,0:T(8,128)(2,1)} fusion(bf16[8,384,640]{1,2,0:T(8,128)(2,1)} %all-to-all-done, f32[8,640]{1,0:T(8,128)S(1)} %add.260, f32[8,640]{1,0:T(8,128)S(1)} %add.259, f32[384]{0:T(512)S(1)} %add_rsqrt_fusion.2, f32[384]{0:T(512)S(1)} %broadcast_multiply_fusion.1), kind=kLoop, calls=%fused_computation.8 | loop fusion | flops 11796480 | bytes 7908352 | tf_op jit(solution)/shard_map/convert_element_type | solution.py:98
  99.2 10.1 %fusion = f32[384,3,384,1,1]{0,2,3,1,4:T(8,128)S(1)} fusion(bf16[384,8,2,320,1]{0,3,1,4,2:T(8,128)(2,1)} %bitcast.213, bf16[8,2,320,3,384]{4,2,3,1,0:T(8,128)(2,1)} %bitcast.220), kind=kOutput, calls=%fused_computation | convolution fusion | flops 4529848320 | bytes 17498112 | tf_op jit(solution)/shard_map/tabi,abiqe->tqe/dot_general | solution.py:113
  110.3 0.7 fusion.51
  111.0 0.9 pad_maximum_fusion.2
  111.8 1.6 collective-permute-start.2
  113.4 1.6 collective-permute-start.3
  115.2 1.5 broadcast_compare_fusion
  117.3 20.5 %collective-permute-done.2 = bf16[384,2,3,128]{3,0,2,1:T(8,128)(2,1)S(1)} collective-permute-done((bf16[384,2,3,128]{3,0,2,1:T(8,128)(2,1)}, bf16[384,2,3,128]{3,0,2,1:T(8,128)(2,1)S(1)}, u32[]{:S(2)}, u32[]{:S(2)}) %collective-permute-start.2) | collective-permute-done | bytes 589856 | tf_op jit(solution)/shard_map/ppermute | solution.py:136
  137.8 2.0 collective-permute-done.3
  140.1 1.8 collective-permute-start.4
  141.8 0.7 fusion.38
  142.6 0.6 fusion.153
  143.1 8.3 %collective-permute-done.4 = bf16[384,2,3,128]{3,0,2,1:T(8,128)(2,1)S(1)} collective-permute-done((bf16[384,2,3,128]{3,0,2,1:T(8,128)(2,1)S(1)}, bf16[384,2,3,128]{3,0,2,1:T(8,128)(2,1)S(1)}, u32[]{:S(2)}, u32[]{:S(2)}) %collective-permute-start.4) | collective-permute-done | bytes 589856 | tf_op jit(solution)/shard_map/ppermute | solution.py:141
  151.4 0.7 pad_maximum_fusion
  152.3 0.6 fusion.147
  153.2 0.5 copy-done.16
  153.7 0.5 fusion.154
  154.3 0.5 fusion.148
  154.8 0.3 copy-done.14
  155.2 0.5 fusion.152
  155.7 0.5 fusion.146
  157.8 0.5 fusion.145
  158.4 0.5 fusion.144
  159.2 0.5 fusion.143
  160.7 0.3 fusion.54
  161.1 1.4 collective-permute-start.6
  162.5 0.5 fusion.151
  163.1 0.6 fusion.150
  163.7 0.3 copy-done.7
  164.0 0.5 fusion.149
  165.8 1.8 collective-permute-done.6
  167.6 3.8 %fusion.85 = f32[192,8,640]{2,0,1:T(8,128)S(1)} fusion(bf16[384,8,640]{0,2,1:T(8,128)(2,1)} %bitcast.211, bf16[192,384]{1,0:T(8,128)(2,1)S(1)} %collective-permute-done.6, pred[]{:T(512)S(6)} %eq.182, bf16[3,24,8,128]{3,2,1,0:T(8,128)(2,1)S(1)} %fusion.55), kind=kOutput, calls=%fused_computation.151 | convolution fusion | flops 755048448 | bytes 8159233 | tf_op jit(solution)/shard_map/te,ebn->btn/dot_general | solution.py:198
  171.4 2.9 %fusion.10 = bf16[8,192,640]{2,1,0:T(8,128)(2,1)} fusion(f32[192,8,640]{2,0,1:T(8,128)S(1)} %fusion.85, bf16[384,8,640]{0,2,1:T(8,128)(2,1)S(1)} %bitcast.212, f32[]{:T(128)} %bitcast.210, bf16[192,384]{1,0:T(8,128)(2,1)S(1)} %collective-permute-done.6, pred[]{:T(512)S(6)} %eq.182, bf16[3,24,8,128]{3,2,1,0:T(8,128)(2,1)S(1)} %fusion.55), kind=kOutput, calls=%fused_computation.14 | convolution fusion | flops 758980608 | bytes 10125317 | tf_op jit(solution)/shard_map/te,ebn->btn/dot_general | solution.py:197
  174.3 7.6 %all-to-all-start.1 = ((bf16[8,192,640]{2,1,0:T(8,128)(2,1)}), bf16[8,192,640]{2,1,0:T(8,128)(2,1)S(1)}, u32[]{:S(2)}, u32[]{:S(2)}) async-start(bf16[8,192,640]{2,1,0:T(8,128)(2,1)} %fusion.10), calls=%async_computation.1 | async-start | bytes 3932160 | tf_op jit(solution)/shard_map/all_to_all | solution.py:200
  181.9 26.8 %all-to-all-done.1 = bf16[8,192,640]{2,1,0:T(8,128)(2,1)S(1)} async-done(((bf16[8,192,640]{2,1,0:T(8,128)(2,1)}), bf16[8,192,640]{2,1,0:T(8,128)(2,1)S(1)}, u32[]{:S(2)}, u32[]{:S(2)}) %all-to-all-start.1) | async-done | bytes 1966112 | tf_op jit(solution)/shard_map/all_to_all | solution.py:200
  209.0 0.9 add_bitcast_fusion
  (98 shorter events, 7.8 us)
Async XLA Ops:
  6.5 92.7 %all-gather.6.cloned.1.call-start = ((), (), s32[]{:S(2)}) async-start(), calls=%async_computation.3 | async-start | bytes 13271040 | tf_op jit(solution)/shard_map/all_gather | solution.py:107
  6.5 18.7 %collective-permute-start.1 = (bf16[320,3,384]{2,0,1:T(8,128)(2,1)}, bf16[320,3,384]{2,0,1:T(8,128)(2,1)S(1)}, u32[]{:S(2)}, u32[]{:S(2)}) collective-permute-start(bf16[320,3,384]{2,0,1:T(8,128)(2,1)} %param.11), channel_id=1, source_target_pairs={{0,64},{64,0},{1,65},{65,1},{2,66},{66,2},{3,67},{67,3},{4,68},{68... | collective-permute-start | bytes 2211848 | tf_op jit(solution)/shard_map/ppermute | solution.py:100
  27.8 1.0 copy-start.1
  31.4 9.0 %copy-start.22 = (s32[5]{0:T(128)S(1)}, s32[5]{0:T(128)}, u32[]{:S(2)}) copy-start(s32[5]{0:T(128)} %param.13) | copy-start | bytes 64
  31.4 9.3 %copy-start.19 = (f32[3,5120]{1,0:T(4,128)S(1)}, f32[3,5120]{1,0:T(4,128)}, u32[]{:S(2)}) copy-start(f32[3,5120]{1,0:T(4,128)} %param.10) | copy-start | bytes 184324
  31.4 9.4 %copy-start.20 = (s32[3,384]{1,0:T(4,128)S(1)}, s32[3,384]{1,0:T(4,128)}, u32[]{:S(2)}) copy-start(s32[3,384]{1,0:T(4,128)} %param.14) | copy-start | bytes 13828
  31.4 9.5 %copy-start.21 = (f32[3,128]{1,0:T(4,128)S(1)}, f32[3,128]{1,0:T(4,128)}, u32[]{:S(2)}) copy-start(f32[3,128]{1,0:T(4,128)} %constant.103.clone) | copy-start | bytes 4612
  31.4 56.1 %all-to-all-start = ((bf16[8,384,640]{1,2,0:T(8,128)(2,1)}), bf16[8,384,640]{1,2,0:T(8,128)(2,1)}, u32[]{:S(2)}, u32[]{:S(2)}) async-start(bf16[8,384,640]{1,2,0:T(8,128)(2,1)} %broadcast_in_dim.146), calls=%async_computation | async-start | bytes 7864320 | tf_op jit(solution)/shard_map/all_to_all | solution.py:85
  39.1 126.7 %all-gather.4.cloned.1.call-start = ((), (), s32[]{:S(2)}) async-start(), calls=%async_computation.2 | async-start | bytes 4177920 | tf_op jit(solution)/shard_map/all_gather | solution.py:194
  39.2 48.1 %collective-permute-start = (bf16[192,640]{1,0:T(8,128)(2,1)S(1)}, bf16[192,640]{1,0:T(8,128)(2,1)S(1)}, u32[]{:S(2)}, u32[]{:S(2)}) collective-permute-start(bf16[192,640]{1,0:T(8,128)(2,1)S(1)} %dynamic-slice_bitcast_fusion), channel_id=1, source_target_pairs={{0,64},{64,0},{1,65},{65,1},{2,66},{66,2},{3,67},{67,3},{4,68},{68... | collective-permute-start | bytes 737288 | tf_op jit(solution)/shard_map/ppermute | solution.py:76
  42.8 67.4 %copy-start.2 = (f32[384,128]{1,0:T(8,128)}, f32[384,128]{1,0:T(8,128)S(1)}, u32[]{:S(2)}) copy-start(f32[384,128]{1,0:T(8,128)S(1)} %copy.61) | copy-start | bytes 589828
  42.9 67.3 %copy-start.4 = (f32[384,128]{1,0:T(8,128)}, f32[384,128]{1,0:T(8,128)S(1)}, u32[]{:S(2)}) copy-start(f32[384,128]{1,0:T(8,128)S(1)} %copy.62) | copy-start | bytes 589828
  109.4 0.8 copy-start.6
  111.8 25.9 %collective-permute-start.2 = (bf16[384,2,3,128]{3,0,2,1:T(8,128)(2,1)}, bf16[384,2,3,128]{3,0,2,1:T(8,128)(2,1)S(1)}, u32[]{:S(2)}, u32[]{:S(2)}) collective-permute-start(bf16[384,2,3,128]{3,0,2,1:T(8,128)(2,1)} %pad_maximum_fusion.2), channel_id=1, source_target_pairs={{0,16},{16,32},{32,48},{48,0},{1,17},{17,33},{33,49},{49,1},{2,18}... | collective-permute-start | bytes 1769480 | tf_op jit(solution)/shard_map/ppermute | solution.py:136
  113.4 26.4 %collective-permute-start.3 = (bf16[384,2,3,128]{3,0,2,1:T(8,128)(2,1)}, bf16[384,2,3,128]{3,0,2,1:T(8,128)(2,1)S(1)}, u32[]{:S(2)}, u32[]{:S(2)}) collective-permute-start(bf16[384,2,3,128]{3,0,2,1:T(8,128)(2,1)} %pad_maximum_fusion.2), channel_id=1, source_target_pairs={{0,48},{16,0},{32,16},{48,32},{1,49},{17,1},{33,17},{49,33},{2,50}... | collective-permute-start | bytes 1769480 | tf_op jit(solution)/shard_map/ppermute | solution.py:137
  117.3 24.6 %copy-start.3 = (f32[384,128]{1,0:T(8,128)S(1)}, f32[384,128]{1,0:T(8,128)}, u32[]{:S(2)}) copy-start(f32[384,128]{1,0:T(8,128)} %copy-done.2) | copy-start | bytes 589828
  117.3 24.6 %copy-start.5 = (f32[384,128]{1,0:T(8,128)S(1)}, f32[384,128]{1,0:T(8,128)}, u32[]{:S(2)}) copy-start(f32[384,128]{1,0:T(8,128)} %copy-done.4) | copy-start | bytes 589828
  140.1 2.5 %copy-start.18 = (pred[192,512]{1,0:T(8,128)(4,1)S(1)}, pred[192,512]{1,0:T(8,128)(4,1)}, u32[]{:S(2)}) copy-start(pred[192,512]{1,0:T(8,128)(4,1)} %get-tuple-element.67) | copy-start | bytes 294916
  140.1 11.3 %collective-permute-start.4 = (bf16[384,2,3,128]{3,0,2,1:T(8,128)(2,1)S(1)}, bf16[384,2,3,128]{3,0,2,1:T(8,128)(2,1)S(1)}, u32[]{:S(2)}, u32[]{:S(2)}) collective-permute-start(bf16[384,2,3,128]{3,0,2,1:T(8,128)(2,1)S(1)} %get-tuple-element.18), channel_id=1, source_target_pairs={{0,16},{16,32},{32,48},{48,0},{8,56},{24,8},{40,24},{56,40},{1,17}... | collective-permute-start | bytes 1769480 | tf_op jit(solution)/shard_map/ppermute | solution.py:141
  143.1 9.2 %copy-start.17 = (pred[192,512]{1,0:T(8,128)(4,1)S(1)}, pred[192,512]{1,0:T(8,128)(4,1)}, u32[]{:S(2)}) copy-start(pred[192,512]{1,0:T(8,128)(4,1)} %get-tuple-element.66) | copy-start | bytes 294916
  152.2 5.4 %collective-permute-start.5 = (bf16[1536,2,3,128]{3,0,2,1:T(8,128)(2,1)S(1)}, bf16[1536,2,3,128]{3,0,2,1:T(8,128)(2,1)S(1)}, u32[]{:S(2)}, u32[]{:S(2)}) collective-permute-start(bf16[1536,2,3,128]{3,0,2,1:T(8,128)(2,1)S(1)} %pad_maximum_fusion), channel_id=1, source_target_pairs={{0,8},{8,0},{1,9},{9,1},{2,10},{10,2},{3,11},{11,3},{4,12},{12,4},... | collective-permute-start | bytes 7077896 | tf_op jit(solution)/shard_map/ppermute | solution.py:143
  152.8 0.9 copy-start.16
  153.2 1.1 copy-start.15
  154.3 0.9 copy-start.14
  154.8 0.9 copy-start.13
  156.9 0.9 copy-start.12
  157.5 0.9 copy-start.11
  158.3 0.9 copy-start.10
  160.7 1.8 copy-start.9
  161.1 2.0 copy-start.8
  161.1 6.5 %collective-permute-start.6 = (bf16[192,384]{1,0:T(8,128)(2,1)S(1)}, bf16[192,384]{1,0:T(8,128)(2,1)S(1)}, u32[]{:S(2)}, u32[]{:S(2)}) collective-permute-start(bf16[192,384]{1,0:T(8,128)(2,1)S(1)} %bitcast.217), channel_id=1, source_target_pairs={{0,64},{64,0},{1,65},{65,1},{2,66},{66,2},{3,67},{67,3},{4,68},{68... | collective-permute-start | bytes 442376 | tf_op jit(solution)/shard_map/ppermute | solution.py:190
  163.1 0.9 copy-start.7
  167.6 3.8 %copy-start = (bf16[384,5120]{0,1:T(8,128)(2,1)S(1)}, bf16[384,5120]{0,1:T(8,128)(2,1)}, u32[]{:S(2)}) copy-start(bf16[384,5120]{0,1:T(8,128)(2,1)} %all-gather.4.cloned.1.call-done) | copy-start | bytes 11796484
  174.3 34.4 %all-to-all-start.1 = ((bf16[8,192,640]{2,1,0:T(8,128)(2,1)}), bf16[8,192,640]{2,1,0:T(8,128)(2,1)S(1)}, u32[]{:S(2)}, u32[]{:S(2)}) async-start(bf16[8,192,640]{2,1,0:T(8,128)(2,1)} %fusion.10), calls=%async_computation.1 | async-start | bytes 3932160 | tf_op jit(solution)/shard_map/all_to_all | solution.py:200
Sparse Core Ops, SparseCore 0:
  27.9 66.1 all-gather.5
  95.8 45.1 all-gather.3

commit v18 on v9

--- a/solution.py
+++ b/solution.py
@@ -190,8 +190,10 @@
     out_piece = lax.all_gather(out_projection, ("cfg",) + SEQ, axis=1, tiled=True).reshape(
         inner_width, n_blk, feat_width
     )
-    cond_part = jnp.einsum("te,ebn->btn", cond_att, out_piece, preferred_element_type=jnp.float32)
-    uncond_part = jnp.einsum("te,ebn->btn", uncond_att, out_piece, preferred_element_type=jnp.float32)
+    both_part = jnp.einsum(
+        "cte,ebn->cbtn", jnp.stack([cond_att, uncond_att]), out_piece, preferred_element_type=jnp.float32
+    )
+    cond_part, uncond_part = both_part[0], both_part[1]
     partial = (uncond_part + scale * (cond_part - uncond_part)).astype(jnp.bfloat16)
     arrived = lax.all_to_all(partial, BLK, 0, 0, tiled=False).astype(jnp.float32)
     gate = lax.dynamic_slice_in_dim(modulation[2], blk * feat_width, feat_width, 0)

time: 218 us -> 218 us (level)
  matrix products: 29.4 us -> 27.1 us
    dot_general x2 -> x1, matrix products: 6.66 us -> 4.34 us  [local(): jnp.einsum('cte,ebn->cbtn', jnp.stack([cond_att, uncond_att]), out_piece,...]
where the time goes in v18:
time: 218 us; the launch traced here: 216 us
  waiting for transfers between devices  120 us (55%)
  matrix products  27.1 us (12%)
  starting transfers between devices  25.3 us (12%)
  other arithmetic  22 us (10%)
  between operations  14.6 us (7%)
  local copies, waits for them, and re-layouts  7.06 us (3%)
    ppermute x1, waiting for transfers between devices, local(): other_rows = lax.ppermute(sent_rows, 'cfg', SWAP)  44.4 us
    all_to_all x1, waiting for transfers between devices, local(): lax.all_to_all(partial, BLK, 0, 0, tiled=False).astype(jnp.float32)  26.8 us
    ppermute x1, waiting for transfers between devices, local(): lax.ppermute(kv, 'x', [(i, (i + 1) % n_x) for i in range(n_x)])  20.5 us
    ppermute x1, waiting for transfers between devices, local(): shard_other = lax.ppermute(in_projection, 'cfg', SWAP)  16.7 us
    dot_general x1, matrix products, local(): jnp.einsum('tabi,abiqe->tqe', mod_perm, piece, preferred_element_type=jnp...  10.1 us
    ppermute x1, waiting for transfers between devices, local(): from_far = lax.ppermute(relayed, SEQ, relay_pairs)  8.23 us
    all_to_all x1, starting transfers between devices, local(): full_states = lax.all_to_all(spread, BLK, 0, 0, tiled=False)  7.75 us
    all_to_all x1, starting transfers between devices, local(): lax.all_to_all(partial, BLK, 0, 0, tiled=False).astype(jnp.float32)  7.63 us
  transfers between devices with their start and end apart: 11, of which 7 were waited for; matrix products, arithmetic and copies ran while one was open for 20% of the time, Pallas kernels for 0%

profile of v18, /device:TPU:0, one launch (start us, length us, event | category | flops | bytes accessed | tf_op | source)
XLA Modules:
  0.0 216.4 jit_solution(9650811840364343803)
XLA Ops:
  6.5 2.0 collective-permute-start.1
  8.6 16.7 %collective-permute-done.1 = bf16[320,3,384]{2,0,1:T(8,128)(2,1)S(1)} collective-permute-done((bf16[320,3,384]{2,0,1:T(8,128)(2,1)}, bf16[320,3,384]{2,0,1:T(8,128)(2,1)S(1)}, u32[]{:S(2)}, u32[]{:S(2)}) %collective-permute-start.1) | collective-permute-done | bytes 737312 | tf_op jit(solution)/shard_map/ppermute | solution.py:96
  25.3 1.3 select_bitcast_fusion.1
  26.5 1.3 pad_maximum_fusion.1
  27.8 1.0 copy-done
  29.1 2.3 %broadcast_in_dim.143 = bf16[8,384,640]{1,2,0:T(8,128)(2,1)} broadcast(bf16[384,640]{0,1:T(8,128)(2,1)S(1)} %copy.53), dimensions={1,2} | broadcast | bytes 4423680 | tf_op jit(solution)/shard_map/broadcast_in_dim | solution.py:84
  31.4 7.8 %all-to-all-start = ((bf16[8,384,640]{1,2,0:T(8,128)(2,1)}), bf16[8,384,640]{1,2,0:T(8,128)(2,1)}, u32[]{:S(2)}, u32[]{:S(2)}) async-start(bf16[8,384,640]{1,2,0:T(8,128)(2,1)} %broadcast_in_dim.143), calls=%async_computation | async-start | bytes 7864320 | tf_op jit(solution)/shard_map/all_to_all | solution.py:85
  39.2 1.1 collective-permute-start
  40.8 1.1 cosine_bitcast_fusion
  42.9 44.4 %collective-permute-done = bf16[192,640]{1,0:T(8,128)(2,1)S(1)} collective-permute-done((bf16[192,640]{1,0:T(8,128)(2,1)S(1)}, bf16[192,640]{1,0:T(8,128)(2,1)S(1)}, u32[]{:S(2)}, u32[]{:S(2)}) %collective-permute-start) | collective-permute-done | bytes 245792 | tf_op jit(solution)/shard_map/ppermute | solution.py:76
  87.4 2.8 %convert_reduce_fusion = f32[384]{0:T(512)S(1)} fusion(bf16[8,384,640]{1,2,0:T(8,128)(2,1)} %all-to-all-done), kind=kLoop, calls=%fused_computation.3 | loop fusion | flops 3931776 | bytes 3933696 | tf_op jit(solution)/shard_map/reduce_sum | solution.py:88
  90.3 3.2 %fusion.4 = f32[384]{0:T(512)S(1)} fusion(bf16[8,384,640]{1,2,0:T(8,128)(2,1)} %all-to-all-done, f32[384]{0:T(512)S(1)} %broadcast_multiply_fusion), kind=kLoop, calls=%fused_computation.6 | loop fusion | flops 7863936 | bytes 3935232 | tf_op jit(solution)/shard_map/reduce_sum | solution.py:90
  93.5 5.8 %fusion.7 = bf16[8,384,640]{1,2,0:T(8,128)(2,1)} fusion(bf16[8,384,640]{1,2,0:T(8,128)(2,1)} %all-to-all-done, f32[8,640]{1,0:T(8,128)S(1)} %add.251, f32[8,640]{1,0:T(8,128)S(1)} %add.250, f32[384]{0:T(512)S(1)} %add_rsqrt_fusion.2, f32[384]{0:T(512)S(1)} %broadcast_multiply_fusion), kind=kLoop, calls=%fused_computation.9 | loop fusion | flops 11796480 | bytes 7908352 | tf_op jit(solution)/shard_map/convert_element_type | solution.py:94
  99.3 10.1 %fusion = f32[384,3,384,1,1]{0,2,3,1,4:T(8,128)S(1)} fusion(bf16[384,8,2,320,1]{0,3,1,4,2:T(8,128)(2,1)} %bitcast.214, bf16[8,2,320,3,384]{4,2,3,1,0:T(8,128)(2,1)} %bitcast.221), kind=kOutput, calls=%fused_computation | convolution fusion | flops 4529848320 | bytes 17498112 | tf_op jit(solution)/shard_map/tabi,abiqe->tqe/dot_general | solution.py:109
  110.4 0.7 fusion.52
  111.1 0.9 pad_maximum_fusion.2
  112.0 1.5 collective-permute-start.2
  113.5 1.7 collective-permute-start.3
  115.4 1.5 broadcast_compare_fusion.1
  117.4 20.5 %collective-permute-done.2 = bf16[384,2,3,128]{3,0,2,1:T(8,128)(2,1)S(1)} collective-permute-done((bf16[384,2,3,128]{3,0,2,1:T(8,128)(2,1)}, bf16[384,2,3,128]{3,0,2,1:T(8,128)(2,1)S(1)}, u32[]{:S(2)}, u32[]{:S(2)}) %collective-permute-start.2) | collective-permute-done | bytes 589856 | tf_op jit(solution)/shard_map/ppermute | solution.py:132
  137.9 1.9 collective-permute-done.3
  140.0 1.8 collective-permute-start.4
  141.9 0.7 fusion.39
  142.6 0.6 fusion.147
  143.1 8.2 %collective-permute-done.4 = bf16[384,2,3,128]{3,0,2,1:T(8,128)(2,1)S(1)} collective-permute-done((bf16[384,2,3,128]{3,0,2,1:T(8,128)(2,1)S(1)}, bf16[384,2,3,128]{3,0,2,1:T(8,128)(2,1)S(1)}, u32[]{:S(2)}, u32[]{:S(2)}) %collective-permute-start.4) | collective-permute-done | bytes 589856 | tf_op jit(solution)/shard_map/ppermute | solution.py:137
  151.4 0.7 pad_maximum_fusion
  152.2 0.6 fusion.141
  153.1 0.5 copy-done.15
  153.7 0.5 fusion.148
  154.2 0.5 fusion.142
  154.8 0.3 copy-done.13
  155.1 0.5 fusion.146
  155.7 0.5 fusion.140
  157.7 0.5 fusion.139
  158.4 0.5 fusion.138
  159.2 0.5 fusion.137
  161.1 1.6 collective-permute-start.6
  162.7 0.5 fusion.145
  163.2 0.6 fusion.144
  163.8 0.3 copy-done.6
  164.1 0.5 fusion.143
  165.6 0.3 fusion.55
  165.9 1.7 collective-permute-done.6
  167.7 4.3 %convolution_bitcast_fusion = f32[2,8,192,640]{3,2,1,0:T(8,128)S(1)} fusion(bf16[384,8,640,1]{0,2,1,3:T(8,128)(2,1)} %bitcast.213, bf16[1,192,384]{2,1,0:T(8,128)(2,1)S(1)} %get-tuple-element.20, bf16[1,192,384]{2,1,0:T(8,128)(2,1)S(1)} %get-tuple-element.19), kind=kOutput, calls=%fused_computation.17 | convolution fusion | flops 1510539264 | bytes 12091392 | tf_op jit(solution)/shard_map/cte,ebn->cbtn/dot_general | solution.py:193
  172.0 1.9 fusion.11
  174.0 7.6 %all-to-all-start.1 = ((bf16[8,192,640]{2,1,0:T(8,128)(2,1)}), bf16[8,192,640]{2,1,0:T(8,128)(2,1)S(1)}, u32[]{:S(2)}, u32[]{:S(2)}) async-start(bf16[8,192,640]{2,1,0:T(8,128)(2,1)} %fusion.11), calls=%async_computation.1 | async-start | bytes 3932160 | tf_op jit(solution)/shard_map/all_to_all | solution.py:198
  181.6 26.8 %all-to-all-done.1 = bf16[8,192,640]{2,1,0:T(8,128)(2,1)S(1)} async-done(((bf16[8,192,640]{2,1,0:T(8,128)(2,1)}), bf16[8,192,640]{2,1,0:T(8,128)(2,1)S(1)}, u32[]{:S(2)}, u32[]{:S(2)}) %all-to-all-start.1) | async-done | bytes 1966112 | tf_op jit(solution)/shard_map/all_to_all | solution.py:198
  208.7 0.9 add_bitcast_fusion
  (95 shorter events, 7.8 us)
Async XLA Ops:
  6.5 92.8 %all-gather.6.cloned.1.call-start = ((), (), s32[]{:S(2)}) async-start(), calls=%async_computation.3 | async-start | bytes 13271040 | tf_op jit(solution)/shard_map/all_gather | solution.py:103
  6.5 18.7 %collective-permute-start.1 = (bf16[320,3,384]{2,0,1:T(8,128)(2,1)}, bf16[320,3,384]{2,0,1:T(8,128)(2,1)S(1)}, u32[]{:S(2)}, u32[]{:S(2)}) collective-permute-start(bf16[320,3,384]{2,0,1:T(8,128)(2,1)} %param.11), channel_id=1, source_target_pairs={{0,64},{64,0},{1,65},{65,1},{2,66},{66,2},{3,67},{67,3},{4,68},{68... | collective-permute-start | bytes 2211848 | tf_op jit(solution)/shard_map/ppermute | solution.py:96
  27.8 1.0 copy-start
  31.4 9.0 %copy-start.21 = (s32[5]{0:T(128)S(1)}, s32[5]{0:T(128)}, u32[]{:S(2)}) copy-start(s32[5]{0:T(128)} %param.13) | copy-start | bytes 64
  31.4 9.3 %copy-start.18 = (f32[3,5120]{1,0:T(4,128)S(1)}, f32[3,5120]{1,0:T(4,128)}, u32[]{:S(2)}) copy-start(f32[3,5120]{1,0:T(4,128)} %param.10) | copy-start | bytes 184324
  31.4 9.4 %copy-start.19 = (s32[3,384]{1,0:T(4,128)S(1)}, s32[3,384]{1,0:T(4,128)}, u32[]{:S(2)}) copy-start(s32[3,384]{1,0:T(4,128)} %param.14) | copy-start | bytes 13828
  31.4 9.5 %copy-start.20 = (f32[3,128]{1,0:T(4,128)S(1)}, f32[3,128]{1,0:T(4,128)}, u32[]{:S(2)}) copy-start(f32[3,128]{1,0:T(4,128)} %constant.96.clone) | copy-start | bytes 4612
  31.4 56.1 %all-to-all-start = ((bf16[8,384,640]{1,2,0:T(8,128)(2,1)}), bf16[8,384,640]{1,2,0:T(8,128)(2,1)}, u32[]{:S(2)}, u32[]{:S(2)}) async-start(bf16[8,384,640]{1,2,0:T(8,128)(2,1)} %broadcast_in_dim.143), calls=%async_computation | async-start | bytes 7864320 | tf_op jit(solution)/shard_map/all_to_all | solution.py:85
  39.1 128.5 %all-gather.4.cloned.1.call-start = ((), (), s32[]{:S(2)}) async-start(), calls=%async_computation.2 | async-start | bytes 4177920 | tf_op jit(solution)/shard_map/all_gather | solution.py:190
  39.2 48.1 %collective-permute-start = (bf16[192,640]{1,0:T(8,128)(2,1)S(1)}, bf16[192,640]{1,0:T(8,128)(2,1)S(1)}, u32[]{:S(2)}, u32[]{:S(2)}) collective-permute-start(bf16[192,640]{1,0:T(8,128)(2,1)S(1)} %dynamic-slice_bitcast_fusion), channel_id=1, source_target_pairs={{0,64},{64,0},{1,65},{65,1},{2,66},{66,2},{3,67},{67,3},{4,68},{68... | collective-permute-start | bytes 737288 | tf_op jit(solution)/shard_map/ppermute | solution.py:76
  42.8 67.5 %copy-start.1 = (f32[384,128]{1,0:T(8,128)}, f32[384,128]{1,0:T(8,128)S(1)}, u32[]{:S(2)}) copy-start(f32[384,128]{1,0:T(8,128)S(1)} %copy.58) | copy-start | bytes 589828
  42.9 67.4 %copy-start.3 = (f32[384,128]{1,0:T(8,128)}, f32[384,128]{1,0:T(8,128)S(1)}, u32[]{:S(2)}) copy-start(f32[384,128]{1,0:T(8,128)S(1)} %copy.59) | copy-start | bytes 589828
  109.6 0.8 copy-start.5
  112.0 25.9 %collective-permute-start.2 = (bf16[384,2,3,128]{3,0,2,1:T(8,128)(2,1)}, bf16[384,2,3,128]{3,0,2,1:T(8,128)(2,1)S(1)}, u32[]{:S(2)}, u32[]{:S(2)}) collective-permute-start(bf16[384,2,3,128]{3,0,2,1:T(8,128)(2,1)} %pad_maximum_fusion.2), channel_id=1, source_target_pairs={{0,16},{16,32},{32,48},{48,0},{1,17},{17,33},{33,49},{49,1},{2,18}... | collective-permute-start | bytes 1769480 | tf_op jit(solution)/shard_map/ppermute | solution.py:132
  113.5 26.3 %collective-permute-start.3 = (bf16[384,2,3,128]{3,0,2,1:T(8,128)(2,1)}, bf16[384,2,3,128]{3,0,2,1:T(8,128)(2,1)S(1)}, u32[]{:S(2)}, u32[]{:S(2)}) collective-permute-start(bf16[384,2,3,128]{3,0,2,1:T(8,128)(2,1)} %pad_maximum_fusion.2), channel_id=1, source_target_pairs={{0,48},{16,0},{32,16},{48,32},{1,49},{17,1},{33,17},{49,33},{2,50}... | collective-permute-start | bytes 1769480 | tf_op jit(solution)/shard_map/ppermute | solution.py:133
  117.4 24.5 %copy-start.2 = (f32[384,128]{1,0:T(8,128)S(1)}, f32[384,128]{1,0:T(8,128)}, u32[]{:S(2)}) copy-start(f32[384,128]{1,0:T(8,128)} %copy-done.1) | copy-start | bytes 589828
  117.4 24.5 %copy-start.4 = (f32[384,128]{1,0:T(8,128)S(1)}, f32[384,128]{1,0:T(8,128)}, u32[]{:S(2)}) copy-start(f32[384,128]{1,0:T(8,128)} %copy-done.3) | copy-start | bytes 589828
  140.0 2.6 %copy-start.17 = (pred[192,512]{1,0:T(8,128)(4,1)S(1)}, pred[192,512]{1,0:T(8,128)(4,1)}, u32[]{:S(2)}) copy-start(pred[192,512]{1,0:T(8,128)(4,1)} %get-tuple-element.67) | copy-start | bytes 294916
  140.0 11.3 %collective-permute-start.4 = (bf16[384,2,3,128]{3,0,2,1:T(8,128)(2,1)S(1)}, bf16[384,2,3,128]{3,0,2,1:T(8,128)(2,1)S(1)}, u32[]{:S(2)}, u32[]{:S(2)}) collective-permute-start(bf16[384,2,3,128]{3,0,2,1:T(8,128)(2,1)S(1)} %get-tuple-element.18), channel_id=1, source_target_pairs={{0,16},{16,32},{32,48},{48,0},{8,56},{24,8},{40,24},{56,40},{1,17}... | collective-permute-start | bytes 1769480 | tf_op jit(solution)/shard_map/ppermute | solution.py:137
  143.1 9.1 %copy-start.16 = (pred[192,512]{1,0:T(8,128)(4,1)S(1)}, pred[192,512]{1,0:T(8,128)(4,1)}, u32[]{:S(2)}) copy-start(pred[192,512]{1,0:T(8,128)(4,1)} %get-tuple-element.66) | copy-start | bytes 294916
  152.1 5.4 %collective-permute-start.5 = (bf16[1536,2,3,128]{3,0,2,1:T(8,128)(2,1)S(1)}, bf16[1536,2,3,128]{3,0,2,1:T(8,128)(2,1)S(1)}, u32[]{:S(2)}, u32[]{:S(2)}) collective-permute-start(bf16[1536,2,3,128]{3,0,2,1:T(8,128)(2,1)S(1)} %pad_maximum_fusion), channel_id=1, source_target_pairs={{0,8},{8,0},{1,9},{9,1},{2,10},{10,2},{3,11},{11,3},{4,12},{12,4},... | collective-permute-start | bytes 7077896 | tf_op jit(solution)/shard_map/ppermute | solution.py:139
  152.8 0.9 copy-start.15
  153.1 1.1 copy-start.14
  154.2 0.9 copy-start.13
  154.8 0.9 copy-start.12
  156.9 0.9 copy-start.11
  157.5 0.9 copy-start.10
  158.3 0.9 copy-start.9
  160.7 2.0 copy-start.8
  161.1 2.2 %copy-start.7 = (pred[192,512]{1,0:T(8,128)(4,1)S(1)}, pred[192,512]{1,0:T(8,128)(4,1)}, u32[]{:S(2)}) copy-start(pred[192,512]{1,0:T(8,128)(4,1)} %get-tuple-element.71) | copy-start | bytes 294916
  161.1 6.5 %collective-permute-start.6 = (bf16[192,384]{1,0:T(8,128)(2,1)S(1)}, bf16[192,384]{1,0:T(8,128)(2,1)S(1)}, u32[]{:S(2)}, u32[]{:S(2)}) collective-permute-start(bf16[192,384]{1,0:T(8,128)(2,1)S(1)} %bitcast.218), channel_id=1, source_target_pairs={{0,64},{64,0},{1,65},{65,1},{2,66},{66,2},{3,67},{67,3},{4,68},{68... | collective-permute-start | bytes 442376 | tf_op jit(solution)/shard_map/ppermute | solution.py:186
  163.2 0.9 copy-start.6
  174.0 34.5 %all-to-all-start.1 = ((bf16[8,192,640]{2,1,0:T(8,128)(2,1)}), bf16[8,192,640]{2,1,0:T(8,128)(2,1)S(1)}, u32[]{:S(2)}, u32[]{:S(2)}) async-start(bf16[8,192,640]{2,1,0:T(8,128)(2,1)} %fusion.11), calls=%async_computation.1 | async-start | bytes 3932160 | tf_op jit(solution)/shard_map/all_to_all | solution.py:198
Sparse Core Ops, SparseCore 0:
  27.9 66.1 all-gather.5
  95.8 45.1 all-gather.3

commit v19 on v18

--- a/solution.py
+++ b/solution.py
@@ -131,10 +131,9 @@
     x_index = lax.axis_index("x")
     from_behind = lax.ppermute(kv, "x", [(i, (i + 1) % n_x) for i in range(n_x)])
     from_ahead = lax.ppermute(kv, "x", [(i, (i - 1) % n_x) for i in range(n_x)])
-    relayed = jnp.where(core == 0, from_behind, from_ahead)
-    relay_pairs = [(i * 2, ((i + 1) % n_x) * 2) for i in range(n_x)]
-    relay_pairs += [(i * 2 + 1, ((i - 1) % n_x) * 2 + 1) for i in range(n_x)]
-    from_far = lax.ppermute(relayed, SEQ, relay_pairs)
+    direct = lax.ppermute(kv, SEQ, [(i * 2, ((i + 2) % n_x) * 2) for i in range(n_x)])
+    relay = lax.ppermute(from_ahead, SEQ, [(i * 2 + 1, ((i - 1) % n_x) * 2 + 1) for i in range(n_x)])
+    from_far = jnp.where(core == 0, direct, relay)
     kv_mine = jnp.concatenate([kv, from_behind, from_far, from_ahead], axis=0)
     kv_other = lax.ppermute(kv_mine, "core", SWAP)
     kv_all = jnp.concatenate([kv_mine, kv_other], axis=0)

time: 218 us -> 217 us (level)
  waiting for transfers between devices: 120 us -> 114 us
  starting transfers between devices: 25.3 us -> 31.2 us
  local copies, waits for them, and re-layouts: 7.06 us -> 4.04 us
    ppermute x1, waiting for transfers between devices: 20.5 us -> 0.01 us  [local(): lax.ppermute(kv, 'x', [(i, (i + 1) % n_x) for i in range(n_x)])]
    ppermute x1, waiting for transfers between devices: 1.88 us -> 19.2 us  [local(): from_ahead = lax.ppermute(kv, 'x', [(i, (i - 1) % n_x) for i in range(n_x)])]
    ppermute x1, starting transfers between devices: 0.09 us -> 3.37 us  [local(): kv_other = lax.ppermute(kv_mine, 'core', SWAP)]
    ppermute x1 -> x2, starting transfers between devices: 1.83 us -> 5 us  [the longest x1 4.14 us: local(): lax.ppermute(kv, SEQ, [(i * 2, (i + 2) % n_x * 2) for i in range(n_x)])]
    unnamed x47 -> x43, local copies, waits for them, and re-layouts: 3.68 us -> 0.98 us
    ppermute x1 -> x2, waiting for transfers between devices: 8.23 us -> 5.63 us  [the longest x1 5.63 us: local(): lax.ppermute(kv, SEQ, [(i * 2, (i + 2) % n_x * 2) for i in range(n_x)])]
  transfers between devices with their start and end apart: 11 -> 12, of which waited for: 7 -> 6; matrix products, arithmetic and copies ran while one was open for 20% -> 21% of each run, Pallas kernels for 0% -> 0%
where the time goes in v19:
time: 217 us; the launch traced here: 215 us
  waiting for transfers between devices  114 us (53%)
  starting transfers between devices  31.2 us (14%)
  matrix products  28.2 us (13%)
  other arithmetic  23.1 us (11%)
  between operations  14.6 us (7%)
  local copies, waits for them, and re-layouts  4.04 us (2%)
    ppermute x1, waiting for transfers between devices, local(): other_rows = lax.ppermute(sent_rows, 'cfg', SWAP)  44.3 us
    all_to_all x1, waiting for transfers between devices, local(): lax.all_to_all(partial, BLK, 0, 0, tiled=False).astype(jnp.float32)  26.6 us
    ppermute x1, waiting for transfers between devices, local(): from_ahead = lax.ppermute(kv, 'x', [(i, (i - 1) % n_x) for i in range(n_x)])  19.2 us
    ppermute x1, waiting for transfers between devices, local(): shard_other = lax.ppermute(in_projection, 'cfg', SWAP)  16.7 us
    dot_general x1, matrix products, local(): jnp.einsum('tabi,abiqe->tqe', mod_perm, piece, preferred_element_type=jnp...  10.1 us
    all_to_all x1, starting transfers between devices, local(): full_states = lax.all_to_all(spread, BLK, 0, 0, tiled=False)  7.75 us
    all_to_all x1, starting transfers between devices, local(): lax.all_to_all(partial, BLK, 0, 0, tiled=False).astype(jnp.float32)  7.35 us
    dot_general x12, matrix products, attend(): jnp.einsum('qhd,khd->hqk', query_rows, key_slab, preferred_element_type=j...  6.61 us
  transfers between devices with their start and end apart: 12, of which 6 were waited for; matrix products, arithmetic and copies ran while one was open for 21% of the time, Pallas kernels for 0%

profile of v19, /device:TPU:0, one launch (start us, length us, event | category | flops | bytes accessed | tf_op | source)
XLA Modules:
  0.0 215.2 jit_solution(4790163337790629947)
XLA Ops:
  6.5 2.0 collective-permute-start.1
  8.6 16.7 %collective-permute-done.1 = bf16[320,3,384]{2,0,1:T(8,128)(2,1)S(1)} collective-permute-done((bf16[320,3,384]{2,0,1:T(8,128)(2,1)}, bf16[320,3,384]{2,0,1:T(8,128)(2,1)S(1)}, u32[]{:S(2)}, u32[]{:S(2)}) %collective-permute-start.1) | collective-permute-done | bytes 737312 | tf_op jit(solution)/shard_map/ppermute | solution.py:96
  25.3 1.3 select_bitcast_fusion.1
  26.5 1.3 pad_maximum_fusion.1
  28.1 2.3 %broadcast_in_dim.143 = bf16[8,384,640]{1,2,0:T(8,128)(2,1)} broadcast(bf16[384,640]{0,1:T(8,128)(2,1)S(1)} %copy.53), dimensions={1,2} | broadcast | bytes 4423680 | tf_op jit(solution)/shard_map/broadcast_in_dim | solution.py:84
  30.4 7.8 %all-to-all-start = ((bf16[8,384,640]{1,2,0:T(8,128)(2,1)}), bf16[8,384,640]{1,2,0:T(8,128)(2,1)}, u32[]{:S(2)}, u32[]{:S(2)}) async-start(bf16[8,384,640]{1,2,0:T(8,128)(2,1)} %broadcast_in_dim.143), calls=%async_computation | async-start | bytes 7864320 | tf_op jit(solution)/shard_map/all_to_all | solution.py:85
  38.2 1.1 collective-permute-start
  39.6 1.1 cosine_bitcast_fusion
  42.0 44.3 %collective-permute-done = bf16[192,640]{1,0:T(8,128)(2,1)S(1)} collective-permute-done((bf16[192,640]{1,0:T(8,128)(2,1)S(1)}, bf16[192,640]{1,0:T(8,128)(2,1)S(1)}, u32[]{:S(2)}, u32[]{:S(2)}) %collective-permute-start) | collective-permute-done | bytes 245792 | tf_op jit(solution)/shard_map/ppermute | solution.py:76
  86.5 2.8 %convert_reduce_fusion = f32[384]{0:T(512)S(1)} fusion(bf16[8,384,640]{1,2,0:T(8,128)(2,1)} %all-to-all-done), kind=kLoop, calls=%fused_computation.3 | loop fusion | flops 3931776 | bytes 3933696 | tf_op jit(solution)/shard_map/reduce_sum | solution.py:88
  89.3 3.2 %fusion.4 = f32[384]{0:T(512)S(1)} fusion(bf16[8,384,640]{1,2,0:T(8,128)(2,1)} %all-to-all-done, f32[384]{0:T(512)S(1)} %broadcast_multiply_fusion), kind=kLoop, calls=%fused_computation.6 | loop fusion | flops 7863936 | bytes 3935232 | tf_op jit(solution)/shard_map/reduce_sum | solution.py:90
  92.5 5.9 %fusion.7 = bf16[8,384,640]{1,2,0:T(8,128)(2,1)} fusion(bf16[8,384,640]{1,2,0:T(8,128)(2,1)} %all-to-all-done, f32[8,640]{1,0:T(8,128)S(1)} %add.251, f32[8,640]{1,0:T(8,128)S(1)} %add.250, f32[384]{0:T(512)S(1)} %add_rsqrt_fusion.2, f32[384]{0:T(512)S(1)} %broadcast_multiply_fusion), kind=kLoop, calls=%fused_computation.9 | loop fusion | flops 11796480 | bytes 7908352 | tf_op jit(solution)/shard_map/convert_element_type | solution.py:94
  98.5 10.1 %fusion = f32[384,3,384,1,1]{0,2,3,1,4:T(8,128)S(1)} fusion(bf16[384,8,2,320,1]{0,3,1,4,2:T(8,128)(2,1)} %bitcast.214, bf16[8,2,320,3,384]{4,2,3,1,0:T(8,128)(2,1)} %bitcast.221), kind=kOutput, calls=%fused_computation | convolution fusion | flops 4529848320 | bytes 17498112 | tf_op jit(solution)/shard_map/tabi,abiqe->tqe/dot_general | solution.py:109
  109.5 0.7 fusion.52
  110.2 0.9 pad_maximum_fusion.2
  111.0 2.7 %collective-permute-start.4 = (bf16[384,2,3,128]{3,0,2,1:T(8,128)(2,1)}, bf16[384,2,3,128]{3,0,2,1:T(8,128)(2,1)S(1)}, u32[]{:S(2)}, u32[]{:S(2)}) collective-permute-start(bf16[384,2,3,128]{3,0,2,1:T(8,128)(2,1)} %pad_maximum_fusion.2), channel_id=1, source_target_pairs={{0,48},{16,0},{32,16},{48,32},{1,49},{17,1},{33,17},{49,33},{2,50}... | collective-permute-start | bytes 1769480 | tf_op jit(solution)/shard_map/ppermute | solution.py:133
  113.9 1.5 broadcast_compare_fusion.1
  115.4 4.1 %collective-permute-start.3 = (bf16[384,2,3,128]{3,0,2,1:T(8,128)(2,1)}, bf16[384,2,3,128]{3,0,2,1:T(8,128)(2,1)}, u32[]{:S(2)}, u32[]{:S(2)}) collective-permute-start(bf16[384,2,3,128]{3,0,2,1:T(8,128)(2,1)} %pad_maximum_fusion.2), channel_id=1, source_target_pairs={{0,32},{16,48},{32,0},{48,16},{1,33},{17,49},{33,1},{49,17},{2,34}... | collective-permute-start | bytes 1769480 | tf_op jit(solution)/shard_map/ppermute | solution.py:134
  119.8 19.2 %collective-permute-done.4 = bf16[384,2,3,128]{3,0,2,1:T(8,128)(2,1)S(1)} collective-permute-done((bf16[384,2,3,128]{3,0,2,1:T(8,128)(2,1)}, bf16[384,2,3,128]{3,0,2,1:T(8,128)(2,1)S(1)}, u32[]{:S(2)}, u32[]{:S(2)}) %collective-permute-start.4) | collective-permute-done | bytes 589856 | tf_op jit(solution)/shard_map/ppermute | solution.py:133
  138.9 0.9 collective-permute-start.5
  140.1 1.7 fusion.39
  141.8 5.6 %collective-permute-done.3 = bf16[384,2,3,128]{3,0,2,1:T(8,128)(2,1)} collective-permute-done((bf16[384,2,3,128]{3,0,2,1:T(8,128)(2,1)}, bf16[384,2,3,128]{3,0,2,1:T(8,128)(2,1)}, u32[]{:S(2)}, u32[]{:S(2)}) %collective-permute-start.3) | collective-permute-done | bytes 589856 | tf_op jit(solution)/shard_map/ppermute | solution.py:134
  147.4 1.1 broadcast_select_fusion
  148.6 0.8 pad_maximum_fusion
  149.4 3.4 %collective-permute-start.6 = (bf16[1536,2,3,128]{3,0,2,1:T(8,128)(2,1)S(1)}, bf16[1536,2,3,128]{3,0,2,1:T(8,128)(2,1)S(1)}, u32[]{:S(2)}, u32[]{:S(2)}) collective-permute-start(bf16[1536,2,3,128]{3,0,2,1:T(8,128)(2,1)S(1)} %pad_maximum_fusion), channel_id=1, source_target_pairs={{0,8},{8,0},{1,9},{9,1},{2,10},{10,2},{3,11},{11,3},{4,12},{12,4},... | collective-permute-start | bytes 7077896 | tf_op jit(solution)/shard_map/ppermute | solution.py:138
  152.7 0.5 fusion.153
  153.3 0.6 fusion.147
  153.9 0.6 fusion.154
  154.5 0.6 fusion.152
  155.0 0.6 fusion.148
  155.6 0.6 fusion.146
  156.1 0.3 fusion.78
  156.8 0.3 fusion.67
  157.7 0.5 fusion.145
  158.2 0.6 fusion.144
  158.8 0.6 fusion.143
  160.3 0.3 fusion.56
  160.6 1.8 collective-permute-start.7
  162.5 0.5 fusion.151
  163.0 0.6 fusion.150
  163.6 0.6 fusion.149
  165.1 0.3 fusion.55
  165.4 1.5 collective-permute-done.7
  167.0 4.3 %convolution_bitcast_fusion = f32[2,8,192,640]{3,2,1,0:T(8,128)S(1)} fusion(bf16[384,8,640,1]{0,2,1,3:T(8,128)(2,1)} %bitcast.213, bf16[1,192,384]{2,1,0:T(8,128)(2,1)S(1)} %get-tuple-element.16, bf16[1,192,384]{2,1,0:T(8,128)(2,1)S(1)} %get-tuple-element.15), kind=kOutput, calls=%fused_computation.17 | convolution fusion | flops 1510539264 | bytes 12091392 | tf_op jit(solution)/shard_map/cte,ebn->cbtn/dot_general | solution.py:192
  171.4 1.9 fusion.11
  173.3 7.3 %all-to-all-start.1 = ((bf16[8,192,640]{2,1,0:T(8,128)(2,1)}), bf16[8,192,640]{2,1,0:T(8,128)(2,1)S(1)}, u32[]{:S(2)}, u32[]{:S(2)}) async-start(bf16[8,192,640]{2,1,0:T(8,128)(2,1)} %fusion.11), calls=%async_computation.1 | async-start | bytes 3932160 | tf_op jit(solution)/shard_map/all_to_all | solution.py:197
  180.7 26.6 %all-to-all-done.1 = bf16[8,192,640]{2,1,0:T(8,128)(2,1)S(1)} async-done(((bf16[8,192,640]{2,1,0:T(8,128)(2,1)}), bf16[8,192,640]{2,1,0:T(8,128)(2,1)S(1)}, u32[]{:S(2)}, u32[]{:S(2)}) %all-to-all-start.1) | async-done | bytes 1966112 | tf_op jit(solution)/shard_map/all_to_all | solution.py:197
  207.5 0.9 add_bitcast_fusion
  (91 shorter events, 5.8 us)
Async XLA Ops:
  6.5 91.9 %all-gather.6.cloned.1.call-start = ((), (), s32[]{:S(2)}) async-start(), calls=%async_computation.3 | async-start | bytes 13271040 | tf_op jit(solution)/shard_map/all_gather | solution.py:103
  6.5 18.7 %collective-permute-start.1 = (bf16[320,3,384]{2,0,1:T(8,128)(2,1)}, bf16[320,3,384]{2,0,1:T(8,128)(2,1)S(1)}, u32[]{:S(2)}, u32[]{:S(2)}) collective-permute-start(bf16[320,3,384]{2,0,1:T(8,128)(2,1)} %param.11), channel_id=1, source_target_pairs={{0,64},{64,0},{1,65},{65,1},{2,66},{66,2},{3,67},{67,3},{4,68},{68... | collective-permute-start | bytes 2211848 | tf_op jit(solution)/shard_map/ppermute | solution.py:96
  26.5 1.3 copy-start
  30.4 9.0 %copy-start.16 = (f32[3,5120]{1,0:T(4,128)S(1)}, f32[3,5120]{1,0:T(4,128)}, u32[]{:S(2)}) copy-start(f32[3,5120]{1,0:T(4,128)} %param.10) | copy-start | bytes 184324
  30.4 9.2 %copy-start.17 = (s32[3,384]{1,0:T(4,128)S(1)}, s32[3,384]{1,0:T(4,128)}, u32[]{:S(2)}) copy-start(s32[3,384]{1,0:T(4,128)} %param.14) | copy-start | bytes 13828
  30.4 9.2 %copy-start.18 = (f32[3,128]{1,0:T(4,128)S(1)}, f32[3,128]{1,0:T(4,128)}, u32[]{:S(2)}) copy-start(f32[3,128]{1,0:T(4,128)} %constant.96.clone) | copy-start | bytes 4612
  30.4 11.2 %copy-start.19 = (s32[5]{0:T(128)S(1)}, s32[5]{0:T(128)}, u32[]{:S(2)}) copy-start(s32[5]{0:T(128)} %param.13) | copy-start | bytes 64
  30.4 56.1 %all-to-all-start = ((bf16[8,384,640]{1,2,0:T(8,128)(2,1)}), bf16[8,384,640]{1,2,0:T(8,128)(2,1)}, u32[]{:S(2)}, u32[]{:S(2)}) async-start(bf16[8,384,640]{1,2,0:T(8,128)(2,1)} %broadcast_in_dim.143), calls=%async_computation | async-start | bytes 7864320 | tf_op jit(solution)/shard_map/all_to_all | solution.py:85
  38.2 128.9 %all-gather.4.cloned.1.call-start = ((), (), s32[]{:S(2)}) async-start(), calls=%async_computation.2 | async-start | bytes 4177920 | tf_op jit(solution)/shard_map/all_gather | solution.py:189
  38.2 48.1 %collective-permute-start = (bf16[192,640]{1,0:T(8,128)(2,1)S(1)}, bf16[192,640]{1,0:T(8,128)(2,1)S(1)}, u32[]{:S(2)}, u32[]{:S(2)}) collective-permute-start(bf16[192,640]{1,0:T(8,128)(2,1)S(1)} %dynamic-slice_bitcast_fusion), channel_id=1, source_target_pairs={{0,64},{64,0},{1,65},{65,1},{2,66},{66,2},{3,67},{67,3},{4,68},{68... | collective-permute-start | bytes 737288 | tf_op jit(solution)/shard_map/ppermute | solution.py:76
  41.5 68.0 %copy-start.1 = (f32[384,128]{1,0:T(8,128)}, f32[384,128]{1,0:T(8,128)S(1)}, u32[]{:S(2)}) copy-start(f32[384,128]{1,0:T(8,128)S(1)} %copy.58) | copy-start | bytes 589828
  41.6 67.9 %copy-start.2 = (f32[384,128]{1,0:T(8,128)}, f32[384,128]{1,0:T(8,128)S(1)}, u32[]{:S(2)}) copy-start(f32[384,128]{1,0:T(8,128)S(1)} %copy.59) | copy-start | bytes 589828
  108.6 0.9 copy-start.3
  111.0 27.9 %collective-permute-start.4 = (bf16[384,2,3,128]{3,0,2,1:T(8,128)(2,1)}, bf16[384,2,3,128]{3,0,2,1:T(8,128)(2,1)S(1)}, u32[]{:S(2)}, u32[]{:S(2)}) collective-permute-start(bf16[384,2,3,128]{3,0,2,1:T(8,128)(2,1)} %pad_maximum_fusion.2), channel_id=1, source_target_pairs={{0,48},{16,0},{32,16},{48,32},{1,49},{17,1},{33,17},{49,33},{2,50}... | collective-permute-start | bytes 1769480 | tf_op jit(solution)/shard_map/ppermute | solution.py:133
  115.4 33.2 %collective-permute-start.2 = (bf16[384,2,3,128]{3,0,2,1:T(8,128)(2,1)}, bf16[384,2,3,128]{3,0,2,1:T(8,128)(2,1)S(1)}, u32[]{:S(2)}, u32[]{:S(2)}) collective-permute-start(bf16[384,2,3,128]{3,0,2,1:T(8,128)(2,1)} %pad_maximum_fusion.2), channel_id=1, source_target_pairs={{0,16},{16,32},{32,48},{48,0},{1,17},{17,33},{33,49},{49,1},{2,18}... | collective-permute-start | bytes 1769480 | tf_op jit(solution)/shard_map/ppermute | solution.py:132
  115.4 32.0 %collective-permute-start.3 = (bf16[384,2,3,128]{3,0,2,1:T(8,128)(2,1)}, bf16[384,2,3,128]{3,0,2,1:T(8,128)(2,1)}, u32[]{:S(2)}, u32[]{:S(2)}) collective-permute-start(bf16[384,2,3,128]{3,0,2,1:T(8,128)(2,1)} %pad_maximum_fusion.2), channel_id=1, source_target_pairs={{0,32},{16,48},{32,0},{48,16},{1,33},{17,49},{33,1},{49,17},{2,34}... | collective-permute-start | bytes 1769480 | tf_op jit(solution)/shard_map/ppermute | solution.py:134
  138.9 8.5 %collective-permute-start.5 = (bf16[384,2,3,128]{3,0,2,1:T(8,128)(2,1)S(1)}, bf16[384,2,3,128]{3,0,2,1:T(8,128)(2,1)S(1)}, u32[]{:S(2)}, u32[]{:S(2)}) collective-permute-start(bf16[384,2,3,128]{3,0,2,1:T(8,128)(2,1)S(1)} %collective-permute-done.4), channel_id=1, source_target_pairs={{8,56},{24,8},{40,24},{56,40},{9,57},{25,9},{41,25},{57,41},{10,58... | collective-permute-start | bytes 1769480 | tf_op jit(solution)/shard_map/ppermute | solution.py:135
  148.6 4.2 %copy-start.15 = (pred[192,512]{1,0:T(8,128)(4,1)S(1)}, pred[192,512]{1,0:T(8,128)(4,1)}, u32[]{:S(2)}) copy-start(pred[192,512]{1,0:T(8,128)(4,1)} %get-tuple-element.63) | copy-start | bytes 294916
  149.4 3.9 %copy-start.14 = (pred[192,512]{1,0:T(8,128)(4,1)S(1)}, pred[192,512]{1,0:T(8,128)(4,1)}, u32[]{:S(2)}) copy-start(pred[192,512]{1,0:T(8,128)(4,1)} %get-tuple-element.62) | copy-start | bytes 294916
  149.4 8.1 %collective-permute-start.6 = (bf16[1536,2,3,128]{3,0,2,1:T(8,128)(2,1)S(1)}, bf16[1536,2,3,128]{3,0,2,1:T(8,128)(2,1)S(1)}, u32[]{:S(2)}, u32[]{:S(2)}) collective-permute-start(bf16[1536,2,3,128]{3,0,2,1:T(8,128)(2,1)S(1)} %pad_maximum_fusion), channel_id=1, source_target_pairs={{0,8},{8,0},{1,9},{9,1},{2,10},{10,2},{3,11},{11,3},{4,12},{12,4},... | collective-permute-start | bytes 7077896 | tf_op jit(solution)/shard_map/ppermute | solution.py:138
  152.7 1.1 copy-start.13
  153.3 1.1 copy-start.12
  153.9 1.1 copy-start.11
  154.4 1.1 copy-start.10
  156.8 0.9 copy-start.9
  157.1 1.1 copy-start.8
  157.4 1.4 copy-start.7
  160.0 2.5 %copy-start.6 = (pred[192,512]{1,0:T(8,128)(4,1)S(1)}, pred[192,512]{1,0:T(8,128)(4,1)}, u32[]{:S(2)}) copy-start(pred[192,512]{1,0:T(8,128)(4,1)} %get-tuple-element.58) | copy-start | bytes 294916
  160.3 2.8 %copy-start.5 = (pred[192,512]{1,0:T(8,128)(4,1)S(1)}, pred[192,512]{1,0:T(8,128)(4,1)}, u32[]{:S(2)}) copy-start(pred[192,512]{1,0:T(8,128)(4,1)} %get-tuple-element.67) | copy-start | bytes 294916
  160.6 3.0 %copy-start.4 = (pred[192,512]{1,0:T(8,128)(4,1)S(1)}, pred[192,512]{1,0:T(8,128)(4,1)}, u32[]{:S(2)}) copy-start(pred[192,512]{1,0:T(8,128)(4,1)} %get-tuple-element.56) | copy-start | bytes 294916
  160.6 6.3 %collective-permute-start.7 = (bf16[192,384]{1,0:T(8,128)(2,1)S(1)}, bf16[192,384]{1,0:T(8,128)(2,1)S(1)}, u32[]{:S(2)}, u32[]{:S(2)}) collective-permute-start(bf16[192,384]{1,0:T(8,128)(2,1)S(1)} %bitcast.218), channel_id=1, source_target_pairs={{0,64},{64,0},{1,65},{65,1},{2,66},{66,2},{3,67},{67,3},{4,68},{68... | collective-permute-start | bytes 442376 | tf_op jit(solution)/shard_map/ppermute | solution.py:185
  173.3 33.9 %all-to-all-start.1 = ((bf16[8,192,640]{2,1,0:T(8,128)(2,1)}), bf16[8,192,640]{2,1,0:T(8,128)(2,1)S(1)}, u32[]{:S(2)}, u32[]{:S(2)}) async-start(bf16[8,192,640]{2,1,0:T(8,128)(2,1)} %fusion.11), calls=%async_computation.1 | async-start | bytes 3932160 | tf_op jit(solution)/shard_map/all_to_all | solution.py:197
Sparse Core Ops, SparseCore 0:
  28.0 66.1 all-gather.5
  95.8 46.0 all-gather.3
